TPU v7x, 128 devices: a whole 4x4x4 slice. The times are simulated.
128 devices in a mesh: sx: 16 (over z, x), sy: 8 (over y, core).
Axes of the slice: x: 4, y: 4, z: 4, core: 2. Of those that a mesh axis runs over, the one named last changes fastest.
Arguments:
- features: bfloat16 [128, 128, 32, 256], P('sx', 'sy'), may hold values from -6 to 6
- conv_weight: bfloat16 [27, 32, 32], replicated, may hold values from -0.21875 to 0.21875
- conv_bias: float32 [32], replicated, may hold values from -3 to 3
- occupancy: int32 [128, 128, 256], P('sx', 'sy'), may hold values 0 or 1
- block_ids: int32 [128, 128, 2, 27], P('sx', 'sy'), may hold values from -1 to 32767, as said below
- ridge: float32 [128, 128, 256], P('sx', 'sy'), may hold values from 0.5 to 2
- target: float32 [128, 128, 256], P('sx', 'sy'), may hold values from -6 to 6
Outputs:
- solution: float32 [128, 128, 256], P('sx', 'sy')
- residual: float32 [128, 128, 256], P('sx', 'sy')
Inputs may be any that keep to these rules, and one draw needn't show every extreme that they name: `block_ids`: entry t of block (x, y, z) is the id (x' 128 + y') * 2 + z' of the block (x', y', z') = (x + a, y + b, z + c) at offset t when that block lies in the grid and is present, else -1; a block is present exactly when its own entry 13 is its id, and every entry naming a block agrees on its presence.
All inputs are finite; a program needn't handle non-finite values. No bound on the sum of `occupancy` on one device may be relied on, other than what follows from the above.
Results may differ from a plain program's by a relative error of at most 0.0047.
Values may be sent and summed in bfloat16 or wider, within the bound.
No kernel may reach another device: no remote copies, remote signals or barrier semaphores. Data moves between devices by JAX's collectives and lax.ppermute only.
A program may use at most 192 MiB of HBM per device.

v0:
```python
import jax
import jax.numpy as jnp
from jax import lax
from jax.sharding import PartitionSpec as P

ITERS = 2


def with_halo(value, sides, width):
    for axis, dim in sides:
        peers, length = (lax.axis_size(axis), value.shape[dim])
        up = [(i, (i + 1) % peers) for i in range(peers - 1)]
        down = [(j, i) for i, j in up]
        last = lax.slice_in_dim(value, length - width, length, axis=dim)
        initial = lax.slice_in_dim(value, 0, width, axis=dim)
        before = lax.ppermute(last, axis, up)
        after = lax.ppermute(initial, axis, down)
        value = jnp.concatenate([before, value, after], axis=dim)
    return value


def offset_list():
    return [
        (off_x, off_y, off_z)
        for off_x in (-1, 0, 1)
        for off_y in (-1, 0, 1)
        for off_z in (-1, 0, 1)
    ]


def spline_weight(off_x, off_y, off_z):
    return 0.5 ** (abs(off_x) + abs(off_y) + abs(off_z))


def convolve(source, out_x, out_y, kernel_mats, bias_col):
    depth = source.shape[3]
    channels = source.shape[2]
    padded = jnp.pad(source, ((0, 0), (0, 0), (0, 0), (1, 1)))
    total = jnp.zeros((out_x, out_y, channels, depth), jnp.float32)
    for slot_x in range(3):
        for slot_y in range(3):
            window_part = jnp.concatenate(
                [
                    padded[
                        slot_x : slot_x + out_x, slot_y : slot_y + out_y, :, slot_z : slot_z + depth
                    ]
                    for slot_z in range(3)
                ],
                axis=2,
            )
            total = total + jnp.einsum(
                "oc,xycz->xyoz",
                kernel_mats[slot_x, slot_y],
                window_part,
                preferred_element_type=jnp.float32,
            )
    return total + bias_col


def squares(residual):
    return lax.psum(jnp.sum(residual * residual), ("sx", "sy"))


def per_device(features, conv_weight, conv_bias, occupancy, block_ids, ridge, target):
    width_x, width_y, channels, depth = features.shape
    voxels = depth // block_ids.shape[2]
    present = (block_ids[:, :, :, 13] >= 0).astype(jnp.float32)
    weight_mask = occupancy.astype(jnp.float32) * jnp.repeat(present, voxels, axis=2)
    mask_half = weight_mask.astype(jnp.bfloat16)
    masked = features * mask_half[:, :, None, :]
    kernel_mats = (
        conv_weight.reshape(3, 3, 3, channels, channels)
        .transpose(0, 1, 3, 2, 4)
        .reshape(3, 3, channels, 3 * channels)
    )
    bias_col = conv_bias[:, None]
    rim_inputs = with_halo(masked, (("sx", 0), ("sy", 1)), 1)
    own_field = (
        weight_mask[:, :, None, :] * convolve(rim_inputs, width_x, width_y, kernel_mats, bias_col)
    ).astype(jnp.bfloat16)
    feature_field = with_halo(own_field, (("sx", 0), ("sy", 1)), 1)
    field_pad = jnp.pad(feature_field, ((0, 0), (0, 0), (0, 0), (1, 1)))
    center = feature_field[1:-1, 1:-1]
    coupling_list = []
    for off_x, off_y, off_z in offset_list():
        beside = field_pad[
            off_x + 1 : off_x + 1 + width_x,
            off_y + 1 : off_y + 1 + width_y,
            :,
            off_z + 1 : off_z + 1 + depth,
        ]
        inner = jnp.einsum("xycz,xycz->xyz", center, beside, preferred_element_type=jnp.float32)
        coupling_list.append(inner * (spline_weight(off_x, off_y, off_z) / channels))
    residual = weight_mask * target
    solution = jnp.zeros_like(residual)
    direction = residual
    norm_now = squares(residual)
    for step in range(ITERS):
        value_rims = with_halo(direction, (("sx", 0), ("sy", 1)), 1)
        value_pad = jnp.pad(value_rims, ((0, 0), (0, 0), (1, 1)))
        total = ridge * direction
        for tap, (operate_off_x, operate_off_y, operate_off_z) in enumerate(offset_list()):
            total = (
                total
                + coupling_list[tap]
                * value_pad[
                    operate_off_x + 1 : operate_off_x + 1 + width_x,
                    operate_off_y + 1 : operate_off_y + 1 + width_y,
                    operate_off_z + 1 : operate_off_z + 1 + depth,
                ]
            )
        alpha = norm_now / lax.psum(jnp.sum(direction * total), ("sx", "sy"))
        solution = solution + alpha * direction
        residual = residual - alpha * total
        norm_next = squares(residual)
        direction = residual + norm_next / norm_now * direction
        norm_now = norm_next
    return (solution, residual)


def solution(mesh):
    placed = (
        P("sx", "sy", None, None),
        P(),
        P(),
        P("sx", "sy", None),
        P("sx", "sy", None, None),
        P("sx", "sy", None),
        P("sx", "sy", None),
    )
    return jax.shard_map(
        per_device,
        mesh=mesh,
        in_specs=placed,
        out_specs=(P("sx", "sy", None), P("sx", "sy", None)),
        check_vma=False,
    )
```

profile of v0, /device:TPU:1, one launch (start us, length us, event | category | flops | bytes accessed | tf_op | source)
XLA Modules:
  0.0 387.4 jit_solution(11064581585786667548)
XLA Ops:
  5.1 4.0 %collective-permute-start = (bf16[1,16,32,256]{3,2,1,0:T(8,128)(2,1)S(1)}, bf16[1,16,32,256]{3,2,1,0:T(8,128)(2,1)S(1)}, u32[]{:S(2)}, u32[]{:S(2)}) collective-permute-start(bf16[1,16,32,256]{3,2,1,0:T(8,128)(2,1)S(1)} %get-tuple-element.77), channel_id=1, source_target_pairs={{0,8},{8,16},{16,24},{24,32},{32,40},{40,48},{48,56},{56,64},{64,7... | collective-permute-start | bytes 786440 | tf_op jit(solution)/shard_map/ppermute | solution.py:16
  10.4 3.6 collective-permute-done
  14.1 3.8 collective-permute-done.1
  18.6 4.9 %collective-permute-start.2 = (bf16[10,1,32,256]{3,2,1,0:T(8,128)(2,1)}, bf16[10,1,32,256]{3,2,1,0:T(8,128)(2,1)S(1)}, u32[]{:S(2)}, u32[]{:S(2)}) collective-permute-start(bf16[10,1,32,256]{3,2,1,0:T(8,128)(2,1)} %get-tuple-element.73), channel_id=1, source_target_pairs={{0,1},{1,2},{2,3},{3,4},{4,5},{5,6},{6,7},{8,9},{9,10},{10,11},{11... | collective-permute-start | bytes 491528 | tf_op jit(solution)/shard_map/ppermute | solution.py:16
  27.4 3.0 collective-permute-done.3
  30.4 4.2 %select_maximum_fusion.4 = bf16[10,18,32,258]{3,2,1,0:T(8,128)(2,1)S(1)} fusion(bf16[10,1,32,256]{3,2,1,0:T(8,128)(2,1)S(1)} %collective-permute-done.3, bf16[10,1,32,256]{3,2,1,0:T(8,128)(2,1)S(1)} %collective-permute-done.2, bf16[1,16,32,256]{3,2,1,0:T(8,128)(2,1)S(1)} %collective-permute-done.1, bf16[8,16,32,256]{3,2,1,0:T(8,128)(2,1)S(1)} %broadcast_multiply_fusion, ...), kind=kLoop, calls=%fused_computation.90 | loop fusion | flops 26749440 | bytes 5921280 | tf_op jit(solution)/shard_map/concatenate | solution.py:18
  34.7 14.1 %fusion.164 = (bf16[8,16,32,256]{3,2,1,0:T(8,128)(2,1)}, bf16[8,16,32,256]{3,2,1,0:T(8,128)(2,1)S(1)}, bf16[8,16,32,256]{3,2,1,0:T(8,128)(2,1)S(1)}, bf16[8,16,3...) fusion(bf16[10,18,32,258]{3,2,1,0:T(8,128)(2,1)S(1)} %select_ma, ...), kind=kLoop, calls=%fused_computation.325 | loop fusion | bytes 75497472 | tf_op jit(solution)/shard_map/slice | solution.py:44
  49.7 2.9 fusion.165
  52.6 2.7 fusion.31
  56.4 2.7 fusion.11
  60.1 2.7 fusion.19
  63.8 2.7 fusion.25
  71.3 2.7 fusion.43
  75.0 3.2 fusion.8
  78.2 3.1 fusion.3
  81.4 14.2 %multiply_convert_fusion = bf16[8,16,256,32]{2,3,1,0:T(8,128)(2,1)S(1)} fusion(f32[8,16,256,32]{2,3,1,0:T(8,128)} %fusion.3, f32[8,16,256,32]{2,3,1,0:T(8,128)} %fusion.43, f32[8,16,256,32]{2,3,1,0:T(8,128)} %fusion.37, f32[8,16,256,32]{2,3,1,0:T(8,128)} %fusion.31, f32[8,16,256,32]{2,3,1,0:T(8,128)} %fusion.25, f32[8,16,256,32]{2,3,1,0:T(8,128)} %fusion.19, ...), kind=kOutput, calls=%fused_computation.124 | convolution fusion | flops 231735296 | bytes 42082816 | tf_op jit(solution)/shard_map/oc,xycz->xyoz/dot_general | solution.py:51
  95.6 3.1 collective-permute-start.4
  100.1 4.0 %collective-permute-start.8 = (f32[1,16,256]{2,1,0:T(8,128)S(1)}, f32[1,16,256]{2,1,0:T(8,128)S(1)}, u32[]{:S(2)}, u32[]{:S(2)}) collective-permute-start(f32[1,16,256]{2,1,0:T(8,128)S(1)} %get-tuple-element.91), channel_id=1, source_target_pairs={{0,8},{8,16},{16,24},{24,32},{32,40},{40,48},{48,56},{56,64},{64,7... | collective-permute-start | bytes 49160 | tf_op jit(solution)/shard_map/ppermute | solution.py:16
  105.4 4.8 %collective-permute-done.9 = f32[1,16,256]{2,1,0:T(8,128)S(1)} collective-permute-done((f32[1,16,256]{2,1,0:T(8,128)S(1)}, f32[1,16,256]{2,1,0:T(8,128)S(1)}, u32[]{:S(2)}, u32[]{:S(2)}) %collective-permute-start.9) | collective-permute-done | bytes 16416 | tf_op jit(solution)/shard_map/ppermute | solution.py:17
  110.2 3.3 collective-permute-start.10
  115.5 3.6 collective-permute-start.6
  121.6 4.2 %collective-permute-done.7 = bf16[10,1,32,256]{3,2,1,0:T(8,128)(2,1)S(1)} collective-permute-done((bf16[10,1,32,256]{3,2,1,0:T(8,128)(2,1)S(1)}, bf16[10,1,32,256]{3,2,1,0:T(8,128)(2,1)S(1)}, u32[]{:S(2)}, u32[]{:S(2)}) %collective-permute-start.7) | collective-permute-done | bytes 163872 | tf_op jit(solution)/shard_map/ppermute | solution.py:17
  125.8 4.2 %select_maximum_fusion = bf16[10,18,32,258]{3,2,1,0:T(8,128)(2,1)S(1)} fusion(bf16[10,1,32,256]{3,2,1,0:T(8,128)(2,1)S(1)} %collective-permute-done.7, bf16[10,1,32,256]{3,2,1,0:T(8,128)(2,1)S(1)} %collective-permute-done.6, bf16[1,16,32,256]{3,2,1,0:T(8,128)(2,1)S(1)} %collective-permute-done.5, bf16[8,16,32,256]{3,2,1,0:T(8,128)(2,1)S(1)} %bitcast.234, ...), kind=kLoop, calls=%fused_computation.86 | loop fusion | flops 26749440 | bytes 5921280 | tf_op jit(solution)/shard_map/concatenate | solution.py:18
  130.0 24.0 %fusion.62 = (f32[8,16,256]{2,1,0:T(8,128)S(1)}, f32[8,16,256]{2,1,0:T(8,128)S(1)}, f32[8,16,256]{2,1,0:T(8,128)S(1)}, f32[8,16,256]{2,1,0:T(8,128)S(1)}, f32[8,...) fusion(bf16[8,16,256,32]{2,3,1,0:T(8,128)(2,1)S(1)} %multiply_c, ...), kind=kLoop, calls=%fused_computation.97 | loop fusion | flops 59146240 | bytes 42336256 | tf_op jit(solution)/shard_map/xycz,xycz->xyz/dot_general | solution.py:92
  155.0 7.5 %fusion.63 = (f32[8,16,256]{2,1,0:T(8,128)S(1)}, f32[8,16,256]{2,1,0:T(8,128)S(1)}, f32[8,16,256]{2,1,0:T(8,128)S(1)}, f32[8,16,256]{2,1,0:T(8,128)S(1)}, f32[8,...) fusion(bf16[8,16,256,32]{2,3,1,0:T(8,128)(2,1)S(1)} %multiply_convert, ...), kind=kLoop, calls=%fused_computation.98 | loop fusion | flops 28049408 | bytes 18350080 | tf_op jit(solution)/shard_map/xycz,xycz->xyz/dot_general | solution.py:92
  164.2 69.5 %all-reduce.4 = (f32[]{:T(128)}, f32[]{:T(128)}) all-reduce(f32[]{:T(128)} %get-tuple-element.35, f32[]{:T(128)} %get-tuple-element.34), channel_id=1, replica_groups=mesh['sx'=16,'sy'=8] {'sx','sy'}, use_global_device_ids=true, to_apply=%region_1.2 | all-reduce | flops 2 | bytes 16 | tf_op jit(solution)/shard_map/psum | solution.py:61
  235.7 63.1 %psum.30 = f32[]{:T(128)} all-reduce(f32[]{:T(128)} %multiply_reduce_fusion.1), channel_id=1, replica_groups=mesh['sx'=16,'sy'=8] {'sx','sy'}, use_global_device_ids=true, to_apply=%region_5.6 | all-reduce | flops 1 | bytes 8 | tf_op jit(solution)/shard_map/psum | solution.py:61
  303.7 3.2 collective-permute-done.13
  306.9 3.9 %collective-permute-start.14 = (f32[10,1,256]{2,1,0:T(1,128)S(1)}, f32[10,1,256]{2,1,0:T(1,128)S(1)}, u32[]{:S(2)}, u32[]{:S(2)}) collective-permute-start(f32[10,1,256]{2,1,0:T(1,128)S(1)} %get-tuple-element.83), channel_id=1, source_target_pairs={{0,1},{1,2},{2,3},{3,4},{4,5},{5,6},{6,7},{8,9},{9,10},{10,11},{11... | collective-permute-start | bytes 30728 | tf_op jit(solution)/shard_map/ppermute | solution.py:16
  312.7 3.1 collective-permute-done.15
  316.1 2.9 multiply_reduce_fusion
  318.9 66.4 %psum.31 = f32[]{:T(128)} all-reduce(f32[]{:T(128)} %get-tuple-element.38), channel_id=1, replica_groups=mesh['sx'=16,'sy'=8] {'sx','sy'}, use_global_device_ids=true, to_apply=%region_7.8 | all-reduce | flops 1 | bytes 8 | tf_op jit(solution)/shard_map/psum | solution.py:112
  (120 shorter events, 36.7 us)
Async XLA Ops:
  3.3 22.2 %copy-start.33 = (bf16[27,32,32]{2,1,0:T(8,128)(2,1)S(1)}, bf16[27,32,32]{2,1,0:T(8,128)(2,1)}, u32[]{:S(2)}) copy-start(bf16[27,32,32]{2,1,0:T(8,128)(2,1)} %param.8) | copy-start | bytes 165892
  5.1 8.9 %collective-permute-start = (bf16[1,16,32,256]{3,2,1,0:T(8,128)(2,1)S(1)}, bf16[1,16,32,256]{3,2,1,0:T(8,128)(2,1)S(1)}, u32[]{:S(2)}, u32[]{:S(2)}) collective-permute-start(bf16[1,16,32,256]{3,2,1,0:T(8,128)(2,1)S(1)} %get-tuple-element.77), channel_id=1, source_target_pairs={{0,8},{8,16},{16,24},{24,32},{32,40},{40,48},{48,56},{56,64},{64,7... | collective-permute-start | bytes 786440 | tf_op jit(solution)/shard_map/ppermute | solution.py:16
  9.1 8.8 %collective-permute-start.1 = (bf16[1,16,32,256]{3,2,1,0:T(8,128)(2,1)S(1)}, bf16[1,16,32,256]{3,2,1,0:T(8,128)(2,1)S(1)}, u32[]{:S(2)}, u32[]{:S(2)}) collective-permute-start(bf16[1,16,32,256]{3,2,1,0:T(8,128)(2,1)S(1)} %get-tuple-element.78), channel_id=1, source_target_pairs={{8,0},{16,8},{24,16},{32,24},{40,32},{48,40},{56,48},{64,56},{72,6... | collective-permute-start | bytes 786440 | tf_op jit(solution)/shard_map/ppermute | solution.py:17
  18.6 8.8 %collective-permute-start.2 = (bf16[10,1,32,256]{3,2,1,0:T(8,128)(2,1)}, bf16[10,1,32,256]{3,2,1,0:T(8,128)(2,1)S(1)}, u32[]{:S(2)}, u32[]{:S(2)}) collective-permute-start(bf16[10,1,32,256]{3,2,1,0:T(8,128)(2,1)} %get-tuple-element.73), channel_id=1, source_target_pairs={{0,1},{1,2},{2,3},{3,4},{4,5},{5,6},{6,7},{8,9},{9,10},{10,11},{11... | collective-permute-start | bytes 491528 | tf_op jit(solution)/shard_map/ppermute | solution.py:16
  23.6 6.8 %collective-permute-start.3 = (bf16[10,1,32,256]{3,2,1,0:T(8,128)(2,1)}, bf16[10,1,32,256]{3,2,1,0:T(8,128)(2,1)S(1)}, u32[]{:S(2)}, u32[]{:S(2)}) collective-permute-start(bf16[10,1,32,256]{3,2,1,0:T(8,128)(2,1)} %get-tuple-element.74), channel_id=1, source_target_pairs={{1,0},{2,1},{3,2},{4,3},{5,4},{6,5},{7,6},{9,8},{10,9},{11,10},{12... | collective-permute-start | bytes 491528 | tf_op jit(solution)/shard_map/ppermute | solution.py:17
  56.4 3.7 copy-start.9
  60.1 3.7 copy-start.7
  63.8 3.7 copy-start.5
  67.6 3.7 copy-start.3
  95.6 19.8 %collective-permute-start.4 = (bf16[1,16,32,256]{3,2,1,0:T(8,128)(2,1)S(1)}, bf16[1,16,32,256]{3,2,1,0:T(8,128)(2,1)S(1)}, u32[]{:S(2)}, u32[]{:S(2)}) collective-permute-start(bf16[1,16,32,256]{3,2,1,0:T(8,128)(2,1)S(1)} %get-tuple-element.75), channel_id=1, source_target_pairs={{0,8},{8,16},{16,24},{24,32},{32,40},{40,48},{48,56},{56,64},{64,7... | collective-permute-start | bytes 786440 | tf_op jit(solution)/shard_map/ppermute | solution.py:16
  98.7 16.7 %collective-permute-start.5 = (bf16[1,16,32,256]{3,2,1,0:T(8,128)(2,1)S(1)}, bf16[1,16,32,256]{3,2,1,0:T(8,128)(2,1)S(1)}, u32[]{:S(2)}, u32[]{:S(2)}) collective-permute-start(bf16[1,16,32,256]{3,2,1,0:T(8,128)(2,1)S(1)} %get-tuple-element.76), channel_id=1, source_target_pairs={{8,0},{16,8},{24,16},{32,24},{40,32},{48,40},{56,48},{64,56},{72,6... | collective-permute-start | bytes 786440 | tf_op jit(solution)/shard_map/ppermute | solution.py:17
  100.1 5.3 %collective-permute-start.8 = (f32[1,16,256]{2,1,0:T(8,128)S(1)}, f32[1,16,256]{2,1,0:T(8,128)S(1)}, u32[]{:S(2)}, u32[]{:S(2)}) collective-permute-start(f32[1,16,256]{2,1,0:T(8,128)S(1)} %get-tuple-element.91), channel_id=1, source_target_pairs={{0,8},{8,16},{16,24},{24,32},{32,40},{40,48},{48,56},{56,64},{64,7... | collective-permute-start | bytes 49160 | tf_op jit(solution)/shard_map/ppermute | solution.py:16
  104.0 6.1 %collective-permute-start.9 = (f32[1,16,256]{2,1,0:T(8,128)S(1)}, f32[1,16,256]{2,1,0:T(8,128)S(1)}, u32[]{:S(2)}, u32[]{:S(2)}) collective-permute-start(f32[1,16,256]{2,1,0:T(8,128)S(1)} %get-tuple-element.92), channel_id=1, source_target_pairs={{8,0},{16,8},{24,16},{32,24},{40,32},{48,40},{56,48},{64,56},{72,6... | collective-permute-start | bytes 49160 | tf_op jit(solution)/shard_map/ppermute | solution.py:17
  110.2 11.1 %collective-permute-start.10 = (f32[10,1,256]{2,1,0:T(1,128)S(1)}, f32[10,1,256]{2,1,0:T(1,128)S(1)}, u32[]{:S(2)}, u32[]{:S(2)}) collective-permute-start(f32[10,1,256]{2,1,0:T(1,128)S(1)} %get-tuple-element.87), channel_id=1, source_target_pairs={{0,1},{1,2},{2,3},{3,4},{4,5},{5,6},{6,7},{8,9},{9,10},{10,11},{11... | collective-permute-start | bytes 30728 | tf_op jit(solution)/shard_map/ppermute | solution.py:16
  113.5 7.8 %collective-permute-start.11 = (f32[10,1,256]{2,1,0:T(1,128)S(1)}, f32[10,1,256]{2,1,0:T(1,128)S(1)}, u32[]{:S(2)}, u32[]{:S(2)}) collective-permute-start(f32[10,1,256]{2,1,0:T(1,128)S(1)} %get-tuple-element.88), channel_id=1, source_target_pairs={{1,0},{2,1},{3,2},{4,3},{5,4},{6,5},{7,6},{9,8},{10,9},{11,10},{12... | collective-permute-start | bytes 30728 | tf_op jit(solution)/shard_map/ppermute | solution.py:17
  115.5 6.1 %collective-permute-start.6 = (bf16[10,1,32,256]{3,2,1,0:T(8,128)(2,1)S(1)}, bf16[10,1,32,256]{3,2,1,0:T(8,128)(2,1)S(1)}, u32[]{:S(2)}, u32[]{:S(2)}) collective-permute-start(bf16[10,1,32,256]{3,2,1,0:T(8,128)(2,1)S(1)} %get-tuple-element.69), channel_id=1, source_target_pairs={{0,1},{1,2},{2,3},{3,4},{4,5},{5,6},{6,7},{8,9},{9,10},{10,11},{11... | collective-permute-start | bytes 491528 | tf_op jit(solution)/shard_map/ppermute | solution.py:16
  119.2 6.6 %collective-permute-start.7 = (bf16[10,1,32,256]{3,2,1,0:T(8,128)(2,1)S(1)}, bf16[10,1,32,256]{3,2,1,0:T(8,128)(2,1)S(1)}, u32[]{:S(2)}, u32[]{:S(2)}) collective-permute-start(bf16[10,1,32,256]{3,2,1,0:T(8,128)(2,1)S(1)} %get-tuple-element.70), channel_id=1, source_target_pairs={{1,0},{2,1},{3,2},{4,3},{5,4},{6,5},{7,6},{9,8},{10,9},{11,10},{12... | collective-permute-start | bytes 491528 | tf_op jit(solution)/shard_map/ppermute | solution.py:17
  154.0 8.7 %copy-start.14 = (f32[8,16,256]{2,1,0:T(8,128)}, f32[8,16,256]{2,1,0:T(8,128)S(1)}, u32[]{:S(2)}) copy-start(f32[8,16,256]{2,1,0:T(8,128)S(1)} %get-tuple-element.12) | copy-start | bytes 393220
  154.0 8.7 %copy-start.15 = (f32[8,16,256]{2,1,0:T(8,128)}, f32[8,16,256]{2,1,0:T(8,128)S(1)}, u32[]{:S(2)}) copy-start(f32[8,16,256]{2,1,0:T(8,128)S(1)} %get-tuple-element.13) | copy-start | bytes 393220
  154.0 8.7 %copy-start.16 = (f32[8,16,256]{2,1,0:T(8,128)}, f32[8,16,256]{2,1,0:T(8,128)S(1)}, u32[]{:S(2)}) copy-start(f32[8,16,256]{2,1,0:T(8,128)S(1)} %get-tuple-element.14) | copy-start | bytes 393220
  154.0 8.7 %copy-start.17 = (f32[8,16,256]{2,1,0:T(8,128)}, f32[8,16,256]{2,1,0:T(8,128)S(1)}, u32[]{:S(2)}) copy-start(f32[8,16,256]{2,1,0:T(8,128)S(1)} %get-tuple-element.15) | copy-start | bytes 393220
  154.0 8.7 %copy-start.18 = (f32[8,16,256]{2,1,0:T(8,128)}, f32[8,16,256]{2,1,0:T(8,128)S(1)}, u32[]{:S(2)}) copy-start(f32[8,16,256]{2,1,0:T(8,128)S(1)} %get-tuple-element.16) | copy-start | bytes 393220
  154.1 8.7 %copy-start.19 = (f32[8,16,256]{2,1,0:T(8,128)}, f32[8,16,256]{2,1,0:T(8,128)S(1)}, u32[]{:S(2)}) copy-start(f32[8,16,256]{2,1,0:T(8,128)S(1)} %get-tuple-element.17) | copy-start | bytes 393220
  154.1 8.7 %copy-start.20 = (f32[8,16,256]{2,1,0:T(8,128)}, f32[8,16,256]{2,1,0:T(8,128)S(1)}, u32[]{:S(2)}) copy-start(f32[8,16,256]{2,1,0:T(8,128)S(1)} %get-tuple-element.18) | copy-start | bytes 393220
  154.1 8.7 %copy-start.21 = (f32[8,16,256]{2,1,0:T(8,128)}, f32[8,16,256]{2,1,0:T(8,128)S(1)}, u32[]{:S(2)}) copy-start(f32[8,16,256]{2,1,0:T(8,128)S(1)} %get-tuple-element.19) | copy-start | bytes 393220
  154.1 8.7 %copy-start.22 = (f32[8,16,256]{2,1,0:T(8,128)}, f32[8,16,256]{2,1,0:T(8,128)S(1)}, u32[]{:S(2)}) copy-start(f32[8,16,256]{2,1,0:T(8,128)S(1)} %get-tuple-element.28) | copy-start | bytes 393220
  155.0 7.7 %copy-start.31 = (f32[8,16,256]{2,1,0:T(8,128)S(1)}, f32[8,16,256]{2,1,0:T(8,128)}, u32[]{:S(2)}) copy-start(f32[8,16,256]{2,1,0:T(8,128)} %param.12) | copy-start | bytes 393220
  162.8 153.3 %copy-start.32 = (f32[8,16,256]{2,1,0:T(8,128)S(1)}, f32[8,16,256]{2,1,0:T(8,128)}, u32[]{:S(2)}) copy-start(f32[8,16,256]{2,1,0:T(8,128)} %param.12) | copy-start | bytes 393220
  300.1 3.6 collective-permute-start.12
  302.4 4.5 %collective-permute-start.13 = (f32[1,16,256]{2,1,0:T(8,128)S(1)}, f32[1,16,256]{2,1,0:T(8,128)S(1)}, u32[]{:S(2)}, u32[]{:S(2)}) collective-permute-start(f32[1,16,256]{2,1,0:T(8,128)S(1)} %get-tuple-element.90), channel_id=1, source_target_pairs={{8,0},{16,8},{24,16},{32,24},{40,32},{48,40},{56,48},{64,56},{72,6... | collective-permute-start | bytes 49160 | tf_op jit(solution)/shard_map/ppermute | solution.py:17
  306.9 5.8 %collective-permute-start.14 = (f32[10,1,256]{2,1,0:T(1,128)S(1)}, f32[10,1,256]{2,1,0:T(1,128)S(1)}, u32[]{:S(2)}, u32[]{:S(2)}) collective-permute-start(f32[10,1,256]{2,1,0:T(1,128)S(1)} %get-tuple-element.83), channel_id=1, source_target_pairs={{0,1},{1,2},{2,3},{3,4},{4,5},{5,6},{6,7},{8,9},{9,10},{10,11},{11... | collective-permute-start | bytes 30728 | tf_op jit(solution)/shard_map/ppermute | solution.py:16
  310.8 5.0 %collective-permute-start.15 = (f32[10,1,256]{2,1,0:T(1,128)S(1)}, f32[10,1,256]{2,1,0:T(1,128)S(1)}, u32[]{:S(2)}, u32[]{:S(2)}) collective-permute-start(f32[10,1,256]{2,1,0:T(1,128)S(1)} %get-tuple-element.84), channel_id=1, source_target_pairs={{1,0},{2,1},{3,2},{4,3},{5,4},{6,5},{7,6},{9,8},{10,9},{11,10},{12... | collective-permute-start | bytes 30728 | tf_op jit(solution)/shard_map/ppermute | solution.py:17
  (20 other events, 48.2 us)
where the time goes:
time: 388 us; the launch traced here: 387 us
  blocking collectives  199 us (51%)
  other arithmetic  52.6 us (14%)
  starting transfers between devices  42.1 us (11%)
  matrix products  36.8 us (9%)
  local copies, waits for them, and re-layouts  26 us (7%)
  waiting for transfers between devices  25.8 us (7%)
  between operations  5.29 us (1%)
    psum x2, blocking collectives, squares(): return lax.psum(jnp.sum(residual * residual), ('sx', 'sy'))  133 us
    psum x1, blocking collectives, per_device(): alpha = norm_now / lax.psum(jnp.sum(direction * total), ('sx', 'sy'))  66.4 us
    dot_general x9, matrix products, convolve(): jnp.einsum('oc,xycz->xyoz', kernel_mats[slot_x, slot_y], window_part, pre...  36.8 us
    dot_general x2, other arithmetic, per_device(): jnp.einsum('xycz,xycz->xyz', center, beside, preferred_element_type=jnp.f...  31.5 us
    ppermute x8, starting transfers between devices, with_halo(): before = lax.ppermute(last, axis, up)  29.1 us
    ppermute x8, waiting for transfers between devices, with_halo(): after = lax.ppermute(initial, axis, down)  22.1 us
    slice x2, local copies, waits for them, and re-layouts, convolve(): padded[slot_x:slot_x + out_x, slot_y:slot_y + out_y, :, slot_z:slot_z + d...  17 us
    ppermute x8, starting transfers between devices, with_halo(): after = lax.ppermute(initial, axis, down)  13 us
  transfers between devices with their start and end apart: 16, of which 7 were waited for; matrix products, arithmetic and copies ran while one was open for 1% of the time, Pallas kernels for 0%

commit v1 on v0

v1 whole, which is shorter than its diff:
```python
import jax
import jax.numpy as jnp
from jax import lax
from jax.experimental import pallas as pl
from jax.experimental.pallas import tpu as pltpu
from jax.sharding import PartitionSpec as P

AXES = ("sx", "sy")
VMEM_LIMIT = 56 * 1024 * 1024


def shift(value, axis, step):
    peers = lax.axis_size(axis)
    return lax.ppermute(value, axis, [(i, (i + step) % peers) for i in range(peers)])


def halo(value, axis, dim, width):
    length = value.shape[dim]
    before = shift(lax.slice_in_dim(value, length - width, length, axis=dim), axis, 1)
    after = shift(lax.slice_in_dim(value, 0, width, axis=dim), axis, -1)
    return before, after


def clear_ends(before, after, axis):
    where = lax.axis_index(axis)
    before = jnp.where(where == 0, jnp.zeros_like(before), before)
    after = jnp.where(where == lax.axis_size(axis) - 1, jnp.zeros_like(after), after)
    return before, after


def extend(value, axis, dim, width):
    before, after = clear_ends(*halo(value, axis, dim, width), axis)
    return jnp.concatenate([before, value, after], axis=dim)


def block_weights(conv_weight):
    channels = conv_weight.shape[1]
    taps = conv_weight.reshape(3, 3, 3, channels, channels).transpose(2, 3, 0, 1, 4)
    rows = []
    for out_x in range(2):
        for out_y in range(2):
            rows.append(
                jnp.pad(taps, ((0, 0), (0, 0), (out_x, 1 - out_x), (out_y, 1 - out_y), (0, 0)))
            )
    block = jnp.stack(rows, axis=1)
    return block.reshape(3 * 4 * channels, 16 * channels)


def conv_kernel(own, y_lo, y_hi, x_lo, x_hi, mask, weights, bias, out, grid, sems):
    rows, cols = (own.shape[0], own.shape[1])
    channels, depth = (own.shape[2], own.shape[3])
    copies = [
        pltpu.make_async_copy(own, grid.at[2 : 2 + rows, 1 : 1 + cols], sems.at[0]),
        pltpu.make_async_copy(y_lo, grid.at[2 : 2 + rows, 0:1], sems.at[1]),
        pltpu.make_async_copy(y_hi, grid.at[2 : 2 + rows, 1 + cols : 2 + cols], sems.at[2]),
        pltpu.make_async_copy(x_lo, grid.at[0:2], sems.at[3]),
        pltpu.make_async_copy(x_hi, grid.at[2 + rows : 4 + rows], sems.at[4]),
    ]
    for copy in copies:
        copy.start()
    for copy in copies:
        copy.wait()

    def mask_row(x, carry):
        for y in range(cols + 2):
            keep = mask[x, y : y + 1, :].astype(jnp.bfloat16)
            grid[x, y] = grid[x, y] * keep
        return carry

    lax.fori_loop(0, rows + 4, mask_row, 0)
    lane = lax.broadcasted_iota(jnp.int32, (4 * channels, depth), 1)
    bias_all = jnp.broadcast_to(bias[...], (channels, depth))
    wide = weights[...]

    def block(step, carry):
        i = step // (cols // 2)
        j = step % (cols // 2)
        window = jnp.concatenate(
            [grid[2 * i + k, pl.ds(2 * j, 4)].reshape(4 * channels, depth) for k in range(4)], axis=0
        )
        parts = jnp.dot(wide, window, preferred_element_type=jnp.float32)
        low = pltpu.roll(parts[0 : 4 * channels], 1, 1)
        high = pltpu.roll(parts[8 * channels :], depth - 1, 1)
        total = parts[4 * channels : 8 * channels]
        total = total + jnp.where(lane == 0, 0.0, low) + jnp.where(lane == depth - 1, 0.0, high)
        for out_x in range(2):
            for out_y in range(2):
                at = (out_x * 2 + out_y) * channels
                keep = mask[2 * i + out_x + 1, pl.ds(2 * j + out_y + 1, 1), :]
                value = keep * (total[at : at + channels] + bias_all)
                out[2 * i + out_x, 2 * j + out_y] = value.astype(jnp.bfloat16)
        return carry

    lax.fori_loop(0, (rows + 2) // 2 * (cols // 2), block, 0)


def two_sum(a, b):
    s = a + b
    t = s - a
    return s, (a - (s - t)) + (b - t)


def split(a):
    c = a * 4097.0
    high = c - (c - a)
    return high, a - high


def two_prod(a, b):
    p = a * b
    a_hi, a_lo = split(a)
    b_hi, b_lo = split(b)
    return p, ((a_hi * b_hi - p) + a_hi * b_lo + a_lo * b_hi) + a_lo * b_lo


def pair_add(a, b):
    s, t = two_sum(a[0], b[0])
    return two_sum(s, t + (a[1] + b[1]))


def pair_scale(a, c):
    p, t = two_prod(a[0], c)
    return two_sum(p, t + a[1] * c)


def apply_rows(field, f_lo, f_hi, values, ridge, out, smooth):
    rows, cols, depth = out.shape
    channels = field.shape[2]

    def along_y(x, carry):
        def product(y):
            ref, at = (f_lo, 0) if y == 0 else (f_hi, 0) if y == cols + 1 else (field, y - 1)
            return ref[x, at].astype(jnp.float32) * values[x, y : y + 1, :]

        last = product(0)
        here = product(1)
        pair = last + here
        for y in range(cols):
            following = product(y + 2)
            pair_next = here + following
            smooth[x, y] = pair + pair_next
            here = following
            pair = pair_next
        return carry

    lax.fori_loop(0, rows + 2, along_y, 0)
    lane = lax.broadcasted_iota(jnp.int32, (channels, depth), 1)

    def along_x(x, carry):
        sums = []
        for y in range(cols):
            mid = smooth[x + 1, y]
            both = (smooth[x, y] + mid) + (mid + smooth[x + 2, y])
            up = jnp.where(lane == depth - 1, 0.0, pltpu.roll(both, depth - 1, 1))
            down = jnp.where(lane == 0, 0.0, pltpu.roll(both, 1, 1))
            both = (both + both) + (up + down)
            prod = both * field[x + 1, y].astype(jnp.float32)
            sums.append(jnp.sum(prod, axis=0, keepdims=True))
        inner = jnp.concatenate(sums, axis=0)
        own = values[x + 1, 1 : 1 + cols, :]
        out[x] = ridge[x] * own + inner * (1.0 / (8 * channels))
        return carry

    lax.fori_loop(0, rows, along_x, 0)


def first_kernel(field, f_lo, f_hi, values, ridge, out, smooth):
    apply_rows(field, f_lo, f_hi, values, ridge, out, smooth)


def second_kernel(field, f_lo, f_hi, values, ridge, start, out, share, smooth):
    apply_rows(field, f_lo, f_hi, values, ridge, out, smooth)
    rows, cols, depth = out.shape
    zero = jnp.zeros((cols, depth), jnp.float32)
    sums = [(zero, zero) for _ in range(5)]
    for x in range(rows):
        w0 = start[x]
        w1 = values[x + 1, 1 : 1 + cols, :]
        w2 = out[x]
        for k, (a, b) in enumerate(((w0, w0), (w0, w1), (w1, w1), (w0, w2), (w1, w2))):
            p, e = two_prod(a, b)
            s, t = two_sum(sums[k][0], p)
            sums[k] = (s, sums[k][1] + (t + e))
    row = jnp.zeros((8, 128), jnp.float32)
    lane = lax.broadcasted_iota(jnp.int32, (8, 128), 1)
    for k, (s, e) in enumerate(sums):
        while s.shape[0] > 8:
            half = s.shape[0] // 2
            t, d = two_sum(s[:half], s[half:])
            s, e = (t, e[:half] + e[half:] + d)
        while s.shape[1] > 128:
            half = s.shape[1] // 2
            t, d = two_sum(s[:, :half], s[:, half:])
            s, e = (t, e[:, :half] + e[:, half:] + d)
        for axis, steps in ((0, (4, 2, 1)), (1, (64, 32, 16, 8, 4, 2, 1))):
            for step in steps:
                t, d = two_sum(s, pltpu.roll(s, step, axis))
                s, e = (t, (e + pltpu.roll(e, step, axis)) + d)
        row = jnp.where(lane == k, s, row)
        row = jnp.where(lane == 8 + k, e, row)
    share[...] = row[0:1]


def final_kernel(shares, start, first, second, solution_out, residual_out):
    s = shares[...]
    e = jnp.zeros_like(s)
    while s.shape[0] > 8:
        half = s.shape[0] // 2
        t, d = two_sum(s[:half], s[half:])
        s, e = (t, e[:half] + e[half:] + d)
    for step in (4, 2, 1):
        t, d = two_sum(s, pltpu.roll(s, step, 0))
        s, e = (t, (e + pltpu.roll(e, step, 0)) + d)
    lane = lax.broadcasted_iota(jnp.int32, s.shape, 1)

    def pick(value, k):
        return jnp.broadcast_to(
            jnp.sum(jnp.where(lane == k, value, 0.0), axis=1, keepdims=True), s.shape
        )

    g00, g01, g11, g02, g12 = [
        two_sum(pick(s, k), pick(e, k) + pick(s, 8 + k)) for k in range(5)
    ]
    alpha = g00[0] / g01[0]
    fresh = pair_add(pair_add(g00, pair_scale(g01, -2.0 * alpha)), pair_scale(pair_scale(g11, alpha), alpha))
    grow = 1.0 + fresh[0] / g00[0]
    curve = pair_add(
        pair_add(
            pair_scale(pair_scale(g01, grow), grow),
            pair_scale(pair_scale(pair_add(g02, g11), -alpha), grow),
        ),
        pair_scale(pair_scale(g12, alpha), alpha),
    )
    beta = fresh[0] / curve[0]
    near = (alpha + beta * grow)[0:1, 0:1]
    far = (alpha * beta)[0:1, 0:1]
    for x in range(start.shape[0]):
        w0, w1, w2 = (start[x], first[x], second[x])
        solution_out[x] = near * w0 - far * w1
        residual_out[x] = (w0 - near * w1) + far * w2


def per_device(features, conv_weight, conv_bias, occupancy, block_ids, ridge, target):
    rows, cols, channels, depth = features.shape
    voxels = depth // block_ids.shape[2]
    f32 = jnp.float32
    vmem = pl.BlockSpec(memory_space=pltpu.VMEM)
    anywhere = pl.BlockSpec(memory_space=pl.ANY)
    params = pltpu.CompilerParams(vmem_limit_bytes=VMEM_LIMIT)

    feat_y = halo(features, "sy", 1, 1)
    edges_lo = jnp.concatenate([feat_y[0][:2], features[:2], feat_y[1][:2]], axis=1)
    edges_hi = jnp.concatenate([feat_y[0][-2:], features[-2:], feat_y[1][-2:]], axis=1)
    feat_x = (shift(edges_hi, "sx", 1), shift(edges_lo, "sx", -1))

    present = (block_ids[:, :, :, 13] >= 0).astype(f32)
    weight_mask = occupancy.astype(f32) * jnp.repeat(present, voxels, axis=2)
    residual = weight_mask * target
    both = jnp.stack([weight_mask, residual])
    both = extend(extend(both, "sy", 2, 1), "sx", 1, 2)
    mask_ext = both[0]
    start_ext = both[1, 1:-1]

    field = pl.pallas_call(
        conv_kernel,
        out_shape=jax.ShapeDtypeStruct((rows + 2, cols, channels, depth), jnp.bfloat16),
        in_specs=[anywhere] * 5 + [vmem] * 3,
        out_specs=vmem,
        scratch_shapes=[
            pltpu.VMEM((rows + 4, cols + 2, channels, depth), jnp.bfloat16),
            pltpu.SemaphoreType.DMA((5,)),
        ],
        compiler_params=params,
        name="conv",
    )(
        features,
        *feat_y,
        *feat_x,
        mask_ext,
        block_weights(conv_weight),
        conv_bias[:, None],
    )
    field_y = halo(field, "sy", 1, 1)

    grid_shape = jax.ShapeDtypeStruct((rows, cols, depth), f32)
    smooth = pltpu.VMEM((rows + 2, cols, channels, depth), f32)
    first = pl.pallas_call(
        first_kernel,
        out_shape=grid_shape,
        in_specs=[vmem] * 5,
        out_specs=vmem,
        scratch_shapes=[smooth],
        compiler_params=params,
        name="first",
    )(field, *field_y, start_ext, ridge)
    first_ext = extend(extend(first, "sy", 1, 1), "sx", 0, 1)
    second, share = pl.pallas_call(
        second_kernel,
        out_shape=(grid_shape, jax.ShapeDtypeStruct((1, 128), f32)),
        in_specs=[vmem] * 6,
        out_specs=(vmem, vmem),
        scratch_shapes=[smooth],
        compiler_params=params,
        name="second",
    )(field, *field_y, first_ext, ridge, residual)

    peers = lax.axis_size("sx") * lax.axis_size("sy")
    shares = lax.all_to_all(jnp.broadcast_to(share[None], (peers, 1, 128)), AXES, 0, 0)
    return pl.pallas_call(
        final_kernel,
        out_shape=(grid_shape, grid_shape),
        in_specs=[vmem] * 4,
        out_specs=(vmem, vmem),
        compiler_params=params,
        name="final",
    )(shares.reshape(peers, 128), residual, first, second)


def solution(mesh):
    placed = (
        P("sx", "sy", None, None),
        P(),
        P(),
        P("sx", "sy", None),
        P("sx", "sy", None, None),
        P("sx", "sy", None),
        P("sx", "sy", None),
    )
    return jax.shard_map(
        per_device,
        mesh=mesh,
        in_specs=placed,
        out_specs=(P("sx", "sy", None), P("sx", "sy", None)),
        check_vma=False,
    )
```

time: 388 us -> 122 us (0.31)
  blocking collectives: 199 us -> 19.9 us
  other arithmetic: 52.6 us -> 6.76 us
  matrix products: 36.8 us -> 0 us
  Pallas kernels: 0 us -> 34.3 us
  starting transfers between devices: 42.1 us -> 26.1 us
  local copies, waits for them, and re-layouts: 26 us -> 12.7 us
  waiting for transfers between devices: 25.8 us -> 21.2 us
  between operations: 5.29 us -> 0.92 us
    psum x3 -> x0, blocking collectives: 199 us -> none  [the longest x2 133 us: squares(): return lax.psum(jnp.sum(residual * residual), ('sx', 'sy'))]
    dot_general x9 -> x0, matrix products: 36.8 us -> none  [convolve(): jnp.einsum('oc,xycz->xyoz', kernel_mats[slot_x, slot_y], window_part, pre...]
    pallas_call x0 -> x4, Pallas kernels: none -> 34.3 us  [the longest x1 18.9 us: per_device(): pl.pallas_call(conv_kernel, out_shape=jax.ShapeDtypeStruct((rows + 2, col...]
    dot_general x2 -> x0, other arithmetic: 31.5 us -> none  [per_device(): jnp.einsum('xycz,xycz->xyz', center, beside, preferred_element_type=jnp.f...]
    all_to_all x0 -> x1, blocking collectives: none -> 19.9 us  [per_device(): lax.all_to_all(jnp.broadcast_to(share[None], (peers, 1, 128)), AXES, 0, 0)]
    ppermute x16 -> x14, starting transfers between devices: 42.1 us -> 26.1 us  [shift(): lax.ppermute(value, axis, [(i, (i + step) % peers) for i in range(peers)])]
    slice x7, local copies, waits for them, and re-layouts: 18.2 us -> 5.32 us  [the longest x2 2.01 us: halo(): after = shift(lax.slice_in_dim(value, 0, width, axis=dim), axis, -1)]
    concatenate x8 -> x4, other arithmetic: 10.8 us -> 1.86 us  [the longest x2 1.71 us: extend(): return jnp.concatenate([before, value, after], axis=dim)]
  transfers between devices with their start and end apart: 16 -> 14, of which waited for: 7 -> 8; matrix products, arithmetic and copies ran while one was open for 1% -> 8% of each run, Pallas kernels for 0% -> 0%
where the time goes in v1:
time: 122 us
  Pallas kernels  34.3 us (28%)
  starting transfers between devices  26.1 us (21%)
  waiting for transfers between devices  21.2 us (17%)
  blocking collectives  19.9 us (16%)
  local copies, waits for them, and re-layouts  12.7 us (10%)
  other arithmetic  6.76 us (6%)
    ppermute x14, starting transfers between devices, shift(): lax.ppermute(value, axis, [(i, (i + step) % peers) for i in range(peers)])  26.1 us
    ppermute x14, waiting for transfers between devices, shift(): lax.ppermute(value, axis, [(i, (i + step) % peers) for i in range(peers)])  21.2 us
    all_to_all x1, blocking collectives, per_device(): lax.all_to_all(jnp.broadcast_to(share[None], (peers, 1, 128)), AXES, 0, 0)  19.9 us
    pallas_call x1, Pallas kernels, per_device(): pl.pallas_call(conv_kernel, out_shape=jax.ShapeDtypeStruct((rows + 2, col...  18.9 us
    pallas_call x1, Pallas kernels, per_device(): pl.pallas_call(second_kernel, out_shape=(grid_shape, jax.ShapeDtypeStruct...  7.24 us
    pallas_call x1, Pallas kernels, per_device(): pl.pallas_call(first_kernel, out_shape=grid_shape, in_specs=[vmem] * 5, o...  6.26 us
  transfers between devices with their start and end apart: 14, of which 8 were waited for; matrix products, arithmetic and copies ran while one was open for 8% of the time, Pallas kernels for 0%

profile of v1, /device:TPU:1, one launch (start us, length us, event | category | flops | bytes accessed | tf_op | source)
XLA Modules:
  0.0 122.0 jit_solution(11291953116586495876)
XLA Ops:
  0.6 1.1 slice.71
  2.4 1.0 fusion.1
  3.5 1.4 %collective-permute-start.5 = (f32[2,8,1,256]{3,2,1,0:T(1,128)S(1)}, f32[2,8,1,256]{3,2,1,0:T(1,128)S(1)}, u32[]{:S(2)}, u32[]{:S(2)}) collective-permute-start(f32[2,8,1,256]{3,2,1,0:T(1,128)S(1)} %get-tuple-element.19), channel_id=1, source_target_pairs={{0,7},{1,0},{2,1},{3,2},{4,3},{5,4},{6,5},{7,6},{8,15},{9,8},{10,9... | collective-permute-start | bytes 49160 | tf_op jit(solution)/shard_map/ppermute | solution.py:14
  4.9 1.3 %collective-permute-start.4 = (f32[2,8,1,256]{3,2,1,0:T(1,128)S(1)}, f32[2,8,1,256]{3,2,1,0:T(1,128)S(1)}, u32[]{:S(2)}, u32[]{:S(2)}) collective-permute-start(f32[2,8,1,256]{3,2,1,0:T(1,128)S(1)} %get-tuple-element.18), channel_id=1, source_target_pairs={{0,1},{1,2},{2,3},{3,4},{4,5},{5,6},{6,7},{7,0},{8,9},{9,10},{10,1... | collective-permute-start | bytes 49160 | tf_op jit(solution)/shard_map/ppermute | solution.py:14
  6.2 1.0 fusion.4
  7.7 0.8 collective-permute-start.1
  8.6 0.8 pad_bitcast_fusion.3
  9.4 1.6 %pad_maximum_fusion = bf16[3,4,32,4,4,32]{5,4,3,2,1,0:T(4,128)(2,1)S(1)} fusion(bf16[3,1,32,4,4,32]{5,4,3,2,1,0:T(4,128)(2,1)S(1)} %get-tuple-element.13, bf16[3,1,32,4,4,32]{5,4,3,2,1,0:T(4,128)(2,1)S(1)} %get-tuple-element.14, bf16[3,1,32,4,4,32]{5,4,3,2,1,0:T(4,128)(2,1)S(1)} %get-tuple-element.15, bf16[3,1,32,4,4,32]{5,4,3,2,1,0:T(4,128)(2,1)S(1)} %get-tuple-element.12), kind=kLoop, calls=%fused_computation | loop fusion | flops 589824 | bytes 786432 | tf_op jit(solution)/shard_map/stack | solution.py:45
  11.8 6.0 %collective-permute-start.7 = (f32[2,2,18,256]{3,2,1,0:T(8,128)}, f32[2,2,18,256]{3,2,1,0:T(8,128)S(1)}, u32[]{:S(2)}, u32[]{:S(2)}) collective-permute-start(f32[2,2,18,256]{3,2,1,0:T(8,128)} %get-tuple-element.17), channel_id=1, source_target_pairs={{0,120},{8,0},{16,8},{24,16},{32,24},{40,32},{48,40},{56,48},{64,5... | collective-permute-start | bytes 221192 | tf_op jit(solution)/shard_map/ppermute | solution.py:14
  17.8 1.3 %fusion.3 = (bf16[2,16,32,256]{3,2,1,0:T(8,128)(2,1)S(1)}, bf16[2,16,32,256]{3,2,1,0:T(8,128)(2,1)S(1)}) fusion(bf16[8,16,32,256]{3,2,1,0:T(8,128)(2,1)} %own.1), kind=kLoop, calls=%fused_computation.34 | loop fusion | bytes 2097152 | tf_op jit(solution)/shard_map/slice | solution.py:252
  19.0 2.3 %reshape.25.weights = bf16[384,512]{1,0:T(8,128)(2,1)} reshape(bf16[3,4,32,4,4,32]{5,4,3,2,1,0:T(4,128)(2,1)S(1)} %pad_maximum_fusion) | data formatting | bytes 786432 | tf_op jit(solution)/shard_map/reshape | solution.py:46
  22.2 4.9 %collective-permute-start.3 = (bf16[2,18,32,256]{3,2,1,0:T(8,128)(2,1)S(1)}, bf16[2,18,32,256]{3,2,1,0:T(8,128)(2,1)S(1)}, u32[]{:S(2)}, u32[]{:S(2)}) collective-permute-start(bf16[2,18,32,256]{3,2,1,0:T(8,128)(2,1)S(1)} %pad_maximum_fusion.2), channel_id=1, source_target_pairs={{0,120},{8,0},{16,8},{24,16},{32,24},{40,32},{48,40},{56,48},{64,5... | collective-permute-start | bytes 1769480 | tf_op jit(solution)/shard_map/ppermute | solution.py:14
  27.2 1.8 %collective-permute-done.6 = f32[2,2,18,256]{3,2,1,0:T(8,128)S(1)} collective-permute-done((f32[2,2,18,256]{3,2,1,0:T(8,128)}, f32[2,2,18,256]{3,2,1,0:T(8,128)S(1)}, u32[]{:S(2)}, u32[]{:S(2)}) %collective-permute-start.6) | collective-permute-done | bytes 73760 | tf_op jit(solution)/shard_map/ppermute | solution.py:14
  29.1 0.8 slice_bitcast_fusion.mask
  29.8 6.3 %collective-permute-done.3.x_hi = bf16[2,18,32,256]{3,2,1,0:T(8,128)(2,1)S(1)} collective-permute-done((bf16[2,18,32,256]{3,2,1,0:T(8,128)(2,1)S(1)}, bf16[2,18,32,256]{3,2,1,0:T(8,128)(2,1)S(1)}, u32[]{:S(2)}, u32[]{:S(2)}) %collective-permute-start.3) | collective-permute-done | bytes 589856 | tf_op jit(solution)/shard_map/ppermute | solution.py:14
  36.1 5.4 %collective-permute-done.2.x_lo = bf16[2,18,32,256]{3,2,1,0:T(8,128)(2,1)S(1)} collective-permute-done((bf16[2,18,32,256]{3,2,1,0:T(8,128)(2,1)S(1)}, bf16[2,18,32,256]{3,2,1,0:T(8,128)(2,1)S(1)}, u32[]{:S(2)}, u32[]{:S(2)}) %collective-permute-start.2) | collective-permute-done | bytes 589856 | tf_op jit(solution)/shard_map/ppermute | solution.py:14
  41.5 0.8 copy-done.4
  42.3 18.9 %conv.1.field = bf16[10,16,32,256]{3,2,1,0:T(8,128)(2,1)} custom-call(bf16[8,16,32,256]{3,2,1,0:T(8,128)(2,1)} %own.1, bf16[8,1,32,256]{3,2,1,0:T(8,128)(2,1)} %copy-done.5, bf16[8,1,32,256]{3,2,1,0:T(8,128)(2,1)} %copy-done.6, bf16[2,18,32,256]{3,2,1,0:T(8,128)(2,1)} %copy-done.4, bf16[2,18,32,256]{3,2,1,0:T(8,128)(2,1)} %copy-done.3, ...), custom_call_target="tpu_custom_call" | custom-call | tf_op jit(solution)/shard_map/conv/pallas_call | solution.py:264
  61.2 1.0 fusion.2
  62.2 5.1 %collective-permute-start.8 = (bf16[10,1,32,256]{3,2,1,0:T(8,128)(2,1)S(1)}, bf16[10,1,32,256]{3,2,1,0:T(8,128)(2,1)S(1)}, u32[]{:S(2)}, u32[]{:S(2)}) collective-permute-start(bf16[10,1,32,256]{3,2,1,0:T(8,128)(2,1)S(1)} %get-tuple-element.7), channel_id=1, source_target_pairs={{0,1},{1,2},{2,3},{3,4},{4,5},{5,6},{6,7},{7,0},{8,9},{9,10},{10,1... | collective-permute-start | bytes 491528 | tf_op jit(solution)/shard_map/ppermute | solution.py:14
  68.1 1.5 %collective-permute-done.8.f_lo = bf16[10,1,32,256]{3,2,1,0:T(8,128)(2,1)S(1)} collective-permute-done((bf16[10,1,32,256]{3,2,1,0:T(8,128)(2,1)S(1)}, bf16[10,1,32,256]{3,2,1,0:T(8,128)(2,1)S(1)}, u32[]{:S(2)}, u32[]{:S(2)}) %collective-permute-start.8) | collective-permute-done | bytes 163872 | tf_op jit(solution)/shard_map/ppermute | solution.py:14
  69.6 2.8 %collective-permute-done.9.f_hi = bf16[10,1,32,256]{3,2,1,0:T(8,128)(2,1)S(1)} collective-permute-done((bf16[10,1,32,256]{3,2,1,0:T(8,128)(2,1)S(1)}, bf16[10,1,32,256]{3,2,1,0:T(8,128)(2,1)S(1)}, u32[]{:S(2)}, u32[]{:S(2)}) %collective-permute-start.9) | collective-permute-done | bytes 163872 | tf_op jit(solution)/shard_map/ppermute | solution.py:14
  73.1 6.3 %first.1 = f32[8,16,256]{2,1,0:T(8,128)} custom-call(bf16[10,16,32,256]{3,2,1,0:T(8,128)(2,1)} %conv.1.field, bf16[10,1,32,256]{3,2,1,0:T(8,128)(2,1)} %copy-done.1, bf16[10,1,32,256]{3,2,1,0:T(8,128)(2,1)} %copy-done.2, f32[10,18,256]{2,1,0:T(8,128)} %maximum_bitcast_fusion.values, f32[8,16,256]{2,1,0:T(8,128)} %ridge.3), custom_call_target="tpu_custom_call" | custom-call | tf_op jit(solution)/shard_map/first/pallas_call | solution.py:287
  79.3 0.9 fusion.5
  80.6 0.8 collective-permute-start.11
  82.1 1.6 %collective-permute-done.11 = f32[8,1,256]{2,1,0:T(1,128)S(1)} collective-permute-done((f32[8,1,256]{2,1,0:T(1,128)S(1)}, f32[8,1,256]{2,1,0:T(1,128)S(1)}, u32[]{:S(2)}, u32[]{:S(2)}) %collective-permute-start.11) | collective-permute-done | bytes 8224 | tf_op jit(solution)/shard_map/ppermute | solution.py:14
  84.5 4.8 %collective-permute-start.13 = (f32[1,18,256]{2,1,0:T(8,128)S(1)}, f32[1,18,256]{2,1,0:T(8,128)S(1)}, u32[]{:S(2)}, u32[]{:S(2)}) collective-permute-start(f32[1,18,256]{2,1,0:T(8,128)S(1)} %get-tuple-element.23), channel_id=1, source_target_pairs={{0,120},{8,0},{16,8},{24,16},{32,24},{40,32},{48,40},{56,48},{64,5... | collective-permute-start | bytes 55304 | tf_op jit(solution)/shard_map/ppermute | solution.py:14
  89.3 1.2 collective-permute-done.12
  90.5 1.6 %pad_maximum_fusion.4.values = f32[10,18,256]{2,1,0:T(8,128)} fusion(f32[1,18,256]{2,1,0:T(8,128)S(1)} %broadcast_select_fusion.6, f32[8,1,256]{2,1,0:T(1,128)S(1)} %broadcast_select_fusion.4, f32[8,16,256]{2,1,0:T(8,128)} %first.1, f32[8,1,256]{2,1,0:T(1,128)S(1)} %broadcast_select_fusion.5, f32[1,18,256]{2,1,0:T(8,128)S(1)} %broadcast_select_fusion.7), kind=kLoop, calls=%fused_computation.11 | loop fusion | flops 184320 | bytes 368640 | tf_op jit(solution)/shard_map/concatenate | solution.py:33
  92.2 7.2 %second.1 = (f32[8,16,256]{2,1,0:T(8,128)}, f32[1,128]{1,0:T(1,128)}) custom-call(bf16[10,16,32,256]{3,2,1,0:T(8,128)(2,1)} %conv.1.field, bf16[10,1,32,256]{3,2,1,0:T(8,128)(2,1)} %copy-done.1, bf16[10,1,32,256]{3,2,1,0:T(8,128)(2,1)} %copy-done.2, f32[10,18,256]{2,1,0:T(8,128)} %pad_maximum_fusion.4.values, f32[8,16,256]{2,1,0:T(8,128)} %ridge.3, ...), custom_call_target="tpu_custom_call" | custom-call | tf_op jit(solution)/shard_map/second/pallas_call | solution.py:297
  100.1 19.9 %all_to_all.5 = f32[128,1,128]{2,1,0:T(1,128)} all-to-all(f32[128,1,128]{2,1,0:T(1,128)S(1)} %broadcast_in_dim.17), channel_id=1, replica_groups=mesh['sx'=16,'sy'=8] {'sx','sy'}, dimensions={0} | all-to-all | bytes 131072 | tf_op jit(solution)/shard_map/all_to_all | solution.py:308
  120.0 2.0 %final.1 = (f32[8,16,256]{2,1,0:T(8,128)}, f32[8,16,256]{2,1,0:T(8,128)}) custom-call(f32[128,128]{1,0:T(8,128)} %bitcast.35, f32[8,16,256]{2,1,0:T(8,128)} %copy-done, f32[8,16,256]{2,1,0:T(8,128)} %first.1, f32[8,16,256]{2,1,0:T(8,128)} %get-tuple-element.5.second), custom_call_target="tpu_custom_call" | custom-call | tf_op jit(solution)/shard_map/final/pallas_call | solution.py:309
  (55 shorter events, 7.1 us)
Async XLA Ops:
  0.6 7.8 %copy-start.7 = (bf16[27,32,32]{2,1,0:T(8,128)(2,1)S(1)}, bf16[27,32,32]{2,1,0:T(8,128)(2,1)}, u32[]{:S(2)}) copy-start(bf16[27,32,32]{2,1,0:T(8,128)(2,1)} %param.8) | copy-start | bytes 165892
  3.4 64.0 %copy-start = (f32[8,16,256]{2,1,0:T(8,128)}, f32[8,16,256]{2,1,0:T(8,128)S(1)}, u32[]{:S(2)}) copy-start(f32[8,16,256]{2,1,0:T(8,128)S(1)} %get-tuple-element.21.start) | copy-start | bytes 393220
  3.5 7.6 %collective-permute-start.5 = (f32[2,8,1,256]{3,2,1,0:T(1,128)S(1)}, f32[2,8,1,256]{3,2,1,0:T(1,128)S(1)}, u32[]{:S(2)}, u32[]{:S(2)}) collective-permute-start(f32[2,8,1,256]{3,2,1,0:T(1,128)S(1)} %get-tuple-element.19), channel_id=1, source_target_pairs={{0,7},{1,0},{2,1},{3,2},{4,3},{5,4},{6,5},{7,6},{8,15},{9,8},{10,9... | collective-permute-start | bytes 49160 | tf_op jit(solution)/shard_map/ppermute | solution.py:14
  4.9 6.2 %collective-permute-start.4 = (f32[2,8,1,256]{3,2,1,0:T(1,128)S(1)}, f32[2,8,1,256]{3,2,1,0:T(1,128)S(1)}, u32[]{:S(2)}, u32[]{:S(2)}) collective-permute-start(f32[2,8,1,256]{3,2,1,0:T(1,128)S(1)} %get-tuple-element.18), channel_id=1, source_target_pairs={{0,1},{1,2},{2,3},{3,4},{4,5},{5,6},{6,7},{7,0},{8,9},{9,10},{10,1... | collective-permute-start | bytes 49160 | tf_op jit(solution)/shard_map/ppermute | solution.py:14
  7.2 14.8 %collective-permute-start = (bf16[8,1,32,256]{3,2,1,0:T(8,128)(2,1)S(1)}, bf16[8,1,32,256]{3,2,1,0:T(8,128)(2,1)S(1)}, u32[]{:S(2)}, u32[]{:S(2)}) collective-permute-start(bf16[8,1,32,256]{3,2,1,0:T(8,128)(2,1)S(1)} %get-tuple-element.11), channel_id=1, source_target_pairs={{0,1},{1,2},{2,3},{3,4},{4,5},{5,6},{6,7},{7,0},{8,9},{9,10},{10,1... | collective-permute-start | bytes 393224 | tf_op jit(solution)/shard_map/ppermute | solution.py:14
  7.7 14.4 %collective-permute-start.1 = (bf16[8,1,32,256]{3,2,1,0:T(8,128)(2,1)S(1)}, bf16[8,1,32,256]{3,2,1,0:T(8,128)(2,1)S(1)}, u32[]{:S(2)}, u32[]{:S(2)}) collective-permute-start(bf16[8,1,32,256]{3,2,1,0:T(8,128)(2,1)S(1)} %get-tuple-element.10), channel_id=1, source_target_pairs={{0,7},{1,0},{2,1},{3,2},{4,3},{5,4},{6,5},{7,6},{8,15},{9,8},{10,9... | collective-permute-start | bytes 393224 | tf_op jit(solution)/shard_map/ppermute | solution.py:14
  11.8 9.5 %copy-start.8 = (f32[32]{0:T(128)S(1)}, f32[32]{0:T(128)}, u32[]{:S(2)}) copy-start(f32[32]{0:T(128)} %param.9) | copy-start | bytes 388
  11.8 10.2 %collective-permute-start.7 = (f32[2,2,18,256]{3,2,1,0:T(8,128)}, f32[2,2,18,256]{3,2,1,0:T(8,128)S(1)}, u32[]{:S(2)}, u32[]{:S(2)}) collective-permute-start(f32[2,2,18,256]{3,2,1,0:T(8,128)} %get-tuple-element.17), channel_id=1, source_target_pairs={{0,120},{8,0},{16,8},{24,16},{32,24},{40,32},{48,40},{56,48},{64,5... | collective-permute-start | bytes 221192 | tf_op jit(solution)/shard_map/ppermute | solution.py:14
  22.0 7.0 %collective-permute-start.6 = (f32[2,2,18,256]{3,2,1,0:T(8,128)}, f32[2,2,18,256]{3,2,1,0:T(8,128)S(1)}, u32[]{:S(2)}, u32[]{:S(2)}) collective-permute-start(f32[2,2,18,256]{3,2,1,0:T(8,128)} %get-tuple-element.16), channel_id=1, source_target_pairs={{0,8},{8,16},{16,24},{24,32},{32,40},{40,48},{48,56},{56,64},{64,7... | collective-permute-start | bytes 221192 | tf_op jit(solution)/shard_map/ppermute | solution.py:14
  22.0 7.1 %copy-start.5 = (bf16[8,1,32,256]{3,2,1,0:T(8,128)(2,1)}, bf16[8,1,32,256]{3,2,1,0:T(8,128)(2,1)S(1)}, u32[]{:S(2)}) copy-start(bf16[8,1,32,256]{3,2,1,0:T(8,128)(2,1)S(1)} %collective-permute-done.y_lo) | copy-start | bytes 393220
  22.1 7.0 %copy-start.6 = (bf16[8,1,32,256]{3,2,1,0:T(8,128)(2,1)}, bf16[8,1,32,256]{3,2,1,0:T(8,128)(2,1)S(1)}, u32[]{:S(2)}) copy-start(bf16[8,1,32,256]{3,2,1,0:T(8,128)(2,1)S(1)} %collective-permute-done.1.y_hi) | copy-start | bytes 393220
  22.2 14.0 %collective-permute-start.3 = (bf16[2,18,32,256]{3,2,1,0:T(8,128)(2,1)S(1)}, bf16[2,18,32,256]{3,2,1,0:T(8,128)(2,1)S(1)}, u32[]{:S(2)}, u32[]{:S(2)}) collective-permute-start(bf16[2,18,32,256]{3,2,1,0:T(8,128)(2,1)S(1)} %pad_maximum_fusion.2), channel_id=1, source_target_pairs={{0,120},{8,0},{16,8},{24,16},{32,24},{40,32},{48,40},{56,48},{64,5... | collective-permute-start | bytes 1769480 | tf_op jit(solution)/shard_map/ppermute | solution.py:14
  27.1 14.4 %collective-permute-start.2 = (bf16[2,18,32,256]{3,2,1,0:T(8,128)(2,1)S(1)}, bf16[2,18,32,256]{3,2,1,0:T(8,128)(2,1)S(1)}, u32[]{:S(2)}, u32[]{:S(2)}) collective-permute-start(bf16[2,18,32,256]{3,2,1,0:T(8,128)(2,1)S(1)} %pad_maximum_fusion.1), channel_id=1, source_target_pairs={{0,8},{8,16},{16,24},{24,32},{32,40},{40,48},{48,56},{56,64},{64,7... | collective-permute-start | bytes 1769480 | tf_op jit(solution)/shard_map/ppermute | solution.py:14
  36.1 5.4 %copy-start.3 = (bf16[2,18,32,256]{3,2,1,0:T(8,128)(2,1)}, bf16[2,18,32,256]{3,2,1,0:T(8,128)(2,1)S(1)}, u32[]{:S(2)}) copy-start(bf16[2,18,32,256]{3,2,1,0:T(8,128)(2,1)S(1)} %collective-permute-done.3.x_hi) | copy-start | bytes 1769476
  41.5 0.8 copy-start.4
  62.2 7.4 %collective-permute-start.8 = (bf16[10,1,32,256]{3,2,1,0:T(8,128)(2,1)S(1)}, bf16[10,1,32,256]{3,2,1,0:T(8,128)(2,1)S(1)}, u32[]{:S(2)}, u32[]{:S(2)}) collective-permute-start(bf16[10,1,32,256]{3,2,1,0:T(8,128)(2,1)S(1)} %get-tuple-element.7), channel_id=1, source_target_pairs={{0,1},{1,2},{2,3},{3,4},{4,5},{5,6},{6,7},{7,0},{8,9},{9,10},{10,1... | collective-permute-start | bytes 491528 | tf_op jit(solution)/shard_map/ppermute | solution.py:14
  67.4 5.0 %collective-permute-start.9 = (bf16[10,1,32,256]{3,2,1,0:T(8,128)(2,1)S(1)}, bf16[10,1,32,256]{3,2,1,0:T(8,128)(2,1)S(1)}, u32[]{:S(2)}, u32[]{:S(2)}) collective-permute-start(bf16[10,1,32,256]{3,2,1,0:T(8,128)(2,1)S(1)} %get-tuple-element.6), channel_id=1, source_target_pairs={{0,7},{1,0},{2,1},{3,2},{4,3},{5,4},{6,5},{7,6},{8,15},{9,8},{10,9... | collective-permute-start | bytes 491528 | tf_op jit(solution)/shard_map/ppermute | solution.py:14
  69.6 2.8 %copy-start.1 = (bf16[10,1,32,256]{3,2,1,0:T(8,128)(2,1)}, bf16[10,1,32,256]{3,2,1,0:T(8,128)(2,1)S(1)}, u32[]{:S(2)}) copy-start(bf16[10,1,32,256]{3,2,1,0:T(8,128)(2,1)S(1)} %collective-permute-done.8.f_lo) | copy-start | bytes 491524
  72.4 0.7 copy-start.2
  80.2 1.9 %collective-permute-start.10 = (f32[8,1,256]{2,1,0:T(1,128)S(1)}, f32[8,1,256]{2,1,0:T(1,128)S(1)}, u32[]{:S(2)}, u32[]{:S(2)}) collective-permute-start(f32[8,1,256]{2,1,0:T(1,128)S(1)} %get-tuple-element.24), channel_id=1, source_target_pairs={{0,1},{1,2},{2,3},{3,4},{4,5},{5,6},{6,7},{7,0},{8,9},{9,10},{10,1... | collective-permute-start | bytes 24584 | tf_op jit(solution)/shard_map/ppermute | solution.py:14
  80.6 3.1 %collective-permute-start.11 = (f32[8,1,256]{2,1,0:T(1,128)S(1)}, f32[8,1,256]{2,1,0:T(1,128)S(1)}, u32[]{:S(2)}, u32[]{:S(2)}) collective-permute-start(f32[8,1,256]{2,1,0:T(1,128)S(1)} %get-tuple-element.25), channel_id=1, source_target_pairs={{0,7},{1,0},{2,1},{3,2},{4,3},{5,4},{6,5},{7,6},{8,15},{9,8},{10,9... | collective-permute-start | bytes 24584 | tf_op jit(solution)/shard_map/ppermute | solution.py:14
  84.4 6.1 %collective-permute-start.12 = (f32[1,18,256]{2,1,0:T(8,128)S(1)}, f32[1,18,256]{2,1,0:T(8,128)S(1)}, u32[]{:S(2)}, u32[]{:S(2)}) collective-permute-start(f32[1,18,256]{2,1,0:T(8,128)S(1)} %get-tuple-element.22), channel_id=1, source_target_pairs={{0,8},{8,16},{16,24},{24,32},{32,40},{40,48},{48,56},{56,64},{64,7... | collective-permute-start | bytes 55304 | tf_op jit(solution)/shard_map/ppermute | solution.py:14
  84.5 6.0 %collective-permute-start.13 = (f32[1,18,256]{2,1,0:T(8,128)S(1)}, f32[1,18,256]{2,1,0:T(8,128)S(1)}, u32[]{:S(2)}, u32[]{:S(2)}) collective-permute-start(f32[1,18,256]{2,1,0:T(8,128)S(1)} %get-tuple-element.23), channel_id=1, source_target_pairs={{0,120},{8,0},{16,8},{24,16},{32,24},{40,32},{48,40},{56,48},{64,5... | collective-permute-start | bytes 55304 | tf_op jit(solution)/shard_map/ppermute | solution.py:14

commit v2 on v1

v2 whole, which is shorter than its diff:
```python
import jax
import jax.numpy as jnp
from jax import lax
from jax.experimental import pallas as pl
from jax.experimental.pallas import tpu as pltpu
from jax.sharding import PartitionSpec as P

AXES = ("sx", "sy")


def shift(value, axis, step):
    peers = lax.axis_size(axis)
    return lax.ppermute(value, axis, [(i, (i + step) % peers) for i in range(peers)])


def halo(value, axis, dim, width):
    length = value.shape[dim]
    before = shift(lax.slice_in_dim(value, length - width, length, axis=dim), axis, 1)
    after = shift(lax.slice_in_dim(value, 0, width, axis=dim), axis, -1)
    return before, after


def clear_ends(before, after, axis):
    where = lax.axis_index(axis)
    before = jnp.where(where == 0, jnp.zeros_like(before), before)
    after = jnp.where(where == lax.axis_size(axis) - 1, jnp.zeros_like(after), after)
    return before, after


def block_weights(conv_weight):
    channels = conv_weight.shape[1]
    taps = conv_weight.reshape(3, 3, 3, channels, channels).transpose(2, 3, 0, 1, 4)
    rows = []
    for out_x in range(2):
        for out_y in range(2):
            rows.append(
                jnp.pad(taps, ((0, 0), (0, 0), (out_x, 1 - out_x), (out_y, 1 - out_y), (0, 0)))
            )
    block = jnp.stack(rows, axis=1)
    return block.reshape(3 * 4 * channels, 16 * channels)


def conv_block(grid, mask, wide, bias_all, lane, grid_x, mask_x, y, out, out_x):
    channels, depth = bias_all.shape
    window = jnp.concatenate(
        [grid[grid_x + k, y : y + 4].reshape(4 * channels, depth) for k in range(4)], axis=0
    )
    parts = jnp.dot(wide[...], window, preferred_element_type=jnp.float32)
    low = pltpu.roll(parts[0 : 4 * channels], 1, 1)
    high = pltpu.roll(parts[8 * channels :], depth - 1, 1)
    total = parts[4 * channels : 8 * channels]
    total = total + jnp.where(lane == 0, 0.0, low) + jnp.where(lane == depth - 1, 0.0, high)
    for step_x in range(2):
        for step_y in range(2):
            at = (step_x * 2 + step_y) * channels
            at_y = y + step_y + 1
            keep = mask[mask_x + step_x + 1, at_y : at_y + 1, :]
            value = keep * (total[at : at + channels] + bias_all)
            out[out_x + step_x, y + step_y] = value.astype(jnp.bfloat16)


def mask_columns(grid, grid_x, mask, mask_x, pieces):
    for y, ref, x, at in pieces:
        grid[grid_x, y] = ref[x, at] * mask[mask_x, y : y + 1, :].astype(jnp.bfloat16)


def own_pieces(own, y_lo, y_hi, x):
    cols = own.shape[1]
    inner = [(y + 1, own, x, y) for y in range(cols)]
    return [(0, y_lo, x, 0)] + inner + [(cols + 1, y_hi, x, 0)]


def side_pieces(side, corner, x):
    cols = side.shape[1]
    inner = [(y + 1, side, x, y) for y in range(cols)]
    return [(0, corner, x, 0)] + inner + [(cols + 1, corner, x, 1)]


def conv_inner_kernel(own, y_lo, y_hi, mask, wide, bias, out, grid):
    rows, cols, channels, depth = own.shape

    def mask_row(x, carry):
        mask_columns(grid, x, mask, x, own_pieces(own, y_lo, y_hi, x))
        return carry

    lax.fori_loop(0, rows, mask_row, 0)
    lane = lax.broadcasted_iota(jnp.int32, (4 * channels, depth), 1)
    bias_all = jnp.broadcast_to(bias[...], (channels, depth))

    def pair(i, carry):
        for y in range(0, cols, 2):
            conv_block(grid, mask, wide, bias_all, lane, 2 * i, 2 * i, y, out, 2 * i)
        return carry

    lax.fori_loop(0, rows // 2 - 1, pair, 0)


def conv_edge_kernel(own, y_lo, y_hi, x_lo, x_hi, c_lo, c_hi, mask, wide, bias, out, grid):
    rows, cols, channels, depth = own.shape
    for x in range(2):
        mask_columns(grid, x, mask, x, side_pieces(x_lo, c_lo, x))
        mask_columns(grid, 2 + x, mask, 2 + x, own_pieces(own, y_lo, y_hi, x))
        mask_columns(grid, 4 + x, mask, rows + x, own_pieces(own, y_lo, y_hi, rows - 2 + x))
        mask_columns(grid, 6 + x, mask, rows + 2 + x, side_pieces(x_hi, c_hi, x))
    lane = lax.broadcasted_iota(jnp.int32, (4 * channels, depth), 1)
    bias_all = jnp.broadcast_to(bias[...], (channels, depth))
    for side in range(2):
        for y in range(0, cols, 2):
            conv_block(grid, mask, wide, bias_all, lane, 4 * side, rows * side, y, out, 2 * side)


def two_sum(a, b):
    s = a + b
    t = s - a
    return s, (a - (s - t)) + (b - t)


def split(a):
    c = a * 4097.0
    high = c - (c - a)
    return high, a - high


def two_prod(a, b):
    p = a * b
    a_hi, a_lo = split(a)
    b_hi, b_lo = split(b)
    return p, ((a_hi * b_hi - p) + a_hi * b_lo + a_lo * b_hi) + a_lo * b_lo


def pair_add(a, b):
    s, t = two_sum(a[0], b[0])
    return two_sum(s, t + (a[1] + b[1]))


def pair_scale(a, c):
    p, t = two_prod(a[0], c)
    return two_sum(p, t + a[1] * c)


def along_y(smooth, dst, field, f_lo, f_hi, row, flags, value_at):
    cols = smooth.shape[1]

    def product(y):
        if y == 0:
            return f_lo[row, 0].astype(jnp.float32) * (value_at(y) * flags[0])
        if y == cols + 1:
            return f_hi[row, 0].astype(jnp.float32) * (value_at(y) * flags[1])
        return field[row, y - 1].astype(jnp.float32) * value_at(y)

    here = product(1)
    pair = product(0) + here
    for y in range(cols):
        following = product(y + 2)
        pair_next = here + following
        smooth[dst, y] = pair + pair_next
        here = following
        pair = pair_next


def own_row(own, lo, hi, x):
    cols = own.shape[1]

    def at(y):
        if y == 0:
            return lo[x]
        if y == cols + 1:
            return hi[x]
        return own[x, y - 1 : y, :]

    return at


def side_row(side):
    return lambda y: side[0, y : y + 1, :]


def along_x(before, here, after, field, row, ridge_row, value_row):
    ref, x = here
    cols, channels, depth = ref.shape[1:]
    lane = lax.broadcasted_iota(jnp.int32, (channels, depth), 1)
    sums = []
    for y in range(cols):
        mid = ref[x, y]
        both = (before[0][before[1], y] + mid) + (mid + after[0][after[1], y])
        up = jnp.where(lane == depth - 1, 0.0, pltpu.roll(both, depth - 1, 1))
        down = jnp.where(lane == 0, 0.0, pltpu.roll(both, 1, 1))
        both = (both + both) + (up + down)
        prod = both * field[row, y].astype(jnp.float32)
        sums.append(jnp.sum(prod, axis=0, keepdims=True))
    inner = jnp.concatenate(sums, axis=0)
    return ridge_row * value_row + inner * (1.0 / (8 * channels))


def first_inner_kernel(inner, i_lo, i_hi, flags, start, s_lo, s_hi, ridge, smooth, out):
    rows = inner.shape[0]

    def stage_y(k, carry):
        along_y(smooth, k, inner, i_lo, i_hi, k, flags, own_row(start, s_lo, s_hi, k + 1))
        return carry

    lax.fori_loop(0, rows, stage_y, 0)

    def stage_x(k, carry):
        out[k] = along_x(
            (smooth, k), (smooth, k + 1), (smooth, k + 2), inner, k + 1, ridge[k + 2], start[k + 2]
        )
        return carry

    lax.fori_loop(0, rows - 2, stage_x, 0)


def first_edge_kernel(
    inner, edge, e_lo, e_hi, flags, start, s_lo, s_hi, x_lo, x_hi, ridge, smooth, part, out, rim
):
    n = inner.shape[0]
    last = n + 1
    along_y(rim, 0, edge, e_lo, e_hi, 0, flags, side_row(x_lo))
    along_y(rim, 1, edge, e_lo, e_hi, 1, flags, own_row(start, s_lo, s_hi, 0))
    along_y(rim, 2, edge, e_lo, e_hi, 2, flags, own_row(start, s_lo, s_hi, last))
    along_y(rim, 3, edge, e_lo, e_hi, 3, flags, side_row(x_hi))
    for x, before, here, after, field, row in (
        (0, (rim, 0), (rim, 1), (smooth, 0), edge, 1),
        (1, (rim, 1), (smooth, 0), (smooth, 1), inner, 0),
        (last - 1, (smooth, n - 2), (smooth, n - 1), (rim, 2), inner, n - 1),
        (last, (smooth, n - 1), (rim, 2), (rim, 3), edge, 2),
    ):
        out[x] = along_x(before, here, after, field, row, ridge[x], start[x])
    for x in range(n - 2):
        out[x + 2] = part[x]


PRODUCTS = ((0, 0), (0, 1), (1, 1), (0, 2), (1, 2))


def add_products(sums, which, fields):
    for k in which:
        a, b = PRODUCTS[k]
        p, e = two_prod(fields[a], fields[b])
        s, t = two_sum(sums[k][0], p)
        sums[k] = (s, sums[k][1] + (t + e))


def second_inner_kernel(
    inner, edge, i_lo, i_hi, e_lo, e_hi, flags, start, first, w_lo, w_hi, ridge, smooth, out, grams
):
    n = inner.shape[0]

    def stage_y(k, carry):
        along_y(smooth, k + 1, inner, i_lo, i_hi, k, flags, own_row(first, w_lo, w_hi, k + 1))
        return carry

    lax.fori_loop(0, n, stage_y, 0)
    along_y(smooth, 0, edge, e_lo, e_hi, 1, flags, own_row(first, w_lo, w_hi, 0))
    along_y(smooth, n + 1, edge, e_lo, e_hi, 2, flags, own_row(first, w_lo, w_hi, n + 1))

    def stage_x(k, carry):
        out[k] = along_x(
            (smooth, k), (smooth, k + 1), (smooth, k + 2), inner, k, ridge[k + 1], first[k + 1]
        )
        return carry

    lax.fori_loop(0, n, stage_x, 0)
    zero = jnp.zeros(start.shape[1:], jnp.float32)
    sums = [(zero, zero) for _ in PRODUCTS]
    for x in range(n + 2):
        inside = 0 < x < n + 1
        fields = (start[x], first[x], out[x - 1] if inside else None)
        add_products(sums, range(5) if inside else range(3), fields)
    for k, (s, e) in enumerate(sums):
        grams[2 * k] = s
        grams[2 * k + 1] = e


def second_edge_kernel(
    edge, e_lo, e_hi, flags, start, first, x_lo, x_hi, ridge, smooth, grams, out, share, rim
):
    n = smooth.shape[0]
    along_y(rim, 0, edge, e_lo, e_hi, 0, flags, side_row(x_lo))
    along_y(rim, 1, edge, e_lo, e_hi, 3, flags, side_row(x_hi))
    out[0] = along_x((rim, 0), (smooth, 0), (smooth, 1), edge, 1, ridge[0], first[0])
    out[1] = along_x(
        (smooth, n - 2), (smooth, n - 1), (rim, 1), edge, 2, ridge[n - 1], first[n - 1]
    )
    sums = [(grams[2 * k], grams[2 * k + 1]) for k in range(5)]
    for x, k in ((0, 0), (n - 1, 1)):
        add_products(sums, (3, 4), (start[x], first[x], out[k]))
    row = jnp.zeros((8, 128), jnp.float32)
    lane = lax.broadcasted_iota(jnp.int32, (8, 128), 1)
    for k, (s, e) in enumerate(sums):
        while s.shape[0] > 8:
            half = s.shape[0] // 2
            t, d = two_sum(s[:half], s[half:])
            s, e = (t, e[:half] + e[half:] + d)
        while s.shape[1] > 128:
            half = s.shape[1] // 2
            t, d = two_sum(s[:, :half], s[:, half:])
            s, e = (t, e[:, :half] + e[:, half:] + d)
        for axis, steps in ((0, (4, 2, 1)), (1, (64, 32, 16, 8, 4, 2, 1))):
            for step in steps:
                t, d = two_sum(s, pltpu.roll(s, step, axis))
                s, e = (t, (e + pltpu.roll(e, step, axis)) + d)
        row = jnp.where(lane == k, s, row)
        row = jnp.where(lane == 8 + k, e, row)
    share[...] = row[0:1]


def final_kernel(shares, start, first, inside, sides, solution_out, residual_out):
    s = shares[...]
    e = jnp.zeros_like(s)
    while s.shape[0] > 8:
        half = s.shape[0] // 2
        t, d = two_sum(s[:half], s[half:])
        s, e = (t, e[:half] + e[half:] + d)
    for step in (4, 2, 1):
        t, d = two_sum(s, pltpu.roll(s, step, 0))
        s, e = (t, (e + pltpu.roll(e, step, 0)) + d)
    lane = lax.broadcasted_iota(jnp.int32, s.shape, 1)

    def pick(value, k):
        return jnp.broadcast_to(
            jnp.sum(jnp.where(lane == k, value, 0.0), axis=1, keepdims=True), s.shape
        )

    g00, g01, g11, g02, g12 = [
        two_sum(pick(s, k), pick(e, k) + pick(s, 8 + k)) for k in range(5)
    ]
    alpha = g00[0] / g01[0]
    fresh = pair_add(pair_add(g00, pair_scale(g01, -2.0 * alpha)), pair_scale(pair_scale(g11, alpha), alpha))
    grow = 1.0 + fresh[0] / g00[0]
    curve = pair_add(
        pair_add(
            pair_scale(pair_scale(g01, grow), grow),
            pair_scale(pair_scale(pair_add(g02, g11), -alpha), grow),
        ),
        pair_scale(pair_scale(g12, alpha), alpha),
    )
    beta = fresh[0] / curve[0]
    near = (alpha + beta * grow)[0:1, 0:1]
    far = (alpha * beta)[0:1, 0:1]
    last = start.shape[0] - 1
    for x in range(last + 1):
        w2 = sides[0] if x == 0 else sides[1] if x == last else inside[x - 1]
        w0, w1 = (start[x], first[x])
        solution_out[x] = near * w0 - far * w1
        residual_out[x] = (w0 - near * w1) + far * w2


def per_device(features, conv_weight, conv_bias, occupancy, block_ids, ridge, target):
    rows, cols, channels, depth = features.shape
    voxels = depth // block_ids.shape[2]
    f32, bf16 = (jnp.float32, jnp.bfloat16)
    vmem = pl.BlockSpec(memory_space=pltpu.VMEM)
    smem = pl.BlockSpec(memory_space=pltpu.SMEM)

    def call(kernel, specs, outs, scratch, limit, name):
        return pl.pallas_call(
            kernel,
            out_shape=[jax.ShapeDtypeStruct(shape, dtype) for shape, dtype in outs],
            in_specs=[smem if s == "s" else vmem for s in specs],
            out_specs=[vmem for _ in outs],
            scratch_shapes=[pltpu.VMEM(shape, dtype) for shape, dtype in scratch],
            compiler_params=pltpu.CompilerParams(vmem_limit_bytes=limit << 20),
            name=name,
        )

    edges = (features[-2:], features[:2], features[:, -1:], features[:, :1])
    edges, occupancy, block_ids, target, conv_weight = lax.optimization_barrier(
        (edges, occupancy, block_ids, target, conv_weight)
    )
    x_lo, x_hi = (shift(edges[0], "sx", 1), shift(edges[1], "sx", -1))
    y_lo, y_hi = (shift(edges[2], "sy", 1), shift(edges[3], "sy", -1))
    c_lo = shift(jnp.concatenate([y_lo[-2:], y_hi[-2:]], axis=1), "sx", 1)
    c_hi = shift(jnp.concatenate([y_lo[:2], y_hi[:2]], axis=1), "sx", -1)

    present = (block_ids[:, :, :, 13] >= 0).astype(f32)
    weight_mask = occupancy.astype(f32) * jnp.repeat(present, voxels, axis=2)
    residual = weight_mask * target
    both = jnp.stack([weight_mask, residual])
    both_lo, both_hi = clear_ends(*halo(both, "sy", 2, 1), "sy")
    both_y = jnp.concatenate([both_lo, both, both_hi], axis=2)
    side_lo, side_hi = clear_ends(*halo(both_y, "sx", 1, 2), "sx")
    mask_y = both_y[0]
    mask_all = jnp.concatenate([side_lo[0], mask_y, side_hi[0]], axis=0)
    where = lax.axis_index("sy")
    flags = jnp.stack([where > 0, where < lax.axis_size("sy") - 1]).astype(f32)

    wide = block_weights(conv_weight)
    bias = conv_bias[:, None]
    grid_scratch = [((rows, cols + 2, channels, depth), bf16)]
    inner_shape = (rows - 2, cols, channels, depth)
    edge_shape = (4, cols, channels, depth)
    (inner,) = call(conv_inner_kernel, "vvvvvv", [(inner_shape, bf16)], grid_scratch, 12, "conv_inner")(
        features, y_lo, y_hi, mask_y, wide, bias
    )
    i_lo, i_hi = halo(inner, "sy", 1, 1)
    smooth, part = call(
        first_inner_kernel,
        "vvvsvvvv",
        [(inner_shape, f32), ((rows - 4, cols, depth), f32)],
        [],
        8,
        "first_inner",
    )(inner, i_lo, i_hi, flags, residual, both_lo[1], both_hi[1], ridge)
    (edge,) = call(conv_edge_kernel, "vvvvvvvvvv", [(edge_shape, bf16)], grid_scratch, 12, "conv_edge")(
        features, y_lo, y_hi, x_lo, x_hi, c_lo, c_hi, mask_all, wide, bias
    )
    e_lo, e_hi = halo(edge, "sy", 1, 1)
    plane = ((rows, cols, depth), f32)
    (first,) = call(
        first_edge_kernel, "vvvvsvvvvvvvv", [plane], [(edge_shape, f32)], 8, "first_edge"
    )(
        inner,
        edge,
        e_lo,
        e_hi,
        flags,
        residual,
        both_lo[1],
        both_hi[1],
        side_lo[1, 1:],
        side_hi[1, :1],
        ridge,
        smooth,
        part,
    )
    w_lo, w_hi = halo(first, "sy", 1, 1)
    rims = [jnp.concatenate([w_lo[x], first[x], w_hi[x]], axis=0)[None] for x in (-1, 0)]
    r_lo, r_hi = (shift(rims[0], "sx", 1), shift(rims[1], "sx", -1))
    smooth, inside, grams = call(
        second_inner_kernel,
        "vvvvvvsvvvvv",
        [
            ((rows, cols, channels, depth), f32),
            ((rows - 2, cols, depth), f32),
            ((2 * len(PRODUCTS), cols, depth), f32),
        ],
        [],
        8,
        "second_inner",
    )(inner, edge, i_lo, i_hi, e_lo, e_hi, flags, residual, first, w_lo, w_hi, ridge)
    sides, share = call(
        second_edge_kernel,
        "vvvsvvvvvvv",
        [((2, cols, depth), f32), ((1, 128), f32)],
        [((2, cols, channels, depth), f32)],
        8,
        "second_edge",
    )(edge, e_lo, e_hi, flags, residual, first, r_lo, r_hi, ridge, smooth, grams)

    peers = lax.axis_size("sx") * lax.axis_size("sy")
    shares = lax.all_to_all(jnp.broadcast_to(share[None], (peers, 1, 128)), AXES, 0, 0)
    return tuple(
        call(final_kernel, "vvvvv", [plane, plane], [], 8, "final")(
            shares.reshape(peers, 128), residual, first, inside, sides
        )
    )


def solution(mesh):
    placed = (
        P("sx", "sy", None, None),
        P(),
        P(),
        P("sx", "sy", None),
        P("sx", "sy", None, None),
        P("sx", "sy", None),
        P("sx", "sy", None),
    )
    return jax.shard_map(
        per_device,
        mesh=mesh,
        in_specs=placed,
        out_specs=(P("sx", "sy", None), P("sx", "sy", None)),
        check_vma=False,
    )
```

time: 122 us -> 89 us (0.73)
  Pallas kernels: 34.3 us -> 16.8 us
  waiting for transfers between devices: 21.2 us -> 12.5 us
  local copies, waits for them, and re-layouts: 12.7 us -> 6.74 us
  starting transfers between devices: 26.1 us -> 31.3 us
  other arithmetic: 6.76 us -> 1.96 us
  blocking collectives: 19.9 us -> 18.5 us
    pallas_call x4 -> x7, Pallas kernels: 34.3 us -> 16.8 us  [the longest x1 3.85 us: per_device(): call(second_inner_kernel, 'vvvvvvsvvvvv', [((rows, cols, channels, depth)...]
    ppermute x14 -> x18, waiting for transfers between devices: 21.2 us -> 12.5 us  [shift(): lax.ppermute(value, axis, [(i, (i + step) % peers) for i in range(peers)])]
    ppermute x14 -> x18, starting transfers between devices: 26.1 us -> 31.3 us  [shift(): lax.ppermute(value, axis, [(i, (i + step) % peers) for i in range(peers)])]
    slice x2, local copies, waits for them, and re-layouts: 2.01 us -> 0.03 us  [halo(): after = shift(lax.slice_in_dim(value, 0, width, axis=dim), axis, -1)]
    concatenate x4, other arithmetic: 1.86 us -> 0.11 us  [the longest x1 0.07 us: per_device(): both_y = jnp.concatenate([both_lo, both, both_hi], axis=2)]
    unnamed x19 -> x14, local copies, waits for them, and re-layouts: 1.66 us -> 0.04 us
    all_to_all x1, blocking collectives: 19.9 us -> 18.5 us  [per_device(): lax.all_to_all(jnp.broadcast_to(share[None], (peers, 1, 128)), AXES, 0, 0)]
    slice x3 -> x2, other arithmetic: 1.48 us -> 0.06 us  [halo(): lax.slice_in_dim(value, length - width, length, axis=dim)]
  transfers between devices with their start and end apart: 14 -> 18, of which waited for: 8 -> 4; matrix products, arithmetic and copies ran while one was open for 8% -> 6% of each run, Pallas kernels for 0% -> 14%
where the time goes in v2:
time: 89 us; the launch traced here: 88.8 us
  starting transfers between devices  31.3 us (35%)
  blocking collectives  18.5 us (21%)
  Pallas kernels  16.8 us (19%)
  waiting for transfers between devices  12.5 us (14%)
  local copies, waits for them, and re-layouts  6.74 us (8%)
  other arithmetic  1.96 us (2%)
  between operations  1.08 us (1%)
    ppermute x18, starting transfers between devices, shift(): lax.ppermute(value, axis, [(i, (i + step) % peers) for i in range(peers)])  31.3 us
    all_to_all x1, blocking collectives, per_device(): lax.all_to_all(jnp.broadcast_to(share[None], (peers, 1, 128)), AXES, 0, 0)  18.5 us
    ppermute x18, waiting for transfers between devices, shift(): lax.ppermute(value, axis, [(i, (i + step) % peers) for i in range(peers)])  12.5 us
    pallas_call x1, Pallas kernels, per_device(): call(second_inner_kernel, 'vvvvvvsvvvvv', [((rows, cols, channels, depth)...  3.85 us
    pallas_call x1, Pallas kernels, per_device(): call(conv_inner_kernel, 'vvvvvv', [(inner_shape, bf16)], grid_scratch, 12...  3.69 us
    slice x2, local copies, waits for them, and re-layouts, per_device(): edges = (features[-2:], features[:2], features[:, -1:], features[:, :1])  3.34 us
    pallas_call x1, Pallas kernels, per_device(): call(first_inner_kernel, 'vvvsvvvv', [(inner_shape, f32), ((rows - 4, col...  2.5 us
    pallas_call x1, Pallas kernels, per_device(): call(conv_edge_kernel, 'vvvvvvvvvv', [(edge_shape, bf16)], grid_scratch,...  2.02 us
  transfers between devices with their start and end apart: 18, of which 4 were waited for; matrix products, arithmetic and copies ran while one was open for 6% of the time, Pallas kernels for 14%

profile of v2, /device:TPU:1, one launch (start us, length us, event | category | flops | bytes accessed | tf_op | source)
XLA Modules:
  0.0 88.8 jit_solution(5584242836469349834)
XLA Ops:
  0.6 1.0 %fusion.2 = (bf16[8,1,32,256]{3,2,1,0:T(8,128)(2,1)S(1)}, bf16[8,1,32,256]{3,2,1,0:T(8,128)(2,1)S(1)}) fusion(bf16[8,16,32,256]{3,2,1,0:T(8,128)(2,1)} %own.3), kind=kLoop, calls=%fused_computation.39 | loop fusion | bytes 524288 | tf_op jit(solution)/shard_map/slice | solution.py:367
  1.7 2.3 %fusion.3 = (bf16[2,16,32,256]{3,2,1,0:T(8,128)(2,1)}, bf16[2,16,32,256]{3,2,1,0:T(8,128)(2,1)}) fusion(bf16[8,16,32,256]{3,2,1,0:T(8,128)(2,1)} %own.3), kind=kLoop, calls=%fused_computation.40 | loop fusion | bytes 2097152 | tf_op jit(solution)/shard_map/slice | solution.py:367
  4.0 2.7 %collective-permute-start = (bf16[8,1,32,256]{3,2,1,0:T(8,128)(2,1)S(1)}, bf16[8,1,32,256]{3,2,1,0:T(8,128)(2,1)S(1)}, u32[]{:S(2)}, u32[]{:S(2)}) collective-permute-start(bf16[8,1,32,256]{3,2,1,0:T(8,128)(2,1)S(1)} %get-tuple-element.17), channel_id=1, source_target_pairs={{0,1},{1,2},{2,3},{3,4},{4,5},{5,6},{6,7},{7,0},{8,9},{9,10},{10,1... | collective-permute-start | bytes 393224 | tf_op jit(solution)/shard_map/ppermute | solution.py:13
  6.7 0.2 copy.23
  7.0 0.2 broadcast_in_dim.20
  7.4 1.8 %collective-permute-start.6 = (f32[2,8,1,256]{3,2,1,0:T(1,128)S(1)}, f32[2,8,1,256]{3,2,1,0:T(1,128)S(1)}, u32[]{:S(2)}, u32[]{:S(2)}) collective-permute-start(f32[2,8,1,256]{3,2,1,0:T(1,128)S(1)} %get-tuple-element.46), channel_id=1, source_target_pairs={{0,1},{1,2},{2,3},{3,4},{4,5},{5,6},{6,7},{7,0},{8,9},{9,10},{10,1... | collective-permute-start | bytes 49160 | tf_op jit(solution)/shard_map/ppermute | solution.py:13
  9.2 1.3 %collective-permute-start.2 = (bf16[2,16,32,256]{3,2,1,0:T(8,128)(2,1)}, bf16[2,16,32,256]{3,2,1,0:T(8,128)(2,1)S(1)}, u32[]{:S(2)}, u32[]{:S(2)}) collective-permute-start(bf16[2,16,32,256]{3,2,1,0:T(8,128)(2,1)} %get-tuple-element.19), channel_id=1, source_target_pairs={{0,8},{8,16},{16,24},{24,32},{32,40},{40,48},{48,56},{56,64},{64,7... | collective-permute-start | bytes 1572872 | tf_op jit(solution)/shard_map/ppermute | solution.py:13
  10.5 0.2 copy.32
  10.6 0.8 pad_bitcast_fusion.3
  11.4 1.6 %pad_maximum_fusion = bf16[3,4,32,4,4,32]{5,4,3,2,1,0:T(4,128)(2,1)S(1)} fusion(bf16[3,1,32,4,4,32]{5,4,3,2,1,0:T(4,128)(2,1)S(1)} %get-tuple-element.41, bf16[3,1,32,4,4,32]{5,4,3,2,1,0:T(4,128)(2,1)S(1)} %get-tuple-element.42, bf16[3,1,32,4,4,32]{5,4,3,2,1,0:T(4,128)(2,1)S(1)} %get-tuple-element.43, bf16[3,1,32,4,4,32]{5,4,3,2,1,0:T(4,128)(2,1)S(1)} %get-tuple-element.40), kind=kLoop, calls=%fused_computation | loop fusion | flops 589824 | bytes 786432 | tf_op jit(solution)/shard_map/stack | solution.py:39
  13.2 1.6 %reshape.25.wide = bf16[384,512]{1,0:T(8,128)(2,1)S(1)} reshape(bf16[3,4,32,4,4,32]{5,4,3,2,1,0:T(4,128)(2,1)S(1)} %pad_maximum_fusion) | data formatting | bytes 786432 | tf_op jit(solution)/shard_map/reshape | solution.py:40
  14.8 4.8 %collective-permute-start.3 = (bf16[2,16,32,256]{3,2,1,0:T(8,128)(2,1)}, bf16[2,16,32,256]{3,2,1,0:T(8,128)(2,1)S(1)}, u32[]{:S(2)}, u32[]{:S(2)}) collective-permute-start(bf16[2,16,32,256]{3,2,1,0:T(8,128)(2,1)} %get-tuple-element.20), channel_id=1, source_target_pairs={{0,120},{8,0},{16,8},{24,16},{32,24},{40,32},{48,40},{56,48},{64,5... | collective-permute-start | bytes 1572872 | tf_op jit(solution)/shard_map/ppermute | solution.py:13
  19.9 8.2 %collective-permute-done.8 = f32[2,2,18,256]{3,2,1,0:T(8,128)S(1)} collective-permute-done((f32[2,2,18,256]{3,2,1,0:T(8,128)S(1)}, f32[2,2,18,256]{3,2,1,0:T(8,128)S(1)}, u32[]{:S(2)}, u32[]{:S(2)}) %collective-permute-start.8) | collective-permute-done | bytes 73760 | tf_op jit(solution)/shard_map/ppermute | solution.py:13
  28.1 3.4 %collective-permute-done.9 = f32[2,2,18,256]{3,2,1,0:T(8,128)S(1)} collective-permute-done((f32[2,2,18,256]{3,2,1,0:T(8,128)S(1)}, f32[2,2,18,256]{3,2,1,0:T(8,128)S(1)}, u32[]{:S(2)}, u32[]{:S(2)}) %collective-permute-start.9) | collective-permute-done | bytes 73760 | tf_op jit(solution)/shard_map/ppermute | solution.py:13
  31.8 4.8 %collective-permute-start.5 = (bf16[2,2,32,256]{3,2,1,0:T(8,128)(2,1)S(1)}, bf16[2,2,32,256]{3,2,1,0:T(8,128)(2,1)S(1)}, u32[]{:S(2)}, u32[]{:S(2)}) collective-permute-start(bf16[2,2,32,256]{3,2,1,0:T(8,128)(2,1)S(1)} %pad_maximum_fusion.6), channel_id=1, source_target_pairs={{0,120},{8,0},{16,8},{24,16},{32,24},{40,32},{48,40},{56,48},{64,5... | collective-permute-start | bytes 196616 | tf_op jit(solution)/shard_map/ppermute | solution.py:13
  36.6 3.7 %conv_inner.1.inner = bf16[6,16,32,256]{3,2,1,0:T(8,128)(2,1)S(1)} custom-call(bf16[8,16,32,256]{3,2,1,0:T(8,128)(2,1)S(1)} %copy-done, bf16[8,1,32,256]{3,2,1,0:T(8,128)(2,1)S(1)} %collective-permute-done.y_lo, bf16[8,1,32,256]{3,2,1,0:T(8,128)(2,1)S(1)} %collective-permute-done.1.y_hi, f32[8,18,256]{2,1,0:T(8,128)S(1)} %slice_bitcast_fusion.mask, ...), custom_call_target="tpu_custom_call" | custom-call | tf_op jit(solution)/shard_map/conv_inner/pallas_call | solution.py:393
  40.3 5.4 %collective-permute-start.13 = (bf16[6,1,32,256]{3,2,1,0:T(8,128)(2,1)S(1)}, bf16[6,1,32,256]{3,2,1,0:T(8,128)(2,1)S(1)}, u32[]{:S(2)}, u32[]{:S(2)}) collective-permute-start(bf16[6,1,32,256]{3,2,1,0:T(8,128)(2,1)S(1)} %get-tuple-element.36), channel_id=1, source_target_pairs={{0,7},{1,0},{2,1},{3,2},{4,3},{5,4},{6,5},{7,6},{8,15},{9,8},{10,9... | collective-permute-start | bytes 294920 | tf_op jit(solution)/shard_map/ppermute | solution.py:13
  45.8 2.0 %conv_edge.1.edge = bf16[4,16,32,256]{3,2,1,0:T(8,128)(2,1)S(1)} custom-call(bf16[8,16,32,256]{3,2,1,0:T(8,128)(2,1)S(1)} %copy-done, bf16[8,1,32,256]{3,2,1,0:T(8,128)(2,1)S(1)} %collective-permute-done.y_lo, bf16[8,1,32,256]{3,2,1,0:T(8,128)(2,1)S(1)} %collective-permute-done.1.y_hi, bf16[2,16,32,256]{3,2,1,0:T(8,128)(2,1)S(1)} %collective-permute-done.2.x_lo, ...), custom_call_target="tpu_custom_call" | custom-call | tf_op jit(solution)/shard_map/conv_edge/pallas_call | solution.py:405
  47.8 0.5 collective-permute-start.11
  48.3 1.3 %collective-permute-start.10 = (bf16[4,1,32,256]{3,2,1,0:T(8,128)(2,1)S(1)}, bf16[4,1,32,256]{3,2,1,0:T(8,128)(2,1)S(1)}, u32[]{:S(2)}, u32[]{:S(2)}) collective-permute-start(bf16[4,1,32,256]{3,2,1,0:T(8,128)(2,1)S(1)} %get-tuple-element.39), channel_id=1, source_target_pairs={{0,1},{1,2},{2,3},{3,4},{4,5},{5,6},{6,7},{7,0},{8,9},{9,10},{10,1... | collective-permute-start | bytes 196616 | tf_op jit(solution)/shard_map/ppermute | solution.py:13
  49.6 2.5 %first_inner.1 = (f32[6,16,32,256]{3,2,1,0:T(8,128)S(1)}, f32[4,16,256]{2,1,0:T(8,128)S(1)}) custom-call(bf16[6,16,32,256]{3,2,1,0:T(8,128)(2,1)S(1)} %conv_inner.1.inner, bf16[6,1,32,256]{3,2,1,0:T(8,128)(2,1)S(1)} %collective-permute-done.12.i_lo, bf16[6,1,32,256]{3,2,1,0:T(8,128)(2,1)S(1)} %collective-permute-done.13.i_hi, f32[2]{0:T(128)S(1)} %add_convert_fusion.flags, ...), custom_call_target="tpu_custom_call" | custom-call | tf_op jit(solution)/shard_map/first_inner/pallas_call | solution.py:397
  52.1 2.0 %first_edge.1.first = f32[8,16,256]{2,1,0:T(8,128)S(1)} custom-call(bf16[6,16,32,256]{3,2,1,0:T(8,128)(2,1)S(1)} %conv_inner.1.inner, bf16[4,16,32,256]{3,2,1,0:T(8,128)(2,1)S(1)} %conv_edge.1.edge, bf16[4,1,32,256]{3,2,1,0:T(8,128)(2,1)S(1)} %collective-permute-done.10.e_lo, bf16[4,1,32,256]{3,2,1,0:T(8,128)(2,1)S(1)} %collective-permute-done.11.e_hi, ...), custom_call_target="tpu_custom_call" | custom-call | tf_op jit(solution)/shard_map/first_edge/pallas_call | solution.py:410
  54.1 1.1 %collective-permute-start.14 = (f32[8,1,256]{2,1,0:T(1,128)S(1)}, f32[8,1,256]{2,1,0:T(1,128)S(1)}, u32[]{:S(2)}, u32[]{:S(2)}) collective-permute-start(f32[8,1,256]{2,1,0:T(1,128)S(1)} %get-tuple-element.52), channel_id=1, source_target_pairs={{0,1},{1,2},{2,3},{3,4},{4,5},{5,6},{6,7},{7,0},{8,9},{9,10},{10,1... | collective-permute-start | bytes 24584 | tf_op jit(solution)/shard_map/ppermute | solution.py:13
  55.3 2.5 %collective-permute-start.15 = (f32[8,1,256]{2,1,0:T(1,128)S(1)}, f32[8,1,256]{2,1,0:T(1,128)S(1)}, u32[]{:S(2)}, u32[]{:S(2)}) collective-permute-start(f32[8,1,256]{2,1,0:T(1,128)S(1)} %get-tuple-element.53), channel_id=1, source_target_pairs={{0,7},{1,0},{2,1},{3,2},{4,3},{5,4},{6,5},{7,6},{8,15},{9,8},{10,9... | collective-permute-start | bytes 24584 | tf_op jit(solution)/shard_map/ppermute | solution.py:13
  57.8 0.6 collective-permute-done.14.w_lo
  58.4 0.2 collective-permute-done.15.w_hi
  58.6 0.3 collective-permute-start.16
  58.9 4.8 %collective-permute-start.17 = (f32[1,18,256]{2,1,0:T(8,128)S(1)}, f32[1,18,256]{2,1,0:T(8,128)S(1)}, u32[]{:S(2)}, u32[]{:S(2)}) collective-permute-start(f32[1,18,256]{2,1,0:T(8,128)S(1)} %maximum_bitcast_fusion.1), channel_id=1, source_target_pairs={{0,120},{8,0},{16,8},{24,16},{32,24},{40,32},{48,40},{56,48},{64,5... | collective-permute-start | bytes 55304 | tf_op jit(solution)/shard_map/ppermute | solution.py:13
  63.7 3.9 %second_inner.1 = (f32[8,16,32,256]{3,2,1,0:T(8,128)S(1)}, f32[6,16,256]{2,1,0:T(8,128)S(1)}, f32[10,16,256]{2,1,0:T(8,128)S(1)}) custom-call(bf16[6,16,32,256]{3,2,1,0:T(8,128)(2,1)S(1)} %conv_inner.1.inner, bf16[4,16,32,256]{3,2,1,0:T(8,128)(2,1)S(1)} %conv_edge.1.edge, bf16[6,1,32,256]{3,2,1,0:T(8,128)(2,1)S(1)} %collective-permute-done.12.i_lo, ...), custom_call_target="tpu_custom_call" | custom-call | tf_op jit(solution)/shard_map/second_inner/pallas_call | solution.py:430
  67.5 1.8 %second_edge.1 = (f32[2,16,256]{2,1,0:T(8,128)S(1)}, f32[1,128]{1,0:T(1,128)S(1)}) custom-call(bf16[4,16,32,256]{3,2,1,0:T(8,128)(2,1)S(1)} %conv_edge.1.edge, bf16[4,1,32,256]{3,2,1,0:T(8,128)(2,1)S(1)} %collective-permute-done.10.e_lo, bf16[4,1,32,256]{3,2,1,0:T(8,128)(2,1)S(1)} %collective-permute-done.11.e_hi, f32[2]{0:T(128)S(1)} %add_convert_fusion.flags, ...), custom_call_target="tpu_custom_call" | custom-call | tf_op jit(solution)/shard_map/second_edge/pallas_call | solution.py:442
  69.4 18.5 %all_to_all.5 = f32[128,1,128]{2,1,0:T(1,128)S(1)} all-to-all(f32[128,1,128]{2,1,0:T(1,128)S(1)} %broadcast_in_dim.25), channel_id=1, replica_groups=mesh['sx'=16,'sy'=8] {'sx','sy'}, dimensions={0} | all-to-all | bytes 131072 | tf_op jit(solution)/shard_map/all_to_all | solution.py:452
  87.9 0.9 %final.1 = (f32[8,16,256]{2,1,0:T(8,128)}, f32[8,16,256]{2,1,0:T(8,128)}) custom-call(f32[128,128]{1,0:T(8,128)S(1)} %bitcast.61, f32[8,16,256]{2,1,0:T(8,128)S(1)} %get-tuple-element.49.start, f32[8,16,256]{2,1,0:T(8,128)S(1)} %first_edge.1.first, f32[6,16,256]{2,1,0:T(8,128)S(1)} %get-tuple-element.30.inside, f32[2,16,256]{2,1,0:T(8,128)S(1)} %get-tuple-element.31.sides), custom_call_target="tpu_custom_call" | custom-call | tf_op jit(solution)/shard_map/final/pallas_call | solution.py:454
  (68 shorter events, 1.0 us)
Async XLA Ops:
  0.6 6.1 %copy-start.5 = (s32[8,16,2,27]{3,2,1,0:T(2,128)S(1)}, s32[8,16,2,27]{3,2,1,0:T(2,128)}, u32[]{:S(2)}) copy-start(s32[8,16,2,27]{3,2,1,0:T(2,128)} %param.11) | copy-start | bytes 82948
  1.7 5.7 %copy-start.3 = (s32[8,16,256]{2,1,0:T(8,128)S(1)}, s32[8,16,256]{2,1,0:T(8,128)}, u32[]{:S(2)}) copy-start(s32[8,16,256]{2,1,0:T(8,128)} %param.10) | copy-start | bytes 393220
  1.7 5.7 %copy-start.4 = (f32[8,16,256]{2,1,0:T(8,128)S(1)}, f32[8,16,256]{2,1,0:T(8,128)}, u32[]{:S(2)}) copy-start(f32[8,16,256]{2,1,0:T(8,128)} %param.13) | copy-start | bytes 393220
  1.7 8.8 %copy-start.2 = (bf16[27,32,32]{2,1,0:T(8,128)(2,1)S(1)}, bf16[27,32,32]{2,1,0:T(8,128)(2,1)}, u32[]{:S(2)}) copy-start(bf16[27,32,32]{2,1,0:T(8,128)(2,1)} %param.8) | copy-start | bytes 165892
  4.0 27.6 %collective-permute-start = (bf16[8,1,32,256]{3,2,1,0:T(8,128)(2,1)S(1)}, bf16[8,1,32,256]{3,2,1,0:T(8,128)(2,1)S(1)}, u32[]{:S(2)}, u32[]{:S(2)}) collective-permute-start(bf16[8,1,32,256]{3,2,1,0:T(8,128)(2,1)S(1)} %get-tuple-element.17), channel_id=1, source_target_pairs={{0,1},{1,2},{2,3},{3,4},{4,5},{5,6},{6,7},{7,0},{8,9},{9,10},{10,1... | collective-permute-start | bytes 393224 | tf_op jit(solution)/shard_map/ppermute | solution.py:13
  6.7 24.9 %collective-permute-start.1 = (bf16[8,1,32,256]{3,2,1,0:T(8,128)(2,1)S(1)}, bf16[8,1,32,256]{3,2,1,0:T(8,128)(2,1)S(1)}, u32[]{:S(2)}, u32[]{:S(2)}) collective-permute-start(bf16[8,1,32,256]{3,2,1,0:T(8,128)(2,1)S(1)} %get-tuple-element.18), channel_id=1, source_target_pairs={{0,7},{1,0},{2,1},{3,2},{4,3},{5,4},{6,5},{7,6},{8,15},{9,8},{10,9... | collective-permute-start | bytes 393224 | tf_op jit(solution)/shard_map/ppermute | solution.py:13
  7.4 7.4 %collective-permute-start.6 = (f32[2,8,1,256]{3,2,1,0:T(1,128)S(1)}, f32[2,8,1,256]{3,2,1,0:T(1,128)S(1)}, u32[]{:S(2)}, u32[]{:S(2)}) collective-permute-start(f32[2,8,1,256]{3,2,1,0:T(1,128)S(1)} %get-tuple-element.46), channel_id=1, source_target_pairs={{0,1},{1,2},{2,3},{3,4},{4,5},{5,6},{6,7},{7,0},{8,9},{9,10},{10,1... | collective-permute-start | bytes 49160 | tf_op jit(solution)/shard_map/ppermute | solution.py:13
  9.2 10.5 %collective-permute-start.7 = (f32[2,8,1,256]{3,2,1,0:T(1,128)S(1)}, f32[2,8,1,256]{3,2,1,0:T(1,128)S(1)}, u32[]{:S(2)}, u32[]{:S(2)}) collective-permute-start(f32[2,8,1,256]{3,2,1,0:T(1,128)S(1)} %get-tuple-element.47), channel_id=1, source_target_pairs={{0,7},{1,0},{2,1},{3,2},{4,3},{5,4},{6,5},{7,6},{8,15},{9,8},{10,9... | collective-permute-start | bytes 49160 | tf_op jit(solution)/shard_map/ppermute | solution.py:13
  9.2 36.5 %collective-permute-start.2 = (bf16[2,16,32,256]{3,2,1,0:T(8,128)(2,1)}, bf16[2,16,32,256]{3,2,1,0:T(8,128)(2,1)S(1)}, u32[]{:S(2)}, u32[]{:S(2)}) collective-permute-start(bf16[2,16,32,256]{3,2,1,0:T(8,128)(2,1)} %get-tuple-element.19), channel_id=1, source_target_pairs={{0,8},{8,16},{16,24},{24,32},{32,40},{40,48},{48,56},{56,64},{64,7... | collective-permute-start | bytes 1572872 | tf_op jit(solution)/shard_map/ppermute | solution.py:13
  11.4 1.7 %copy-start.6 = (f32[32]{0:T(128)S(1)}, f32[32]{0:T(128)}, u32[]{:S(2)}) copy-start(f32[32]{0:T(128)} %param.9) | copy-start | bytes 388
  14.8 30.9 %collective-permute-start.3 = (bf16[2,16,32,256]{3,2,1,0:T(8,128)(2,1)}, bf16[2,16,32,256]{3,2,1,0:T(8,128)(2,1)S(1)}, u32[]{:S(2)}, u32[]{:S(2)}) collective-permute-start(bf16[2,16,32,256]{3,2,1,0:T(8,128)(2,1)} %get-tuple-element.20), channel_id=1, source_target_pairs={{0,120},{8,0},{16,8},{24,16},{32,24},{40,32},{48,40},{56,48},{64,5... | collective-permute-start | bytes 1572872 | tf_op jit(solution)/shard_map/ppermute | solution.py:13
  19.7 16.9 %copy-start = (bf16[8,16,32,256]{3,2,1,0:T(8,128)(2,1)S(1)}, bf16[8,16,32,256]{3,2,1,0:T(8,128)(2,1)}, u32[]{:S(2)}) copy-start(bf16[8,16,32,256]{3,2,1,0:T(8,128)(2,1)} %own.3) | copy-start | bytes 6291460
  19.8 8.3 %collective-permute-start.8 = (f32[2,2,18,256]{3,2,1,0:T(8,128)S(1)}, f32[2,2,18,256]{3,2,1,0:T(8,128)S(1)}, u32[]{:S(2)}, u32[]{:S(2)}) collective-permute-start(f32[2,2,18,256]{3,2,1,0:T(8,128)S(1)} %get-tuple-element.44), channel_id=1, source_target_pairs={{0,8},{8,16},{16,24},{24,32},{32,40},{40,48},{48,56},{56,64},{64,7... | collective-permute-start | bytes 221192 | tf_op jit(solution)/shard_map/ppermute | solution.py:13
  28.1 3.5 %collective-permute-start.9 = (f32[2,2,18,256]{3,2,1,0:T(8,128)S(1)}, f32[2,2,18,256]{3,2,1,0:T(8,128)S(1)}, u32[]{:S(2)}, u32[]{:S(2)}) collective-permute-start(f32[2,2,18,256]{3,2,1,0:T(8,128)S(1)} %get-tuple-element.45), channel_id=1, source_target_pairs={{0,120},{8,0},{16,8},{24,16},{32,24},{40,32},{48,40},{56,48},{64,5... | collective-permute-start | bytes 221192 | tf_op jit(solution)/shard_map/ppermute | solution.py:13
  31.7 14.0 %collective-permute-start.4 = (bf16[2,2,32,256]{3,2,1,0:T(8,128)(2,1)S(1)}, bf16[2,2,32,256]{3,2,1,0:T(8,128)(2,1)S(1)}, u32[]{:S(2)}, u32[]{:S(2)}) collective-permute-start(bf16[2,2,32,256]{3,2,1,0:T(8,128)(2,1)S(1)} %pad_maximum_fusion.5), channel_id=1, source_target_pairs={{0,8},{8,16},{16,24},{24,32},{32,40},{40,48},{48,56},{56,64},{64,7... | collective-permute-start | bytes 196616 | tf_op jit(solution)/shard_map/ppermute | solution.py:13
  31.8 13.9 %collective-permute-start.5 = (bf16[2,2,32,256]{3,2,1,0:T(8,128)(2,1)S(1)}, bf16[2,2,32,256]{3,2,1,0:T(8,128)(2,1)S(1)}, u32[]{:S(2)}, u32[]{:S(2)}) collective-permute-start(bf16[2,2,32,256]{3,2,1,0:T(8,128)(2,1)S(1)} %pad_maximum_fusion.6), channel_id=1, source_target_pairs={{0,120},{8,0},{16,8},{24,16},{32,24},{40,32},{48,40},{56,48},{64,5... | collective-permute-start | bytes 196616 | tf_op jit(solution)/shard_map/ppermute | solution.py:13
  40.3 9.2 %collective-permute-start.13 = (bf16[6,1,32,256]{3,2,1,0:T(8,128)(2,1)S(1)}, bf16[6,1,32,256]{3,2,1,0:T(8,128)(2,1)S(1)}, u32[]{:S(2)}, u32[]{:S(2)}) collective-permute-start(bf16[6,1,32,256]{3,2,1,0:T(8,128)(2,1)S(1)} %get-tuple-element.36), channel_id=1, source_target_pairs={{0,7},{1,0},{2,1},{3,2},{4,3},{5,4},{6,5},{7,6},{8,15},{9,8},{10,9... | collective-permute-start | bytes 294920 | tf_op jit(solution)/shard_map/ppermute | solution.py:13
  45.7 3.9 %copy-start.1 = (f32[8,16,256]{2,1,0:T(8,128)S(1)}, f32[8,16,256]{2,1,0:T(8,128)}, u32[]{:S(2)}) copy-start(f32[8,16,256]{2,1,0:T(8,128)} %ridge.7) | copy-start | bytes 393220
  45.7 3.8 %collective-permute-start.12 = (bf16[6,1,32,256]{3,2,1,0:T(8,128)(2,1)S(1)}, bf16[6,1,32,256]{3,2,1,0:T(8,128)(2,1)S(1)}, u32[]{:S(2)}, u32[]{:S(2)}) collective-permute-start(bf16[6,1,32,256]{3,2,1,0:T(8,128)(2,1)S(1)} %get-tuple-element.37), channel_id=1, source_target_pairs={{0,1},{1,2},{2,3},{3,4},{4,5},{5,6},{6,7},{7,0},{8,9},{9,10},{10,1... | collective-permute-start | bytes 294920 | tf_op jit(solution)/shard_map/ppermute | solution.py:13
  47.8 4.3 %collective-permute-start.11 = (bf16[4,1,32,256]{3,2,1,0:T(8,128)(2,1)S(1)}, bf16[4,1,32,256]{3,2,1,0:T(8,128)(2,1)S(1)}, u32[]{:S(2)}, u32[]{:S(2)}) collective-permute-start(bf16[4,1,32,256]{3,2,1,0:T(8,128)(2,1)S(1)} %get-tuple-element.38), channel_id=1, source_target_pairs={{0,7},{1,0},{2,1},{3,2},{4,3},{5,4},{6,5},{7,6},{8,15},{9,8},{10,9... | collective-permute-start | bytes 196616 | tf_op jit(solution)/shard_map/ppermute | solution.py:13
  48.3 3.8 %collective-permute-start.10 = (bf16[4,1,32,256]{3,2,1,0:T(8,128)(2,1)S(1)}, bf16[4,1,32,256]{3,2,1,0:T(8,128)(2,1)S(1)}, u32[]{:S(2)}, u32[]{:S(2)}) collective-permute-start(bf16[4,1,32,256]{3,2,1,0:T(8,128)(2,1)S(1)} %get-tuple-element.39), channel_id=1, source_target_pairs={{0,1},{1,2},{2,3},{3,4},{4,5},{5,6},{6,7},{7,0},{8,9},{9,10},{10,1... | collective-permute-start | bytes 196616 | tf_op jit(solution)/shard_map/ppermute | solution.py:13
  54.1 4.3 %collective-permute-start.14 = (f32[8,1,256]{2,1,0:T(1,128)S(1)}, f32[8,1,256]{2,1,0:T(1,128)S(1)}, u32[]{:S(2)}, u32[]{:S(2)}) collective-permute-start(f32[8,1,256]{2,1,0:T(1,128)S(1)} %get-tuple-element.52), channel_id=1, source_target_pairs={{0,1},{1,2},{2,3},{3,4},{4,5},{5,6},{6,7},{7,0},{8,9},{9,10},{10,1... | collective-permute-start | bytes 24584 | tf_op jit(solution)/shard_map/ppermute | solution.py:13
  55.3 3.3 %collective-permute-start.15 = (f32[8,1,256]{2,1,0:T(1,128)S(1)}, f32[8,1,256]{2,1,0:T(1,128)S(1)}, u32[]{:S(2)}, u32[]{:S(2)}) collective-permute-start(f32[8,1,256]{2,1,0:T(1,128)S(1)} %get-tuple-element.53), channel_id=1, source_target_pairs={{0,7},{1,0},{2,1},{3,2},{4,3},{5,4},{6,5},{7,6},{8,15},{9,8},{10,9... | collective-permute-start | bytes 24584 | tf_op jit(solution)/shard_map/ppermute | solution.py:13
  58.6 8.9 %collective-permute-start.16 = (f32[1,18,256]{2,1,0:T(8,128)S(1)}, f32[1,18,256]{2,1,0:T(8,128)S(1)}, u32[]{:S(2)}, u32[]{:S(2)}) collective-permute-start(f32[1,18,256]{2,1,0:T(8,128)S(1)} %maximum_bitcast_fusion), channel_id=1, source_target_pairs={{0,8},{8,16},{16,24},{24,32},{32,40},{40,48},{48,56},{56,64},{64,7... | collective-permute-start | bytes 55304 | tf_op jit(solution)/shard_map/ppermute | solution.py:13
  58.9 8.6 %collective-permute-start.17 = (f32[1,18,256]{2,1,0:T(8,128)S(1)}, f32[1,18,256]{2,1,0:T(8,128)S(1)}, u32[]{:S(2)}, u32[]{:S(2)}) collective-permute-start(f32[1,18,256]{2,1,0:T(8,128)S(1)} %maximum_bitcast_fusion.1), channel_id=1, source_target_pairs={{0,120},{8,0},{16,8},{24,16},{32,24},{40,32},{48,40},{56,48},{64,5... | collective-permute-start | bytes 55304 | tf_op jit(solution)/shard_map/ppermute | solution.py:13

commit v3 on v2

--- a/solution.py
+++ b/solution.py
@@ -17,13 +17,6 @@
     length = value.shape[dim]
     before = shift(lax.slice_in_dim(value, length - width, length, axis=dim), axis, 1)
     after = shift(lax.slice_in_dim(value, 0, width, axis=dim), axis, -1)
-    return before, after
-
-
-def clear_ends(before, after, axis):
-    where = lax.axis_index(axis)
-    before = jnp.where(where == 0, jnp.zeros_like(before), before)
-    after = jnp.where(where == lax.axis_size(axis) - 1, jnp.zeros_like(after), after)
     return before, after
 
 
@@ -40,7 +33,7 @@
     return block.reshape(3 * 4 * channels, 16 * channels)
 
 
-def conv_block(grid, mask, wide, bias_all, lane, grid_x, mask_x, y, out, out_x):
+def conv_block(grid, masks, wide, bias_all, lane, grid_x, y, out, out_x):
     channels, depth = bias_all.shape
     window = jnp.concatenate(
         [grid[grid_x + k, y : y + 4].reshape(4 * channels, depth) for k in range(4)], axis=0
@@ -53,60 +46,118 @@
     for step_x in range(2):
         for step_y in range(2):
             at = (step_x * 2 + step_y) * channels
-            at_y = y + step_y + 1
-            keep = mask[mask_x + step_x + 1, at_y : at_y + 1, :]
+            keep = masks[step_x](y + step_y)
             value = keep * (total[at : at + channels] + bias_all)
             out[out_x + step_x, y + step_y] = value.astype(jnp.bfloat16)
 
 
-def mask_columns(grid, grid_x, mask, mask_x, pieces):
-    for y, ref, x, at in pieces:
-        grid[grid_x, y] = ref[x, at] * mask[mask_x, y : y + 1, :].astype(jnp.bfloat16)
-
-
-def own_pieces(own, y_lo, y_hi, x):
-    cols = own.shape[1]
-    inner = [(y + 1, own, x, y) for y in range(cols)]
-    return [(0, y_lo, x, 0)] + inner + [(cols + 1, y_hi, x, 0)]
-
-
-def side_pieces(side, corner, x):
-    cols = side.shape[1]
-    inner = [(y + 1, side, x, y) for y in range(cols)]
-    return [(0, corner, x, 0)] + inner + [(cols + 1, corner, x, 1)]
-
-
-def conv_inner_kernel(own, y_lo, y_hi, mask, wide, bias, out, grid):
+def as_bf16(row, flag):
+    return (row * flag).astype(jnp.bfloat16)
+
+
+def fill_row(grid, grid_x, mask, middle, low, high):
+    cols = grid.shape[1] - 2
+    grid[grid_x, 0] = low
+    for y in range(cols):
+        grid[grid_x, y + 1] = middle(y) * mask(y).astype(jnp.bfloat16)
+    grid[grid_x, cols + 1] = high
+
+
+def fill_own(grid, grid_x, own, mask, y_lo, y_hi, m_lo, m_hi, flags, x):
+    low = y_lo[x, 0] * as_bf16(m_lo[0, x], flags[0])
+    high = y_hi[x, 0] * as_bf16(m_hi[0, x], flags[1])
+    fill_row(grid, grid_x, mask_of(mask, x), lambda y: own[x, y], low, high)
+
+
+def mask_of(mask, x):
+    return lambda y: mask[x, y : y + 1, :]
+
+
+def conv_inner_kernel(own, y_lo, y_hi, m_lo, m_hi, mask, flags, wide, bias, out, grid):
     rows, cols, channels, depth = own.shape
 
-    def mask_row(x, carry):
-        mask_columns(grid, x, mask, x, own_pieces(own, y_lo, y_hi, x))
+    def fill(x, carry):
+        fill_own(grid, x, own, mask, y_lo, y_hi, m_lo, m_hi, flags, x)
         return carry
 
-    lax.fori_loop(0, rows, mask_row, 0)
+    lax.fori_loop(0, rows, fill, 0)
     lane = lax.broadcasted_iota(jnp.int32, (4 * channels, depth), 1)
     bias_all = jnp.broadcast_to(bias[...], (channels, depth))
 
     def pair(i, carry):
+        masks = (mask_of(mask, 2 * i + 1), mask_of(mask, 2 * i + 2))
         for y in range(0, cols, 2):
-            conv_block(grid, mask, wide, bias_all, lane, 2 * i, 2 * i, y, out, 2 * i)
+            conv_block(grid, masks, wide, bias_all, lane, 2 * i, y, out, 2 * i)
         return carry
 
     lax.fori_loop(0, rows // 2 - 1, pair, 0)
 
 
-def conv_edge_kernel(own, y_lo, y_hi, x_lo, x_hi, c_lo, c_hi, mask, wide, bias, out, grid):
+def sides_kernel(y_lo, y_hi, m_lo, m_hi, mask, start, flags, out_hi, out_lo):
+    rows, cols, depth = mask.shape
+
+    def three(value):
+        high = value.astype(jnp.bfloat16).astype(jnp.float32)
+        rest = value - high
+        mid = rest.astype(jnp.bfloat16).astype(jnp.float32)
+        return high, mid, rest - mid
+
+    for out, pair, row in ((out_hi, (rows - 2, rows - 1), rows - 1), (out_lo, (0, 1), 0)):
+        for k, x in enumerate(pair):
+            out[2 * k] = y_lo[x, 0] * as_bf16(m_lo[0, x], flags[0])
+            out[2 * k + 1] = y_hi[x, 0] * as_bf16(m_hi[0, x], flags[1])
+        out[4] = jnp.concatenate([mask[x] for x in pair], axis=0).astype(jnp.bfloat16)
+        high, mid, low = three(start[row])
+        rims = three(jnp.concatenate([m_lo[1, row], m_hi[1, row]], axis=0))
+        blank = jnp.zeros((10, depth), jnp.float32)
+        out[5] = jnp.concatenate([high, mid], axis=0).astype(jnp.bfloat16)
+        out[6] = jnp.concatenate([low, *rims, blank], axis=0).astype(jnp.bfloat16)
+
+
+def conv_edge_kernel(
+    own,
+    y_lo,
+    y_hi,
+    m_lo,
+    m_hi,
+    x_lo,
+    x_hi,
+    side_lo,
+    side_hi,
+    mask,
+    flags,
+    wide,
+    bias,
+    out,
+    grid,
+    side_mask,
+):
     rows, cols, channels, depth = own.shape
+    for k, side in enumerate((side_lo, side_hi)):
+        both = side[4].astype(jnp.float32) * flags[2 + k]
+        side_mask[2 * k] = both[:cols]
+        side_mask[2 * k + 1] = both[cols:]
     for x in range(2):
-        mask_columns(grid, x, mask, x, side_pieces(x_lo, c_lo, x))
-        mask_columns(grid, 2 + x, mask, 2 + x, own_pieces(own, y_lo, y_hi, x))
-        mask_columns(grid, 4 + x, mask, rows + x, own_pieces(own, y_lo, y_hi, rows - 2 + x))
-        mask_columns(grid, 6 + x, mask, rows + 2 + x, side_pieces(x_hi, c_hi, x))
+        for k, ref, side in ((0, x_lo, side_lo), (1, x_hi, side_hi)):
+            clear = jnp.full((channels, depth), flags[2 + k], jnp.float32).astype(jnp.bfloat16)
+            fill_row(
+                grid,
+                6 * k + x,
+                mask_of(side_mask, 2 * k + x),
+                lambda y: ref[x, y],
+                side[2 * x] * clear,
+                side[2 * x + 1] * clear,
+            )
+        fill_own(grid, 2 + x, own, mask, y_lo, y_hi, m_lo, m_hi, flags, x)
+        fill_own(grid, 4 + x, own, mask, y_lo, y_hi, m_lo, m_hi, flags, rows - 2 + x)
     lane = lax.broadcasted_iota(jnp.int32, (4 * channels, depth), 1)
     bias_all = jnp.broadcast_to(bias[...], (channels, depth))
-    for side in range(2):
+    for side, masks in (
+        (0, (mask_of(side_mask, 1), mask_of(mask, 0))),
+        (1, (mask_of(mask, rows - 1), mask_of(side_mask, 2))),
+    ):
         for y in range(0, cols, 2):
-            conv_block(grid, mask, wide, bias_all, lane, 4 * side, rows * side, y, out, 2 * side)
+            conv_block(grid, masks, wide, bias_all, lane, 4 * side, y, out, 2 * side)
 
 
 def two_sum(a, b):
@@ -163,16 +214,20 @@
 
     def at(y):
         if y == 0:
-            return lo[x]
+            return lo(x)
         if y == cols + 1:
-            return hi[x]
+            return hi(x)
         return own[x, y - 1 : y, :]
 
     return at
 
 
 def side_row(side):
-    return lambda y: side[0, y : y + 1, :]
+    return lambda y: side[y : y + 1, :]
+
+
+def rim_of(ref, *index):
+    return lambda x: ref[(*index, x)]
 
 
 def along_x(before, here, after, field, row, ridge_row, value_row):
@@ -192,8 +247,9 @@
     return ridge_row * value_row + inner * (1.0 / (8 * channels))
 
 
-def first_inner_kernel(inner, i_lo, i_hi, flags, start, s_lo, s_hi, ridge, smooth, out):
+def first_inner_kernel(inner, i_lo, i_hi, flags, start, m_lo, m_hi, ridge, smooth, out):
     rows = inner.shape[0]
+    s_lo, s_hi = (rim_of(m_lo, 1), rim_of(m_hi, 1))
 
     def stage_y(k, carry):
         along_y(smooth, k, inner, i_lo, i_hi, k, flags, own_row(start, s_lo, s_hi, k + 1))
@@ -211,14 +267,49 @@
 
 
 def first_edge_kernel(
-    inner, edge, e_lo, e_hi, flags, start, s_lo, s_hi, x_lo, x_hi, ridge, smooth, part, out, rim
+    inner,
+    edge,
+    e_lo,
+    e_hi,
+    flags,
+    start,
+    m_lo,
+    m_hi,
+    side_lo,
+    side_hi,
+    ridge,
+    smooth,
+    part,
+    out,
+    rim,
+    side_start,
+    side_rims,
 ):
     n = inner.shape[0]
     last = n + 1
-    along_y(rim, 0, edge, e_lo, e_hi, 0, flags, side_row(x_lo))
+    cols = inner.shape[1]
+    s_lo, s_hi = (rim_of(m_lo, 1), rim_of(m_hi, 1))
+    for k, side in enumerate((side_lo, side_hi)):
+        upper = side[5].astype(jnp.float32)
+        lower = side[6].astype(jnp.float32)
+        side_start[k] = (upper[:cols] + upper[cols:]) + lower[:cols]
+        ends = lower[cols : cols + 8]
+        side_rims[k, 0:2] = (ends[0:2] + ends[2:4]) + ends[4:6]
+
+    def side_values(k):
+        def at(y):
+            if y == 0:
+                return side_rims[k, 0:1]
+            if y == cols + 1:
+                return side_rims[k, 1:2]
+            return side_start[k, y - 1 : y]
+
+        return at
+
+    along_y(rim, 0, edge, e_lo, e_hi, 0, flags, side_values(0))
     along_y(rim, 1, edge, e_lo, e_hi, 1, flags, own_row(start, s_lo, s_hi, 0))
     along_y(rim, 2, edge, e_lo, e_hi, 2, flags, own_row(start, s_lo, s_hi, last))
-    along_y(rim, 3, edge, e_lo, e_hi, 3, flags, side_row(x_hi))
+    along_y(rim, 3, edge, e_lo, e_hi, 3, flags, side_values(1))
     for x, before, here, after, field, row in (
         (0, (rim, 0), (rim, 1), (smooth, 0), edge, 1),
         (1, (rim, 1), (smooth, 0), (smooth, 1), inner, 0),
@@ -245,6 +336,7 @@
     inner, edge, i_lo, i_hi, e_lo, e_hi, flags, start, first, w_lo, w_hi, ridge, smooth, out, grams
 ):
     n = inner.shape[0]
+    w_lo, w_hi = (rim_of(w_lo), rim_of(w_hi))
 
     def stage_y(k, carry):
         along_y(smooth, k + 1, inner, i_lo, i_hi, k, flags, own_row(first, w_lo, w_hi, k + 1))
@@ -364,35 +456,41 @@
             name=name,
         )
 
-    edges = (features[-2:], features[:2], features[:, -1:], features[:, :1])
+    edges = (features[-2:], features[:2])
     edges, occupancy, block_ids, target, conv_weight = lax.optimization_barrier(
         (edges, occupancy, block_ids, target, conv_weight)
     )
     x_lo, x_hi = (shift(edges[0], "sx", 1), shift(edges[1], "sx", -1))
-    y_lo, y_hi = (shift(edges[2], "sy", 1), shift(edges[3], "sy", -1))
-    c_lo = shift(jnp.concatenate([y_lo[-2:], y_hi[-2:]], axis=1), "sx", 1)
-    c_hi = shift(jnp.concatenate([y_lo[:2], y_hi[:2]], axis=1), "sx", -1)
 
     present = (block_ids[:, :, :, 13] >= 0).astype(f32)
     weight_mask = occupancy.astype(f32) * jnp.repeat(present, voxels, axis=2)
     residual = weight_mask * target
-    both = jnp.stack([weight_mask, residual])
-    both_lo, both_hi = clear_ends(*halo(both, "sy", 2, 1), "sy")
-    both_y = jnp.concatenate([both_lo, both, both_hi], axis=2)
-    side_lo, side_hi = clear_ends(*halo(both_y, "sx", 1, 2), "sx")
-    mask_y = both_y[0]
-    mask_all = jnp.concatenate([side_lo[0], mask_y, side_hi[0]], axis=0)
-    where = lax.axis_index("sy")
-    flags = jnp.stack([where > 0, where < lax.axis_size("sy") - 1]).astype(f32)
+    y_lo, y_hi = halo(features, "sy", 1, 1)
+    weight_mask, residual, y_lo, y_hi = lax.optimization_barrier(
+        (weight_mask, residual, y_lo, y_hi)
+    )
+    m_lo, m_hi = halo(jnp.stack([weight_mask, residual]), "sy", 2, 1)
+    flags = jnp.stack(
+        [
+            keep
+            for axis in ("sy", "sx")
+            for keep in (lax.axis_index(axis) > 0, lax.axis_index(axis) < lax.axis_size(axis) - 1)
+        ]
+    ).astype(f32)
 
     wide = block_weights(conv_weight)
     bias = conv_bias[:, None]
-    grid_scratch = [((rows, cols + 2, channels, depth), bf16)]
+    grid_scratch = ((rows, cols + 2, channels, depth), bf16)
     inner_shape = (rows - 2, cols, channels, depth)
     edge_shape = (4, cols, channels, depth)
-    (inner,) = call(conv_inner_kernel, "vvvvvv", [(inner_shape, bf16)], grid_scratch, 12, "conv_inner")(
-        features, y_lo, y_hi, mask_y, wide, bias
-    )
+    side_shape = (7, channels, depth)
+    side_hi, side_lo = call(
+        sides_kernel, "vvvvvvs", [(side_shape, bf16), (side_shape, bf16)], [], 4, "sides"
+    )(y_lo, y_hi, m_lo, m_hi, weight_mask, residual, flags)
+    side_lo, side_hi = (shift(side_hi, "sx", 1), shift(side_lo, "sx", -1))
+    (inner,) = call(
+        conv_inner_kernel, "vvvvvvsvv", [(inner_shape, bf16)], [grid_scratch], 12, "conv_inner"
+    )(features, y_lo, y_hi, m_lo, m_hi, weight_mask, flags, wide, bias)
     i_lo, i_hi = halo(inner, "sy", 1, 1)
     smooth, part = call(
         first_inner_kernel,
@@ -401,14 +499,24 @@
         [],
         8,
         "first_inner",
-    )(inner, i_lo, i_hi, flags, residual, both_lo[1], both_hi[1], ridge)
-    (edge,) = call(conv_edge_kernel, "vvvvvvvvvv", [(edge_shape, bf16)], grid_scratch, 12, "conv_edge")(
-        features, y_lo, y_hi, x_lo, x_hi, c_lo, c_hi, mask_all, wide, bias
-    )
+    )(inner, i_lo, i_hi, flags, residual, m_lo, m_hi, ridge)
+    (edge,) = call(
+        conv_edge_kernel,
+        "vvvvvvvvvvsvv",
+        [(edge_shape, bf16)],
+        [grid_scratch, ((4, cols, depth), f32)],
+        12,
+        "conv_edge",
+    )(features, y_lo, y_hi, m_lo, m_hi, x_lo, x_hi, side_lo, side_hi, weight_mask, flags, wide, bias)
     e_lo, e_hi = halo(edge, "sy", 1, 1)
     plane = ((rows, cols, depth), f32)
     (first,) = call(
-        first_edge_kernel, "vvvvsvvvvvvvv", [plane], [(edge_shape, f32)], 8, "first_edge"
+        first_edge_kernel,
+        "vvvvsvvvvvvvv",
+        [plane],
+        [(edge_shape, f32), ((2, cols, depth), f32), ((2, 8, depth), f32)],
+        8,
+        "first_edge",
     )(
         inner,
         edge,
@@ -416,16 +524,16 @@
         e_hi,
         flags,
         residual,
-        both_lo[1],
-        both_hi[1],
-        side_lo[1, 1:],
-        side_hi[1, :1],
+        m_lo,
+        m_hi,
+        side_lo,
+        side_hi,
         ridge,
         smooth,
         part,
     )
     w_lo, w_hi = halo(first, "sy", 1, 1)
-    rims = [jnp.concatenate([w_lo[x], first[x], w_hi[x]], axis=0)[None] for x in (-1, 0)]
+    rims = [jnp.concatenate([w_lo[x], first[x], w_hi[x]], axis=0) for x in (-1, 0)]
     r_lo, r_hi = (shift(rims[0], "sx", 1), shift(rims[1], "sx", -1))
     smooth, inside, grams = call(
         second_inner_kernel,

time: 89 us -> 86.5 us (0.972)
  waiting for transfers between devices: 12.5 us -> 1.79 us
  local copies, waits for them, and re-layouts: 6.74 us -> 11.5 us
  Pallas kernels: 16.8 us -> 19.5 us
  other arithmetic: 1.96 us -> 3.76 us
  starting transfers between devices: 31.3 us -> 29.8 us
    ppermute x18 -> x16, waiting for transfers between devices: 12.5 us -> 1.79 us  [shift(): lax.ppermute(value, axis, [(i, (i + step) % peers) for i in range(peers)])]
    pallas_call x3 -> x4, Pallas kernels: 7.72 us -> 10.3 us  [the longest x1 4.36 us: per_device(): call(conv_inner_kernel, 'vvvvvvsvv', [(inner_shape, bf16)], [grid_scratch...]
    reshape x1, local copies, waits for them, and re-layouts: 1.6 us -> 3.9 us  [block_weights(): return block.reshape(3 * 4 * channels, 16 * channels)]
    unnamed x14 -> x22, local copies, waits for them, and re-layouts: 0.04 us -> 2 us
    ppermute x18 -> x16, starting transfers between devices: 31.3 us -> 29.8 us  [shift(): lax.ppermute(value, axis, [(i, (i + step) % peers) for i in range(peers)])]
    slice x4 -> x1, local copies, waits for them, and re-layouts: 3.35 us -> 2.26 us  [per_device(): edges = (features[-2:], features[:2])]
    slice x2 -> x3, local copies, waits for them, and re-layouts: 0.03 us -> 1.05 us  [halo(): after = shift(lax.slice_in_dim(value, 0, width, axis=dim), axis, -1)]
  transfers between devices with their start and end apart: 18 -> 16, of which waited for: 4 -> 3; matrix products, arithmetic and copies ran while one was open for 6% -> 14% of each run, Pallas kernels for 14% -> 17%
where the time goes in v3:
time: 86.5 us; the launch traced here: 85.8 us
  starting transfers between devices  29.8 us (34%)
  Pallas kernels  19.5 us (23%)
  blocking collectives  18.5 us (21%)
  local copies, waits for them, and re-layouts  11.5 us (13%)
  other arithmetic  3.76 us (4%)
  waiting for transfers between devices  1.79 us (2%)
  between operations  0.98 us (1%)
    ppermute x16, starting transfers between devices, shift(): lax.ppermute(value, axis, [(i, (i + step) % peers) for i in range(peers)])  29.8 us
    all_to_all x1, blocking collectives, per_device(): lax.all_to_all(jnp.broadcast_to(share[None], (peers, 1, 128)), AXES, 0, 0)  18.5 us
    pallas_call x1, Pallas kernels, per_device(): call(conv_inner_kernel, 'vvvvvvsvv', [(inner_shape, bf16)], [grid_scratch...  4.36 us
    reshape x1, local copies, waits for them, and re-layouts, block_weights(): return block.reshape(3 * 4 * channels, 16 * channels)  3.9 us
    pallas_call x1, Pallas kernels, per_device(): call(second_inner_kernel, 'vvvvvvsvvvvv', [((rows, cols, channels, depth)...  3.8 us
    pallas_call x1, Pallas kernels, per_device(): call(conv_edge_kernel, 'vvvvvvvvvvsvv', [(edge_shape, bf16)], [grid_scrat...  3.03 us
    pallas_call x1, Pallas kernels, per_device(): call(first_inner_kernel, 'vvvsvvvv', [(inner_shape, f32), ((rows - 4, col...  2.68 us
    another operation x1, other arithmetic, block_weights(): block = jnp.stack(rows, axis=1)  2.46 us
  transfers between devices with their start and end apart: 16, of which 3 were waited for; matrix products, arithmetic and copies ran while one was open for 14% of the time, Pallas kernels for 17%

profile of v3, /device:TPU:1, one launch (start us, length us, event | category | flops | bytes accessed | tf_op | source)
XLA Modules:
  0.0 85.8 jit_solution(6981816347872422251)
XLA Ops:
  0.6 1.0 %fusion.1 = (bf16[8,1,32,256]{3,2,1,0:T(8,128)(2,1)S(1)}, bf16[8,1,32,256]{3,2,1,0:T(8,128)(2,1)S(1)}) fusion(bf16[8,16,32,256]{3,2,1,0:T(8,128)(2,1)} %own.3), kind=kLoop, calls=%fused_computation.21 | loop fusion | bytes 524288 | tf_op jit(solution)/shard_map/slice | solution.py:19
  1.7 1.4 %collective-permute-start.1 = (bf16[8,1,32,256]{3,2,1,0:T(8,128)(2,1)S(1)}, bf16[8,1,32,256]{3,2,1,0:T(8,128)(2,1)S(1)}, u32[]{:S(2)}, u32[]{:S(2)}) collective-permute-start(bf16[8,1,32,256]{3,2,1,0:T(8,128)(2,1)S(1)} %get-tuple-element.42), channel_id=1, source_target_pairs={{0,7},{1,0},{2,1},{3,2},{4,3},{5,4},{6,5},{7,6},{8,15},{9,8},{10,9... | collective-permute-start | bytes 393224 | tf_op jit(solution)/shard_map/ppermute | solution.py:13
  3.1 1.3 %collective-permute-start = (bf16[8,1,32,256]{3,2,1,0:T(8,128)(2,1)S(1)}, bf16[8,1,32,256]{3,2,1,0:T(8,128)(2,1)S(1)}, u32[]{:S(2)}, u32[]{:S(2)}) collective-permute-start(bf16[8,1,32,256]{3,2,1,0:T(8,128)(2,1)S(1)} %get-tuple-element.43), channel_id=1, source_target_pairs={{0,1},{1,2},{2,3},{3,4},{4,5},{5,6},{6,7},{7,0},{8,9},{9,10},{10,1... | collective-permute-start | bytes 393224 | tf_op jit(solution)/shard_map/ppermute | solution.py:13
  4.4 2.3 %fusion.2 = (bf16[2,16,32,256]{3,2,1,0:T(8,128)(2,1)}, bf16[2,16,32,256]{3,2,1,0:T(8,128)(2,1)}) fusion(bf16[8,16,32,256]{3,2,1,0:T(8,128)(2,1)} %own.3), kind=kLoop, calls=%fused_computation.22 | loop fusion | bytes 2097152 | tf_op jit(solution)/shard_map/slice | solution.py:459
  6.7 1.2 %collective-permute-start.4 = (bf16[2,16,32,256]{3,2,1,0:T(8,128)(2,1)}, bf16[2,16,32,256]{3,2,1,0:T(8,128)(2,1)S(1)}, u32[]{:S(2)}, u32[]{:S(2)}) collective-permute-start(bf16[2,16,32,256]{3,2,1,0:T(8,128)(2,1)} %get-tuple-element.28), channel_id=1, source_target_pairs={{0,8},{8,16},{16,24},{24,32},{32,40},{40,48},{48,56},{56,64},{64,7... | collective-permute-start | bytes 1572872 | tf_op jit(solution)/shard_map/ppermute | solution.py:13
  7.9 4.7 %collective-permute-start.5 = (bf16[2,16,32,256]{3,2,1,0:T(8,128)(2,1)}, bf16[2,16,32,256]{3,2,1,0:T(8,128)(2,1)}, u32[]{:S(2)}, u32[]{:S(2)}) collective-permute-start(bf16[2,16,32,256]{3,2,1,0:T(8,128)(2,1)} %get-tuple-element.29), channel_id=1, source_target_pairs={{0,120},{8,0},{16,8},{24,16},{32,24},{40,32},{48,40},{56,48},{64,5... | collective-permute-start | bytes 1572872 | tf_op jit(solution)/shard_map/ppermute | solution.py:13
  13.4 0.8 pad_bitcast_fusion.3
  14.3 2.5 %pad_maximum_fusion = bf16[3,4,32,4,4,32]{5,4,3,2,1,0:T(4,128)(2,1)} fusion(bf16[3,1,32,4,4,32]{5,4,3,2,1,0:T(4,128)(2,1)S(1)} %get-tuple-element.51, bf16[3,1,32,4,4,32]{5,4,3,2,1,0:T(4,128)(2,1)S(1)} %get-tuple-element.52, bf16[3,1,32,4,4,32]{5,4,3,2,1,0:T(4,128)(2,1)S(1)} %get-tuple-element.53, bf16[3,1,32,4,4,32]{5,4,3,2,1,0:T(4,128)(2,1)S(1)} %get-tuple-element.50), kind=kLoop, calls=%fused_computation | loop fusion | flops 589824 | bytes 786432 | tf_op jit(solution)/shard_map/stack | solution.py:32
  16.8 0.6 pad_maximum_fusion.3
  17.4 1.5 %collective-permute-start.3 = (f32[2,8,1,256]{3,2,1,0:T(1,128)}, f32[2,8,1,256]{3,2,1,0:T(1,128)S(1)}, u32[]{:S(2)}, u32[]{:S(2)}) collective-permute-start(f32[2,8,1,256]{3,2,1,0:T(1,128)} %get-tuple-element.54), channel_id=1, source_target_pairs={{0,7},{1,0},{2,1},{3,2},{4,3},{5,4},{6,5},{7,6},{8,15},{9,8},{10,9... | collective-permute-start | bytes 49160 | tf_op jit(solution)/shard_map/ppermute | solution.py:13
  19.2 0.6 add_convert_fusion.flags
  19.8 0.7 copy.29.bias
  20.5 3.9 %reshape.25.wide = bf16[384,512]{1,0:T(8,128)(2,1)S(1)} reshape(bf16[3,4,32,4,4,32]{5,4,3,2,1,0:T(4,128)(2,1)} %pad_maximum_fusion) | data formatting | bytes 786432 | tf_op jit(solution)/shard_map/reshape | solution.py:33
  24.4 0.6 copy-done.3
  25.0 0.8 sides.1
  25.9 4.8 %collective-permute-start.7 = (bf16[7,32,256]{2,1,0:T(8,128)(2,1)S(1)}, bf16[7,32,256]{2,1,0:T(8,128)(2,1)S(1)}, u32[]{:S(2)}, u32[]{:S(2)}) collective-permute-start(bf16[7,32,256]{2,1,0:T(8,128)(2,1)S(1)} %get-tuple-element.31), channel_id=1, source_target_pairs={{0,120},{8,0},{16,8},{24,16},{32,24},{40,32},{48,40},{56,48},{64,5... | collective-permute-start | bytes 344072 | tf_op jit(solution)/shard_map/ppermute | solution.py:13
  30.7 0.7 copy-done.2
  31.4 0.6 copy-done.4
  32.0 4.4 %conv_inner.1.inner = bf16[6,16,32,256]{3,2,1,0:T(8,128)(2,1)S(1)} custom-call(bf16[8,16,32,256]{3,2,1,0:T(8,128)(2,1)S(1)} %copy-done, bf16[8,1,32,256]{3,2,1,0:T(8,128)(2,1)S(1)} %collective-permute-done.y_lo, bf16[8,1,32,256]{3,2,1,0:T(8,128)(2,1)S(1)} %collective-permute-done.1.y_hi, f32[2,8,1,256]{3,2,1,0:T(1,128)} %collective-permute-done.2.m_lo, ...), custom_call_target="tpu_custom_call" | custom-call | tf_op jit(solution)/shard_map/conv_inner/pallas_call | solution.py:491
  36.4 3.0 %collective-permute-start.11 = (bf16[6,1,32,256]{3,2,1,0:T(8,128)(2,1)S(1)}, bf16[6,1,32,256]{3,2,1,0:T(8,128)(2,1)S(1)}, u32[]{:S(2)}, u32[]{:S(2)}) collective-permute-start(bf16[6,1,32,256]{3,2,1,0:T(8,128)(2,1)S(1)} %get-tuple-element.46), channel_id=1, source_target_pairs={{0,7},{1,0},{2,1},{3,2},{4,3},{5,4},{6,5},{7,6},{8,15},{9,8},{10,9... | collective-permute-start | bytes 294920 | tf_op jit(solution)/shard_map/ppermute | solution.py:13
  39.5 3.0 %conv_edge.1.edge = bf16[4,16,32,256]{3,2,1,0:T(8,128)(2,1)S(1)} custom-call(bf16[8,16,32,256]{3,2,1,0:T(8,128)(2,1)S(1)} %copy-done, bf16[8,1,32,256]{3,2,1,0:T(8,128)(2,1)S(1)} %collective-permute-done.y_lo, bf16[8,1,32,256]{3,2,1,0:T(8,128)(2,1)S(1)} %collective-permute-done.1.y_hi, f32[2,8,1,256]{3,2,1,0:T(1,128)} %collective-permute-done.2.m_lo, ...), custom_call_target="tpu_custom_call" | custom-call | tf_op jit(solution)/shard_map/conv_edge/pallas_call | solution.py:503
  42.5 2.4 %collective-permute-start.9 = (bf16[4,1,32,256]{3,2,1,0:T(8,128)(2,1)S(1)}, bf16[4,1,32,256]{3,2,1,0:T(8,128)(2,1)S(1)}, u32[]{:S(2)}, u32[]{:S(2)}) collective-permute-start(bf16[4,1,32,256]{3,2,1,0:T(8,128)(2,1)S(1)} %get-tuple-element.48), channel_id=1, source_target_pairs={{0,7},{1,0},{2,1},{3,2},{4,3},{5,4},{6,5},{7,6},{8,15},{9,8},{10,9... | collective-permute-start | bytes 196616 | tf_op jit(solution)/shard_map/ppermute | solution.py:13
  45.0 2.7 %first_inner.1 = (f32[6,16,32,256]{3,2,1,0:T(8,128)S(1)}, f32[4,16,256]{2,1,0:T(8,128)S(1)}) custom-call(bf16[6,16,32,256]{3,2,1,0:T(8,128)(2,1)S(1)} %conv_inner.1.inner, bf16[6,1,32,256]{3,2,1,0:T(8,128)(2,1)S(1)} %collective-permute-done.10.i_lo, bf16[6,1,32,256]{3,2,1,0:T(8,128)(2,1)S(1)} %collective-permute-done.11.i_hi, f32[4]{0:T(128)S(1)} %copy-done.5, ...), custom_call_target="tpu_custom_call" | custom-call | tf_op jit(solution)/shard_map/first_inner/pallas_call | solution.py:495
  47.7 0.9 %collective-permute-done.8.e_lo = bf16[4,1,32,256]{3,2,1,0:T(8,128)(2,1)S(1)} collective-permute-done((bf16[4,1,32,256]{3,2,1,0:T(8,128)(2,1)S(1)}, bf16[4,1,32,256]{3,2,1,0:T(8,128)(2,1)S(1)}, u32[]{:S(2)}, u32[]{:S(2)}) %collective-permute-start.8) | collective-permute-done | bytes 65568 | tf_op jit(solution)/shard_map/ppermute | solution.py:13
  48.6 2.1 %first_edge.1.first = f32[8,16,256]{2,1,0:T(8,128)S(1)} custom-call(bf16[6,16,32,256]{3,2,1,0:T(8,128)(2,1)S(1)} %conv_inner.1.inner, bf16[4,16,32,256]{3,2,1,0:T(8,128)(2,1)S(1)} %conv_edge.1.edge, bf16[4,1,32,256]{3,2,1,0:T(8,128)(2,1)S(1)} %collective-permute-done.8.e_lo, bf16[4,1,32,256]{3,2,1,0:T(8,128)(2,1)S(1)} %collective-permute-done.9.e_hi, ...), custom_call_target="tpu_custom_call" | custom-call | tf_op jit(solution)/shard_map/first_edge/pallas_call | solution.py:513
  50.8 4.1 %collective-permute-start.13 = (f32[8,1,256]{2,1,0:T(1,128)S(1)}, f32[8,1,256]{2,1,0:T(1,128)S(1)}, u32[]{:S(2)}, u32[]{:S(2)}) collective-permute-start(f32[8,1,256]{2,1,0:T(1,128)S(1)} %get-tuple-element.59), channel_id=1, source_target_pairs={{0,7},{1,0},{2,1},{3,2},{4,3},{5,4},{6,5},{7,6},{8,15},{9,8},{10,9... | collective-permute-start | bytes 24584 | tf_op jit(solution)/shard_map/ppermute | solution.py:13
  55.0 0.6 collective-permute-done.12.w_lo
  55.9 4.8 %collective-permute-start.15 = (f32[18,256]{1,0:T(8,128)S(1)}, f32[18,256]{1,0:T(8,128)S(1)}, u32[]{:S(2)}, u32[]{:S(2)}) collective-permute-start(f32[18,256]{1,0:T(8,128)S(1)} %pad_maximum_fusion.2), channel_id=1, source_target_pairs={{0,120},{8,0},{16,8},{24,16},{32,24},{40,32},{48,40},{56,48},{64,5... | collective-permute-start | bytes 55304 | tf_op jit(solution)/shard_map/ppermute | solution.py:13
  60.7 3.8 %second_inner.1 = (f32[8,16,32,256]{3,2,1,0:T(8,128)S(1)}, f32[6,16,256]{2,1,0:T(8,128)S(1)}, f32[10,16,256]{2,1,0:T(8,128)S(1)}) custom-call(bf16[6,16,32,256]{3,2,1,0:T(8,128)(2,1)S(1)} %conv_inner.1.inner, bf16[4,16,32,256]{3,2,1,0:T(8,128)(2,1)S(1)} %conv_edge.1.edge, bf16[6,1,32,256]{3,2,1,0:T(8,128)(2,1)S(1)} %collective-permute-done.10.i_lo, ...), custom_call_target="tpu_custom_call" | custom-call | tf_op jit(solution)/shard_map/second_inner/pallas_call | solution.py:538
  64.5 1.8 %second_edge.1 = (f32[2,16,256]{2,1,0:T(8,128)S(1)}, f32[1,128]{1,0:T(1,128)S(1)}) custom-call(bf16[4,16,32,256]{3,2,1,0:T(8,128)(2,1)S(1)} %conv_edge.1.edge, bf16[4,1,32,256]{3,2,1,0:T(8,128)(2,1)S(1)} %collective-permute-done.8.e_lo, bf16[4,1,32,256]{3,2,1,0:T(8,128)(2,1)S(1)} %collective-permute-done.9.e_hi, f32[4]{0:T(128)S(1)} %copy-done.5, ...), custom_call_target="tpu_custom_call" | custom-call | tf_op jit(solution)/shard_map/second_edge/pallas_call | solution.py:550
  66.4 18.5 %all_to_all.5 = f32[128,1,128]{2,1,0:T(1,128)S(1)} all-to-all(f32[128,1,128]{2,1,0:T(1,128)S(1)} %broadcast_in_dim.17), channel_id=1, replica_groups=mesh['sx'=16,'sy'=8] {'sx','sy'}, dimensions={0} | all-to-all | bytes 131072 | tf_op jit(solution)/shard_map/all_to_all | solution.py:560
  84.9 0.9 %final.1 = (f32[8,16,256]{2,1,0:T(8,128)}, f32[8,16,256]{2,1,0:T(8,128)}) custom-call(f32[128,128]{1,0:T(8,128)S(1)} %bitcast.43, f32[8,16,256]{2,1,0:T(8,128)S(1)} %get-tuple-element.27.start, f32[8,16,256]{2,1,0:T(8,128)S(1)} %first_edge.1.first, f32[6,16,256]{2,1,0:T(8,128)S(1)} %get-tuple-element.38.inside, f32[2,16,256]{2,1,0:T(8,128)S(1)} %get-tuple-element.39.sides), custom_call_target="tpu_custom_call" | custom-call | tf_op jit(solution)/shard_map/final/pallas_call | solution.py:562
  (55 shorter events, 1.6 us)
Async XLA Ops:
  0.6 12.0 %copy-start.9 = (s32[8,16,2,27]{3,2,1,0:T(2,128)S(1)}, s32[8,16,2,27]{3,2,1,0:T(2,128)}, u32[]{:S(2)}) copy-start(s32[8,16,2,27]{3,2,1,0:T(2,128)} %param.11) | copy-start | bytes 82948
  1.7 11.6 %copy-start.6 = (bf16[27,32,32]{2,1,0:T(8,128)(2,1)S(1)}, bf16[27,32,32]{2,1,0:T(8,128)(2,1)}, u32[]{:S(2)}) copy-start(bf16[27,32,32]{2,1,0:T(8,128)(2,1)} %param.8) | copy-start | bytes 165892
  1.7 15.1 %collective-permute-start.1 = (bf16[8,1,32,256]{3,2,1,0:T(8,128)(2,1)S(1)}, bf16[8,1,32,256]{3,2,1,0:T(8,128)(2,1)S(1)}, u32[]{:S(2)}, u32[]{:S(2)}) collective-permute-start(bf16[8,1,32,256]{3,2,1,0:T(8,128)(2,1)S(1)} %get-tuple-element.42), channel_id=1, source_target_pairs={{0,7},{1,0},{2,1},{3,2},{4,3},{5,4},{6,5},{7,6},{8,15},{9,8},{10,9... | collective-permute-start | bytes 393224 | tf_op jit(solution)/shard_map/ppermute | solution.py:13
  3.1 13.7 %collective-permute-start = (bf16[8,1,32,256]{3,2,1,0:T(8,128)(2,1)S(1)}, bf16[8,1,32,256]{3,2,1,0:T(8,128)(2,1)S(1)}, u32[]{:S(2)}, u32[]{:S(2)}) collective-permute-start(bf16[8,1,32,256]{3,2,1,0:T(8,128)(2,1)S(1)} %get-tuple-element.43), channel_id=1, source_target_pairs={{0,1},{1,2},{2,3},{3,4},{4,5},{5,6},{6,7},{7,0},{8,9},{9,10},{10,1... | collective-permute-start | bytes 393224 | tf_op jit(solution)/shard_map/ppermute | solution.py:13
  6.7 32.8 %collective-permute-start.4 = (bf16[2,16,32,256]{3,2,1,0:T(8,128)(2,1)}, bf16[2,16,32,256]{3,2,1,0:T(8,128)(2,1)S(1)}, u32[]{:S(2)}, u32[]{:S(2)}) collective-permute-start(bf16[2,16,32,256]{3,2,1,0:T(8,128)(2,1)} %get-tuple-element.28), channel_id=1, source_target_pairs={{0,8},{8,16},{16,24},{24,32},{32,40},{40,48},{48,56},{56,64},{64,7... | collective-permute-start | bytes 1572872 | tf_op jit(solution)/shard_map/ppermute | solution.py:13
  7.9 31.6 %collective-permute-start.5 = (bf16[2,16,32,256]{3,2,1,0:T(8,128)(2,1)}, bf16[2,16,32,256]{3,2,1,0:T(8,128)(2,1)}, u32[]{:S(2)}, u32[]{:S(2)}) collective-permute-start(bf16[2,16,32,256]{3,2,1,0:T(8,128)(2,1)} %get-tuple-element.29), channel_id=1, source_target_pairs={{0,120},{8,0},{16,8},{24,16},{32,24},{40,32},{48,40},{56,48},{64,5... | collective-permute-start | bytes 1572872 | tf_op jit(solution)/shard_map/ppermute | solution.py:13
  14.2 2.5 %copy-start.7 = (f32[8,16,256]{2,1,0:T(8,128)S(1)}, f32[8,16,256]{2,1,0:T(8,128)}, u32[]{:S(2)}) copy-start(f32[8,16,256]{2,1,0:T(8,128)} %param.13) | copy-start | bytes 393220
  14.2 2.5 %copy-start.8 = (s32[8,16,256]{2,1,0:T(8,128)S(1)}, s32[8,16,256]{2,1,0:T(8,128)}, u32[]{:S(2)}) copy-start(s32[8,16,256]{2,1,0:T(8,128)} %param.10) | copy-start | bytes 393220
  14.2 5.6 %copy-start.10 = (f32[32]{0:T(128)S(1)}, f32[32]{0:T(128)}, u32[]{:S(2)}) copy-start(f32[32]{0:T(128)} %param.9) | copy-start | bytes 388
  16.8 13.9 %copy-start = (bf16[8,16,32,256]{3,2,1,0:T(8,128)(2,1)S(1)}, bf16[8,16,32,256]{3,2,1,0:T(8,128)(2,1)}, u32[]{:S(2)}) copy-start(bf16[8,16,32,256]{3,2,1,0:T(8,128)(2,1)} %own.3) | copy-start | bytes 6291460
  17.4 7.0 %collective-permute-start.3 = (f32[2,8,1,256]{3,2,1,0:T(1,128)}, f32[2,8,1,256]{3,2,1,0:T(1,128)S(1)}, u32[]{:S(2)}, u32[]{:S(2)}) collective-permute-start(f32[2,8,1,256]{3,2,1,0:T(1,128)} %get-tuple-element.54), channel_id=1, source_target_pairs={{0,7},{1,0},{2,1},{3,2},{4,3},{5,4},{6,5},{7,6},{8,15},{9,8},{10,9... | collective-permute-start | bytes 49160 | tf_op jit(solution)/shard_map/ppermute | solution.py:13
  19.0 5.4 %collective-permute-start.2 = (f32[2,8,1,256]{3,2,1,0:T(1,128)}, f32[2,8,1,256]{3,2,1,0:T(1,128)}, u32[]{:S(2)}, u32[]{:S(2)}) collective-permute-start(f32[2,8,1,256]{3,2,1,0:T(1,128)} %get-tuple-element.55), channel_id=1, source_target_pairs={{0,1},{1,2},{2,3},{3,4},{4,5},{5,6},{6,7},{7,0},{8,9},{9,10},{10,1... | collective-permute-start | bytes 49160 | tf_op jit(solution)/shard_map/ppermute | solution.py:13
  24.4 0.6 copy-start.3
  25.8 13.6 %collective-permute-start.6 = (bf16[7,32,256]{2,1,0:T(8,128)(2,1)S(1)}, bf16[7,32,256]{2,1,0:T(8,128)(2,1)S(1)}, u32[]{:S(2)}, u32[]{:S(2)}) collective-permute-start(bf16[7,32,256]{2,1,0:T(8,128)(2,1)S(1)} %get-tuple-element.30), channel_id=1, source_target_pairs={{0,8},{8,16},{16,24},{24,32},{32,40},{40,48},{48,56},{56,64},{64,7... | collective-permute-start | bytes 344072 | tf_op jit(solution)/shard_map/ppermute | solution.py:13
  25.9 13.6 %collective-permute-start.7 = (bf16[7,32,256]{2,1,0:T(8,128)(2,1)S(1)}, bf16[7,32,256]{2,1,0:T(8,128)(2,1)S(1)}, u32[]{:S(2)}, u32[]{:S(2)}) collective-permute-start(bf16[7,32,256]{2,1,0:T(8,128)(2,1)S(1)} %get-tuple-element.31), channel_id=1, source_target_pairs={{0,120},{8,0},{16,8},{24,16},{32,24},{40,32},{48,40},{56,48},{64,5... | collective-permute-start | bytes 344072 | tf_op jit(solution)/shard_map/ppermute | solution.py:13
  30.7 0.7 copy-start.2
  31.4 0.6 copy-start.4
  32.0 7.5 %copy-start.5 = (f32[4]{0:T(128)S(1)}, f32[4]{0:T(128)}, u32[]{:S(2)}) copy-start(f32[4]{0:T(128)} %add_convert_fusion.flags) | copy-start | bytes 52
  36.4 8.6 %collective-permute-start.11 = (bf16[6,1,32,256]{3,2,1,0:T(8,128)(2,1)S(1)}, bf16[6,1,32,256]{3,2,1,0:T(8,128)(2,1)S(1)}, u32[]{:S(2)}, u32[]{:S(2)}) collective-permute-start(bf16[6,1,32,256]{3,2,1,0:T(8,128)(2,1)S(1)} %get-tuple-element.46), channel_id=1, source_target_pairs={{0,7},{1,0},{2,1},{3,2},{4,3},{5,4},{6,5},{7,6},{8,15},{9,8},{10,9... | collective-permute-start | bytes 294920 | tf_op jit(solution)/shard_map/ppermute | solution.py:13
  39.4 5.5 %copy-start.1 = (f32[8,16,256]{2,1,0:T(8,128)S(1)}, f32[8,16,256]{2,1,0:T(8,128)}, u32[]{:S(2)}) copy-start(f32[8,16,256]{2,1,0:T(8,128)} %ridge.7) | copy-start | bytes 393220
  39.4 5.5 %collective-permute-start.10 = (bf16[6,1,32,256]{3,2,1,0:T(8,128)(2,1)S(1)}, bf16[6,1,32,256]{3,2,1,0:T(8,128)(2,1)S(1)}, u32[]{:S(2)}, u32[]{:S(2)}) collective-permute-start(bf16[6,1,32,256]{3,2,1,0:T(8,128)(2,1)S(1)} %get-tuple-element.47), channel_id=1, source_target_pairs={{0,1},{1,2},{2,3},{3,4},{4,5},{5,6},{6,7},{7,0},{8,9},{9,10},{10,1... | collective-permute-start | bytes 294920 | tf_op jit(solution)/shard_map/ppermute | solution.py:13
  42.5 5.1 %collective-permute-start.9 = (bf16[4,1,32,256]{3,2,1,0:T(8,128)(2,1)S(1)}, bf16[4,1,32,256]{3,2,1,0:T(8,128)(2,1)S(1)}, u32[]{:S(2)}, u32[]{:S(2)}) collective-permute-start(bf16[4,1,32,256]{3,2,1,0:T(8,128)(2,1)S(1)} %get-tuple-element.48), channel_id=1, source_target_pairs={{0,7},{1,0},{2,1},{3,2},{4,3},{5,4},{6,5},{7,6},{8,15},{9,8},{10,9... | collective-permute-start | bytes 196616 | tf_op jit(solution)/shard_map/ppermute | solution.py:13
  44.9 3.6 %collective-permute-start.8 = (bf16[4,1,32,256]{3,2,1,0:T(8,128)(2,1)S(1)}, bf16[4,1,32,256]{3,2,1,0:T(8,128)(2,1)S(1)}, u32[]{:S(2)}, u32[]{:S(2)}) collective-permute-start(bf16[4,1,32,256]{3,2,1,0:T(8,128)(2,1)S(1)} %get-tuple-element.49), channel_id=1, source_target_pairs={{0,1},{1,2},{2,3},{3,4},{4,5},{5,6},{6,7},{7,0},{8,9},{9,10},{10,1... | collective-permute-start | bytes 196616 | tf_op jit(solution)/shard_map/ppermute | solution.py:13
  50.8 4.8 %collective-permute-start.12 = (f32[8,1,256]{2,1,0:T(1,128)S(1)}, f32[8,1,256]{2,1,0:T(1,128)S(1)}, u32[]{:S(2)}, u32[]{:S(2)}) collective-permute-start(f32[8,1,256]{2,1,0:T(1,128)S(1)} %get-tuple-element.58), channel_id=1, source_target_pairs={{0,1},{1,2},{2,3},{3,4},{4,5},{5,6},{6,7},{7,0},{8,9},{9,10},{10,1... | collective-permute-start | bytes 24584 | tf_op jit(solution)/shard_map/ppermute | solution.py:13
  50.8 5.0 %collective-permute-start.13 = (f32[8,1,256]{2,1,0:T(1,128)S(1)}, f32[8,1,256]{2,1,0:T(1,128)S(1)}, u32[]{:S(2)}, u32[]{:S(2)}) collective-permute-start(f32[8,1,256]{2,1,0:T(1,128)S(1)} %get-tuple-element.59), channel_id=1, source_target_pairs={{0,7},{1,0},{2,1},{3,2},{4,3},{5,4},{6,5},{7,6},{8,15},{9,8},{10,9... | collective-permute-start | bytes 24584 | tf_op jit(solution)/shard_map/ppermute | solution.py:13
  55.8 8.7 %collective-permute-start.14 = (f32[18,256]{1,0:T(8,128)S(1)}, f32[18,256]{1,0:T(8,128)S(1)}, u32[]{:S(2)}, u32[]{:S(2)}) collective-permute-start(f32[18,256]{1,0:T(8,128)S(1)} %pad_maximum_fusion.1), channel_id=1, source_target_pairs={{0,8},{8,16},{16,24},{24,32},{32,40},{40,48},{48,56},{56,64},{64,7... | collective-permute-start | bytes 55304 | tf_op jit(solution)/shard_map/ppermute | solution.py:13
  55.9 8.6 %collective-permute-start.15 = (f32[18,256]{1,0:T(8,128)S(1)}, f32[18,256]{1,0:T(8,128)S(1)}, u32[]{:S(2)}, u32[]{:S(2)}) collective-permute-start(f32[18,256]{1,0:T(8,128)S(1)} %pad_maximum_fusion.2), channel_id=1, source_target_pairs={{0,120},{8,0},{16,8},{24,16},{32,24},{40,32},{48,40},{56,48},{64,5... | collective-permute-start | bytes 55304 | tf_op jit(solution)/shard_map/ppermute | solution.py:13

commit v4 on v3

--- a/solution.py
+++ b/solution.py
@@ -20,17 +20,51 @@
     return before, after
 
 
-def block_weights(conv_weight):
-    channels = conv_weight.shape[1]
-    taps = conv_weight.reshape(3, 3, 3, channels, channels).transpose(2, 3, 0, 1, 4)
-    rows = []
-    for out_x in range(2):
-        for out_y in range(2):
-            rows.append(
-                jnp.pad(taps, ((0, 0), (0, 0), (out_x, 1 - out_x), (out_y, 1 - out_y), (0, 0)))
-            )
-    block = jnp.stack(rows, axis=1)
-    return block.reshape(3 * 4 * channels, 16 * channels)
+def edges_kernel(own, x_hi, x_lo, y_hi, y_lo, sems):
+    rows, cols = own.shape[:2]
+    copies = [
+        pltpu.make_async_copy(own.at[rows - 2 : rows], x_hi, sems.at[0]),
+        pltpu.make_async_copy(own.at[0:2], x_lo, sems.at[1]),
+        pltpu.make_async_copy(own.at[:, cols - 1 : cols], y_hi, sems.at[2]),
+        pltpu.make_async_copy(own.at[:, 0:1], y_lo, sems.at[3]),
+    ]
+    for copy in copies:
+        copy.start()
+    for copy in copies:
+        copy.wait()
+
+
+def weights_kernel(taps, bias, wide, bias_col):
+    channels = taps.shape[1]
+    width = 16 * channels
+    row = lax.broadcasted_iota(jnp.int32, (channels, width), 0)
+    lane = lax.broadcasted_iota(jnp.int32, (channels, width), 1)
+    repeat = jnp.where(lane % channels == row, 1.0, 0.0).astype(jnp.bfloat16)
+    group = lane // channels
+    for z in range(3):
+        every = [
+            jnp.dot(taps[3 * k + z], repeat, preferred_element_type=jnp.float32) for k in range(9)
+        ]
+        for out_x in range(2):
+            for out_y in range(2):
+                total = jnp.zeros((channels, width), jnp.float32)
+                for k in range(9):
+                    at = (out_x + k // 3) * 4 + out_y + k % 3
+                    total = jnp.where(group == at, every[k], total)
+                start = ((z * 2 + out_x) * 2 + out_y) * channels
+                wide[start : start + channels] = total.astype(jnp.bfloat16)
+    square = (channels, channels)
+    same = lax.broadcasted_iota(jnp.int32, square, 0) == lax.broadcasted_iota(jnp.int32, square, 1)
+    column = jnp.sum(jnp.where(same, bias[...], 0.0), axis=1, keepdims=True)
+    bias_col[...] = jnp.broadcast_to(column, bias_col.shape)
+
+
+def mesh_flags():
+    keep = []
+    for axis in ("sy", "sx"):
+        where = lax.axis_index(axis)
+        keep += [where > 0, where < lax.axis_size(axis) - 1]
+    return [jnp.where(k, 1.0, 0.0) for k in keep]
 
 
 def conv_block(grid, masks, wide, bias_all, lane, grid_x, y, out, out_x):
@@ -64,8 +98,8 @@
 
 
 def fill_own(grid, grid_x, own, mask, y_lo, y_hi, m_lo, m_hi, flags, x):
-    low = y_lo[x, 0] * as_bf16(m_lo[0, x], flags[0])
-    high = y_hi[x, 0] * as_bf16(m_hi[0, x], flags[1])
+    low = y_lo[x, 0] * as_bf16(m_lo[0, pl.ds(x, 1)], flags[0])
+    high = y_hi[x, 0] * as_bf16(m_hi[0, pl.ds(x, 1)], flags[1])
     fill_row(grid, grid_x, mask_of(mask, x), lambda y: own[x, y], low, high)
 
 
@@ -73,8 +107,9 @@
     return lambda y: mask[x, y : y + 1, :]
 
 
-def conv_inner_kernel(own, y_lo, y_hi, m_lo, m_hi, mask, flags, wide, bias, out, grid):
+def conv_inner_kernel(own, y_lo, y_hi, m_lo, m_hi, mask, wide, bias, out, grid):
     rows, cols, channels, depth = own.shape
+    flags = mesh_flags()
 
     def fill(x, carry):
         fill_own(grid, x, own, mask, y_lo, y_hi, m_lo, m_hi, flags, x)
@@ -82,7 +117,7 @@
 
     lax.fori_loop(0, rows, fill, 0)
     lane = lax.broadcasted_iota(jnp.int32, (4 * channels, depth), 1)
-    bias_all = jnp.broadcast_to(bias[...], (channels, depth))
+    bias_all = bias[...]
 
     def pair(i, carry):
         masks = (mask_of(mask, 2 * i + 1), mask_of(mask, 2 * i + 2))
@@ -93,8 +128,9 @@
     lax.fori_loop(0, rows // 2 - 1, pair, 0)
 
 
-def sides_kernel(y_lo, y_hi, m_lo, m_hi, mask, start, flags, out_hi, out_lo):
+def sides_kernel(y_lo, y_hi, m_lo, m_hi, mask, start, out_hi, out_lo):
     rows, cols, depth = mask.shape
+    flags = mesh_flags()
 
     def three(value):
         high = value.astype(jnp.bfloat16).astype(jnp.float32)
@@ -104,11 +140,11 @@
 
     for out, pair, row in ((out_hi, (rows - 2, rows - 1), rows - 1), (out_lo, (0, 1), 0)):
         for k, x in enumerate(pair):
-            out[2 * k] = y_lo[x, 0] * as_bf16(m_lo[0, x], flags[0])
-            out[2 * k + 1] = y_hi[x, 0] * as_bf16(m_hi[0, x], flags[1])
+            out[2 * k] = y_lo[x, 0] * as_bf16(m_lo[0, pl.ds(x, 1)], flags[0])
+            out[2 * k + 1] = y_hi[x, 0] * as_bf16(m_hi[0, pl.ds(x, 1)], flags[1])
         out[4] = jnp.concatenate([mask[x] for x in pair], axis=0).astype(jnp.bfloat16)
         high, mid, low = three(start[row])
-        rims = three(jnp.concatenate([m_lo[1, row], m_hi[1, row]], axis=0))
+        rims = three(jnp.concatenate([m_lo[1, row : row + 1], m_hi[1, row : row + 1]], axis=0))
         blank = jnp.zeros((10, depth), jnp.float32)
         out[5] = jnp.concatenate([high, mid], axis=0).astype(jnp.bfloat16)
         out[6] = jnp.concatenate([low, *rims, blank], axis=0).astype(jnp.bfloat16)
@@ -125,7 +161,6 @@
     side_lo,
     side_hi,
     mask,
-    flags,
     wide,
     bias,
     out,
@@ -133,6 +168,7 @@
     side_mask,
 ):
     rows, cols, channels, depth = own.shape
+    flags = mesh_flags()
     for k, side in enumerate((side_lo, side_hi)):
         both = side[4].astype(jnp.float32) * flags[2 + k]
         side_mask[2 * k] = both[:cols]
@@ -151,7 +187,7 @@
         fill_own(grid, 2 + x, own, mask, y_lo, y_hi, m_lo, m_hi, flags, x)
         fill_own(grid, 4 + x, own, mask, y_lo, y_hi, m_lo, m_hi, flags, rows - 2 + x)
     lane = lax.broadcasted_iota(jnp.int32, (4 * channels, depth), 1)
-    bias_all = jnp.broadcast_to(bias[...], (channels, depth))
+    bias_all = bias[...]
     for side, masks in (
         (0, (mask_of(side_mask, 1), mask_of(mask, 0))),
         (1, (mask_of(mask, rows - 1), mask_of(side_mask, 2))),
@@ -227,7 +263,7 @@
 
 
 def rim_of(ref, *index):
-    return lambda x: ref[(*index, x)]
+    return lambda x: ref[(*index, pl.ds(x, 1))]
 
 
 def along_x(before, here, after, field, row, ridge_row, value_row):
@@ -247,8 +283,9 @@
     return ridge_row * value_row + inner * (1.0 / (8 * channels))
 
 
-def first_inner_kernel(inner, i_lo, i_hi, flags, start, m_lo, m_hi, ridge, smooth, out):
+def first_inner_kernel(inner, i_lo, i_hi, start, m_lo, m_hi, ridge, smooth, out):
     rows = inner.shape[0]
+    flags = mesh_flags()
     s_lo, s_hi = (rim_of(m_lo, 1), rim_of(m_hi, 1))
 
     def stage_y(k, carry):
@@ -271,7 +308,6 @@
     edge,
     e_lo,
     e_hi,
-    flags,
     start,
     m_lo,
     m_hi,
@@ -286,6 +322,7 @@
     side_rims,
 ):
     n = inner.shape[0]
+    flags = mesh_flags()
     last = n + 1
     cols = inner.shape[1]
     s_lo, s_hi = (rim_of(m_lo, 1), rim_of(m_hi, 1))
@@ -333,9 +370,10 @@
 
 
 def second_inner_kernel(
-    inner, edge, i_lo, i_hi, e_lo, e_hi, flags, start, first, w_lo, w_hi, ridge, smooth, out, grams
+    inner, edge, i_lo, i_hi, e_lo, e_hi, start, first, w_lo, w_hi, ridge, smooth, out, grams
 ):
     n = inner.shape[0]
+    flags = mesh_flags()
     w_lo, w_hi = (rim_of(w_lo), rim_of(w_hi))
 
     def stage_y(k, carry):
@@ -365,9 +403,10 @@
 
 
 def second_edge_kernel(
-    edge, e_lo, e_hi, flags, start, first, x_lo, x_hi, ridge, smooth, grams, out, share, rim
+    edge, e_lo, e_hi, start, first, x_lo, x_hi, ridge, smooth, grams, out, share, rim
 ):
     n = smooth.shape[0]
+    flags = mesh_flags()
     along_y(rim, 0, edge, e_lo, e_hi, 0, flags, side_row(x_lo))
     along_y(rim, 1, edge, e_lo, e_hi, 3, flags, side_row(x_hi))
     out[0] = along_x((rim, 0), (smooth, 0), (smooth, 1), edge, 1, ridge[0], first[0])
@@ -443,101 +482,109 @@
     voxels = depth // block_ids.shape[2]
     f32, bf16 = (jnp.float32, jnp.bfloat16)
     vmem = pl.BlockSpec(memory_space=pltpu.VMEM)
-    smem = pl.BlockSpec(memory_space=pltpu.SMEM)
-
-    def call(kernel, specs, outs, scratch, limit, name):
+    anywhere = pl.BlockSpec(memory_space=pl.ANY)
+
+    def call(kernel, args, outs, scratch, limit, name):
         return pl.pallas_call(
             kernel,
             out_shape=[jax.ShapeDtypeStruct(shape, dtype) for shape, dtype in outs],
-            in_specs=[smem if s == "s" else vmem for s in specs],
+            in_specs=[vmem for _ in args],
             out_specs=[vmem for _ in outs],
             scratch_shapes=[pltpu.VMEM(shape, dtype) for shape, dtype in scratch],
             compiler_params=pltpu.CompilerParams(vmem_limit_bytes=limit << 20),
             name=name,
-        )
-
-    edges = (features[-2:], features[:2])
+        )(*args)
+
+    edges = pl.pallas_call(
+        edges_kernel,
+        out_shape=[
+            jax.ShapeDtypeStruct(shape + (channels, depth), bf16)
+            for shape in ((2, cols), (2, cols), (rows, 1), (rows, 1))
+        ],
+        in_specs=[pl.BlockSpec(memory_space=pltpu.HBM)],
+        out_specs=[anywhere] * 4,
+        scratch_shapes=[pltpu.SemaphoreType.DMA((4,))],
+        compiler_params=pltpu.CompilerParams(vmem_limit_bytes=1 << 20),
+        name="edges",
+    )(features)
     edges, occupancy, block_ids, target, conv_weight = lax.optimization_barrier(
         (edges, occupancy, block_ids, target, conv_weight)
     )
     x_lo, x_hi = (shift(edges[0], "sx", 1), shift(edges[1], "sx", -1))
+    y_lo, y_hi = (shift(edges[2], "sy", 1), shift(edges[3], "sy", -1))
 
     present = (block_ids[:, :, :, 13] >= 0).astype(f32)
     weight_mask = occupancy.astype(f32) * jnp.repeat(present, voxels, axis=2)
     residual = weight_mask * target
-    y_lo, y_hi = halo(features, "sy", 1, 1)
     weight_mask, residual, y_lo, y_hi = lax.optimization_barrier(
         (weight_mask, residual, y_lo, y_hi)
     )
-    m_lo, m_hi = halo(jnp.stack([weight_mask, residual]), "sy", 2, 1)
-    flags = jnp.stack(
-        [
-            keep
-            for axis in ("sy", "sx")
-            for keep in (lax.axis_index(axis) > 0, lax.axis_index(axis) < lax.axis_size(axis) - 1)
-        ]
-    ).astype(f32)
-
-    wide = block_weights(conv_weight)
-    bias = conv_bias[:, None]
+    m_lo, m_hi = [
+        shift(jnp.stack([weight_mask[:, y], residual[:, y]]), "sy", step)
+        for y, step in ((cols - 1, 1), (0, -1))
+    ]
+    wide, bias = call(
+        weights_kernel,
+        (conv_weight, conv_bias[None]),
+        [((12 * channels, 16 * channels), bf16), ((channels, depth), f32)],
+        [],
+        8,
+        "weights",
+    )
     grid_scratch = ((rows, cols + 2, channels, depth), bf16)
     inner_shape = (rows - 2, cols, channels, depth)
     edge_shape = (4, cols, channels, depth)
     side_shape = (7, channels, depth)
+    plane = ((rows, cols, depth), f32)
     side_hi, side_lo = call(
-        sides_kernel, "vvvvvvs", [(side_shape, bf16), (side_shape, bf16)], [], 4, "sides"
-    )(y_lo, y_hi, m_lo, m_hi, weight_mask, residual, flags)
+        sides_kernel,
+        (y_lo, y_hi, m_lo, m_hi, weight_mask, residual),
+        [(side_shape, bf16), (side_shape, bf16)],
+        [],
+        4,
+        "sides",
+    )
     side_lo, side_hi = (shift(side_hi, "sx", 1), shift(side_lo, "sx", -1))
     (inner,) = call(
-        conv_inner_kernel, "vvvvvvsvv", [(inner_shape, bf16)], [grid_scratch], 12, "conv_inner"
-    )(features, y_lo, y_hi, m_lo, m_hi, weight_mask, flags, wide, bias)
+        conv_inner_kernel,
+        (features, y_lo, y_hi, m_lo, m_hi, weight_mask, wide, bias),
+        [(inner_shape, bf16)],
+        [grid_scratch],
+        12,
+        "conv_inner",
+    )
     i_lo, i_hi = halo(inner, "sy", 1, 1)
     smooth, part = call(
         first_inner_kernel,
-        "vvvsvvvv",
+        (inner, i_lo, i_hi, residual, m_lo, m_hi, ridge),
         [(inner_shape, f32), ((rows - 4, cols, depth), f32)],
         [],
         8,
         "first_inner",
-    )(inner, i_lo, i_hi, flags, residual, m_lo, m_hi, ridge)
+    )
     (edge,) = call(
         conv_edge_kernel,
-        "vvvvvvvvvvsvv",
+        (features, y_lo, y_hi, m_lo, m_hi, x_lo, x_hi, side_lo, side_hi, weight_mask, wide, bias),
         [(edge_shape, bf16)],
         [grid_scratch, ((4, cols, depth), f32)],
         12,
         "conv_edge",
-    )(features, y_lo, y_hi, m_lo, m_hi, x_lo, x_hi, side_lo, side_hi, weight_mask, flags, wide, bias)
+    )
     e_lo, e_hi = halo(edge, "sy", 1, 1)
-    plane = ((rows, cols, depth), f32)
     (first,) = call(
         first_edge_kernel,
-        "vvvvsvvvvvvvv",
+        (inner, edge, e_lo, e_hi, residual, m_lo, m_hi, side_lo, side_hi, ridge, smooth, part),
         [plane],
         [(edge_shape, f32), ((2, cols, depth), f32), ((2, 8, depth), f32)],
         8,
         "first_edge",
-    )(
-        inner,
-        edge,
-        e_lo,
-        e_hi,
-        flags,
-        residual,
-        m_lo,
-        m_hi,
-        side_lo,
-        side_hi,
-        ridge,
-        smooth,
-        part,
-    )
-    w_lo, w_hi = halo(first, "sy", 1, 1)
-    rims = [jnp.concatenate([w_lo[x], first[x], w_hi[x]], axis=0) for x in (-1, 0)]
+    )
+    w_lo, w_hi = (shift(first[:, -1], "sy", 1), shift(first[:, 0], "sy", -1))
+    rims = [jnp.concatenate([w_lo[x : x + 1], first[x], w_hi[x : x + 1]]) for x in (rows - 1, 0)]
     r_lo, r_hi = (shift(rims[0], "sx", 1), shift(rims[1], "sx", -1))
     smooth, inside, grams = call(
         second_inner_kernel,
-        "vvvvvvsvvvvv",
+        (inner, edge, i_lo, i_hi, e_lo, e_hi, residual, first, w_lo, w_hi, ridge),
         [
             ((rows, cols, channels, depth), f32),
             ((rows - 2, cols, depth), f32),
@@ -546,21 +593,26 @@
         [],
         8,
         "second_inner",
-    )(inner, edge, i_lo, i_hi, e_lo, e_hi, flags, residual, first, w_lo, w_hi, ridge)
+    )
     sides, share = call(
         second_edge_kernel,
-        "vvvsvvvvvvv",
+        (edge, e_lo, e_hi, residual, first, r_lo, r_hi, ridge, smooth, grams),
         [((2, cols, depth), f32), ((1, 128), f32)],
         [((2, cols, channels, depth), f32)],
         8,
         "second_edge",
-    )(edge, e_lo, e_hi, flags, residual, first, r_lo, r_hi, ridge, smooth, grams)
+    )
 
     peers = lax.axis_size("sx") * lax.axis_size("sy")
     shares = lax.all_to_all(jnp.broadcast_to(share[None], (peers, 1, 128)), AXES, 0, 0)
     return tuple(
-        call(final_kernel, "vvvvv", [plane, plane], [], 8, "final")(
-            shares.reshape(peers, 128), residual, first, inside, sides
+        call(
+            final_kernel,
+            (shares.reshape(peers, 128), residual, first, inside, sides),
+            [plane, plane],
+            [],
+            8,
+            "final",
         )
     )
 

time: 86.5 us -> 78.6 us (0.909)
  Pallas kernels: 19.5 us -> 15.6 us
  waiting for transfers between devices: 1.79 us -> 4.94 us
  local copies, waits for them, and re-layouts: 11.5 us -> 8.53 us
  other arithmetic: 3.76 us -> 1.81 us
  starting transfers between devices: 29.8 us -> 28.6 us
    reshape x2 -> x0, local copies, waits for them, and re-layouts: 4.05 us -> none  [the longest x1 3.9 us: block_weights(): return block.reshape(3 * 4 * channels, 16 * channels)]
    pallas_call x8 -> x10, Pallas kernels: 19.5 us -> 15.6 us  [the longest x9 14.5 us: call(): pl.pallas_call(kernel, out_shape=[jax.ShapeDtypeStruct(shape, dtype) for...]
    ppermute x16, waiting for transfers between devices: 1.79 us -> 4.94 us  [shift(): lax.ppermute(value, axis, [(i, (i + step) % peers) for i in range(peers)])]
    another operation x2, other arithmetic: 3.1 us -> 0.04 us  [per_device(): jnp.stack([weight_mask[:, y], residual[:, y]])]
    slice x2 -> x3, local copies, waits for them, and re-layouts: 2.27 us -> 0.02 us  [the longest x1 0.01 us: per_device(): w_lo, w_hi = (shift(first[:, -1], 'sy', 1), shift(first[:, 0], 'sy', -1))]
    optimization_barrier x1, local copies, waits for them, and re-layouts: 0.18 us -> 1.77 us  [per_device(): lax.optimization_barrier((edges, occupancy, block_ids, target, conv_weight))]
    reshape x1, local copies, waits for them, and re-layouts: 0.11 us -> 1.66 us  [per_device(): weight_mask = occupancy.astype(f32) * jnp.repeat(present, voxels, axis=2)]
    broadcast_in_dim x1, local copies, waits for them, and re-layouts: 0.2 us -> 1.69 us  [per_device(): weight_mask = occupancy.astype(f32) * jnp.repeat(present, voxels, axis=2)]
  transfers between devices with their start and end apart: 16 -> 16, of which waited for: 3 -> 4; matrix products, arithmetic and copies ran while one was open for 14% -> 10% of each run, Pallas kernels for 17% -> 14%
where the time goes in v4:
time: 78.6 us; the launch traced here: 78.3 us
  starting transfers between devices  28.6 us (36%)
  blocking collectives  18 us (23%)
  Pallas kernels  15.6 us (20%)
  local copies, waits for them, and re-layouts  8.53 us (11%)
  waiting for transfers between devices  4.94 us (6%)
  other arithmetic  1.81 us (2%)
  between operations  0.87 us (1%)
    ppermute x16, starting transfers between devices, shift(): lax.ppermute(value, axis, [(i, (i + step) % peers) for i in range(peers)])  28.6 us
    all_to_all x1, blocking collectives, per_device(): lax.all_to_all(jnp.broadcast_to(share[None], (peers, 1, 128)), AXES, 0, 0)  18 us
    pallas_call x9, Pallas kernels, call(): pl.pallas_call(kernel, out_shape=[jax.ShapeDtypeStruct(shape, dtype) for...  14.5 us
    ppermute x16, waiting for transfers between devices, shift(): lax.ppermute(value, axis, [(i, (i + step) % peers) for i in range(peers)])  4.94 us
    unnamed x12, local copies, waits for them, and re-layouts  2.54 us
    optimization_barrier x1, local copies, waits for them, and re-layouts, per_device(): lax.optimization_barrier((edges, occupancy, block_ids, target, conv_weight))  1.77 us
    broadcast_in_dim x1, local copies, waits for them, and re-layouts, per_device(): weight_mask = occupancy.astype(f32) * jnp.repeat(present, voxels, axis=2)  1.69 us
    reshape x1, local copies, waits for them, and re-layouts, per_device(): weight_mask = occupancy.astype(f32) * jnp.repeat(present, voxels, axis=2)  1.66 us
  transfers between devices with their start and end apart: 16, of which 4 were waited for; matrix products, arithmetic and copies ran while one was open for 10% of the time, Pallas kernels for 14%

profile of v4, /device:TPU:1, one launch (start us, length us, event | category | flops | bytes accessed | tf_op | source)
XLA Modules:
  0.0 78.3 jit_solution(9205140339450013093)
XLA Ops:
  0.6 1.6 %copy-done = bf16[8,16,32,256]{3,2,1,0:T(8,128)(2,1)S(1)} copy-done((bf16[8,16,32,256]{3,2,1,0:T(8,128)(2,1)S(1)}, bf16[8,16,32,256]{3,2,1,0:T(8,128)(2,1)}, u32[]{:S(2)}) %copy-start) | copy-done | bytes 2097176
  2.2 1.0 %edges.1 = (bf16[2,16,32,256]{3,2,1,0:T(8,128)(2,1)}, bf16[2,16,32,256]{3,2,1,0:T(8,128)(2,1)}, bf16[8,1,32,256]{3,2,1,0:T(8,128)(2,1)}, bf16[8,1,32,256]{3,2,1,0:T(8,128)(2,1)S(1)}) custom-call(bf16[8,16,32,256]{3,2,1,0:T(8,128)(2,1)S(1)} %copy-done), custom_call_target="tpu_custom_call" | custom-call | tf_op jit(solution)/shard_map/edges/pallas_call | solution.py:498
  3.3 2.7 %collective-permute-start = (bf16[8,1,32,256]{3,2,1,0:T(8,128)(2,1)}, bf16[8,1,32,256]{3,2,1,0:T(8,128)(2,1)S(1)}, u32[]{:S(2)}, u32[]{:S(2)}) collective-permute-start(bf16[8,1,32,256]{3,2,1,0:T(8,128)(2,1)} %get-tuple-element.36), channel_id=1, source_target_pairs={{0,1},{1,2},{2,3},{3,4},{4,5},{5,6},{6,7},{7,0},{8,9},{9,10},{10,1... | collective-permute-start | bytes 393224 | tf_op jit(solution)/shard_map/ppermute | solution.py:13
  6.0 1.2 %collective-permute-start.4 = (bf16[2,16,32,256]{3,2,1,0:T(8,128)(2,1)}, bf16[2,16,32,256]{3,2,1,0:T(8,128)(2,1)S(1)}, u32[]{:S(2)}, u32[]{:S(2)}) collective-permute-start(bf16[2,16,32,256]{3,2,1,0:T(8,128)(2,1)} %get-tuple-element.42), channel_id=1, source_target_pairs={{0,8},{8,16},{16,24},{24,32},{32,40},{40,48},{48,56},{56,64},{64,7... | collective-permute-start | bytes 1572872 | tf_op jit(solution)/shard_map/ppermute | solution.py:13
  7.2 4.7 %collective-permute-start.5 = (bf16[2,16,32,256]{3,2,1,0:T(8,128)(2,1)}, bf16[2,16,32,256]{3,2,1,0:T(8,128)(2,1)S(1)}, u32[]{:S(2)}, u32[]{:S(2)}) collective-permute-start(bf16[2,16,32,256]{3,2,1,0:T(8,128)(2,1)} %get-tuple-element.43), channel_id=1, source_target_pairs={{0,120},{8,0},{16,8},{24,16},{32,24},{40,32},{48,40},{56,48},{64,5... | collective-permute-start | bytes 1572872 | tf_op jit(solution)/shard_map/ppermute | solution.py:13
  11.9 1.8 %copy.35 = s32[8,16,2,27]{1,0,3,2:T(8,128)} copy(s32[8,16,2,27]{3,2,1,0:T(2,128)} %param.11) | data formatting | bytes 55296 | tf_op jit(solution)/shard_map/optimization_barrier | solution.py:510
  13.7 0.7 convert_bitcast_fusion
  14.4 0.7 copy.36
  15.1 1.7 %broadcast_in_dim.14 = f32[8,16,2,128]{3,2,1,0:T(2,128)} broadcast(f32[8,16,2]{2,1,0:T(8,128)} %copy.36), dimensions={0,1,2} | broadcast | bytes 132096 | tf_op jit(solution)/shard_map/broadcast_in_dim | solution.py:517
  16.8 1.7 %reshape.17 = f32[8,16,256]{2,1,0:T(8,128)} reshape(f32[8,16,2,128]{3,2,1,0:T(2,128)} %broadcast_in_dim.14) | data formatting | bytes 262144 | tf_op jit(solution)/shard_map/reshape | solution.py:517
  18.5 1.1 %fusion = (f32[8,16,256]{2,1,0:T(8,128)S(1)}, f32[8,16,256]{2,1,0:T(8,128)S(1)}) fusion(f32[8,16,256]{2,1,0:T(8,128)} %param.13, f32[8,16,256]{2,1,0:T(8,128)} %reshape.17, s32[8,16,256]{2,1,0:T(8,128)} %param.10), kind=kLoop, calls=%fused_computation.15 | loop fusion | flops 98304 | bytes 655360 | tf_op jit(solution)/shard_map/mul | solution.py:518
  19.6 2.0 %collective-permute-start.2 = (f32[2,8,256]{2,0,1:T(2,128)S(1)}, f32[2,8,256]{2,0,1:T(2,128)S(1)}, u32[]{:S(2)}, u32[]{:S(2)}) collective-permute-start(f32[2,8,256]{2,0,1:T(2,128)S(1)} %pad_maximum_fusion.2), channel_id=1, source_target_pairs={{0,1},{1,2},{2,3},{3,4},{4,5},{5,6},{6,7},{7,0},{8,9},{9,10},{10,1... | collective-permute-start | bytes 49160 | tf_op jit(solution)/shard_map/ppermute | solution.py:13
  21.8 0.9 %copy-done.3 = bf16[27,32,32]{2,1,0:T(8,128)(2,1)S(1)} copy-done((bf16[27,32,32]{2,1,0:T(8,128)(2,1)S(1)}, bf16[27,32,32]{2,1,0:T(8,128)(2,1)}, u32[]{:S(2)}) %copy-start.3) | copy-done | bytes 55320
  22.7 0.4 weights.1
  23.2 2.0 %collective-permute-done.3 = f32[2,8,256]{2,0,1:T(2,128)S(1)} collective-permute-done((f32[2,8,256]{2,0,1:T(2,128)S(1)}, f32[2,8,256]{2,0,1:T(2,128)S(1)}, u32[]{:S(2)}, u32[]{:S(2)}) %collective-permute-start.3) | collective-permute-done | bytes 16416 | tf_op jit(solution)/shard_map/ppermute | solution.py:13
  25.3 4.8 %collective-permute-start.7 = (bf16[7,32,256]{2,1,0:T(8,128)(2,1)S(1)}, bf16[7,32,256]{2,1,0:T(8,128)(2,1)S(1)}, u32[]{:S(2)}, u32[]{:S(2)}) collective-permute-start(bf16[7,32,256]{2,1,0:T(8,128)(2,1)S(1)} %get-tuple-element.45), channel_id=1, source_target_pairs={{0,120},{8,0},{16,8},{24,16},{32,24},{40,32},{48,40},{56,48},{64,5... | collective-permute-start | bytes 344072 | tf_op jit(solution)/shard_map/ppermute | solution.py:13
  30.1 3.6 %conv_inner.1.inner = bf16[6,16,32,256]{3,2,1,0:T(8,128)(2,1)S(1)} custom-call(bf16[8,16,32,256]{3,2,1,0:T(8,128)(2,1)S(1)} %copy-done.1, bf16[8,1,32,256]{3,2,1,0:T(8,128)(2,1)S(1)} %collective-permute-done.y_lo, bf16[8,1,32,256]{3,2,1,0:T(8,128)(2,1)S(1)} %collective-permute-done.1.y_hi, f32[2,8,256]{2,1,0:T(8,128)S(1)} %copy.39.m_lo, ...), custom_call_target="tpu_custom_call" | custom-call | tf_op jit(solution)/shard_map/conv_inner/pallas_call | solution.py:488
  33.7 1.5 %collective-permute-start.11 = (bf16[6,1,32,256]{3,2,1,0:T(8,128)(2,1)S(1)}, bf16[6,1,32,256]{3,2,1,0:T(8,128)(2,1)S(1)}, u32[]{:S(2)}, u32[]{:S(2)}) collective-permute-start(bf16[6,1,32,256]{3,2,1,0:T(8,128)(2,1)S(1)} %get-tuple-element.58), channel_id=1, source_target_pairs={{0,7},{1,0},{2,1},{3,2},{4,3},{5,4},{6,5},{7,6},{8,15},{9,8},{10,9... | collective-permute-start | bytes 294920 | tf_op jit(solution)/shard_map/ppermute | solution.py:13
  35.2 0.2 collective-permute-start.10
  35.5 1.9 %conv_edge.1.edge = bf16[4,16,32,256]{3,2,1,0:T(8,128)(2,1)S(1)} custom-call(bf16[8,16,32,256]{3,2,1,0:T(8,128)(2,1)S(1)} %copy-done.1, bf16[8,1,32,256]{3,2,1,0:T(8,128)(2,1)S(1)} %collective-permute-done.y_lo, bf16[8,1,32,256]{3,2,1,0:T(8,128)(2,1)S(1)} %collective-permute-done.1.y_hi, f32[2,8,256]{2,1,0:T(8,128)S(1)} %copy.39.m_lo, ...), custom_call_target="tpu_custom_call" | custom-call | tf_op jit(solution)/shard_map/conv_edge/pallas_call | solution.py:488
  37.4 2.2 %collective-permute-start.9 = (bf16[4,1,32,256]{3,2,1,0:T(8,128)(2,1)S(1)}, bf16[4,1,32,256]{3,2,1,0:T(8,128)(2,1)S(1)}, u32[]{:S(2)}, u32[]{:S(2)}) collective-permute-start(bf16[4,1,32,256]{3,2,1,0:T(8,128)(2,1)S(1)} %get-tuple-element.60), channel_id=1, source_target_pairs={{0,7},{1,0},{2,1},{3,2},{4,3},{5,4},{6,5},{7,6},{8,15},{9,8},{10,9... | collective-permute-start | bytes 196616 | tf_op jit(solution)/shard_map/ppermute | solution.py:13
  39.6 1.9 %first_inner.1 = (f32[6,16,32,256]{3,2,1,0:T(8,128)S(1)}, f32[4,16,256]{2,1,0:T(8,128)S(1)}) custom-call(bf16[6,16,32,256]{3,2,1,0:T(8,128)(2,1)S(1)} %conv_inner.1.inner, bf16[6,1,32,256]{3,2,1,0:T(8,128)(2,1)S(1)} %collective-permute-done.10.i_lo, bf16[6,1,32,256]{3,2,1,0:T(8,128)(2,1)S(1)} %collective-permute-done.11.i_hi, ...), custom_call_target="tpu_custom_call" | custom-call | tf_op jit(solution)/shard_map/first_inner/pallas_call | solution.py:488
  41.6 1.7 %collective-permute-done.8.e_lo = bf16[4,1,32,256]{3,2,1,0:T(8,128)(2,1)S(1)} collective-permute-done((bf16[4,1,32,256]{3,2,1,0:T(8,128)(2,1)S(1)}, bf16[4,1,32,256]{3,2,1,0:T(8,128)(2,1)S(1)}, u32[]{:S(2)}, u32[]{:S(2)}) %collective-permute-start.8) | collective-permute-done | bytes 65568 | tf_op jit(solution)/shard_map/ppermute | solution.py:13
  43.3 1.4 %first_edge.1.first = f32[8,16,256]{2,1,0:T(8,128)S(1)} custom-call(bf16[6,16,32,256]{3,2,1,0:T(8,128)(2,1)S(1)} %conv_inner.1.inner, bf16[4,16,32,256]{3,2,1,0:T(8,128)(2,1)S(1)} %conv_edge.1.edge, bf16[4,1,32,256]{3,2,1,0:T(8,128)(2,1)S(1)} %collective-permute-done.8.e_lo, bf16[4,1,32,256]{3,2,1,0:T(8,128)(2,1)S(1)} %collective-permute-done.9.e_hi, ...), custom_call_target="tpu_custom_call" | custom-call | tf_op jit(solution)/shard_map/first_edge/pallas_call | solution.py:488
  44.7 4.2 %collective-permute-start.13 = (f32[8,256]{1,0:T(8,128)S(1)}, f32[8,256]{1,0:T(8,128)S(1)}, u32[]{:S(2)}, u32[]{:S(2)}) collective-permute-start(f32[8,256]{1,0:T(8,128)S(1)} %bitcast.26), channel_id=1, source_target_pairs={{0,7},{1,0},{2,1},{3,2},{4,3},{5,4},{6,5},{7,6},{8,15},{9,8},{10,9... | collective-permute-start | bytes 24584 | tf_op jit(solution)/shard_map/ppermute | solution.py:13
  48.9 0.8 %collective-permute-done.13.w_hi = f32[8,256]{1,0:T(8,128)S(1)} collective-permute-done((f32[8,256]{1,0:T(8,128)S(1)}, f32[8,256]{1,0:T(8,128)S(1)}, u32[]{:S(2)}, u32[]{:S(2)}) %collective-permute-start.13) | collective-permute-done | bytes 8224 | tf_op jit(solution)/shard_map/ppermute | solution.py:13
  49.7 0.3 collective-permute-done.12.w_lo
  50.1 4.8 %collective-permute-start.15 = (f32[18,256]{1,0:T(8,128)S(1)}, f32[18,256]{1,0:T(8,128)S(1)}, u32[]{:S(2)}, u32[]{:S(2)}) collective-permute-start(f32[18,256]{1,0:T(8,128)S(1)} %pad_maximum_fusion.1), channel_id=1, source_target_pairs={{0,120},{8,0},{16,8},{24,16},{32,24},{40,32},{48,40},{56,48},{64,5... | collective-permute-start | bytes 55304 | tf_op jit(solution)/shard_map/ppermute | solution.py:13
  54.9 3.1 %second_inner.1 = (f32[8,16,32,256]{3,2,1,0:T(8,128)S(1)}, f32[6,16,256]{2,1,0:T(8,128)S(1)}, f32[10,16,256]{2,1,0:T(8,128)S(1)}) custom-call(bf16[6,16,32,256]{3,2,1,0:T(8,128)(2,1)S(1)} %conv_inner.1.inner, bf16[4,16,32,256]{3,2,1,0:T(8,128)(2,1)S(1)} %conv_edge.1.edge, bf16[6,1,32,256]{3,2,1,0:T(8,128)(2,1)S(1)} %collective-permute-done.10.i_lo, ...), custom_call_target="tpu_custom_call" | custom-call | tf_op jit(solution)/shard_map/second_inner/pallas_call | solution.py:488
  58.1 1.2 %second_edge.1 = (f32[2,16,256]{2,1,0:T(8,128)S(1)}, f32[1,128]{1,0:T(1,128)S(1)}) custom-call(bf16[4,16,32,256]{3,2,1,0:T(8,128)(2,1)S(1)} %conv_edge.1.edge, bf16[4,1,32,256]{3,2,1,0:T(8,128)(2,1)S(1)} %collective-permute-done.8.e_lo, bf16[4,1,32,256]{3,2,1,0:T(8,128)(2,1)S(1)} %collective-permute-done.9.e_hi, f32[8,16,256]{2,1,0:T(8,128)S(1)} %get-tuple-element.41.start, ...), custom_call_target="tpu_custom_call" | custom-call | tf_op jit(solution)/shard_map/second_edge/pallas_call | solution.py:488
  59.4 18.0 %all_to_all.5 = f32[128,1,128]{2,1,0:T(1,128)S(1)} all-to-all(f32[128,1,128]{2,1,0:T(1,128)S(1)} %broadcast_in_dim.17), channel_id=1, replica_groups=mesh['sx'=16,'sy'=8] {'sx','sy'}, dimensions={0} | all-to-all | bytes 131072 | tf_op jit(solution)/shard_map/all_to_all | solution.py:607
  77.3 0.9 %final.1 = (f32[8,16,256]{2,1,0:T(8,128)}, f32[8,16,256]{2,1,0:T(8,128)}) custom-call(f32[128,128]{1,0:T(8,128)S(1)} %bitcast.23, f32[8,16,256]{2,1,0:T(8,128)S(1)} %get-tuple-element.41.start, f32[8,16,256]{2,1,0:T(8,128)S(1)} %first_edge.1.first, f32[6,16,256]{2,1,0:T(8,128)S(1)} %get-tuple-element.54.inside, f32[2,16,256]{2,1,0:T(8,128)S(1)} %get-tuple-element.55.sides), custom_call_target="tpu_custom_call" | custom-call | tf_op jit(solution)/shard_map/final/pallas_call | solution.py:488
  (43 shorter events, 0.5 us)
Async XLA Ops:
  0.6 1.6 %copy-start = (bf16[8,16,32,256]{3,2,1,0:T(8,128)(2,1)S(1)}, bf16[8,16,32,256]{3,2,1,0:T(8,128)(2,1)}, u32[]{:S(2)}) copy-start(bf16[8,16,32,256]{3,2,1,0:T(8,128)(2,1)} %own.5) | copy-start | bytes 6291460
  2.2 19.5 %copy-start.4 = (f32[32]{0:T(128)S(1)}, f32[32]{0:T(128)}, u32[]{:S(2)}) copy-start(f32[32]{0:T(128)} %param.9) | copy-start | bytes 388
  2.2 27.9 %copy-start.1 = (bf16[8,16,32,256]{3,2,1,0:T(8,128)(2,1)S(1)}, bf16[8,16,32,256]{3,2,1,0:T(8,128)(2,1)}, u32[]{:S(2)}) copy-start(bf16[8,16,32,256]{3,2,1,0:T(8,128)(2,1)} %own.5) | copy-start | bytes 6291460
  3.3 16.3 %collective-permute-start = (bf16[8,1,32,256]{3,2,1,0:T(8,128)(2,1)}, bf16[8,1,32,256]{3,2,1,0:T(8,128)(2,1)S(1)}, u32[]{:S(2)}, u32[]{:S(2)}) collective-permute-start(bf16[8,1,32,256]{3,2,1,0:T(8,128)(2,1)} %get-tuple-element.36), channel_id=1, source_target_pairs={{0,1},{1,2},{2,3},{3,4},{4,5},{5,6},{6,7},{7,0},{8,9},{9,10},{10,1... | collective-permute-start | bytes 393224 | tf_op jit(solution)/shard_map/ppermute | solution.py:13
  6.0 13.6 %collective-permute-start.1 = (bf16[8,1,32,256]{3,2,1,0:T(8,128)(2,1)S(1)}, bf16[8,1,32,256]{3,2,1,0:T(8,128)(2,1)S(1)}, u32[]{:S(2)}, u32[]{:S(2)}) collective-permute-start(bf16[8,1,32,256]{3,2,1,0:T(8,128)(2,1)S(1)} %get-tuple-element.37), channel_id=1, source_target_pairs={{0,7},{1,0},{2,1},{3,2},{4,3},{5,4},{6,5},{7,6},{8,15},{9,8},{10,9... | collective-permute-start | bytes 393224 | tf_op jit(solution)/shard_map/ppermute | solution.py:13
  6.0 29.5 %collective-permute-start.4 = (bf16[2,16,32,256]{3,2,1,0:T(8,128)(2,1)}, bf16[2,16,32,256]{3,2,1,0:T(8,128)(2,1)S(1)}, u32[]{:S(2)}, u32[]{:S(2)}) collective-permute-start(bf16[2,16,32,256]{3,2,1,0:T(8,128)(2,1)} %get-tuple-element.42), channel_id=1, source_target_pairs={{0,8},{8,16},{16,24},{24,32},{32,40},{40,48},{48,56},{56,64},{64,7... | collective-permute-start | bytes 1572872 | tf_op jit(solution)/shard_map/ppermute | solution.py:13
  7.2 28.3 %collective-permute-start.5 = (bf16[2,16,32,256]{3,2,1,0:T(8,128)(2,1)}, bf16[2,16,32,256]{3,2,1,0:T(8,128)(2,1)S(1)}, u32[]{:S(2)}, u32[]{:S(2)}) collective-permute-start(bf16[2,16,32,256]{3,2,1,0:T(8,128)(2,1)} %get-tuple-element.43), channel_id=1, source_target_pairs={{0,120},{8,0},{16,8},{24,16},{32,24},{40,32},{48,40},{56,48},{64,5... | collective-permute-start | bytes 1572872 | tf_op jit(solution)/shard_map/ppermute | solution.py:13
  19.6 3.5 %collective-permute-start.2 = (f32[2,8,256]{2,0,1:T(2,128)S(1)}, f32[2,8,256]{2,0,1:T(2,128)S(1)}, u32[]{:S(2)}, u32[]{:S(2)}) collective-permute-start(f32[2,8,256]{2,0,1:T(2,128)S(1)} %pad_maximum_fusion.2), channel_id=1, source_target_pairs={{0,1},{1,2},{2,3},{3,4},{4,5},{5,6},{6,7},{7,0},{8,9},{9,10},{10,1... | collective-permute-start | bytes 49160 | tf_op jit(solution)/shard_map/ppermute | solution.py:13
  21.7 3.5 %collective-permute-start.3 = (f32[2,8,256]{2,0,1:T(2,128)S(1)}, f32[2,8,256]{2,0,1:T(2,128)S(1)}, u32[]{:S(2)}, u32[]{:S(2)}) collective-permute-start(f32[2,8,256]{2,0,1:T(2,128)S(1)} %pad_maximum_fusion.3), channel_id=1, source_target_pairs={{0,7},{1,0},{2,1},{3,2},{4,3},{5,4},{6,5},{7,6},{8,15},{9,8},{10,9... | collective-permute-start | bytes 49160 | tf_op jit(solution)/shard_map/ppermute | solution.py:13
  21.8 0.9 %copy-start.3 = (bf16[27,32,32]{2,1,0:T(8,128)(2,1)S(1)}, bf16[27,32,32]{2,1,0:T(8,128)(2,1)}, u32[]{:S(2)}) copy-start(bf16[27,32,32]{2,1,0:T(8,128)(2,1)} %taps) | copy-start | bytes 165892
  25.2 10.0 %collective-permute-start.6 = (bf16[7,32,256]{2,1,0:T(8,128)(2,1)S(1)}, bf16[7,32,256]{2,1,0:T(8,128)(2,1)S(1)}, u32[]{:S(2)}, u32[]{:S(2)}) collective-permute-start(bf16[7,32,256]{2,1,0:T(8,128)(2,1)S(1)} %get-tuple-element.44), channel_id=1, source_target_pairs={{0,8},{8,16},{16,24},{24,32},{32,40},{40,48},{48,56},{56,64},{64,7... | collective-permute-start | bytes 344072 | tf_op jit(solution)/shard_map/ppermute | solution.py:13
  25.3 10.1 %collective-permute-start.7 = (bf16[7,32,256]{2,1,0:T(8,128)(2,1)S(1)}, bf16[7,32,256]{2,1,0:T(8,128)(2,1)S(1)}, u32[]{:S(2)}, u32[]{:S(2)}) collective-permute-start(bf16[7,32,256]{2,1,0:T(8,128)(2,1)S(1)} %get-tuple-element.45), channel_id=1, source_target_pairs={{0,120},{8,0},{16,8},{24,16},{32,24},{40,32},{48,40},{56,48},{64,5... | collective-permute-start | bytes 344072 | tf_op jit(solution)/shard_map/ppermute | solution.py:13
  33.7 5.9 %collective-permute-start.11 = (bf16[6,1,32,256]{3,2,1,0:T(8,128)(2,1)S(1)}, bf16[6,1,32,256]{3,2,1,0:T(8,128)(2,1)S(1)}, u32[]{:S(2)}, u32[]{:S(2)}) collective-permute-start(bf16[6,1,32,256]{3,2,1,0:T(8,128)(2,1)S(1)} %get-tuple-element.58), channel_id=1, source_target_pairs={{0,7},{1,0},{2,1},{3,2},{4,3},{5,4},{6,5},{7,6},{8,15},{9,8},{10,9... | collective-permute-start | bytes 294920 | tf_op jit(solution)/shard_map/ppermute | solution.py:13
  35.2 4.4 %copy-start.2 = (f32[8,16,256]{2,1,0:T(8,128)S(1)}, f32[8,16,256]{2,1,0:T(8,128)}, u32[]{:S(2)}) copy-start(f32[8,16,256]{2,1,0:T(8,128)} %ridge.7) | copy-start | bytes 393220
  35.2 4.4 %collective-permute-start.10 = (bf16[6,1,32,256]{3,2,1,0:T(8,128)(2,1)S(1)}, bf16[6,1,32,256]{3,2,1,0:T(8,128)(2,1)S(1)}, u32[]{:S(2)}, u32[]{:S(2)}) collective-permute-start(bf16[6,1,32,256]{3,2,1,0:T(8,128)(2,1)S(1)} %get-tuple-element.59), channel_id=1, source_target_pairs={{0,1},{1,2},{2,3},{3,4},{4,5},{5,6},{6,7},{7,0},{8,9},{9,10},{10,1... | collective-permute-start | bytes 294920 | tf_op jit(solution)/shard_map/ppermute | solution.py:13
  37.4 4.1 %collective-permute-start.9 = (bf16[4,1,32,256]{3,2,1,0:T(8,128)(2,1)S(1)}, bf16[4,1,32,256]{3,2,1,0:T(8,128)(2,1)S(1)}, u32[]{:S(2)}, u32[]{:S(2)}) collective-permute-start(bf16[4,1,32,256]{3,2,1,0:T(8,128)(2,1)S(1)} %get-tuple-element.60), channel_id=1, source_target_pairs={{0,7},{1,0},{2,1},{3,2},{4,3},{5,4},{6,5},{7,6},{8,15},{9,8},{10,9... | collective-permute-start | bytes 196616 | tf_op jit(solution)/shard_map/ppermute | solution.py:13
  39.6 3.7 %collective-permute-start.8 = (bf16[4,1,32,256]{3,2,1,0:T(8,128)(2,1)S(1)}, bf16[4,1,32,256]{3,2,1,0:T(8,128)(2,1)S(1)}, u32[]{:S(2)}, u32[]{:S(2)}) collective-permute-start(bf16[4,1,32,256]{3,2,1,0:T(8,128)(2,1)S(1)} %get-tuple-element.61), channel_id=1, source_target_pairs={{0,1},{1,2},{2,3},{3,4},{4,5},{5,6},{6,7},{7,0},{8,9},{9,10},{10,1... | collective-permute-start | bytes 196616 | tf_op jit(solution)/shard_map/ppermute | solution.py:13
  44.7 5.0 %collective-permute-start.13 = (f32[8,256]{1,0:T(8,128)S(1)}, f32[8,256]{1,0:T(8,128)S(1)}, u32[]{:S(2)}, u32[]{:S(2)}) collective-permute-start(f32[8,256]{1,0:T(8,128)S(1)} %bitcast.26), channel_id=1, source_target_pairs={{0,7},{1,0},{2,1},{3,2},{4,3},{5,4},{6,5},{7,6},{8,15},{9,8},{10,9... | collective-permute-start | bytes 24584 | tf_op jit(solution)/shard_map/ppermute | solution.py:13
  48.9 1.2 %collective-permute-start.12 = (f32[8,256]{1,0:T(8,128)S(1)}, f32[8,256]{1,0:T(8,128)S(1)}, u32[]{:S(2)}, u32[]{:S(2)}) collective-permute-start(f32[8,256]{1,0:T(8,128)S(1)} %bitcast.27), channel_id=1, source_target_pairs={{0,1},{1,2},{2,3},{3,4},{4,5},{5,6},{6,7},{7,0},{8,9},{9,10},{10,1... | collective-permute-start | bytes 24584 | tf_op jit(solution)/shard_map/ppermute | solution.py:13
  50.0 8.0 %collective-permute-start.14 = (f32[18,256]{1,0:T(8,128)S(1)}, f32[18,256]{1,0:T(8,128)S(1)}, u32[]{:S(2)}, u32[]{:S(2)}) collective-permute-start(f32[18,256]{1,0:T(8,128)S(1)} %pad_maximum_fusion), channel_id=1, source_target_pairs={{0,8},{8,16},{16,24},{24,32},{32,40},{40,48},{48,56},{56,64},{64,7... | collective-permute-start | bytes 55304 | tf_op jit(solution)/shard_map/ppermute | solution.py:13
  50.1 7.9 %collective-permute-start.15 = (f32[18,256]{1,0:T(8,128)S(1)}, f32[18,256]{1,0:T(8,128)S(1)}, u32[]{:S(2)}, u32[]{:S(2)}) collective-permute-start(f32[18,256]{1,0:T(8,128)S(1)} %pad_maximum_fusion.1), channel_id=1, source_target_pairs={{0,120},{8,0},{16,8},{24,16},{32,24},{40,32},{48,40},{56,48},{64,5... | collective-permute-start | bytes 55304 | tf_op jit(solution)/shard_map/ppermute | solution.py:13

commit v5 on v4

--- a/solution.py
+++ b/solution.py
@@ -20,18 +20,49 @@
     return before, after
 
 
-def edges_kernel(own, x_hi, x_lo, y_hi, y_lo, sems):
-    rows, cols = own.shape[:2]
+def edges_kernel(own, x_hi, x_lo, token, sems):
+    rows = own.shape[0]
     copies = [
         pltpu.make_async_copy(own.at[rows - 2 : rows], x_hi, sems.at[0]),
         pltpu.make_async_copy(own.at[0:2], x_lo, sems.at[1]),
-        pltpu.make_async_copy(own.at[:, cols - 1 : cols], y_hi, sems.at[2]),
-        pltpu.make_async_copy(own.at[:, 0:1], y_lo, sems.at[3]),
     ]
     for copy in copies:
         copy.start()
+    token[...] = jnp.zeros_like(token)
     for copy in copies:
         copy.wait()
+
+
+def three(value):
+    high = value.astype(jnp.bfloat16).astype(jnp.float32)
+    rest = value - high
+    mid = rest.astype(jnp.bfloat16).astype(jnp.float32)
+    return high, mid, rest - mid
+
+
+def prep_kernel(token, own, ids, occupancy, target, mask, start, out_hi, out_lo, present):
+    rows, cols, channels, depth = own.shape
+    half = present.shape[1]
+    present[...] = jnp.broadcast_to(
+        jnp.where(ids[:, 13:14] >= 0, 1.0, 0.0).astype(jnp.float32), present.shape
+    )
+    for x in range(rows):
+        blocks = [present[pl.ds(2 * cols * x + z, cols, stride=2), :] for z in range(depth // half)]
+        mask[x] = occupancy[x].astype(jnp.float32) * jnp.concatenate(blocks, axis=1)
+        start[x] = mask[x] * target[x]
+    for out, y in ((out_hi, cols - 1), (out_lo, 0)):
+        for x in range(rows):
+            out[x] = own[x, y] * mask[x, y : y + 1, :].astype(jnp.bfloat16)
+        edge = jnp.concatenate([start[x, y : y + 1, :] for x in range(rows)], axis=0)
+        blank = jnp.zeros((channels - 3 * rows, depth), jnp.float32)
+        out[rows] = jnp.concatenate([*three(edge), blank], axis=0).astype(jnp.bfloat16)
+
+
+def start_rims(y_lo, y_hi, out):
+    rows = y_lo.shape[0] - 1
+    for k, ref in enumerate((y_lo, y_hi)):
+        terms = ref[rows].astype(jnp.float32)
+        out[k] = (terms[:rows] + terms[rows : 2 * rows]) + terms[2 * rows : 3 * rows]
 
 
 def weights_kernel(taps, bias, wide, bias_col):
@@ -85,8 +116,8 @@
             out[out_x + step_x, y + step_y] = value.astype(jnp.bfloat16)
 
 
-def as_bf16(row, flag):
-    return (row * flag).astype(jnp.bfloat16)
+def splat(flag, shape):
+    return jnp.full(shape, flag, jnp.float32).astype(jnp.bfloat16)
 
 
 def fill_row(grid, grid_x, mask, middle, low, high):
@@ -97,9 +128,9 @@
     grid[grid_x, cols + 1] = high
 
 
-def fill_own(grid, grid_x, own, mask, y_lo, y_hi, m_lo, m_hi, flags, x):
-    low = y_lo[x, 0] * as_bf16(m_lo[0, pl.ds(x, 1)], flags[0])
-    high = y_hi[x, 0] * as_bf16(m_hi[0, pl.ds(x, 1)], flags[1])
+def fill_own(grid, grid_x, own, mask, y_lo, y_hi, flags, x):
+    low = y_lo[x] * splat(flags[0], y_lo.shape[1:])
+    high = y_hi[x] * splat(flags[1], y_hi.shape[1:])
     fill_row(grid, grid_x, mask_of(mask, x), lambda y: own[x, y], low, high)
 
 
@@ -107,12 +138,12 @@
     return lambda y: mask[x, y : y + 1, :]
 
 
-def conv_inner_kernel(own, y_lo, y_hi, m_lo, m_hi, mask, wide, bias, out, grid):
+def conv_inner_kernel(own, y_lo, y_hi, mask, wide, bias, out, grid):
     rows, cols, channels, depth = own.shape
     flags = mesh_flags()
 
     def fill(x, carry):
-        fill_own(grid, x, own, mask, y_lo, y_hi, m_lo, m_hi, flags, x)
+        fill_own(grid, x, own, mask, y_lo, y_hi, flags, x)
         return carry
 
     lax.fori_loop(0, rows, fill, 0)
@@ -128,23 +159,23 @@
     lax.fori_loop(0, rows // 2 - 1, pair, 0)
 
 
-def sides_kernel(y_lo, y_hi, m_lo, m_hi, mask, start, out_hi, out_lo):
+def sides_kernel(y_lo, y_hi, mask, start, out_hi, out_lo):
     rows, cols, depth = mask.shape
     flags = mesh_flags()
-
-    def three(value):
-        high = value.astype(jnp.bfloat16).astype(jnp.float32)
-        rest = value - high
-        mid = rest.astype(jnp.bfloat16).astype(jnp.float32)
-        return high, mid, rest - mid
-
+    clear = [splat(flag, y_lo.shape[1:]) for flag in flags[:2]]
+    low_terms = y_lo[rows].astype(jnp.float32)
+    high_terms = y_hi[rows].astype(jnp.float32)
     for out, pair, row in ((out_hi, (rows - 2, rows - 1), rows - 1), (out_lo, (0, 1), 0)):
         for k, x in enumerate(pair):
-            out[2 * k] = y_lo[x, 0] * as_bf16(m_lo[0, pl.ds(x, 1)], flags[0])
-            out[2 * k + 1] = y_hi[x, 0] * as_bf16(m_hi[0, pl.ds(x, 1)], flags[1])
+            out[2 * k] = y_lo[x] * clear[0]
+            out[2 * k + 1] = y_hi[x] * clear[1]
         out[4] = jnp.concatenate([mask[x] for x in pair], axis=0).astype(jnp.bfloat16)
         high, mid, low = three(start[row])
-        rims = three(jnp.concatenate([m_lo[1, row : row + 1], m_hi[1, row : row + 1]], axis=0))
+        rims = [
+            terms[at : at + 1]
+            for at in (row, rows + row, 2 * rows + row)
+            for terms in (low_terms, high_terms)
+        ]
         blank = jnp.zeros((10, depth), jnp.float32)
         out[5] = jnp.concatenate([high, mid], axis=0).astype(jnp.bfloat16)
         out[6] = jnp.concatenate([low, *rims, blank], axis=0).astype(jnp.bfloat16)
@@ -154,8 +185,6 @@
     own,
     y_lo,
     y_hi,
-    m_lo,
-    m_hi,
     x_lo,
     x_hi,
     side_lo,
@@ -175,7 +204,7 @@
         side_mask[2 * k + 1] = both[cols:]
     for x in range(2):
         for k, ref, side in ((0, x_lo, side_lo), (1, x_hi, side_hi)):
-            clear = jnp.full((channels, depth), flags[2 + k], jnp.float32).astype(jnp.bfloat16)
+            clear = splat(flags[2 + k], (channels, depth))
             fill_row(
                 grid,
                 6 * k + x,
@@ -184,8 +213,8 @@
                 side[2 * x] * clear,
                 side[2 * x + 1] * clear,
             )
-        fill_own(grid, 2 + x, own, mask, y_lo, y_hi, m_lo, m_hi, flags, x)
-        fill_own(grid, 4 + x, own, mask, y_lo, y_hi, m_lo, m_hi, flags, rows - 2 + x)
+        fill_own(grid, 2 + x, own, mask, y_lo, y_hi, flags, x)
+        fill_own(grid, 4 + x, own, mask, y_lo, y_hi, flags, rows - 2 + x)
     lane = lax.broadcasted_iota(jnp.int32, (4 * channels, depth), 1)
     bias_all = bias[...]
     for side, masks in (
@@ -283,10 +312,11 @@
     return ridge_row * value_row + inner * (1.0 / (8 * channels))
 
 
-def first_inner_kernel(inner, i_lo, i_hi, start, m_lo, m_hi, ridge, smooth, out):
+def first_inner_kernel(inner, i_lo, i_hi, start, y_lo, y_hi, ridge, smooth, out, rims):
     rows = inner.shape[0]
     flags = mesh_flags()
-    s_lo, s_hi = (rim_of(m_lo, 1), rim_of(m_hi, 1))
+    start_rims(y_lo, y_hi, rims)
+    s_lo, s_hi = (rim_of(rims, 0), rim_of(rims, 1))
 
     def stage_y(k, carry):
         along_y(smooth, k, inner, i_lo, i_hi, k, flags, own_row(start, s_lo, s_hi, k + 1))
@@ -309,23 +339,27 @@
     e_lo,
     e_hi,
     start,
-    m_lo,
-    m_hi,
+    y_lo,
+    y_hi,
     side_lo,
     side_hi,
     ridge,
     smooth,
     part,
     out,
+    out_hi,
+    out_lo,
     rim,
     side_start,
     side_rims,
+    rims,
 ):
     n = inner.shape[0]
     flags = mesh_flags()
     last = n + 1
     cols = inner.shape[1]
-    s_lo, s_hi = (rim_of(m_lo, 1), rim_of(m_hi, 1))
+    start_rims(y_lo, y_hi, rims)
+    s_lo, s_hi = (rim_of(rims, 0), rim_of(rims, 1))
     for k, side in enumerate((side_lo, side_hi)):
         upper = side[5].astype(jnp.float32)
         lower = side[6].astype(jnp.float32)
@@ -356,6 +390,8 @@
         out[x] = along_x(before, here, after, field, row, ridge[x], start[x])
     for x in range(n - 2):
         out[x + 2] = part[x]
+    for ref, y in ((out_hi, cols - 1), (out_lo, 0)):
+        ref[...] = jnp.concatenate([out[x, y : y + 1, :] for x in range(n + 2)], axis=0)
 
 
 PRODUCTS = ((0, 0), (0, 1), (1, 1), (0, 2), (1, 2))
@@ -479,7 +515,6 @@
 
 def per_device(features, conv_weight, conv_bias, occupancy, block_ids, ridge, target):
     rows, cols, channels, depth = features.shape
-    voxels = depth // block_ids.shape[2]
     f32, bf16 = (jnp.float32, jnp.bfloat16)
     vmem = pl.BlockSpec(memory_space=pltpu.VMEM)
     anywhere = pl.BlockSpec(memory_space=pl.ANY)
@@ -495,34 +530,30 @@
             name=name,
         )(*args)
 
-    edges = pl.pallas_call(
+    x_hi, x_lo, token = pl.pallas_call(
         edges_kernel,
-        out_shape=[
-            jax.ShapeDtypeStruct(shape + (channels, depth), bf16)
-            for shape in ((2, cols), (2, cols), (rows, 1), (rows, 1))
-        ],
-        in_specs=[pl.BlockSpec(memory_space=pltpu.HBM)],
-        out_specs=[anywhere] * 4,
-        scratch_shapes=[pltpu.SemaphoreType.DMA((4,))],
-        compiler_params=pltpu.CompilerParams(vmem_limit_bytes=1 << 20),
+        out_shape=[jax.ShapeDtypeStruct((2, cols, channels, depth), bf16) for _ in range(2)]
+        + [jax.ShapeDtypeStruct((8, 128), f32)],
+        in_specs=[anywhere],
+        out_specs=[anywhere, anywhere, vmem],
+        scratch_shapes=[pltpu.SemaphoreType.DMA((2,))],
+        compiler_params=pltpu.CompilerParams(vmem_limit_bytes=60 << 20),
         name="edges",
     )(features)
-    edges, occupancy, block_ids, target, conv_weight = lax.optimization_barrier(
-        (edges, occupancy, block_ids, target, conv_weight)
-    )
-    x_lo, x_hi = (shift(edges[0], "sx", 1), shift(edges[1], "sx", -1))
-    y_lo, y_hi = (shift(edges[2], "sy", 1), shift(edges[3], "sy", -1))
-
-    present = (block_ids[:, :, :, 13] >= 0).astype(f32)
-    weight_mask = occupancy.astype(f32) * jnp.repeat(present, voxels, axis=2)
-    residual = weight_mask * target
-    weight_mask, residual, y_lo, y_hi = lax.optimization_barrier(
-        (weight_mask, residual, y_lo, y_hi)
-    )
-    m_lo, m_hi = [
-        shift(jnp.stack([weight_mask[:, y], residual[:, y]]), "sy", step)
-        for y, step in ((cols - 1, 1), (0, -1))
-    ]
+    x_lo, x_hi = (shift(x_hi, "sx", 1), shift(x_lo, "sx", -1))
+
+    plane = ((rows, cols, depth), f32)
+    blocks = block_ids.reshape(-1, block_ids.shape[3])
+    edge_column = ((rows + 1, channels, depth), bf16)
+    weight_mask, residual, y_hi, y_lo = call(
+        prep_kernel,
+        (token, features, blocks, occupancy, target),
+        [plane, plane, edge_column, edge_column],
+        [((blocks.shape[0], depth // block_ids.shape[2]), f32)],
+        4,
+        "prep",
+    )
+    y_lo, y_hi = (shift(y_hi, "sy", 1), shift(y_lo, "sy", -1))
     wide, bias = call(
         weights_kernel,
         (conv_weight, conv_bias[None]),
@@ -531,14 +562,14 @@
         8,
         "weights",
     )
+    rims_scratch = ((2, rows, depth), f32)
     grid_scratch = ((rows, cols + 2, channels, depth), bf16)
     inner_shape = (rows - 2, cols, channels, depth)
     edge_shape = (4, cols, channels, depth)
     side_shape = (7, channels, depth)
-    plane = ((rows, cols, depth), f32)
     side_hi, side_lo = call(
         sides_kernel,
-        (y_lo, y_hi, m_lo, m_hi, weight_mask, residual),
+        (y_lo, y_hi, weight_mask, residual),
         [(side_shape, bf16), (side_shape, bf16)],
         [],
         4,
@@ -547,7 +578,7 @@
     side_lo, side_hi = (shift(side_hi, "sx", 1), shift(side_lo, "sx", -1))
     (inner,) = call(
         conv_inner_kernel,
-        (features, y_lo, y_hi, m_lo, m_hi, weight_mask, wide, bias),
+        (features, y_lo, y_hi, weight_mask, wide, bias),
         [(inner_shape, bf16)],
         [grid_scratch],
         12,
@@ -556,30 +587,30 @@
     i_lo, i_hi = halo(inner, "sy", 1, 1)
     smooth, part = call(
         first_inner_kernel,
-        (inner, i_lo, i_hi, residual, m_lo, m_hi, ridge),
+        (inner, i_lo, i_hi, residual, y_lo, y_hi, ridge),
         [(inner_shape, f32), ((rows - 4, cols, depth), f32)],
-        [],
+        [rims_scratch],
         8,
         "first_inner",
     )
     (edge,) = call(
         conv_edge_kernel,
-        (features, y_lo, y_hi, m_lo, m_hi, x_lo, x_hi, side_lo, side_hi, weight_mask, wide, bias),
+        (features, y_lo, y_hi, x_lo, x_hi, side_lo, side_hi, weight_mask, wide, bias),
         [(edge_shape, bf16)],
         [grid_scratch, ((4, cols, depth), f32)],
         12,
         "conv_edge",
     )
     e_lo, e_hi = halo(edge, "sy", 1, 1)
-    (first,) = call(
+    first, w_hi, w_lo = call(
         first_edge_kernel,
-        (inner, edge, e_lo, e_hi, residual, m_lo, m_hi, side_lo, side_hi, ridge, smooth, part),
-        [plane],
-        [(edge_shape, f32), ((2, cols, depth), f32), ((2, 8, depth), f32)],
+        (inner, edge, e_lo, e_hi, residual, y_lo, y_hi, side_lo, side_hi, ridge, smooth, part),
+        [plane, ((rows, depth), f32), ((rows, depth), f32)],
+        [(edge_shape, f32), ((2, cols, depth), f32), ((2, 8, depth), f32), rims_scratch],
         8,
         "first_edge",
     )
-    w_lo, w_hi = (shift(first[:, -1], "sy", 1), shift(first[:, 0], "sy", -1))
+    w_lo, w_hi = (shift(w_hi, "sy", 1), shift(w_lo, "sy", -1))
     rims = [jnp.concatenate([w_lo[x : x + 1], first[x], w_hi[x : x + 1]]) for x in (rows - 1, 0)]
     r_lo, r_hi = (shift(rims[0], "sx", 1), shift(rims[1], "sx", -1))
     smooth, inside, grams = call(

time: 78.6 us -> 105 us (1.34)
  Pallas kernels: 15.6 us -> 48.1 us
  local copies, waits for them, and re-layouts: 8.53 us -> 3.49 us
  starting transfers between devices: 28.6 us -> 26.5 us
  other arithmetic: 1.81 us -> 0.02 us
  waiting for transfers between devices: 4.94 us -> 6.53 us
  blocking collectives: 18 us -> 19.2 us
    pallas_call x1, Pallas kernels: 1.03 us -> 33.5 us  [per_device(): pl.pallas_call(edges_kernel, out_shape=[jax.ShapeDtypeStruct((2, cols, ch...]
    ppermute x16 -> x14, starting transfers between devices: 28.6 us -> 26.5 us  [shift(): lax.ppermute(value, axis, [(i, (i + step) % peers) for i in range(peers)])]
    optimization_barrier x1 -> x0, local copies, waits for them, and re-layouts: 1.77 us -> none  [per_device(): lax.optimization_barrier((edges, occupancy, block_ids, target, conv_weight))]
    broadcast_in_dim x1 -> x0, local copies, waits for them, and re-layouts: 1.69 us -> none  [per_device(): weight_mask = occupancy.astype(f32) * jnp.repeat(present, voxels, axis=2)]
    reshape x1 -> x0, local copies, waits for them, and re-layouts: 1.66 us -> none  [per_device(): weight_mask = occupancy.astype(f32) * jnp.repeat(present, voxels, axis=2)]
    ppermute x16 -> x14, waiting for transfers between devices: 4.94 us -> 6.53 us  [shift(): lax.ppermute(value, axis, [(i, (i + step) % peers) for i in range(peers)])]
    all_to_all x1, blocking collectives: 18 us -> 19.2 us  [per_device(): lax.all_to_all(jnp.broadcast_to(share[None], (peers, 1, 128)), AXES, 0, 0)]
    mul x1 -> x0, other arithmetic: 1.06 us -> none  [per_device(): residual = weight_mask * target]
  transfers between devices with their start and end apart: 16 -> 14, of which waited for: 4 -> 6; matrix products, arithmetic and copies ran while one was open for 10% -> 0% of each run, Pallas kernels for 14% -> 11%
where the time goes in v5:
time: 105 us
  Pallas kernels  48.1 us (46%)
  starting transfers between devices  26.5 us (25%)
  blocking collectives  19.2 us (18%)
  waiting for transfers between devices  6.53 us (6%)
  local copies, waits for them, and re-layouts  3.49 us (3%)
    pallas_call x1, Pallas kernels, per_device(): pl.pallas_call(edges_kernel, out_shape=[jax.ShapeDtypeStruct((2, cols, ch...  33.5 us
    ppermute x14, starting transfers between devices, shift(): lax.ppermute(value, axis, [(i, (i + step) % peers) for i in range(peers)])  26.5 us
    all_to_all x1, blocking collectives, per_device(): lax.all_to_all(jnp.broadcast_to(share[None], (peers, 1, 128)), AXES, 0, 0)  19.2 us
    pallas_call x10, Pallas kernels, call(): pl.pallas_call(kernel, out_shape=[jax.ShapeDtypeStruct(shape, dtype) for...  14.6 us
    ppermute x14, waiting for transfers between devices, shift(): lax.ppermute(value, axis, [(i, (i + step) % peers) for i in range(peers)])  6.53 us
    unnamed x16, local copies, waits for them, and re-layouts  3.41 us
  transfers between devices with their start and end apart: 14, of which 6 were waited for; matrix products, arithmetic and copies ran while one was open for 0% of the time, Pallas kernels for 11%

profile of v5, /device:TPU:1, one launch (start us, length us, event | category | flops | bytes accessed | tf_op | source)
XLA Modules:
  0.0 104.6 jit_solution(6546943579840599628)
XLA Ops:
  0.6 33.5 %edges.1 = (bf16[2,16,32,256]{3,2,1,0:T(8,128)(2,1)}, bf16[2,16,32,256]{3,2,1,0:T(8,128)(2,1)}, f32[8,128]{1,0:T(8,128)}) custom-call(bf16[8,16,32,256]{3,2,1,0:T(8,128)(2,1)} %own.7), custom_call_target="tpu_custom_call" | custom-call | tf_op jit(solution)/shard_map/edges/pallas_call | solution.py:533
  34.1 2.1 %collective-permute-start.2 = (bf16[2,16,32,256]{3,2,1,0:T(8,128)(2,1)}, bf16[2,16,32,256]{3,2,1,0:T(8,128)(2,1)S(1)}, u32[]{:S(2)}, u32[]{:S(2)}) collective-permute-start(bf16[2,16,32,256]{3,2,1,0:T(8,128)(2,1)} %get-tuple-element.26), channel_id=1, source_target_pairs={{0,8},{8,16},{16,24},{24,32},{32,40},{40,48},{48,56},{56,64},{64,7... | collective-permute-start | bytes 1572872 | tf_op jit(solution)/shard_map/ppermute | solution.py:13
  36.2 4.8 %collective-permute-start.3 = (bf16[2,16,32,256]{3,2,1,0:T(8,128)(2,1)}, bf16[2,16,32,256]{3,2,1,0:T(8,128)(2,1)S(1)}, u32[]{:S(2)}, u32[]{:S(2)}) collective-permute-start(bf16[2,16,32,256]{3,2,1,0:T(8,128)(2,1)} %get-tuple-element.27), channel_id=1, source_target_pairs={{0,120},{8,0},{16,8},{24,16},{32,24},{40,32},{48,40},{56,48},{64,5... | collective-permute-start | bytes 1572872 | tf_op jit(solution)/shard_map/ppermute | solution.py:13
  41.1 0.9 copy-done.3
  42.0 0.9 copy-done.4
  42.9 0.9 copy-done.5
  43.8 0.7 copy-done.6
  44.5 0.1 prep.1
  44.6 2.1 %collective-permute-start = (bf16[9,32,256]{2,1,0:T(8,128)(2,1)S(1)}, bf16[9,32,256]{2,1,0:T(8,128)(2,1)S(1)}, u32[]{:S(2)}, u32[]{:S(2)}) collective-permute-start(bf16[9,32,256]{2,1,0:T(8,128)(2,1)S(1)} %get-tuple-element.24), channel_id=1, source_target_pairs={{0,1},{1,2},{2,3},{3,4},{4,5},{5,6},{6,7},{7,0},{8,9},{9,10},{10,1... | collective-permute-start | bytes 442376 | tf_op jit(solution)/shard_map/ppermute | solution.py:13
  46.8 0.4 weights.1
  47.2 1.7 %collective-permute-done.y_lo = bf16[9,32,256]{2,1,0:T(8,128)(2,1)S(1)} collective-permute-done((bf16[9,32,256]{2,1,0:T(8,128)(2,1)S(1)}, bf16[9,32,256]{2,1,0:T(8,128)(2,1)S(1)}, u32[]{:S(2)}, u32[]{:S(2)}) %collective-permute-start) | collective-permute-done | bytes 147488 | tf_op jit(solution)/shard_map/ppermute | solution.py:13
  48.9 2.8 %collective-permute-done.1.y_hi = bf16[9,32,256]{2,1,0:T(8,128)(2,1)S(1)} collective-permute-done((bf16[9,32,256]{2,1,0:T(8,128)(2,1)S(1)}, bf16[9,32,256]{2,1,0:T(8,128)(2,1)S(1)}, u32[]{:S(2)}, u32[]{:S(2)}) %collective-permute-start.1) | collective-permute-done | bytes 147488 | tf_op jit(solution)/shard_map/ppermute | solution.py:13
  51.7 4.8 %collective-permute-start.5 = (bf16[7,32,256]{2,1,0:T(8,128)(2,1)S(1)}, bf16[7,32,256]{2,1,0:T(8,128)(2,1)S(1)}, u32[]{:S(2)}, u32[]{:S(2)}) collective-permute-start(bf16[7,32,256]{2,1,0:T(8,128)(2,1)S(1)} %get-tuple-element.31), channel_id=1, source_target_pairs={{0,120},{8,0},{16,8},{24,16},{32,24},{40,32},{48,40},{56,48},{64,5... | collective-permute-start | bytes 344072 | tf_op jit(solution)/shard_map/ppermute | solution.py:13
  56.5 3.5 %conv_inner.1.inner = bf16[6,16,32,256]{3,2,1,0:T(8,128)(2,1)S(1)} custom-call(bf16[8,16,32,256]{3,2,1,0:T(8,128)(2,1)S(1)} %copy-done, bf16[9,32,256]{2,1,0:T(8,128)(2,1)S(1)} %collective-permute-done.y_lo, bf16[9,32,256]{2,1,0:T(8,128)(2,1)S(1)} %collective-permute-done.1.y_hi, f32[8,16,256]{2,1,0:T(8,128)S(1)} %get-tuple-element.28.mask, ...), custom_call_target="tpu_custom_call" | custom-call | tf_op jit(solution)/shard_map/conv_inner/pallas_call | solution.py:523
  60.1 0.3 collective-permute-start.9
  60.4 1.4 %collective-permute-start.8 = (bf16[6,1,32,256]{3,2,1,0:T(8,128)(2,1)S(1)}, bf16[6,1,32,256]{3,2,1,0:T(8,128)(2,1)S(1)}, u32[]{:S(2)}, u32[]{:S(2)}) collective-permute-start(bf16[6,1,32,256]{3,2,1,0:T(8,128)(2,1)S(1)} %get-tuple-element.45), channel_id=1, source_target_pairs={{0,1},{1,2},{2,3},{3,4},{4,5},{5,6},{6,7},{7,0},{8,9},{9,10},{10,1... | collective-permute-start | bytes 294920 | tf_op jit(solution)/shard_map/ppermute | solution.py:13
  61.9 1.9 %conv_edge.1.edge = bf16[4,16,32,256]{3,2,1,0:T(8,128)(2,1)S(1)} custom-call(bf16[8,16,32,256]{3,2,1,0:T(8,128)(2,1)S(1)} %copy-done, bf16[9,32,256]{2,1,0:T(8,128)(2,1)S(1)} %collective-permute-done.y_lo, bf16[9,32,256]{2,1,0:T(8,128)(2,1)S(1)} %collective-permute-done.1.y_hi, bf16[2,16,32,256]{3,2,1,0:T(8,128)(2,1)S(1)} %collective-permute-done.2.x_lo, ...), custom_call_target="tpu_custom_call" | custom-call | tf_op jit(solution)/shard_map/conv_edge/pallas_call | solution.py:523
  63.8 1.3 %collective-permute-start.7 = (bf16[4,1,32,256]{3,2,1,0:T(8,128)(2,1)S(1)}, bf16[4,1,32,256]{3,2,1,0:T(8,128)(2,1)S(1)}, u32[]{:S(2)}, u32[]{:S(2)}) collective-permute-start(bf16[4,1,32,256]{3,2,1,0:T(8,128)(2,1)S(1)} %get-tuple-element.46), channel_id=1, source_target_pairs={{0,7},{1,0},{2,1},{3,2},{4,3},{5,4},{6,5},{7,6},{8,15},{9,8},{10,9... | collective-permute-start | bytes 196616 | tf_op jit(solution)/shard_map/ppermute | solution.py:13
  65.1 0.5 collective-permute-start.6
  65.6 1.9 %first_inner.1 = (f32[6,16,32,256]{3,2,1,0:T(8,128)S(1)}, f32[4,16,256]{2,1,0:T(8,128)S(1)}) custom-call(bf16[6,16,32,256]{3,2,1,0:T(8,128)(2,1)S(1)} %conv_inner.1.inner, bf16[6,1,32,256]{3,2,1,0:T(8,128)(2,1)S(1)} %collective-permute-done.8.i_lo, bf16[6,1,32,256]{3,2,1,0:T(8,128)(2,1)S(1)} %collective-permute-done.9.i_hi, ...), custom_call_target="tpu_custom_call" | custom-call | tf_op jit(solution)/shard_map/first_inner/pallas_call | solution.py:523
  67.5 0.3 collective-permute-done.7.e_hi
  67.8 1.0 collective-permute-done.6.e_lo
  68.8 1.4 %first_edge.1 = (f32[8,16,256]{2,1,0:T(8,128)S(1)}, f32[8,256]{1,0:T(8,128)S(1)}, f32[8,256]{1,0:T(8,128)S(1)}) custom-call(bf16[6,16,32,256]{3,2,1,0:T(8,128)(2,1)S(1)} %conv_inner.1.inner, bf16[4,16,32,256]{3,2,1,0:T(8,128)(2,1)S(1)} %conv_edge.1.edge, bf16[4,1,32,256]{3,2,1,0:T(8,128)(2,1)S(1)} %collective-permute-done.6.e_lo, ...), custom_call_target="tpu_custom_call" | custom-call | tf_op jit(solution)/shard_map/first_edge/pallas_call | solution.py:523
  70.1 0.5 collective-permute-start.10
  70.6 3.7 %collective-permute-start.11 = (f32[8,256]{1,0:T(8,128)S(1)}, f32[8,256]{1,0:T(8,128)S(1)}, u32[]{:S(2)}, u32[]{:S(2)}) collective-permute-start(f32[8,256]{1,0:T(8,128)S(1)} %get-tuple-element.38), channel_id=1, source_target_pairs={{0,7},{1,0},{2,1},{3,2},{4,3},{5,4},{6,5},{7,6},{8,15},{9,8},{10,9... | collective-permute-start | bytes 24584 | tf_op jit(solution)/shard_map/ppermute | solution.py:13
  74.3 0.6 collective-permute-done.10.w_lo
  75.0 0.2 collective-permute-done.11.w_hi
  75.3 4.8 %collective-permute-start.13 = (f32[18,256]{1,0:T(8,128)S(1)}, f32[18,256]{1,0:T(8,128)S(1)}, u32[]{:S(2)}, u32[]{:S(2)}) collective-permute-start(f32[18,256]{1,0:T(8,128)S(1)} %pad_maximum_fusion.1), channel_id=1, source_target_pairs={{0,120},{8,0},{16,8},{24,16},{32,24},{40,32},{48,40},{56,48},{64,5... | collective-permute-start | bytes 55304 | tf_op jit(solution)/shard_map/ppermute | solution.py:13
  80.0 3.1 %second_inner.1 = (f32[8,16,32,256]{3,2,1,0:T(8,128)S(1)}, f32[6,16,256]{2,1,0:T(8,128)S(1)}, f32[10,16,256]{2,1,0:T(8,128)S(1)}) custom-call(bf16[6,16,32,256]{3,2,1,0:T(8,128)(2,1)S(1)} %conv_inner.1.inner, bf16[4,16,32,256]{3,2,1,0:T(8,128)(2,1)S(1)} %conv_edge.1.edge, bf16[6,1,32,256]{3,2,1,0:T(8,128)(2,1)S(1)} %collective-permute-done.8.i_lo, ...), custom_call_target="tpu_custom_call" | custom-call | tf_op jit(solution)/shard_map/second_inner/pallas_call | solution.py:523
  83.2 1.2 %second_edge.1 = (f32[2,16,256]{2,1,0:T(8,128)S(1)}, f32[1,128]{1,0:T(1,128)S(1)}) custom-call(bf16[4,16,32,256]{3,2,1,0:T(8,128)(2,1)S(1)} %conv_edge.1.edge, bf16[4,1,32,256]{3,2,1,0:T(8,128)(2,1)S(1)} %collective-permute-done.6.e_lo, bf16[4,1,32,256]{3,2,1,0:T(8,128)(2,1)S(1)} %collective-permute-done.7.e_hi, f32[8,16,256]{2,1,0:T(8,128)S(1)} %get-tuple-element.29.start, ...), custom_call_target="tpu_custom_call" | custom-call | tf_op jit(solution)/shard_map/second_edge/pallas_call | solution.py:523
  84.5 19.2 %all_to_all.5 = f32[128,1,128]{2,1,0:T(1,128)S(1)} all-to-all(f32[128,1,128]{2,1,0:T(1,128)S(1)} %broadcast_in_dim.13), channel_id=1, replica_groups=mesh['sx'=16,'sy'=8] {'sx','sy'}, dimensions={0} | all-to-all | bytes 131072 | tf_op jit(solution)/shard_map/all_to_all | solution.py:638
  103.7 0.9 final.1
  (32 shorter events, 0.3 us)
Async XLA Ops:
  0.6 40.4 %copy-start = (bf16[8,16,32,256]{3,2,1,0:T(8,128)(2,1)S(1)}, bf16[8,16,32,256]{3,2,1,0:T(8,128)(2,1)}, u32[]{:S(2)}) copy-start(bf16[8,16,32,256]{3,2,1,0:T(8,128)(2,1)} %own.7) | copy-start | bytes 6291460
  0.6 46.1 %copy-start.2 = (bf16[27,32,32]{2,1,0:T(8,128)(2,1)S(1)}, bf16[27,32,32]{2,1,0:T(8,128)(2,1)}, u32[]{:S(2)}) copy-start(bf16[27,32,32]{2,1,0:T(8,128)(2,1)} %taps.1) | copy-start | bytes 165892
  34.1 27.7 %collective-permute-start.2 = (bf16[2,16,32,256]{3,2,1,0:T(8,128)(2,1)}, bf16[2,16,32,256]{3,2,1,0:T(8,128)(2,1)S(1)}, u32[]{:S(2)}, u32[]{:S(2)}) collective-permute-start(bf16[2,16,32,256]{3,2,1,0:T(8,128)(2,1)} %get-tuple-element.26), channel_id=1, source_target_pairs={{0,8},{8,16},{16,24},{24,32},{32,40},{40,48},{48,56},{56,64},{64,7... | collective-permute-start | bytes 1572872 | tf_op jit(solution)/shard_map/ppermute | solution.py:13
  36.2 25.6 %collective-permute-start.3 = (bf16[2,16,32,256]{3,2,1,0:T(8,128)(2,1)}, bf16[2,16,32,256]{3,2,1,0:T(8,128)(2,1)S(1)}, u32[]{:S(2)}, u32[]{:S(2)}) collective-permute-start(bf16[2,16,32,256]{3,2,1,0:T(8,128)(2,1)} %get-tuple-element.27), channel_id=1, source_target_pairs={{0,120},{8,0},{16,8},{24,16},{32,24},{40,32},{48,40},{56,48},{64,5... | collective-permute-start | bytes 1572872 | tf_op jit(solution)/shard_map/ppermute | solution.py:13
  41.1 0.9 copy-start.3
  42.0 0.9 copy-start.4
  42.9 0.9 copy-start.5
  43.8 0.7 copy-start.6
  44.5 2.3 %copy-start.7 = (f32[32]{0:T(128)S(1)}, f32[32]{0:T(128)}, u32[]{:S(2)}) copy-start(f32[32]{0:T(128)} %param.9) | copy-start | bytes 388
  44.6 4.3 %collective-permute-start = (bf16[9,32,256]{2,1,0:T(8,128)(2,1)S(1)}, bf16[9,32,256]{2,1,0:T(8,128)(2,1)S(1)}, u32[]{:S(2)}, u32[]{:S(2)}) collective-permute-start(bf16[9,32,256]{2,1,0:T(8,128)(2,1)S(1)} %get-tuple-element.24), channel_id=1, source_target_pairs={{0,1},{1,2},{2,3},{3,4},{4,5},{5,6},{6,7},{7,0},{8,9},{9,10},{10,1... | collective-permute-start | bytes 442376 | tf_op jit(solution)/shard_map/ppermute | solution.py:13
  46.8 4.9 %collective-permute-start.1 = (bf16[9,32,256]{2,1,0:T(8,128)(2,1)S(1)}, bf16[9,32,256]{2,1,0:T(8,128)(2,1)S(1)}, u32[]{:S(2)}, u32[]{:S(2)}) collective-permute-start(bf16[9,32,256]{2,1,0:T(8,128)(2,1)S(1)} %get-tuple-element.25), channel_id=1, source_target_pairs={{0,7},{1,0},{2,1},{3,2},{4,3},{5,4},{6,5},{7,6},{8,15},{9,8},{10,9... | collective-permute-start | bytes 442376 | tf_op jit(solution)/shard_map/ppermute | solution.py:13
  51.7 8.7 %collective-permute-start.4 = (bf16[7,32,256]{2,1,0:T(8,128)(2,1)S(1)}, bf16[7,32,256]{2,1,0:T(8,128)(2,1)S(1)}, u32[]{:S(2)}, u32[]{:S(2)}) collective-permute-start(bf16[7,32,256]{2,1,0:T(8,128)(2,1)S(1)} %get-tuple-element.30), channel_id=1, source_target_pairs={{0,8},{8,16},{16,24},{24,32},{32,40},{40,48},{48,56},{56,64},{64,7... | collective-permute-start | bytes 344072 | tf_op jit(solution)/shard_map/ppermute | solution.py:13
  51.7 10.1 %collective-permute-start.5 = (bf16[7,32,256]{2,1,0:T(8,128)(2,1)S(1)}, bf16[7,32,256]{2,1,0:T(8,128)(2,1)S(1)}, u32[]{:S(2)}, u32[]{:S(2)}) collective-permute-start(bf16[7,32,256]{2,1,0:T(8,128)(2,1)S(1)} %get-tuple-element.31), channel_id=1, source_target_pairs={{0,120},{8,0},{16,8},{24,16},{32,24},{40,32},{48,40},{56,48},{64,5... | collective-permute-start | bytes 344072 | tf_op jit(solution)/shard_map/ppermute | solution.py:13
  60.1 5.5 %collective-permute-start.9 = (bf16[6,1,32,256]{3,2,1,0:T(8,128)(2,1)S(1)}, bf16[6,1,32,256]{3,2,1,0:T(8,128)(2,1)S(1)}, u32[]{:S(2)}, u32[]{:S(2)}) collective-permute-start(bf16[6,1,32,256]{3,2,1,0:T(8,128)(2,1)S(1)} %get-tuple-element.44), channel_id=1, source_target_pairs={{0,7},{1,0},{2,1},{3,2},{4,3},{5,4},{6,5},{7,6},{8,15},{9,8},{10,9... | collective-permute-start | bytes 294920 | tf_op jit(solution)/shard_map/ppermute | solution.py:13
  60.4 5.2 %copy-start.1 = (f32[8,16,256]{2,1,0:T(8,128)S(1)}, f32[8,16,256]{2,1,0:T(8,128)}, u32[]{:S(2)}) copy-start(f32[8,16,256]{2,1,0:T(8,128)} %ridge.7) | copy-start | bytes 393220
  60.4 5.2 %collective-permute-start.8 = (bf16[6,1,32,256]{3,2,1,0:T(8,128)(2,1)S(1)}, bf16[6,1,32,256]{3,2,1,0:T(8,128)(2,1)S(1)}, u32[]{:S(2)}, u32[]{:S(2)}) collective-permute-start(bf16[6,1,32,256]{3,2,1,0:T(8,128)(2,1)S(1)} %get-tuple-element.45), channel_id=1, source_target_pairs={{0,1},{1,2},{2,3},{3,4},{4,5},{5,6},{6,7},{7,0},{8,9},{9,10},{10,1... | collective-permute-start | bytes 294920 | tf_op jit(solution)/shard_map/ppermute | solution.py:13
  63.8 4.0 %collective-permute-start.7 = (bf16[4,1,32,256]{3,2,1,0:T(8,128)(2,1)S(1)}, bf16[4,1,32,256]{3,2,1,0:T(8,128)(2,1)S(1)}, u32[]{:S(2)}, u32[]{:S(2)}) collective-permute-start(bf16[4,1,32,256]{3,2,1,0:T(8,128)(2,1)S(1)} %get-tuple-element.46), channel_id=1, source_target_pairs={{0,7},{1,0},{2,1},{3,2},{4,3},{5,4},{6,5},{7,6},{8,15},{9,8},{10,9... | collective-permute-start | bytes 196616 | tf_op jit(solution)/shard_map/ppermute | solution.py:13
  65.1 3.7 %collective-permute-start.6 = (bf16[4,1,32,256]{3,2,1,0:T(8,128)(2,1)S(1)}, bf16[4,1,32,256]{3,2,1,0:T(8,128)(2,1)S(1)}, u32[]{:S(2)}, u32[]{:S(2)}) collective-permute-start(bf16[4,1,32,256]{3,2,1,0:T(8,128)(2,1)S(1)} %get-tuple-element.47), channel_id=1, source_target_pairs={{0,1},{1,2},{2,3},{3,4},{4,5},{5,6},{6,7},{7,0},{8,9},{9,10},{10,1... | collective-permute-start | bytes 196616 | tf_op jit(solution)/shard_map/ppermute | solution.py:13
  70.1 4.8 %collective-permute-start.10 = (f32[8,256]{1,0:T(8,128)S(1)}, f32[8,256]{1,0:T(8,128)S(1)}, u32[]{:S(2)}, u32[]{:S(2)}) collective-permute-start(f32[8,256]{1,0:T(8,128)S(1)} %get-tuple-element.37), channel_id=1, source_target_pairs={{0,1},{1,2},{2,3},{3,4},{4,5},{5,6},{6,7},{7,0},{8,9},{9,10},{10,1... | collective-permute-start | bytes 24584 | tf_op jit(solution)/shard_map/ppermute | solution.py:13
  70.6 4.5 %collective-permute-start.11 = (f32[8,256]{1,0:T(8,128)S(1)}, f32[8,256]{1,0:T(8,128)S(1)}, u32[]{:S(2)}, u32[]{:S(2)}) collective-permute-start(f32[8,256]{1,0:T(8,128)S(1)} %get-tuple-element.38), channel_id=1, source_target_pairs={{0,7},{1,0},{2,1},{3,2},{4,3},{5,4},{6,5},{7,6},{8,15},{9,8},{10,9... | collective-permute-start | bytes 24584 | tf_op jit(solution)/shard_map/ppermute | solution.py:13
  75.2 8.0 %collective-permute-start.12 = (f32[18,256]{1,0:T(8,128)S(1)}, f32[18,256]{1,0:T(8,128)S(1)}, u32[]{:S(2)}, u32[]{:S(2)}) collective-permute-start(f32[18,256]{1,0:T(8,128)S(1)} %pad_maximum_fusion), channel_id=1, source_target_pairs={{0,8},{8,16},{16,24},{24,32},{32,40},{40,48},{48,56},{56,64},{64,7... | collective-permute-start | bytes 55304 | tf_op jit(solution)/shard_map/ppermute | solution.py:13
  75.3 7.9 %collective-permute-start.13 = (f32[18,256]{1,0:T(8,128)S(1)}, f32[18,256]{1,0:T(8,128)S(1)}, u32[]{:S(2)}, u32[]{:S(2)}) collective-permute-start(f32[18,256]{1,0:T(8,128)S(1)} %pad_maximum_fusion.1), channel_id=1, source_target_pairs={{0,120},{8,0},{16,8},{24,16},{32,24},{40,32},{48,40},{56,48},{64,5... | collective-permute-start | bytes 55304 | tf_op jit(solution)/shard_map/ppermute | solution.py:13

commit v6 on v5

--- a/solution.py
+++ b/solution.py
@@ -20,19 +20,6 @@
     return before, after
 
 
-def edges_kernel(own, x_hi, x_lo, token, sems):
-    rows = own.shape[0]
-    copies = [
-        pltpu.make_async_copy(own.at[rows - 2 : rows], x_hi, sems.at[0]),
-        pltpu.make_async_copy(own.at[0:2], x_lo, sems.at[1]),
-    ]
-    for copy in copies:
-        copy.start()
-    token[...] = jnp.zeros_like(token)
-    for copy in copies:
-        copy.wait()
-
-
 def three(value):
     high = value.astype(jnp.bfloat16).astype(jnp.float32)
     rest = value - high
@@ -40,7 +27,7 @@
     return high, mid, rest - mid
 
 
-def prep_kernel(token, own, ids, occupancy, target, mask, start, out_hi, out_lo, present):
+def prep_kernel(own, ids, occupancy, target, mask, start, out_hi, out_lo, present):
     rows, cols, channels, depth = own.shape
     half = present.shape[1]
     present[...] = jnp.broadcast_to(
@@ -517,7 +504,6 @@
     rows, cols, channels, depth = features.shape
     f32, bf16 = (jnp.float32, jnp.bfloat16)
     vmem = pl.BlockSpec(memory_space=pltpu.VMEM)
-    anywhere = pl.BlockSpec(memory_space=pl.ANY)
 
     def call(kernel, args, outs, scratch, limit, name):
         return pl.pallas_call(
@@ -530,24 +516,15 @@
             name=name,
         )(*args)
 
-    x_hi, x_lo, token = pl.pallas_call(
-        edges_kernel,
-        out_shape=[jax.ShapeDtypeStruct((2, cols, channels, depth), bf16) for _ in range(2)]
-        + [jax.ShapeDtypeStruct((8, 128), f32)],
-        in_specs=[anywhere],
-        out_specs=[anywhere, anywhere, vmem],
-        scratch_shapes=[pltpu.SemaphoreType.DMA((2,))],
-        compiler_params=pltpu.CompilerParams(vmem_limit_bytes=60 << 20),
-        name="edges",
-    )(features)
-    x_lo, x_hi = (shift(x_hi, "sx", 1), shift(x_lo, "sx", -1))
+    edges, target = lax.optimization_barrier(((features[-2:], features[:2]), target))
+    x_lo, x_hi = (shift(edges[0], "sx", 1), shift(edges[1], "sx", -1))
 
     plane = ((rows, cols, depth), f32)
     blocks = block_ids.reshape(-1, block_ids.shape[3])
     edge_column = ((rows + 1, channels, depth), bf16)
     weight_mask, residual, y_hi, y_lo = call(
         prep_kernel,
-        (token, features, blocks, occupancy, target),
+        (features, blocks, occupancy, target),
         [plane, plane, edge_column, edge_column],
         [((blocks.shape[0], depth // block_ids.shape[2]), f32)],
         4,

time: 105 us -> 72.1 us (0.69)
  Pallas kernels: 48.1 us -> 14.6 us
    pallas_call x1 -> x0, Pallas kernels: 33.5 us -> none  [per_device(): pl.pallas_call(edges_kernel, out_shape=[jax.ShapeDtypeStruct((2, cols, ch...]
    slice x0 -> x1, local copies, waits for them, and re-layouts: none -> 1.42 us  [per_device(): features[:2]]
    unnamed x16 -> x14, local copies, waits for them, and re-layouts: 3.41 us -> 2.73 us
  transfers between devices with their start and end apart: 14 -> 14, of which waited for: 6 -> 6; matrix products, arithmetic and copies ran while one was open for 0% -> 0% of each run, Pallas kernels for 11% -> 15%
where the time goes in v6:
time: 72.1 us; the launch traced here: 71.9 us
  starting transfers between devices  26.5 us (37%)
  blocking collectives  19.2 us (27%)
  Pallas kernels  14.6 us (20%)
  waiting for transfers between devices  6.53 us (9%)
  local copies, waits for them, and re-layouts  4.22 us (6%)
  between operations  0.79 us (1%)
    ppermute x14, starting transfers between devices, shift(): lax.ppermute(value, axis, [(i, (i + step) % peers) for i in range(peers)])  26.5 us
    all_to_all x1, blocking collectives, per_device(): lax.all_to_all(jnp.broadcast_to(share[None], (peers, 1, 128)), AXES, 0, 0)  19.2 us
    pallas_call x10, Pallas kernels, call(): pl.pallas_call(kernel, out_shape=[jax.ShapeDtypeStruct(shape, dtype) for...  14.6 us
    ppermute x14, waiting for transfers between devices, shift(): lax.ppermute(value, axis, [(i, (i + step) % peers) for i in range(peers)])  6.53 us
    unnamed x14, local copies, waits for them, and re-layouts  2.73 us
  transfers between devices with their start and end apart: 14, of which 6 were waited for; matrix products, arithmetic and copies ran while one was open for 0% of the time, Pallas kernels for 15%

profile of v6, /device:TPU:1, one launch (start us, length us, event | category | flops | bytes accessed | tf_op | source)
XLA Modules:
  0.0 71.9 jit_solution(4769464518730976352)
XLA Ops:
  0.6 1.4 %fusion = (bf16[2,16,32,256]{3,2,1,0:T(8,128)(2,1)S(1)}, bf16[2,16,32,256]{3,2,1,0:T(8,128)(2,1)S(1)}) fusion(bf16[8,16,32,256]{3,2,1,0:T(8,128)(2,1)} %own.5), kind=kLoop, calls=%fused_computation.4 | loop fusion | bytes 2097152 | tf_op jit(solution)/shard_map/slice | solution.py:519
  2.1 2.1 %collective-permute-start.2 = (bf16[2,16,32,256]{3,2,1,0:T(8,128)(2,1)S(1)}, bf16[2,16,32,256]{3,2,1,0:T(8,128)(2,1)S(1)}, u32[]{:S(2)}, u32[]{:S(2)}) collective-permute-start(bf16[2,16,32,256]{3,2,1,0:T(8,128)(2,1)S(1)} %get-tuple-element.26), channel_id=1, source_target_pairs={{0,8},{8,16},{16,24},{24,32},{32,40},{40,48},{48,56},{56,64},{64,7... | collective-permute-start | bytes 1572872 | tf_op jit(solution)/shard_map/ppermute | solution.py:13
  4.2 4.8 %collective-permute-start.3 = (bf16[2,16,32,256]{3,2,1,0:T(8,128)(2,1)S(1)}, bf16[2,16,32,256]{3,2,1,0:T(8,128)(2,1)S(1)}, u32[]{:S(2)}, u32[]{:S(2)}) collective-permute-start(bf16[2,16,32,256]{3,2,1,0:T(8,128)(2,1)S(1)} %get-tuple-element.27), channel_id=1, source_target_pairs={{0,120},{8,0},{16,8},{24,16},{32,24},{40,32},{48,40},{56,48},{64,5... | collective-permute-start | bytes 1572872 | tf_op jit(solution)/shard_map/ppermute | solution.py:13
  9.0 0.9 %copy-done.3 = s32[8,16,2,27]{3,2,1,0:T(2,128)S(1)} copy-done((s32[8,16,2,27]{3,2,1,0:T(2,128)S(1)}, s32[8,16,2,27]{3,2,1,0:T(2,128)}, u32[]{:S(2)}) %copy-start.3) | copy-done | bytes 27672
  9.9 0.9 %copy-done.4 = s32[8,16,256]{2,1,0:T(8,128)S(1)} copy-done((s32[8,16,256]{2,1,0:T(8,128)S(1)}, s32[8,16,256]{2,1,0:T(8,128)}, u32[]{:S(2)}) %copy-start.4) | copy-done | bytes 131096
  10.8 0.9 %copy-done.5 = f32[8,16,256]{2,1,0:T(8,128)S(1)} copy-done((f32[8,16,256]{2,1,0:T(8,128)S(1)}, f32[8,16,256]{2,1,0:T(8,128)}, u32[]{:S(2)}) %copy-start.5) | copy-done | bytes 131096
  11.7 0.1 prep.1
  11.9 2.1 %collective-permute-start = (bf16[9,32,256]{2,1,0:T(8,128)(2,1)S(1)}, bf16[9,32,256]{2,1,0:T(8,128)(2,1)S(1)}, u32[]{:S(2)}, u32[]{:S(2)}) collective-permute-start(bf16[9,32,256]{2,1,0:T(8,128)(2,1)S(1)} %get-tuple-element.24), channel_id=1, source_target_pairs={{0,1},{1,2},{2,3},{3,4},{4,5},{5,6},{6,7},{7,0},{8,9},{9,10},{10,1... | collective-permute-start | bytes 442376 | tf_op jit(solution)/shard_map/ppermute | solution.py:13
  14.0 0.4 weights.1
  14.5 1.7 %collective-permute-done.y_lo = bf16[9,32,256]{2,1,0:T(8,128)(2,1)S(1)} collective-permute-done((bf16[9,32,256]{2,1,0:T(8,128)(2,1)S(1)}, bf16[9,32,256]{2,1,0:T(8,128)(2,1)S(1)}, u32[]{:S(2)}, u32[]{:S(2)}) %collective-permute-start) | collective-permute-done | bytes 147488 | tf_op jit(solution)/shard_map/ppermute | solution.py:13
  16.1 2.8 %collective-permute-done.1.y_hi = bf16[9,32,256]{2,1,0:T(8,128)(2,1)S(1)} collective-permute-done((bf16[9,32,256]{2,1,0:T(8,128)(2,1)S(1)}, bf16[9,32,256]{2,1,0:T(8,128)(2,1)S(1)}, u32[]{:S(2)}, u32[]{:S(2)}) %collective-permute-start.1) | collective-permute-done | bytes 147488 | tf_op jit(solution)/shard_map/ppermute | solution.py:13
  18.9 0.1 collective-permute-start.4
  19.0 4.8 %collective-permute-start.5 = (bf16[7,32,256]{2,1,0:T(8,128)(2,1)S(1)}, bf16[7,32,256]{2,1,0:T(8,128)(2,1)S(1)}, u32[]{:S(2)}, u32[]{:S(2)}) collective-permute-start(bf16[7,32,256]{2,1,0:T(8,128)(2,1)S(1)} %get-tuple-element.31), channel_id=1, source_target_pairs={{0,120},{8,0},{16,8},{24,16},{32,24},{40,32},{48,40},{56,48},{64,5... | collective-permute-start | bytes 344072 | tf_op jit(solution)/shard_map/ppermute | solution.py:13
  23.8 3.5 %conv_inner.1.inner = bf16[6,16,32,256]{3,2,1,0:T(8,128)(2,1)S(1)} custom-call(bf16[8,16,32,256]{3,2,1,0:T(8,128)(2,1)S(1)} %copy-done, bf16[9,32,256]{2,1,0:T(8,128)(2,1)S(1)} %collective-permute-done.y_lo, bf16[9,32,256]{2,1,0:T(8,128)(2,1)S(1)} %collective-permute-done.1.y_hi, f32[8,16,256]{2,1,0:T(8,128)S(1)} %get-tuple-element.28.mask, ...), custom_call_target="tpu_custom_call" | custom-call | tf_op jit(solution)/shard_map/conv_inner/pallas_call | solution.py:509
  27.3 0.3 collective-permute-start.9
  27.6 1.4 %collective-permute-start.8 = (bf16[6,1,32,256]{3,2,1,0:T(8,128)(2,1)S(1)}, bf16[6,1,32,256]{3,2,1,0:T(8,128)(2,1)S(1)}, u32[]{:S(2)}, u32[]{:S(2)}) collective-permute-start(bf16[6,1,32,256]{3,2,1,0:T(8,128)(2,1)S(1)} %get-tuple-element.47), channel_id=1, source_target_pairs={{0,1},{1,2},{2,3},{3,4},{4,5},{5,6},{6,7},{7,0},{8,9},{9,10},{10,1... | collective-permute-start | bytes 294920 | tf_op jit(solution)/shard_map/ppermute | solution.py:13
  29.1 1.9 %conv_edge.1.edge = bf16[4,16,32,256]{3,2,1,0:T(8,128)(2,1)S(1)} custom-call(bf16[8,16,32,256]{3,2,1,0:T(8,128)(2,1)S(1)} %copy-done, bf16[9,32,256]{2,1,0:T(8,128)(2,1)S(1)} %collective-permute-done.y_lo, bf16[9,32,256]{2,1,0:T(8,128)(2,1)S(1)} %collective-permute-done.1.y_hi, bf16[2,16,32,256]{3,2,1,0:T(8,128)(2,1)S(1)} %collective-permute-done.2.x_lo, ...), custom_call_target="tpu_custom_call" | custom-call | tf_op jit(solution)/shard_map/conv_edge/pallas_call | solution.py:509
  31.1 1.3 %collective-permute-start.7 = (bf16[4,1,32,256]{3,2,1,0:T(8,128)(2,1)S(1)}, bf16[4,1,32,256]{3,2,1,0:T(8,128)(2,1)S(1)}, u32[]{:S(2)}, u32[]{:S(2)}) collective-permute-start(bf16[4,1,32,256]{3,2,1,0:T(8,128)(2,1)S(1)} %get-tuple-element.48), channel_id=1, source_target_pairs={{0,7},{1,0},{2,1},{3,2},{4,3},{5,4},{6,5},{7,6},{8,15},{9,8},{10,9... | collective-permute-start | bytes 196616 | tf_op jit(solution)/shard_map/ppermute | solution.py:13
  32.3 0.5 collective-permute-start.6
  32.8 1.9 %first_inner.1 = (f32[6,16,32,256]{3,2,1,0:T(8,128)S(1)}, f32[4,16,256]{2,1,0:T(8,128)S(1)}) custom-call(bf16[6,16,32,256]{3,2,1,0:T(8,128)(2,1)S(1)} %conv_inner.1.inner, bf16[6,1,32,256]{3,2,1,0:T(8,128)(2,1)S(1)} %collective-permute-done.8.i_lo, bf16[6,1,32,256]{3,2,1,0:T(8,128)(2,1)S(1)} %collective-permute-done.9.i_hi, ...), custom_call_target="tpu_custom_call" | custom-call | tf_op jit(solution)/shard_map/first_inner/pallas_call | solution.py:509
  34.7 0.3 collective-permute-done.7.e_hi
  35.1 1.0 %collective-permute-done.6.e_lo = bf16[4,1,32,256]{3,2,1,0:T(8,128)(2,1)S(1)} collective-permute-done((bf16[4,1,32,256]{3,2,1,0:T(8,128)(2,1)S(1)}, bf16[4,1,32,256]{3,2,1,0:T(8,128)(2,1)S(1)}, u32[]{:S(2)}, u32[]{:S(2)}) %collective-permute-start.6) | collective-permute-done | bytes 65568 | tf_op jit(solution)/shard_map/ppermute | solution.py:13
  36.0 1.4 %first_edge.1 = (f32[8,16,256]{2,1,0:T(8,128)S(1)}, f32[8,256]{1,0:T(8,128)S(1)}, f32[8,256]{1,0:T(8,128)S(1)}) custom-call(bf16[6,16,32,256]{3,2,1,0:T(8,128)(2,1)S(1)} %conv_inner.1.inner, bf16[4,16,32,256]{3,2,1,0:T(8,128)(2,1)S(1)} %conv_edge.1.edge, bf16[4,1,32,256]{3,2,1,0:T(8,128)(2,1)S(1)} %collective-permute-done.6.e_lo, ...), custom_call_target="tpu_custom_call" | custom-call | tf_op jit(solution)/shard_map/first_edge/pallas_call | solution.py:509
  37.4 0.5 collective-permute-start.10
  37.9 3.7 %collective-permute-start.11 = (f32[8,256]{1,0:T(8,128)S(1)}, f32[8,256]{1,0:T(8,128)S(1)}, u32[]{:S(2)}, u32[]{:S(2)}) collective-permute-start(f32[8,256]{1,0:T(8,128)S(1)} %get-tuple-element.38), channel_id=1, source_target_pairs={{0,7},{1,0},{2,1},{3,2},{4,3},{5,4},{6,5},{7,6},{8,15},{9,8},{10,9... | collective-permute-start | bytes 24584 | tf_op jit(solution)/shard_map/ppermute | solution.py:13
  41.6 0.6 collective-permute-done.10.w_lo
  42.2 0.2 collective-permute-done.11.w_hi
  42.5 4.8 %collective-permute-start.13 = (f32[18,256]{1,0:T(8,128)S(1)}, f32[18,256]{1,0:T(8,128)S(1)}, u32[]{:S(2)}, u32[]{:S(2)}) collective-permute-start(f32[18,256]{1,0:T(8,128)S(1)} %pad_maximum_fusion.1), channel_id=1, source_target_pairs={{0,120},{8,0},{16,8},{24,16},{32,24},{40,32},{48,40},{56,48},{64,5... | collective-permute-start | bytes 55304 | tf_op jit(solution)/shard_map/ppermute | solution.py:13
  47.3 3.1 %second_inner.1 = (f32[8,16,32,256]{3,2,1,0:T(8,128)S(1)}, f32[6,16,256]{2,1,0:T(8,128)S(1)}, f32[10,16,256]{2,1,0:T(8,128)S(1)}) custom-call(bf16[6,16,32,256]{3,2,1,0:T(8,128)(2,1)S(1)} %conv_inner.1.inner, bf16[4,16,32,256]{3,2,1,0:T(8,128)(2,1)S(1)} %conv_edge.1.edge, bf16[6,1,32,256]{3,2,1,0:T(8,128)(2,1)S(1)} %collective-permute-done.8.i_lo, ...), custom_call_target="tpu_custom_call" | custom-call | tf_op jit(solution)/shard_map/second_inner/pallas_call | solution.py:509
  50.4 1.2 %second_edge.1 = (f32[2,16,256]{2,1,0:T(8,128)S(1)}, f32[1,128]{1,0:T(1,128)S(1)}) custom-call(bf16[4,16,32,256]{3,2,1,0:T(8,128)(2,1)S(1)} %conv_edge.1.edge, bf16[4,1,32,256]{3,2,1,0:T(8,128)(2,1)S(1)} %collective-permute-done.6.e_lo, bf16[4,1,32,256]{3,2,1,0:T(8,128)(2,1)S(1)} %collective-permute-done.7.e_hi, f32[8,16,256]{2,1,0:T(8,128)S(1)} %get-tuple-element.29.start, ...), custom_call_target="tpu_custom_call" | custom-call | tf_op jit(solution)/shard_map/second_edge/pallas_call | solution.py:509
  51.7 19.2 %all_to_all.5 = f32[128,1,128]{2,1,0:T(1,128)S(1)} all-to-all(f32[128,1,128]{2,1,0:T(1,128)S(1)} %broadcast_in_dim.13), channel_id=1, replica_groups=mesh['sx'=16,'sy'=8] {'sx','sy'}, dimensions={0} | all-to-all | bytes 131072 | tf_op jit(solution)/shard_map/all_to_all | solution.py:615
  71.0 0.9 %final.1 = (f32[8,16,256]{2,1,0:T(8,128)}, f32[8,16,256]{2,1,0:T(8,128)}) custom-call(f32[128,128]{1,0:T(8,128)S(1)} %bitcast.8, f32[8,16,256]{2,1,0:T(8,128)S(1)} %get-tuple-element.29.start, f32[8,16,256]{2,1,0:T(8,128)S(1)} %get-tuple-element.36.first, f32[6,16,256]{2,1,0:T(8,128)S(1)} %get-tuple-element.42.inside, f32[2,16,256]{2,1,0:T(8,128)S(1)} %get-tuple-element.43.sides), custom_call_target="tpu_custom_call" | custom-call | tf_op jit(solution)/shard_map/final/pallas_call | solution.py:509
  (30 shorter events, 0.2 us)
Async XLA Ops:
  0.6 8.4 %copy-start = (bf16[8,16,32,256]{3,2,1,0:T(8,128)(2,1)S(1)}, bf16[8,16,32,256]{3,2,1,0:T(8,128)(2,1)}, u32[]{:S(2)}) copy-start(bf16[8,16,32,256]{3,2,1,0:T(8,128)(2,1)} %own.5) | copy-start | bytes 6291460
  0.6 13.4 %copy-start.2 = (bf16[27,32,32]{2,1,0:T(8,128)(2,1)S(1)}, bf16[27,32,32]{2,1,0:T(8,128)(2,1)}, u32[]{:S(2)}) copy-start(bf16[27,32,32]{2,1,0:T(8,128)(2,1)} %taps.1) | copy-start | bytes 165892
  2.1 27.0 %collective-permute-start.2 = (bf16[2,16,32,256]{3,2,1,0:T(8,128)(2,1)S(1)}, bf16[2,16,32,256]{3,2,1,0:T(8,128)(2,1)S(1)}, u32[]{:S(2)}, u32[]{:S(2)}) collective-permute-start(bf16[2,16,32,256]{3,2,1,0:T(8,128)(2,1)S(1)} %get-tuple-element.26), channel_id=1, source_target_pairs={{0,8},{8,16},{16,24},{24,32},{32,40},{40,48},{48,56},{56,64},{64,7... | collective-permute-start | bytes 1572872 | tf_op jit(solution)/shard_map/ppermute | solution.py:13
  4.2 24.9 %collective-permute-start.3 = (bf16[2,16,32,256]{3,2,1,0:T(8,128)(2,1)S(1)}, bf16[2,16,32,256]{3,2,1,0:T(8,128)(2,1)S(1)}, u32[]{:S(2)}, u32[]{:S(2)}) collective-permute-start(bf16[2,16,32,256]{3,2,1,0:T(8,128)(2,1)S(1)} %get-tuple-element.27), channel_id=1, source_target_pairs={{0,120},{8,0},{16,8},{24,16},{32,24},{40,32},{48,40},{56,48},{64,5... | collective-permute-start | bytes 1572872 | tf_op jit(solution)/shard_map/ppermute | solution.py:13
  9.0 0.9 %copy-start.3 = (s32[8,16,2,27]{3,2,1,0:T(2,128)S(1)}, s32[8,16,2,27]{3,2,1,0:T(2,128)}, u32[]{:S(2)}) copy-start(s32[8,16,2,27]{3,2,1,0:T(2,128)} %param.11) | copy-start | bytes 82948
  9.9 0.9 %copy-start.4 = (s32[8,16,256]{2,1,0:T(8,128)S(1)}, s32[8,16,256]{2,1,0:T(8,128)}, u32[]{:S(2)}) copy-start(s32[8,16,256]{2,1,0:T(8,128)} %occupancy.1) | copy-start | bytes 393220
  10.8 0.9 %copy-start.5 = (f32[8,16,256]{2,1,0:T(8,128)S(1)}, f32[8,16,256]{2,1,0:T(8,128)}, u32[]{:S(2)}) copy-start(f32[8,16,256]{2,1,0:T(8,128)} %target) | copy-start | bytes 393220
  11.7 2.3 %copy-start.6 = (f32[32]{0:T(128)S(1)}, f32[32]{0:T(128)}, u32[]{:S(2)}) copy-start(f32[32]{0:T(128)} %param.9) | copy-start | bytes 388
  11.9 4.3 %collective-permute-start = (bf16[9,32,256]{2,1,0:T(8,128)(2,1)S(1)}, bf16[9,32,256]{2,1,0:T(8,128)(2,1)S(1)}, u32[]{:S(2)}, u32[]{:S(2)}) collective-permute-start(bf16[9,32,256]{2,1,0:T(8,128)(2,1)S(1)} %get-tuple-element.24), channel_id=1, source_target_pairs={{0,1},{1,2},{2,3},{3,4},{4,5},{5,6},{6,7},{7,0},{8,9},{9,10},{10,1... | collective-permute-start | bytes 442376 | tf_op jit(solution)/shard_map/ppermute | solution.py:13
  14.0 4.9 %collective-permute-start.1 = (bf16[9,32,256]{2,1,0:T(8,128)(2,1)S(1)}, bf16[9,32,256]{2,1,0:T(8,128)(2,1)S(1)}, u32[]{:S(2)}, u32[]{:S(2)}) collective-permute-start(bf16[9,32,256]{2,1,0:T(8,128)(2,1)S(1)} %get-tuple-element.25), channel_id=1, source_target_pairs={{0,7},{1,0},{2,1},{3,2},{4,3},{5,4},{6,5},{7,6},{8,15},{9,8},{10,9... | collective-permute-start | bytes 442376 | tf_op jit(solution)/shard_map/ppermute | solution.py:13
  18.9 8.7 %collective-permute-start.4 = (bf16[7,32,256]{2,1,0:T(8,128)(2,1)S(1)}, bf16[7,32,256]{2,1,0:T(8,128)(2,1)S(1)}, u32[]{:S(2)}, u32[]{:S(2)}) collective-permute-start(bf16[7,32,256]{2,1,0:T(8,128)(2,1)S(1)} %get-tuple-element.30), channel_id=1, source_target_pairs={{0,8},{8,16},{16,24},{24,32},{32,40},{40,48},{48,56},{56,64},{64,7... | collective-permute-start | bytes 344072 | tf_op jit(solution)/shard_map/ppermute | solution.py:13
  19.0 10.1 %collective-permute-start.5 = (bf16[7,32,256]{2,1,0:T(8,128)(2,1)S(1)}, bf16[7,32,256]{2,1,0:T(8,128)(2,1)S(1)}, u32[]{:S(2)}, u32[]{:S(2)}) collective-permute-start(bf16[7,32,256]{2,1,0:T(8,128)(2,1)S(1)} %get-tuple-element.31), channel_id=1, source_target_pairs={{0,120},{8,0},{16,8},{24,16},{32,24},{40,32},{48,40},{56,48},{64,5... | collective-permute-start | bytes 344072 | tf_op jit(solution)/shard_map/ppermute | solution.py:13
  27.3 5.5 %collective-permute-start.9 = (bf16[6,1,32,256]{3,2,1,0:T(8,128)(2,1)S(1)}, bf16[6,1,32,256]{3,2,1,0:T(8,128)(2,1)S(1)}, u32[]{:S(2)}, u32[]{:S(2)}) collective-permute-start(bf16[6,1,32,256]{3,2,1,0:T(8,128)(2,1)S(1)} %get-tuple-element.46), channel_id=1, source_target_pairs={{0,7},{1,0},{2,1},{3,2},{4,3},{5,4},{6,5},{7,6},{8,15},{9,8},{10,9... | collective-permute-start | bytes 294920 | tf_op jit(solution)/shard_map/ppermute | solution.py:13
  27.6 5.2 %copy-start.1 = (f32[8,16,256]{2,1,0:T(8,128)S(1)}, f32[8,16,256]{2,1,0:T(8,128)}, u32[]{:S(2)}) copy-start(f32[8,16,256]{2,1,0:T(8,128)} %ridge.7) | copy-start | bytes 393220
  27.6 5.2 %collective-permute-start.8 = (bf16[6,1,32,256]{3,2,1,0:T(8,128)(2,1)S(1)}, bf16[6,1,32,256]{3,2,1,0:T(8,128)(2,1)S(1)}, u32[]{:S(2)}, u32[]{:S(2)}) collective-permute-start(bf16[6,1,32,256]{3,2,1,0:T(8,128)(2,1)S(1)} %get-tuple-element.47), channel_id=1, source_target_pairs={{0,1},{1,2},{2,3},{3,4},{4,5},{5,6},{6,7},{7,0},{8,9},{9,10},{10,1... | collective-permute-start | bytes 294920 | tf_op jit(solution)/shard_map/ppermute | solution.py:13
  31.1 4.0 %collective-permute-start.7 = (bf16[4,1,32,256]{3,2,1,0:T(8,128)(2,1)S(1)}, bf16[4,1,32,256]{3,2,1,0:T(8,128)(2,1)S(1)}, u32[]{:S(2)}, u32[]{:S(2)}) collective-permute-start(bf16[4,1,32,256]{3,2,1,0:T(8,128)(2,1)S(1)} %get-tuple-element.48), channel_id=1, source_target_pairs={{0,7},{1,0},{2,1},{3,2},{4,3},{5,4},{6,5},{7,6},{8,15},{9,8},{10,9... | collective-permute-start | bytes 196616 | tf_op jit(solution)/shard_map/ppermute | solution.py:13
  32.3 3.7 %collective-permute-start.6 = (bf16[4,1,32,256]{3,2,1,0:T(8,128)(2,1)S(1)}, bf16[4,1,32,256]{3,2,1,0:T(8,128)(2,1)S(1)}, u32[]{:S(2)}, u32[]{:S(2)}) collective-permute-start(bf16[4,1,32,256]{3,2,1,0:T(8,128)(2,1)S(1)} %get-tuple-element.49), channel_id=1, source_target_pairs={{0,1},{1,2},{2,3},{3,4},{4,5},{5,6},{6,7},{7,0},{8,9},{9,10},{10,1... | collective-permute-start | bytes 196616 | tf_op jit(solution)/shard_map/ppermute | solution.py:13
  37.4 4.8 %collective-permute-start.10 = (f32[8,256]{1,0:T(8,128)S(1)}, f32[8,256]{1,0:T(8,128)S(1)}, u32[]{:S(2)}, u32[]{:S(2)}) collective-permute-start(f32[8,256]{1,0:T(8,128)S(1)} %get-tuple-element.37), channel_id=1, source_target_pairs={{0,1},{1,2},{2,3},{3,4},{4,5},{5,6},{6,7},{7,0},{8,9},{9,10},{10,1... | collective-permute-start | bytes 24584 | tf_op jit(solution)/shard_map/ppermute | solution.py:13
  37.9 4.5 %collective-permute-start.11 = (f32[8,256]{1,0:T(8,128)S(1)}, f32[8,256]{1,0:T(8,128)S(1)}, u32[]{:S(2)}, u32[]{:S(2)}) collective-permute-start(f32[8,256]{1,0:T(8,128)S(1)} %get-tuple-element.38), channel_id=1, source_target_pairs={{0,7},{1,0},{2,1},{3,2},{4,3},{5,4},{6,5},{7,6},{8,15},{9,8},{10,9... | collective-permute-start | bytes 24584 | tf_op jit(solution)/shard_map/ppermute | solution.py:13
  42.4 8.0 %collective-permute-start.12 = (f32[18,256]{1,0:T(8,128)S(1)}, f32[18,256]{1,0:T(8,128)S(1)}, u32[]{:S(2)}, u32[]{:S(2)}) collective-permute-start(f32[18,256]{1,0:T(8,128)S(1)} %pad_maximum_fusion), channel_id=1, source_target_pairs={{0,8},{8,16},{16,24},{24,32},{32,40},{40,48},{48,56},{56,64},{64,7... | collective-permute-start | bytes 55304 | tf_op jit(solution)/shard_map/ppermute | solution.py:13
  42.5 7.9 %collective-permute-start.13 = (f32[18,256]{1,0:T(8,128)S(1)}, f32[18,256]{1,0:T(8,128)S(1)}, u32[]{:S(2)}, u32[]{:S(2)}) collective-permute-start(f32[18,256]{1,0:T(8,128)S(1)} %pad_maximum_fusion.1), channel_id=1, source_target_pairs={{0,120},{8,0},{16,8},{24,16},{32,24},{40,32},{48,40},{56,48},{64,5... | collective-permute-start | bytes 55304 | tf_op jit(solution)/shard_map/ppermute | solution.py:13

commit v7 on v6

--- a/solution.py
+++ b/solution.py
@@ -11,13 +11,6 @@
 def shift(value, axis, step):
     peers = lax.axis_size(axis)
     return lax.ppermute(value, axis, [(i, (i + step) % peers) for i in range(peers)])
-
-
-def halo(value, axis, dim, width):
-    length = value.shape[dim]
-    before = shift(lax.slice_in_dim(value, length - width, length, axis=dim), axis, 1)
-    after = shift(lax.slice_in_dim(value, 0, width, axis=dim), axis, -1)
-    return before, after
 
 
 def three(value):
@@ -43,13 +36,6 @@
         edge = jnp.concatenate([start[x, y : y + 1, :] for x in range(rows)], axis=0)
         blank = jnp.zeros((channels - 3 * rows, depth), jnp.float32)
         out[rows] = jnp.concatenate([*three(edge), blank], axis=0).astype(jnp.bfloat16)
-
-
-def start_rims(y_lo, y_hi, out):
-    rows = y_lo.shape[0] - 1
-    for k, ref in enumerate((y_lo, y_hi)):
-        terms = ref[rows].astype(jnp.float32)
-        out[k] = (terms[:rows] + terms[rows : 2 * rows]) + terms[2 * rows : 3 * rows]
 
 
 def weights_kernel(taps, bias, wide, bias_col):
@@ -179,7 +165,10 @@
     mask,
     wide,
     bias,
+    inner,
     out,
+    out_hi,
+    out_lo,
     grid,
     side_mask,
 ):
@@ -210,6 +199,10 @@
     ):
         for y in range(0, cols, 2):
             conv_block(grid, masks, wide, bias_all, lane, 4 * side, y, out, 2 * side)
+    for ref, y in ((out_hi, cols - 1), (out_lo, 0)):
+        for x in range(rows + 2):
+            at = field_at(inner, out, x)
+            ref[x] = at[0][at[1], y]
 
 
 def two_sum(a, b):
@@ -241,144 +234,128 @@
     return two_sum(p, t + a[1] * c)
 
 
-def along_y(smooth, dst, field, f_lo, f_hi, row, flags, value_at):
+def field_at(inner, edge, x):
+    n = inner.shape[0]
+    if x < 2:
+        return edge, x
+    return (inner, x - 2) if x < n + 2 else (edge, x - n)
+
+
+def along_y(smooth, dst, field, row, value_at):
     cols = smooth.shape[1]
 
     def product(y):
-        if y == 0:
-            return f_lo[row, 0].astype(jnp.float32) * (value_at(y) * flags[0])
-        if y == cols + 1:
-            return f_hi[row, 0].astype(jnp.float32) * (value_at(y) * flags[1])
-        return field[row, y - 1].astype(jnp.float32) * value_at(y)
-
-    here = product(1)
-    pair = product(0) + here
+        return field[row, y].astype(jnp.float32) * value_at(y)
+
+    here = product(0)
+    pair = here
     for y in range(cols):
-        following = product(y + 2)
-        pair_next = here + following
+        if y + 1 < cols:
+            following = product(y + 1)
+            pair_next = here + following
+        else:
+            pair_next = here
+            following = here
         smooth[dst, y] = pair + pair_next
         here = following
         pair = pair_next
 
 
-def own_row(own, lo, hi, x):
-    cols = own.shape[1]
-
-    def at(y):
-        if y == 0:
-            return lo(x)
-        if y == cols + 1:
-            return hi(x)
-        return own[x, y - 1 : y, :]
-
-    return at
-
-
-def side_row(side):
-    return lambda y: side[y : y + 1, :]
-
-
-def rim_of(ref, *index):
-    return lambda x: ref[(*index, pl.ds(x, 1))]
-
-
-def along_x(before, here, after, field, row, ridge_row, value_row):
-    ref, x = here
-    cols, channels, depth = ref.shape[1:]
-    lane = lax.broadcasted_iota(jnp.int32, (channels, depth), 1)
+def row_of(ref, x):
+    return lambda y: ref[x, y : y + 1, :]
+
+
+def close_column(both, lane, field):
+    depth = both.shape[1]
+    up = jnp.where(lane == depth - 1, 0.0, pltpu.roll(both, depth - 1, 1))
+    down = jnp.where(lane == 0, 0.0, pltpu.roll(both, 1, 1))
+    prod = ((both + both) + (up + down)) * field.astype(jnp.float32)
+    return jnp.sum(prod, axis=0, keepdims=True)
+
+
+def lanes(shape):
+    return lax.broadcasted_iota(jnp.int32, shape, 1)
+
+
+def along_x(smooth, x, ends, field, row, scale):
+    cols, channels, depth = smooth.shape[1:]
+    lane = lanes((channels, depth))
     sums = []
     for y in range(cols):
-        mid = ref[x, y]
-        both = (before[0][before[1], y] + mid) + (mid + after[0][after[1], y])
-        up = jnp.where(lane == depth - 1, 0.0, pltpu.roll(both, depth - 1, 1))
-        down = jnp.where(lane == 0, 0.0, pltpu.roll(both, 1, 1))
-        both = (both + both) + (up + down)
-        prod = both * field[row, y].astype(jnp.float32)
-        sums.append(jnp.sum(prod, axis=0, keepdims=True))
-    inner = jnp.concatenate(sums, axis=0)
-    return ridge_row * value_row + inner * (1.0 / (8 * channels))
-
-
-def first_inner_kernel(inner, i_lo, i_hi, start, y_lo, y_hi, ridge, smooth, out, rims):
-    rows = inner.shape[0]
-    flags = mesh_flags()
-    start_rims(y_lo, y_hi, rims)
-    s_lo, s_hi = (rim_of(rims, 0), rim_of(rims, 1))
-
-    def stage_y(k, carry):
-        along_y(smooth, k, inner, i_lo, i_hi, k, flags, own_row(start, s_lo, s_hi, k + 1))
-        return carry
-
-    lax.fori_loop(0, rows, stage_y, 0)
-
-    def stage_x(k, carry):
-        out[k] = along_x(
-            (smooth, k), (smooth, k + 1), (smooth, k + 2), inner, k + 1, ridge[k + 2], start[k + 2]
-        )
-        return carry
-
-    lax.fori_loop(0, rows - 2, stage_x, 0)
-
-
-def first_edge_kernel(
-    inner,
-    edge,
-    e_lo,
-    e_hi,
-    start,
-    y_lo,
-    y_hi,
-    side_lo,
-    side_hi,
-    ridge,
-    smooth,
-    part,
-    out,
-    out_hi,
-    out_lo,
-    rim,
-    side_start,
-    side_rims,
-    rims,
-):
-    n = inner.shape[0]
-    flags = mesh_flags()
-    last = n + 1
-    cols = inner.shape[1]
-    start_rims(y_lo, y_hi, rims)
-    s_lo, s_hi = (rim_of(rims, 0), rim_of(rims, 1))
+        mid = smooth[x, y]
+        low = (smooth[x - 1, y] + mid) if ends[0] else mid
+        high = (mid + smooth[x + 1, y]) if ends[1] else mid
+        sums.append(close_column(low + high, lane, field[row, y]))
+    return jnp.concatenate(sums, axis=0) * scale
+
+
+def first_core_kernel(inner, edge, start, side_lo, side_hi, ridge, out, smooth, side_start):
+    n, cols, channels, depth = inner.shape
+    scale = 1.0 / (8 * channels)
     for k, side in enumerate((side_lo, side_hi)):
         upper = side[5].astype(jnp.float32)
         lower = side[6].astype(jnp.float32)
         side_start[k] = (upper[:cols] + upper[cols:]) + lower[:cols]
-        ends = lower[cols : cols + 8]
-        side_rims[k, 0:2] = (ends[0:2] + ends[2:4]) + ends[4:6]
-
-    def side_values(k):
-        def at(y):
-            if y == 0:
-                return side_rims[k, 0:1]
-            if y == cols + 1:
-                return side_rims[k, 1:2]
-            return side_start[k, y - 1 : y]
-
-        return at
-
-    along_y(rim, 0, edge, e_lo, e_hi, 0, flags, side_values(0))
-    along_y(rim, 1, edge, e_lo, e_hi, 1, flags, own_row(start, s_lo, s_hi, 0))
-    along_y(rim, 2, edge, e_lo, e_hi, 2, flags, own_row(start, s_lo, s_hi, last))
-    along_y(rim, 3, edge, e_lo, e_hi, 3, flags, side_values(1))
-    for x, before, here, after, field, row in (
-        (0, (rim, 0), (rim, 1), (smooth, 0), edge, 1),
-        (1, (rim, 1), (smooth, 0), (smooth, 1), inner, 0),
-        (last - 1, (smooth, n - 2), (smooth, n - 1), (rim, 2), inner, n - 1),
-        (last, (smooth, n - 1), (rim, 2), (rim, 3), edge, 2),
+    along_y(smooth, 0, edge, 0, row_of(side_start, 0))
+    along_y(smooth, 1, edge, 1, row_of(start, 0))
+    along_y(smooth, n + 2, edge, 2, row_of(start, n + 1))
+    along_y(smooth, n + 3, edge, 3, row_of(side_start, 1))
+
+    def stage_y(k, carry):
+        along_y(smooth, k + 2, inner, k, row_of(start, k + 1))
+        return carry
+
+    lax.fori_loop(0, n, stage_y, 0)
+
+    def stage_x(k, carry):
+        image = along_x(smooth, k + 2, (True, True), inner, k, scale)
+        out[k + 1] = ridge[k + 1] * start[k + 1] + image
+        return carry
+
+    lax.fori_loop(0, n, stage_x, 0)
+    for x, row in ((0, 1), (n + 1, 2)):
+        image = along_x(smooth, x + 1, (True, True), edge, row, scale)
+        out[x] = ridge[x] * start[x] + image
+
+
+def rim_rows(g, inner, edge, y, lane, scale):
+    sums = []
+    for x in range(inner.shape[0] + 2):
+        low, mid, high = g[x : x + 3]
+        both = mid + mid
+        both = both if low is None else both + low
+        both = both if high is None else both + high
+        at = field_at(inner, edge, x + 1)
+        sums.append(close_column(both, lane, at[0][at[1], y]))
+    return jnp.concatenate(sums, axis=0) * scale
+
+
+def column_of(ref, y):
+    return jnp.concatenate([ref[x, y : y + 1, :] for x in range(ref.shape[0])], axis=0)
+
+
+def first_rim_kernel(
+    inner, edge, f_lo, f_hi, y_lo, y_hi, side_lo, side_hi, core, out, out_hi, out_lo
+):
+    n, cols, channels, depth = inner.shape
+    rows = n + 2
+    lane = lanes((channels, depth))
+    out[...] = core[...]
+    ends = []
+    for side in (side_lo, side_hi):
+        terms = side[6].astype(jnp.float32)[cols : cols + 8]
+        ends.append((terms[0:2] + terms[2:4]) + terms[4:6])
+    for k, (ref, rim, flag, y, send) in enumerate(
+        zip((f_lo, f_hi), (y_lo, y_hi), mesh_flags(), (0, cols - 1), (out_lo, out_hi))
     ):
-        out[x] = along_x(before, here, after, field, row, ridge[x], start[x])
-    for x in range(n - 2):
-        out[x + 2] = part[x]
-    for ref, y in ((out_hi, cols - 1), (out_lo, 0)):
-        ref[...] = jnp.concatenate([out[x, y : y + 1, :] for x in range(n + 2)], axis=0)
+        terms = rim[rows].astype(jnp.float32)
+        values = (terms[:rows] + terms[rows : 2 * rows]) + terms[2 * rows : 3 * rows]
+        values = [ends[0][k : k + 1], *(values[x : x + 1] for x in range(rows)), ends[1][k : k + 1]]
+        g = [ref[x].astype(jnp.float32) * (value * flag) for x, value in enumerate(values)]
+        column = column_of(core, y) + rim_rows(g, inner, edge, y, lane, 1.0 / (8 * channels))
+        send[...] = column
+        for x in range(rows):
+            out[x, y : y + 1, :] = column[x : x + 1]
 
 
 PRODUCTS = ((0, 0), (0, 1), (1, 1), (0, 2), (1, 2))
@@ -392,55 +369,78 @@
         sums[k] = (s, sums[k][1] + (t + e))
 
 
-def second_inner_kernel(
-    inner, edge, i_lo, i_hi, e_lo, e_hi, start, first, w_lo, w_hi, ridge, smooth, out, grams
-):
-    n = inner.shape[0]
-    flags = mesh_flags()
-    w_lo, w_hi = (rim_of(w_lo), rim_of(w_hi))
+def second_core_kernel(inner, edge, start, first, ridge, out, grams, smooth):
+    n, cols, channels, depth = inner.shape
+    scale = 1.0 / (8 * channels)
 
     def stage_y(k, carry):
-        along_y(smooth, k + 1, inner, i_lo, i_hi, k, flags, own_row(first, w_lo, w_hi, k + 1))
+        along_y(smooth, k + 1, inner, k, row_of(first, k + 1))
         return carry
 
     lax.fori_loop(0, n, stage_y, 0)
-    along_y(smooth, 0, edge, e_lo, e_hi, 1, flags, own_row(first, w_lo, w_hi, 0))
-    along_y(smooth, n + 1, edge, e_lo, e_hi, 2, flags, own_row(first, w_lo, w_hi, n + 1))
+    along_y(smooth, 0, edge, 1, row_of(first, 0))
+    along_y(smooth, n + 1, edge, 2, row_of(first, n + 1))
 
     def stage_x(k, carry):
-        out[k] = along_x(
-            (smooth, k), (smooth, k + 1), (smooth, k + 2), inner, k, ridge[k + 1], first[k + 1]
-        )
+        image = along_x(smooth, k + 1, (True, True), inner, k, scale)
+        out[k + 1] = ridge[k + 1] * first[k + 1] + image
         return carry
 
     lax.fori_loop(0, n, stage_x, 0)
-    zero = jnp.zeros(start.shape[1:], jnp.float32)
+    for x, row, ends in ((0, 1, (False, True)), (n + 1, 2, (True, False))):
+        out[x] = ridge[x] * first[x] + along_x(smooth, x, ends, edge, row, scale)
+    zero = jnp.zeros((cols, depth), jnp.float32)
     sums = [(zero, zero) for _ in PRODUCTS]
     for x in range(n + 2):
-        inside = 0 < x < n + 1
-        fields = (start[x], first[x], out[x - 1] if inside else None)
-        add_products(sums, range(5) if inside else range(3), fields)
+        add_products(sums, range(5), (start[x], first[x], out[x]))
     for k, (s, e) in enumerate(sums):
         grams[2 * k] = s
         grams[2 * k + 1] = e
 
 
-def second_edge_kernel(
-    edge, e_lo, e_hi, start, first, x_lo, x_hi, ridge, smooth, grams, out, share, rim
+def second_rim_kernel(
+    inner, edge, f_lo, f_hi, start, first, w_lo, w_hi, x_lo, x_hi, core, grams, out, share
 ):
-    n = smooth.shape[0]
+    n, cols, channels, depth = inner.shape
+    rows = n + 2
+    scale = 1.0 / (8 * channels)
+    lane = lanes((channels, depth))
     flags = mesh_flags()
-    along_y(rim, 0, edge, e_lo, e_hi, 0, flags, side_row(x_lo))
-    along_y(rim, 1, edge, e_lo, e_hi, 3, flags, side_row(x_hi))
-    out[0] = along_x((rim, 0), (smooth, 0), (smooth, 1), edge, 1, ridge[0], first[0])
-    out[1] = along_x(
-        (smooth, n - 2), (smooth, n - 1), (rim, 1), edge, 2, ridge[n - 1], first[n - 1]
-    )
+    out[...] = core[...]
     sums = [(grams[2 * k], grams[2 * k + 1]) for k in range(5)]
-    for x, k in ((0, 0), (n - 1, 1)):
-        add_products(sums, (3, 4), (start[x], first[x], out[k]))
+    added = []
+    for ref, rim, flag, y in ((f_lo, w_lo, flags[0], 0), (f_hi, w_hi, flags[1], cols - 1)):
+        g = [ref[x + 1].astype(jnp.float32) * (rim[x : x + 1] * flag) for x in range(rows)]
+        added.append(rim_rows([None, *g, None], inner, edge, y, lane, scale))
+    columns = [jnp.concatenate([column_of(ref, y) for y in (0, cols - 1)]) for ref in (start, first)]
+    add_products(sums, (3, 4), (*columns, jnp.concatenate(added, axis=0)))
+    for delta, y in zip(added, (0, cols - 1)):
+        for x in range(rows):
+            out[x, y : y + 1, :] = out[x, y : y + 1, :] + delta[x : x + 1]
+    for rim, at, row, x, far in ((x_lo, 0, 1, 0, 0), (x_hi, 3, 2, rows - 1, rows + 1)):
+
+        def product(y):
+            value = rim[y : y + 1]
+            if y == 0:
+                return f_lo[far].astype(jnp.float32) * (value * flags[0])
+            if y == cols + 1:
+                return f_hi[far].astype(jnp.float32) * (value * flags[1])
+            return edge[at, y - 1].astype(jnp.float32) * value
+
+        parts = []
+        here = product(1)
+        pair = product(0) + here
+        for y in range(cols):
+            following = product(y + 2)
+            pair_next = here + following
+            parts.append(close_column(pair + pair_next, lane, edge[row, y]))
+            here = following
+            pair = pair_next
+        delta = jnp.concatenate(parts, axis=0) * scale
+        add_products(sums, (3, 4), (start[x], first[x], delta))
+        out[x] = out[x] + delta
     row = jnp.zeros((8, 128), jnp.float32)
-    lane = lax.broadcasted_iota(jnp.int32, (8, 128), 1)
+    lane = lanes((8, 128))
     for k, (s, e) in enumerate(sums):
         while s.shape[0] > 8:
             half = s.shape[0] // 2
@@ -459,7 +459,7 @@
     share[...] = row[0:1]
 
 
-def final_kernel(shares, start, first, inside, sides, solution_out, residual_out):
+def final_kernel(shares, start, first, second, solution_out, residual_out):
     s = shares[...]
     e = jnp.zeros_like(s)
     while s.shape[0] > 8:
@@ -492,10 +492,8 @@
     beta = fresh[0] / curve[0]
     near = (alpha + beta * grow)[0:1, 0:1]
     far = (alpha * beta)[0:1, 0:1]
-    last = start.shape[0] - 1
-    for x in range(last + 1):
-        w2 = sides[0] if x == 0 else sides[1] if x == last else inside[x - 1]
-        w0, w1 = (start[x], first[x])
+    for x in range(start.shape[0]):
+        w0, w1, w2 = (start[x], first[x], second[x])
         solution_out[x] = near * w0 - far * w1
         residual_out[x] = (w0 - near * w1) + far * w2
 
@@ -539,7 +537,6 @@
         8,
         "weights",
     )
-    rims_scratch = ((2, rows, depth), f32)
     grid_scratch = ((rows, cols + 2, channels, depth), bf16)
     inner_shape = (rows - 2, cols, channels, depth)
     edge_shape = (4, cols, channels, depth)
@@ -561,54 +558,51 @@
         12,
         "conv_inner",
     )
-    i_lo, i_hi = halo(inner, "sy", 1, 1)
-    smooth, part = call(
-        first_inner_kernel,
-        (inner, i_lo, i_hi, residual, y_lo, y_hi, ridge),
-        [(inner_shape, f32), ((rows - 4, cols, depth), f32)],
-        [rims_scratch],
-        8,
-        "first_inner",
-    )
-    (edge,) = call(
+    column = ((rows + 2, channels, depth), bf16)
+    edge, f_hi, f_lo = call(
         conv_edge_kernel,
-        (features, y_lo, y_hi, x_lo, x_hi, side_lo, side_hi, weight_mask, wide, bias),
-        [(edge_shape, bf16)],
+        (features, y_lo, y_hi, x_lo, x_hi, side_lo, side_hi, weight_mask, wide, bias, inner),
+        [(edge_shape, bf16), column, column],
         [grid_scratch, ((4, cols, depth), f32)],
         12,
         "conv_edge",
     )
-    e_lo, e_hi = halo(edge, "sy", 1, 1)
+    f_lo, f_hi = (shift(f_hi, "sy", 1), shift(f_lo, "sy", -1))
+    (core,) = call(
+        first_core_kernel,
+        (inner, edge, residual, side_lo, side_hi, ridge),
+        [plane],
+        [((rows + 2, cols, channels, depth), f32), ((2, cols, depth), f32)],
+        10,
+        "first_core",
+    )
+    line = ((rows, depth), f32)
     first, w_hi, w_lo = call(
-        first_edge_kernel,
-        (inner, edge, e_lo, e_hi, residual, y_lo, y_hi, side_lo, side_hi, ridge, smooth, part),
-        [plane, ((rows, depth), f32), ((rows, depth), f32)],
-        [(edge_shape, f32), ((2, cols, depth), f32), ((2, 8, depth), f32), rims_scratch],
-        8,
-        "first_edge",
+        first_rim_kernel,
+        (inner, edge, f_lo, f_hi, y_lo, y_hi, side_lo, side_hi, core),
+        [plane, line, line],
+        [],
+        4,
+        "first_rim",
     )
     w_lo, w_hi = (shift(w_hi, "sy", 1), shift(w_lo, "sy", -1))
     rims = [jnp.concatenate([w_lo[x : x + 1], first[x], w_hi[x : x + 1]]) for x in (rows - 1, 0)]
     r_lo, r_hi = (shift(rims[0], "sx", 1), shift(rims[1], "sx", -1))
-    smooth, inside, grams = call(
-        second_inner_kernel,
-        (inner, edge, i_lo, i_hi, e_lo, e_hi, residual, first, w_lo, w_hi, ridge),
-        [
-            ((rows, cols, channels, depth), f32),
-            ((rows - 2, cols, depth), f32),
-            ((2 * len(PRODUCTS), cols, depth), f32),
-        ],
+    core, grams = call(
+        second_core_kernel,
+        (inner, edge, residual, first, ridge),
+        [plane, ((2 * len(PRODUCTS), cols, depth), f32)],
+        [((rows, cols, channels, depth), f32)],
+        10,
+        "second_core",
+    )
+    second, share = call(
+        second_rim_kernel,
+        (inner, edge, f_lo, f_hi, residual, first, w_lo, w_hi, r_lo, r_hi, core, grams),
+        [plane, ((1, 128), f32)],
         [],
-        8,
-        "second_inner",
-    )
-    sides, share = call(
-        second_edge_kernel,
-        (edge, e_lo, e_hi, residual, first, r_lo, r_hi, ridge, smooth, grams),
-        [((2, cols, depth), f32), ((1, 128), f32)],
-        [((2, cols, channels, depth), f32)],
-        8,
-        "second_edge",
+        4,
+        "second_rim",
     )
 
     peers = lax.axis_size("sx") * lax.axis_size("sy")
@@ -616,7 +610,7 @@
     return tuple(
         call(
             final_kernel,
-            (shares.reshape(peers, 128), residual, first, inside, sides),
+            (shares.reshape(peers, 128), residual, first, second),
             [plane, plane],
             [],
             8,

time: 72.1 us -> 67.7 us (0.939)
  starting transfers between devices: 26.5 us -> 20.8 us
  waiting for transfers between devices: 6.53 us -> 7.99 us
  blocking collectives: 19.2 us -> 17.8 us
  Pallas kernels: 14.6 us -> 15.9 us
    ppermute x14 -> x12, starting transfers between devices: 26.5 us -> 20.8 us  [shift(): lax.ppermute(value, axis, [(i, (i + step) % peers) for i in range(peers)])]
    all_to_all x1, blocking collectives: 19.2 us -> 17.8 us  [per_device(): lax.all_to_all(jnp.broadcast_to(share[None], (peers, 1, 128)), AXES, 0, 0)]
    ppermute x14 -> x12, waiting for transfers between devices: 6.53 us -> 7.99 us  [shift(): lax.ppermute(value, axis, [(i, (i + step) % peers) for i in range(peers)])]
    pallas_call x10, Pallas kernels: 14.6 us -> 15.9 us  [call(): pl.pallas_call(kernel, out_shape=[jax.ShapeDtypeStruct(shape, dtype) for...]
  transfers between devices with their start and end apart: 14 -> 12, of which waited for: 6 -> 5; matrix products, arithmetic and copies ran while one was open for 0% -> 0% of each run, Pallas kernels for 15% -> 17%
where the time goes in v7:
time: 67.7 us; the launch traced here: 67.5 us
  starting transfers between devices  20.8 us (31%)
  blocking collectives  17.8 us (26%)
  Pallas kernels  15.9 us (23%)
  waiting for transfers between devices  7.99 us (12%)
  local copies, waits for them, and re-layouts  4.2 us (6%)
  between operations  0.81 us (1%)
    ppermute x12, starting transfers between devices, shift(): lax.ppermute(value, axis, [(i, (i + step) % peers) for i in range(peers)])  20.8 us
    all_to_all x1, blocking collectives, per_device(): lax.all_to_all(jnp.broadcast_to(share[None], (peers, 1, 128)), AXES, 0, 0)  17.8 us
    pallas_call x10, Pallas kernels, call(): pl.pallas_call(kernel, out_shape=[jax.ShapeDtypeStruct(shape, dtype) for...  15.9 us
    ppermute x12, waiting for transfers between devices, shift(): lax.ppermute(value, axis, [(i, (i + step) % peers) for i in range(peers)])  7.99 us
    unnamed x14, local copies, waits for them, and re-layouts  2.73 us
    slice x1, local copies, waits for them, and re-layouts, per_device(): features[:2]  1.42 us
  transfers between devices with their start and end apart: 12, of which 5 were waited for; matrix products, arithmetic and copies ran while one was open for 0% of the time, Pallas kernels for 17%

profile of v7, /device:TPU:1, one launch (start us, length us, event | category | flops | bytes accessed | tf_op | source)
XLA Modules:
  0.0 67.5 jit_solution(8259656013010452669)
XLA Ops:
  0.6 1.4 %fusion = (bf16[2,16,32,256]{3,2,1,0:T(8,128)(2,1)S(1)}, bf16[2,16,32,256]{3,2,1,0:T(8,128)(2,1)S(1)}) fusion(bf16[8,16,32,256]{3,2,1,0:T(8,128)(2,1)} %own.5), kind=kLoop, calls=%fused_computation.4 | loop fusion | bytes 2097152 | tf_op jit(solution)/shard_map/slice | solution.py:517
  2.1 2.1 %collective-permute-start.2 = (bf16[2,16,32,256]{3,2,1,0:T(8,128)(2,1)S(1)}, bf16[2,16,32,256]{3,2,1,0:T(8,128)(2,1)S(1)}, u32[]{:S(2)}, u32[]{:S(2)}) collective-permute-start(bf16[2,16,32,256]{3,2,1,0:T(8,128)(2,1)S(1)} %get-tuple-element.29), channel_id=1, source_target_pairs={{0,8},{8,16},{16,24},{24,32},{32,40},{40,48},{48,56},{56,64},{64,7... | collective-permute-start | bytes 1572872 | tf_op jit(solution)/shard_map/ppermute | solution.py:13
  4.2 4.8 %collective-permute-start.3 = (bf16[2,16,32,256]{3,2,1,0:T(8,128)(2,1)S(1)}, bf16[2,16,32,256]{3,2,1,0:T(8,128)(2,1)S(1)}, u32[]{:S(2)}, u32[]{:S(2)}) collective-permute-start(bf16[2,16,32,256]{3,2,1,0:T(8,128)(2,1)S(1)} %get-tuple-element.30), channel_id=1, source_target_pairs={{0,120},{8,0},{16,8},{24,16},{32,24},{40,32},{48,40},{56,48},{64,5... | collective-permute-start | bytes 1572872 | tf_op jit(solution)/shard_map/ppermute | solution.py:13
  9.0 0.9 %copy-done.3 = s32[8,16,2,27]{3,2,1,0:T(2,128)S(1)} copy-done((s32[8,16,2,27]{3,2,1,0:T(2,128)S(1)}, s32[8,16,2,27]{3,2,1,0:T(2,128)}, u32[]{:S(2)}) %copy-start.3) | copy-done | bytes 27672
  9.9 0.9 %copy-done.4 = s32[8,16,256]{2,1,0:T(8,128)S(1)} copy-done((s32[8,16,256]{2,1,0:T(8,128)S(1)}, s32[8,16,256]{2,1,0:T(8,128)}, u32[]{:S(2)}) %copy-start.4) | copy-done | bytes 131096
  10.8 0.9 %copy-done.5 = f32[8,16,256]{2,1,0:T(8,128)S(1)} copy-done((f32[8,16,256]{2,1,0:T(8,128)S(1)}, f32[8,16,256]{2,1,0:T(8,128)}, u32[]{:S(2)}) %copy-start.5) | copy-done | bytes 131096
  11.7 0.1 prep.1
  11.9 2.1 %collective-permute-start = (bf16[9,32,256]{2,1,0:T(8,128)(2,1)S(1)}, bf16[9,32,256]{2,1,0:T(8,128)(2,1)S(1)}, u32[]{:S(2)}, u32[]{:S(2)}) collective-permute-start(bf16[9,32,256]{2,1,0:T(8,128)(2,1)S(1)} %get-tuple-element.24), channel_id=1, source_target_pairs={{0,1},{1,2},{2,3},{3,4},{4,5},{5,6},{6,7},{7,0},{8,9},{9,10},{10,1... | collective-permute-start | bytes 442376 | tf_op jit(solution)/shard_map/ppermute | solution.py:13
  14.0 0.0 collective-permute-start.1
  14.0 2.1 %collective-permute-done.y_lo = bf16[9,32,256]{2,1,0:T(8,128)(2,1)S(1)} collective-permute-done((bf16[9,32,256]{2,1,0:T(8,128)(2,1)S(1)}, bf16[9,32,256]{2,1,0:T(8,128)(2,1)S(1)}, u32[]{:S(2)}, u32[]{:S(2)}) %collective-permute-start) | collective-permute-done | bytes 147488 | tf_op jit(solution)/shard_map/ppermute | solution.py:13
  16.1 2.8 %collective-permute-done.1.y_hi = bf16[9,32,256]{2,1,0:T(8,128)(2,1)S(1)} collective-permute-done((bf16[9,32,256]{2,1,0:T(8,128)(2,1)S(1)}, bf16[9,32,256]{2,1,0:T(8,128)(2,1)S(1)}, u32[]{:S(2)}, u32[]{:S(2)}) %collective-permute-start.1) | collective-permute-done | bytes 147488 | tf_op jit(solution)/shard_map/ppermute | solution.py:13
  18.9 0.1 collective-permute-start.4
  19.0 4.8 %collective-permute-start.5 = (bf16[7,32,256]{2,1,0:T(8,128)(2,1)S(1)}, bf16[7,32,256]{2,1,0:T(8,128)(2,1)S(1)}, u32[]{:S(2)}, u32[]{:S(2)}) collective-permute-start(bf16[7,32,256]{2,1,0:T(8,128)(2,1)S(1)} %get-tuple-element.33), channel_id=1, source_target_pairs={{0,120},{8,0},{16,8},{24,16},{32,24},{40,32},{48,40},{56,48},{64,5... | collective-permute-start | bytes 344072 | tf_op jit(solution)/shard_map/ppermute | solution.py:13
  23.8 0.4 weights.1
  24.2 3.5 %conv_inner.1.inner = bf16[6,16,32,256]{3,2,1,0:T(8,128)(2,1)S(1)} custom-call(bf16[8,16,32,256]{3,2,1,0:T(8,128)(2,1)S(1)} %copy-done, bf16[9,32,256]{2,1,0:T(8,128)(2,1)S(1)} %collective-permute-done.y_lo, bf16[9,32,256]{2,1,0:T(8,128)(2,1)S(1)} %collective-permute-done.1.y_hi, f32[8,16,256]{2,1,0:T(8,128)S(1)} %get-tuple-element.26.mask, ...), custom_call_target="tpu_custom_call" | custom-call | tf_op jit(solution)/shard_map/conv_inner/pallas_call | solution.py:507
  27.8 0.0 copy-start.1
  27.8 1.9 %conv_edge.1 = (bf16[4,16,32,256]{3,2,1,0:T(8,128)(2,1)S(1)}, bf16[10,32,256]{2,1,0:T(8,128)(2,1)S(1)}, bf16[10,32,256]{2,1,0:T(8,128)(2,1)S(1)}) custom-call(bf16[8,16,32,256]{3,2,1,0:T(8,128)(2,1)S(1)} %copy-done, bf16[9,32,256]{2,1,0:T(8,128)(2,1)S(1)} %collective-permute-done.y_lo, bf16[9,32,256]{2,1,0:T(8,128)(2,1)S(1)} %collective-permute-done.1.y_hi, ...), custom_call_target="tpu_custom_call" | custom-call | tf_op jit(solution)/shard_map/conv_edge/pallas_call | solution.py:507
  29.8 0.3 collective-permute-start.6
  30.0 0.2 collective-permute-start.7
  30.3 3.5 %first_core.1.core = f32[8,16,256]{2,1,0:T(8,128)S(1)} custom-call(bf16[6,16,32,256]{3,2,1,0:T(8,128)(2,1)S(1)} %conv_inner.1.inner, bf16[4,16,32,256]{3,2,1,0:T(8,128)(2,1)S(1)} %get-tuple-element.34.edge, f32[8,16,256]{2,1,0:T(8,128)S(1)} %get-tuple-element.31.start, bf16[7,32,256]{2,1,0:T(8,128)(2,1)S(1)} %collective-permute-done.4.side_lo, ...), custom_call_target="tpu_custom_call" | custom-call | tf_op jit(solution)/shard_map/first_core/pallas_call | solution.py:507
  33.8 1.3 %collective-permute-done.7.f_hi = bf16[10,32,256]{2,1,0:T(8,128)(2,1)S(1)} collective-permute-done((bf16[10,32,256]{2,1,0:T(8,128)(2,1)S(1)}, bf16[10,32,256]{2,1,0:T(8,128)(2,1)S(1)}, u32[]{:S(2)}, u32[]{:S(2)}) %collective-permute-start.7) | collective-permute-done | bytes 163872 | tf_op jit(solution)/shard_map/ppermute | solution.py:13
  35.1 0.4 first_rim.1
  35.5 0.2 collective-permute-start.8
  35.7 1.3 %collective-permute-start.9 = (f32[8,256]{1,0:T(8,128)S(1)}, f32[8,256]{1,0:T(8,128)S(1)}, u32[]{:S(2)}, u32[]{:S(2)}) collective-permute-start(f32[8,256]{1,0:T(8,128)S(1)} %get-tuple-element.39), channel_id=1, source_target_pairs={{0,7},{1,0},{2,1},{3,2},{4,3},{5,4},{6,5},{7,6},{8,15},{9,8},{10,9... | collective-permute-start | bytes 24584 | tf_op jit(solution)/shard_map/ppermute | solution.py:13
  36.9 0.6 collective-permute-done.8.w_lo
  37.6 1.2 %collective-permute-done.9.w_hi = f32[8,256]{1,0:T(8,128)S(1)} collective-permute-done((f32[8,256]{1,0:T(8,128)S(1)}, f32[8,256]{1,0:T(8,128)S(1)}, u32[]{:S(2)}, u32[]{:S(2)}) %collective-permute-start.9) | collective-permute-done | bytes 8224 | tf_op jit(solution)/shard_map/ppermute | solution.py:13
  38.8 0.1 collective-permute-start.10
  38.9 4.8 %collective-permute-start.11 = (f32[18,256]{1,0:T(8,128)S(1)}, f32[18,256]{1,0:T(8,128)S(1)}, u32[]{:S(2)}, u32[]{:S(2)}) collective-permute-start(f32[18,256]{1,0:T(8,128)S(1)} %pad_maximum_fusion.1), channel_id=1, source_target_pairs={{0,120},{8,0},{16,8},{24,16},{32,24},{40,32},{48,40},{56,48},{64,5... | collective-permute-start | bytes 55304 | tf_op jit(solution)/shard_map/ppermute | solution.py:13
  43.6 3.6 %second_core.1 = (f32[8,16,256]{2,1,0:T(8,128)S(1)}, f32[10,16,256]{2,1,0:T(8,128)S(1)}) custom-call(bf16[6,16,32,256]{3,2,1,0:T(8,128)(2,1)S(1)} %conv_inner.1.inner, bf16[4,16,32,256]{3,2,1,0:T(8,128)(2,1)S(1)} %get-tuple-element.34.edge, f32[8,16,256]{2,1,0:T(8,128)S(1)} %get-tuple-element.31.start, f32[8,16,256]{2,1,0:T(8,128)S(1)} %get-tuple-element.37.first, ...), custom_call_target="tpu_custom_call" | custom-call | tf_op jit(solution)/shard_map/second_core/pallas_call | solution.py:507
  47.3 1.5 %second_rim.1 = (f32[8,16,256]{2,1,0:T(8,128)S(1)}, f32[1,128]{1,0:T(1,128)S(1)}) custom-call(bf16[6,16,32,256]{3,2,1,0:T(8,128)(2,1)S(1)} %conv_inner.1.inner, bf16[4,16,32,256]{3,2,1,0:T(8,128)(2,1)S(1)} %get-tuple-element.34.edge, bf16[10,32,256]{2,1,0:T(8,128)(2,1)S(1)} %collective-permute-done.6.f_lo, ...), custom_call_target="tpu_custom_call" | custom-call | tf_op jit(solution)/shard_map/second_rim/pallas_call | solution.py:507
  48.8 17.8 %all_to_all.5 = f32[128,1,128]{2,1,0:T(1,128)S(1)} all-to-all(f32[128,1,128]{2,1,0:T(1,128)S(1)} %broadcast_in_dim.13), channel_id=1, replica_groups=mesh['sx'=16,'sy'=8] {'sx','sy'}, dimensions={0} | all-to-all | bytes 131072 | tf_op jit(solution)/shard_map/all_to_all | solution.py:609
  66.6 0.9 %final.1 = (f32[8,16,256]{2,1,0:T(8,128)}, f32[8,16,256]{2,1,0:T(8,128)}) custom-call(f32[128,128]{1,0:T(8,128)S(1)} %bitcast.8, f32[8,16,256]{2,1,0:T(8,128)S(1)} %get-tuple-element.31.start, f32[8,16,256]{2,1,0:T(8,128)S(1)} %get-tuple-element.37.first, f32[8,16,256]{2,1,0:T(8,128)S(1)} %get-tuple-element.43.second), custom_call_target="tpu_custom_call" | custom-call | tf_op jit(solution)/shard_map/final/pallas_call | solution.py:507
  (24 shorter events, 0.1 us)
Async XLA Ops:
  0.6 8.4 %copy-start = (bf16[8,16,32,256]{3,2,1,0:T(8,128)(2,1)S(1)}, bf16[8,16,32,256]{3,2,1,0:T(8,128)(2,1)}, u32[]{:S(2)}) copy-start(bf16[8,16,32,256]{3,2,1,0:T(8,128)(2,1)} %own.5) | copy-start | bytes 6291460
  0.6 23.1 %copy-start.2 = (bf16[27,32,32]{2,1,0:T(8,128)(2,1)S(1)}, bf16[27,32,32]{2,1,0:T(8,128)(2,1)}, u32[]{:S(2)}) copy-start(bf16[27,32,32]{2,1,0:T(8,128)(2,1)} %taps.1) | copy-start | bytes 165892
  2.1 25.7 %collective-permute-start.2 = (bf16[2,16,32,256]{3,2,1,0:T(8,128)(2,1)S(1)}, bf16[2,16,32,256]{3,2,1,0:T(8,128)(2,1)S(1)}, u32[]{:S(2)}, u32[]{:S(2)}) collective-permute-start(bf16[2,16,32,256]{3,2,1,0:T(8,128)(2,1)S(1)} %get-tuple-element.29), channel_id=1, source_target_pairs={{0,8},{8,16},{16,24},{24,32},{32,40},{40,48},{48,56},{56,64},{64,7... | collective-permute-start | bytes 1572872 | tf_op jit(solution)/shard_map/ppermute | solution.py:13
  4.2 23.6 %collective-permute-start.3 = (bf16[2,16,32,256]{3,2,1,0:T(8,128)(2,1)S(1)}, bf16[2,16,32,256]{3,2,1,0:T(8,128)(2,1)S(1)}, u32[]{:S(2)}, u32[]{:S(2)}) collective-permute-start(bf16[2,16,32,256]{3,2,1,0:T(8,128)(2,1)S(1)} %get-tuple-element.30), channel_id=1, source_target_pairs={{0,120},{8,0},{16,8},{24,16},{32,24},{40,32},{48,40},{56,48},{64,5... | collective-permute-start | bytes 1572872 | tf_op jit(solution)/shard_map/ppermute | solution.py:13
  9.0 0.9 %copy-start.3 = (s32[8,16,2,27]{3,2,1,0:T(2,128)S(1)}, s32[8,16,2,27]{3,2,1,0:T(2,128)}, u32[]{:S(2)}) copy-start(s32[8,16,2,27]{3,2,1,0:T(2,128)} %param.11) | copy-start | bytes 82948
  9.9 0.9 %copy-start.4 = (s32[8,16,256]{2,1,0:T(8,128)S(1)}, s32[8,16,256]{2,1,0:T(8,128)}, u32[]{:S(2)}) copy-start(s32[8,16,256]{2,1,0:T(8,128)} %occupancy.1) | copy-start | bytes 393220
  10.8 0.9 %copy-start.5 = (f32[8,16,256]{2,1,0:T(8,128)S(1)}, f32[8,16,256]{2,1,0:T(8,128)}, u32[]{:S(2)}) copy-start(f32[8,16,256]{2,1,0:T(8,128)} %target) | copy-start | bytes 393220
  11.7 12.0 %copy-start.6 = (f32[32]{0:T(128)S(1)}, f32[32]{0:T(128)}, u32[]{:S(2)}) copy-start(f32[32]{0:T(128)} %param.9) | copy-start | bytes 388
  11.9 4.3 %collective-permute-start = (bf16[9,32,256]{2,1,0:T(8,128)(2,1)S(1)}, bf16[9,32,256]{2,1,0:T(8,128)(2,1)S(1)}, u32[]{:S(2)}, u32[]{:S(2)}) collective-permute-start(bf16[9,32,256]{2,1,0:T(8,128)(2,1)S(1)} %get-tuple-element.24), channel_id=1, source_target_pairs={{0,1},{1,2},{2,3},{3,4},{4,5},{5,6},{6,7},{7,0},{8,9},{9,10},{10,1... | collective-permute-start | bytes 442376 | tf_op jit(solution)/shard_map/ppermute | solution.py:13
  14.0 4.9 %collective-permute-start.1 = (bf16[9,32,256]{2,1,0:T(8,128)(2,1)S(1)}, bf16[9,32,256]{2,1,0:T(8,128)(2,1)S(1)}, u32[]{:S(2)}, u32[]{:S(2)}) collective-permute-start(bf16[9,32,256]{2,1,0:T(8,128)(2,1)S(1)} %get-tuple-element.25), channel_id=1, source_target_pairs={{0,7},{1,0},{2,1},{3,2},{4,3},{5,4},{6,5},{7,6},{8,15},{9,8},{10,9... | collective-permute-start | bytes 442376 | tf_op jit(solution)/shard_map/ppermute | solution.py:13
  18.9 8.9 %collective-permute-start.4 = (bf16[7,32,256]{2,1,0:T(8,128)(2,1)S(1)}, bf16[7,32,256]{2,1,0:T(8,128)(2,1)S(1)}, u32[]{:S(2)}, u32[]{:S(2)}) collective-permute-start(bf16[7,32,256]{2,1,0:T(8,128)(2,1)S(1)} %get-tuple-element.32), channel_id=1, source_target_pairs={{0,8},{8,16},{16,24},{24,32},{32,40},{40,48},{48,56},{56,64},{64,7... | collective-permute-start | bytes 344072 | tf_op jit(solution)/shard_map/ppermute | solution.py:13
  19.0 8.8 %collective-permute-start.5 = (bf16[7,32,256]{2,1,0:T(8,128)(2,1)S(1)}, bf16[7,32,256]{2,1,0:T(8,128)(2,1)S(1)}, u32[]{:S(2)}, u32[]{:S(2)}) collective-permute-start(bf16[7,32,256]{2,1,0:T(8,128)(2,1)S(1)} %get-tuple-element.33), channel_id=1, source_target_pairs={{0,120},{8,0},{16,8},{24,16},{32,24},{40,32},{48,40},{56,48},{64,5... | collective-permute-start | bytes 344072 | tf_op jit(solution)/shard_map/ppermute | solution.py:13
  27.8 2.5 %copy-start.1 = (f32[8,16,256]{2,1,0:T(8,128)S(1)}, f32[8,16,256]{2,1,0:T(8,128)}, u32[]{:S(2)}) copy-start(f32[8,16,256]{2,1,0:T(8,128)} %ridge.3) | copy-start | bytes 393220
  29.8 4.0 %collective-permute-start.6 = (bf16[10,32,256]{2,1,0:T(8,128)(2,1)S(1)}, bf16[10,32,256]{2,1,0:T(8,128)(2,1)S(1)}, u32[]{:S(2)}, u32[]{:S(2)}) collective-permute-start(bf16[10,32,256]{2,1,0:T(8,128)(2,1)S(1)} %get-tuple-element.35), channel_id=1, source_target_pairs={{0,1},{1,2},{2,3},{3,4},{4,5},{5,6},{6,7},{7,0},{8,9},{9,10},{10,1... | collective-permute-start | bytes 491528 | tf_op jit(solution)/shard_map/ppermute | solution.py:13
  30.0 5.0 %collective-permute-start.7 = (bf16[10,32,256]{2,1,0:T(8,128)(2,1)S(1)}, bf16[10,32,256]{2,1,0:T(8,128)(2,1)S(1)}, u32[]{:S(2)}, u32[]{:S(2)}) collective-permute-start(bf16[10,32,256]{2,1,0:T(8,128)(2,1)S(1)} %get-tuple-element.36), channel_id=1, source_target_pairs={{0,7},{1,0},{2,1},{3,2},{4,3},{5,4},{6,5},{7,6},{8,15},{9,8},{10,9... | collective-permute-start | bytes 491528 | tf_op jit(solution)/shard_map/ppermute | solution.py:13
  35.5 2.1 %collective-permute-start.8 = (f32[8,256]{1,0:T(8,128)S(1)}, f32[8,256]{1,0:T(8,128)S(1)}, u32[]{:S(2)}, u32[]{:S(2)}) collective-permute-start(f32[8,256]{1,0:T(8,128)S(1)} %get-tuple-element.38), channel_id=1, source_target_pairs={{0,1},{1,2},{2,3},{3,4},{4,5},{5,6},{6,7},{7,0},{8,9},{9,10},{10,1... | collective-permute-start | bytes 24584 | tf_op jit(solution)/shard_map/ppermute | solution.py:13
  35.7 3.1 %collective-permute-start.9 = (f32[8,256]{1,0:T(8,128)S(1)}, f32[8,256]{1,0:T(8,128)S(1)}, u32[]{:S(2)}, u32[]{:S(2)}) collective-permute-start(f32[8,256]{1,0:T(8,128)S(1)} %get-tuple-element.39), channel_id=1, source_target_pairs={{0,7},{1,0},{2,1},{3,2},{4,3},{5,4},{6,5},{7,6},{8,15},{9,8},{10,9... | collective-permute-start | bytes 24584 | tf_op jit(solution)/shard_map/ppermute | solution.py:13
  38.8 8.5 %collective-permute-start.10 = (f32[18,256]{1,0:T(8,128)S(1)}, f32[18,256]{1,0:T(8,128)S(1)}, u32[]{:S(2)}, u32[]{:S(2)}) collective-permute-start(f32[18,256]{1,0:T(8,128)S(1)} %pad_maximum_fusion), channel_id=1, source_target_pairs={{0,8},{8,16},{16,24},{24,32},{32,40},{40,48},{48,56},{56,64},{64,7... | collective-permute-start | bytes 55304 | tf_op jit(solution)/shard_map/ppermute | solution.py:13
  38.9 8.4 %collective-permute-start.11 = (f32[18,256]{1,0:T(8,128)S(1)}, f32[18,256]{1,0:T(8,128)S(1)}, u32[]{:S(2)}, u32[]{:S(2)}) collective-permute-start(f32[18,256]{1,0:T(8,128)S(1)} %pad_maximum_fusion.1), channel_id=1, source_target_pairs={{0,120},{8,0},{16,8},{24,16},{32,24},{40,32},{48,40},{56,48},{64,5... | collective-permute-start | bytes 55304 | tf_op jit(solution)/shard_map/ppermute | solution.py:13

commit v8 on v7

--- a/solution.py
+++ b/solution.py
@@ -6,6 +6,7 @@
 from jax.sharding import PartitionSpec as P
 
 AXES = ("sx", "sy")
+PREP_LIMIT = 58
 
 
 def shift(value, axis, step):
@@ -20,22 +21,70 @@
     return high, mid, rest - mid
 
 
-def prep_kernel(own, ids, occupancy, target, mask, start, out_hi, out_lo, present):
+def prep_kernel(
+    own,
+    ids_in,
+    occupancy_in,
+    target_in,
+    mask,
+    start,
+    y_hi,
+    y_lo,
+    x_hi,
+    x_lo,
+    ids,
+    occupancy,
+    target,
+    columns,
+    present,
+    sems,
+):
     rows, cols, channels, depth = own.shape
     half = present.shape[1]
+    copies = [
+        pltpu.make_async_copy(source, goal, sems.at[k])
+        for k, (source, goal) in enumerate(
+            (
+                (ids_in, ids),
+                (occupancy_in, occupancy),
+                (target_in, target),
+                (own.at[:, 0:1], columns.at[0]),
+                (own.at[:, cols - 1 : cols], columns.at[1]),
+                (own.at[rows - 2], x_hi.at[0:cols]),
+                (own.at[rows - 1], x_hi.at[cols : 2 * cols]),
+                (own.at[0], x_lo.at[0:cols]),
+                (own.at[1], x_lo.at[cols : 2 * cols]),
+            )
+        )
+    ]
+    for copy in copies:
+        copy.start()
+    copies[0].wait()
+    copies[1].wait()
     present[...] = jnp.broadcast_to(
         jnp.where(ids[:, 13:14] >= 0, 1.0, 0.0).astype(jnp.float32), present.shape
     )
     for x in range(rows):
         blocks = [present[pl.ds(2 * cols * x + z, cols, stride=2), :] for z in range(depth // half)]
         mask[x] = occupancy[x].astype(jnp.float32) * jnp.concatenate(blocks, axis=1)
+    copies[2].wait()
+    for x in range(rows):
         start[x] = mask[x] * target[x]
-    for out, y in ((out_hi, cols - 1), (out_lo, 0)):
+    copies[3].wait()
+    copies[4].wait()
+    for k, (out, y) in enumerate(((y_lo, 0), (y_hi, cols - 1))):
         for x in range(rows):
-            out[x] = own[x, y] * mask[x, y : y + 1, :].astype(jnp.bfloat16)
+            out[x] = columns[k, x, 0] * mask[x, y : y + 1, :].astype(jnp.bfloat16)
         edge = jnp.concatenate([start[x, y : y + 1, :] for x in range(rows)], axis=0)
         blank = jnp.zeros((channels - 3 * rows, depth), jnp.float32)
         out[rows] = jnp.concatenate([*three(edge), blank], axis=0).astype(jnp.bfloat16)
+    for out, pair, row in ((x_hi, (rows - 2, rows - 1), rows - 1), (x_lo, (0, 1), 0)):
+        out[2 * cols] = jnp.concatenate([mask[x] for x in pair], axis=0).astype(jnp.bfloat16)
+        high, mid, low = three(start[row])
+        out[2 * cols + 1] = jnp.concatenate([high, mid], axis=0).astype(jnp.bfloat16)
+        out[2 * cols + 2] = jnp.concatenate([low, jnp.zeros_like(low)], axis=0).astype(jnp.bfloat16)
+    for copy in copies[5:]:
+        copy.wait()
 
 
 def weights_kernel(taps, bias, wide, bias_col):
@@ -132,26 +181,23 @@
     lax.fori_loop(0, rows // 2 - 1, pair, 0)
 
 
-def sides_kernel(y_lo, y_hi, mask, start, out_hi, out_lo):
-    rows, cols, depth = mask.shape
-    flags = mesh_flags()
-    clear = [splat(flag, y_lo.shape[1:]) for flag in flags[:2]]
+def sides_kernel(y_lo, y_hi, out_hi, out_lo):
+    rows = y_lo.shape[0] - 1
+    channels, depth = y_lo.shape[1:]
+    clear = [splat(flag, y_lo.shape[1:]) for flag in mesh_flags()[:2]]
     low_terms = y_lo[rows].astype(jnp.float32)
     high_terms = y_hi[rows].astype(jnp.float32)
     for out, pair, row in ((out_hi, (rows - 2, rows - 1), rows - 1), (out_lo, (0, 1), 0)):
         for k, x in enumerate(pair):
             out[2 * k] = y_lo[x] * clear[0]
             out[2 * k + 1] = y_hi[x] * clear[1]
-        out[4] = jnp.concatenate([mask[x] for x in pair], axis=0).astype(jnp.bfloat16)
-        high, mid, low = three(start[row])
         rims = [
             terms[at : at + 1]
             for at in (row, rows + row, 2 * rows + row)
             for terms in (low_terms, high_terms)
         ]
-        blank = jnp.zeros((10, depth), jnp.float32)
-        out[5] = jnp.concatenate([high, mid], axis=0).astype(jnp.bfloat16)
-        out[6] = jnp.concatenate([low, *rims, blank], axis=0).astype(jnp.bfloat16)
+        blank = jnp.zeros((channels - 6, depth), jnp.float32)
+        out[4] = jnp.concatenate([*rims, blank], axis=0).astype(jnp.bfloat16)
 
 
 def conv_edge_kernel(
@@ -174,8 +220,8 @@
 ):
     rows, cols, channels, depth = own.shape
     flags = mesh_flags()
-    for k, side in enumerate((side_lo, side_hi)):
-        both = side[4].astype(jnp.float32) * flags[2 + k]
+    for k, side in enumerate((x_lo, x_hi)):
+        both = side[2 * cols].astype(jnp.float32) * flags[2 + k]
         side_mask[2 * k] = both[:cols]
         side_mask[2 * k + 1] = both[cols:]
     for x in range(2):
@@ -185,7 +231,7 @@
                 grid,
                 6 * k + x,
                 mask_of(side_mask, 2 * k + x),
-                lambda y: ref[x, y],
+                lambda y: ref[x * cols + y],
                 side[2 * x] * clear,
                 side[2 * x + 1] * clear,
             )
@@ -289,12 +335,12 @@
     return jnp.concatenate(sums, axis=0) * scale
 
 
-def first_core_kernel(inner, edge, start, side_lo, side_hi, ridge, out, smooth, side_start):
+def first_core_kernel(inner, edge, start, x_lo, x_hi, ridge, out, smooth, side_start):
     n, cols, channels, depth = inner.shape
     scale = 1.0 / (8 * channels)
-    for k, side in enumerate((side_lo, side_hi)):
-        upper = side[5].astype(jnp.float32)
-        lower = side[6].astype(jnp.float32)
+    for k, side in enumerate((x_lo, x_hi)):
+        upper = side[2 * cols + 1].astype(jnp.float32)
+        lower = side[2 * cols + 2].astype(jnp.float32)
         side_start[k] = (upper[:cols] + upper[cols:]) + lower[:cols]
     along_y(smooth, 0, edge, 0, row_of(side_start, 0))
     along_y(smooth, 1, edge, 1, row_of(start, 0))
@@ -343,7 +389,7 @@
     out[...] = core[...]
     ends = []
     for side in (side_lo, side_hi):
-        terms = side[6].astype(jnp.float32)[cols : cols + 8]
+        terms = side[4].astype(jnp.float32)
         ends.append((terms[0:2] + terms[2:4]) + terms[4:6])
     for k, (ref, rim, flag, y, send) in enumerate(
         zip((f_lo, f_hi), (y_lo, y_hi), mesh_flags(), (0, cols - 1), (out_lo, out_hi))
@@ -514,21 +560,29 @@
             name=name,
         )(*args)
 
-    edges, target = lax.optimization_barrier(((features[-2:], features[:2]), target))
-    x_lo, x_hi = (shift(edges[0], "sx", 1), shift(edges[1], "sx", -1))
-
     plane = ((rows, cols, depth), f32)
     blocks = block_ids.reshape(-1, block_ids.shape[3])
     edge_column = ((rows + 1, channels, depth), bf16)
-    weight_mask, residual, y_hi, y_lo = call(
+    edge_rows = ((2 * cols + 3, channels, depth), bf16)
+    outs = [plane, plane, edge_column, edge_column, edge_rows, edge_rows]
+    weight_mask, residual, y_hi, y_lo, x_hi, x_lo = pl.pallas_call(
         prep_kernel,
-        (features, blocks, occupancy, target),
-        [plane, plane, edge_column, edge_column],
-        [((blocks.shape[0], depth // block_ids.shape[2]), f32)],
-        4,
-        "prep",
-    )
+        out_shape=[jax.ShapeDtypeStruct(shape, dtype) for shape, dtype in outs],
+        in_specs=[pl.BlockSpec(memory_space=pl.ANY)] * 4,
+        out_specs=[vmem for _ in outs],
+        scratch_shapes=[
+            pltpu.VMEM(blocks.shape, jnp.int32),
+            pltpu.VMEM(occupancy.shape, jnp.int32),
+            pltpu.VMEM(target.shape, f32),
+            pltpu.VMEM((2, rows, 1, channels, depth), bf16),
+            pltpu.VMEM((blocks.shape[0], depth // block_ids.shape[2]), f32),
+            pltpu.SemaphoreType.DMA((9,)),
+        ],
+        compiler_params=pltpu.CompilerParams(vmem_limit_bytes=PREP_LIMIT << 20),
+        name="prep",
+    )(features, blocks, occupancy, target)
     y_lo, y_hi = (shift(y_hi, "sy", 1), shift(y_lo, "sy", -1))
+    x_lo, x_hi = (shift(x_hi, "sx", 1), shift(x_lo, "sx", -1))
     wide, bias = call(
         weights_kernel,
         (conv_weight, conv_bias[None]),
@@ -540,10 +594,10 @@
     grid_scratch = ((rows, cols + 2, channels, depth), bf16)
     inner_shape = (rows - 2, cols, channels, depth)
     edge_shape = (4, cols, channels, depth)
-    side_shape = (7, channels, depth)
+    side_shape = (5, channels, depth)
     side_hi, side_lo = call(
         sides_kernel,
-        (y_lo, y_hi, weight_mask, residual),
+        (y_lo, y_hi),
         [(side_shape, bf16), (side_shape, bf16)],
         [],
         4,
@@ -570,7 +624,7 @@
     f_lo, f_hi = (shift(f_hi, "sy", 1), shift(f_lo, "sy", -1))
     (core,) = call(
         first_core_kernel,
-        (inner, edge, residual, side_lo, side_hi, ridge),
+        (inner, edge, residual, x_lo, x_hi, ridge),
         [plane],
         [((rows + 2, cols, channels, depth), f32), ((2, cols, depth), f32)],
         10,

time: 67.7 us -> 67.4 us (level)
  local copies, waits for them, and re-layouts: 4.2 us -> 0.98 us
  Pallas kernels: 15.9 us -> 18.7 us
    pallas_call x0 -> x1, Pallas kernels: none -> 2.9 us  [per_device(): pl.pallas_call(prep_kernel, out_shape=[jax.ShapeDtypeStruct(shape, dtype)...]
    unnamed x14, local copies, waits for them, and re-layouts: 2.73 us -> 0.93 us
    slice x1 -> x0, local copies, waits for them, and re-layouts: 1.42 us -> none  [per_device(): features[:2]]
    pallas_call x10 -> x9, Pallas kernels: 15.9 us -> 15.8 us  [call(): pl.pallas_call(kernel, out_shape=[jax.ShapeDtypeStruct(shape, dtype) for...]
  transfers between devices with their start and end apart: 12 -> 12, of which waited for: 5 -> 5; matrix products, arithmetic and copies ran while one was open for 0% -> 0% of each run, Pallas kernels for 17% -> 16%
where the time goes in v8:
time: 67.4 us; the launch traced here: 67.3 us
  starting transfers between devices  20.9 us (31%)
  Pallas kernels  18.7 us (28%)
  blocking collectives  17.6 us (26%)
  waiting for transfers between devices  8.2 us (12%)
  local copies, waits for them, and re-layouts  0.98 us (1%)
  between operations  0.85 us (1%)
    ppermute x12, starting transfers between devices, shift(): lax.ppermute(value, axis, [(i, (i + step) % peers) for i in range(peers)])  20.9 us
    all_to_all x1, blocking collectives, per_device(): lax.all_to_all(jnp.broadcast_to(share[None], (peers, 1, 128)), AXES, 0, 0)  17.6 us
    pallas_call x9, Pallas kernels, call(): pl.pallas_call(kernel, out_shape=[jax.ShapeDtypeStruct(shape, dtype) for...  15.8 us
    ppermute x12, waiting for transfers between devices, shift(): lax.ppermute(value, axis, [(i, (i + step) % peers) for i in range(peers)])  8.2 us
    pallas_call x1, Pallas kernels, per_device(): pl.pallas_call(prep_kernel, out_shape=[jax.ShapeDtypeStruct(shape, dtype)...  2.9 us
  transfers between devices with their start and end apart: 12, of which 5 were waited for; matrix products, arithmetic and copies ran while one was open for 0% of the time, Pallas kernels for 16%

profile of v8, /device:TPU:1, one launch (start us, length us, event | category | flops | bytes accessed | tf_op | source)
XLA Modules:
  0.0 67.3 jit_solution(9344586207735173731)
XLA Ops:
  0.7 2.9 %prep.1 = (f32[8,16,256]{2,1,0:T(8,128)}, f32[8,16,256]{2,1,0:T(8,128)}, bf16[9,32,256]{2,1,0:T(8,128)(2,1)}, bf16[9,32,256]{2,1,0:T(8,128)(2,1)}, bf16[35,32,25...) custom-call(bf16[8,16,32,256]{3,2,1,0:T(8,128)(2,1)} %own.5, s32[256,27]{1,0:T(8,128)} %bitcast.11, ...), custom_call_target="tpu_custom_call" | custom-call | tf_op jit(solution)/shard_map/prep/pallas_call | solution.py:568
  3.6 2.1 %collective-permute-start.2 = (bf16[35,32,256]{2,1,0:T(8,128)(2,1)}, bf16[35,32,256]{2,1,0:T(8,128)(2,1)S(1)}, u32[]{:S(2)}, u32[]{:S(2)}) collective-permute-start(bf16[35,32,256]{2,1,0:T(8,128)(2,1)} %get-tuple-element.27), channel_id=1, source_target_pairs={{0,8},{8,16},{16,24},{24,32},{32,40},{40,48},{48,56},{56,64},{64,7... | collective-permute-start | bytes 1720328 | tf_op jit(solution)/shard_map/ppermute | solution.py:14
  5.7 4.8 %collective-permute-start.3 = (bf16[35,32,256]{2,1,0:T(8,128)(2,1)}, bf16[35,32,256]{2,1,0:T(8,128)(2,1)S(1)}, u32[]{:S(2)}, u32[]{:S(2)}) collective-permute-start(bf16[35,32,256]{2,1,0:T(8,128)(2,1)} %get-tuple-element.28), channel_id=1, source_target_pairs={{0,120},{8,0},{16,8},{24,16},{32,24},{40,32},{48,40},{56,48},{64,5... | collective-permute-start | bytes 1720328 | tf_op jit(solution)/shard_map/ppermute | solution.py:14
  10.5 2.1 %collective-permute-start = (bf16[9,32,256]{2,1,0:T(8,128)(2,1)}, bf16[9,32,256]{2,1,0:T(8,128)(2,1)S(1)}, u32[]{:S(2)}, u32[]{:S(2)}) collective-permute-start(bf16[9,32,256]{2,1,0:T(8,128)(2,1)} %get-tuple-element.22), channel_id=1, source_target_pairs={{0,1},{1,2},{2,3},{3,4},{4,5},{5,6},{6,7},{7,0},{8,9},{9,10},{10,1... | collective-permute-start | bytes 442376 | tf_op jit(solution)/shard_map/ppermute | solution.py:14
  12.6 0.0 collective-permute-start.1
  12.6 2.4 %collective-permute-done.y_lo = bf16[9,32,256]{2,1,0:T(8,128)(2,1)S(1)} collective-permute-done((bf16[9,32,256]{2,1,0:T(8,128)(2,1)}, bf16[9,32,256]{2,1,0:T(8,128)(2,1)S(1)}, u32[]{:S(2)}, u32[]{:S(2)}) %collective-permute-start) | collective-permute-done | bytes 147488 | tf_op jit(solution)/shard_map/ppermute | solution.py:14
  15.1 2.7 %collective-permute-done.1.y_hi = bf16[9,32,256]{2,1,0:T(8,128)(2,1)S(1)} collective-permute-done((bf16[9,32,256]{2,1,0:T(8,128)(2,1)}, bf16[9,32,256]{2,1,0:T(8,128)(2,1)S(1)}, u32[]{:S(2)}, u32[]{:S(2)}) %collective-permute-start.1) | collective-permute-done | bytes 147488 | tf_op jit(solution)/shard_map/ppermute | solution.py:14
  17.7 0.1 collective-permute-start.4
  17.8 4.8 %collective-permute-start.5 = (bf16[5,32,256]{2,1,0:T(8,128)(2,1)S(1)}, bf16[5,32,256]{2,1,0:T(8,128)(2,1)S(1)}, u32[]{:S(2)}, u32[]{:S(2)}) collective-permute-start(bf16[5,32,256]{2,1,0:T(8,128)(2,1)S(1)} %get-tuple-element.30), channel_id=1, source_target_pairs={{0,120},{8,0},{16,8},{24,16},{32,24},{40,32},{48,40},{56,48},{64,5... | collective-permute-start | bytes 245768 | tf_op jit(solution)/shard_map/ppermute | solution.py:14
  22.6 0.4 weights.1
  23.0 0.0 copy-start.3
  23.1 0.9 %copy-done.3 = f32[8,16,256]{2,1,0:T(8,128)S(1)} copy-done((f32[8,16,256]{2,1,0:T(8,128)S(1)}, f32[8,16,256]{2,1,0:T(8,128)}, u32[]{:S(2)}) %copy-start.3) | copy-done | bytes 131096
  24.0 3.5 %conv_inner.1.inner = bf16[6,16,32,256]{3,2,1,0:T(8,128)(2,1)S(1)} custom-call(bf16[8,16,32,256]{3,2,1,0:T(8,128)(2,1)S(1)} %copy-done, bf16[9,32,256]{2,1,0:T(8,128)(2,1)S(1)} %collective-permute-done.y_lo, bf16[9,32,256]{2,1,0:T(8,128)(2,1)S(1)} %collective-permute-done.1.y_hi, f32[8,16,256]{2,1,0:T(8,128)S(1)} %copy-done.3, ...), custom_call_target="tpu_custom_call" | custom-call | tf_op jit(solution)/shard_map/conv_inner/pallas_call | solution.py:553
  27.5 0.0 copy-start.1
  27.5 0.0 copy-start.2
  27.5 0.0 collective-permute-done.5.side_hi
  27.6 1.9 %conv_edge.1 = (bf16[4,16,32,256]{3,2,1,0:T(8,128)(2,1)S(1)}, bf16[10,32,256]{2,1,0:T(8,128)(2,1)S(1)}, bf16[10,32,256]{2,1,0:T(8,128)(2,1)S(1)}) custom-call(bf16[8,16,32,256]{3,2,1,0:T(8,128)(2,1)S(1)} %copy-done, bf16[9,32,256]{2,1,0:T(8,128)(2,1)S(1)} %collective-permute-done.y_lo, bf16[9,32,256]{2,1,0:T(8,128)(2,1)S(1)} %collective-permute-done.1.y_hi, ...), custom_call_target="tpu_custom_call" | custom-call | tf_op jit(solution)/shard_map/conv_edge/pallas_call | solution.py:553
  29.5 0.3 collective-permute-start.6
  29.8 0.2 collective-permute-start.7
  30.0 3.5 %first_core.1.core = f32[8,16,256]{2,1,0:T(8,128)S(1)} custom-call(bf16[6,16,32,256]{3,2,1,0:T(8,128)(2,1)S(1)} %conv_inner.1.inner, bf16[4,16,32,256]{3,2,1,0:T(8,128)(2,1)S(1)} %get-tuple-element.31.edge, f32[8,16,256]{2,1,0:T(8,128)S(1)} %copy-done.1, bf16[35,32,256]{2,1,0:T(8,128)(2,1)S(1)} %collective-permute-done.2.x_lo, ...), custom_call_target="tpu_custom_call" | custom-call | tf_op jit(solution)/shard_map/first_core/pallas_call | solution.py:553
  33.5 1.3 %collective-permute-done.7.f_hi = bf16[10,32,256]{2,1,0:T(8,128)(2,1)S(1)} collective-permute-done((bf16[10,32,256]{2,1,0:T(8,128)(2,1)S(1)}, bf16[10,32,256]{2,1,0:T(8,128)(2,1)S(1)}, u32[]{:S(2)}, u32[]{:S(2)}) %collective-permute-start.7) | collective-permute-done | bytes 163872 | tf_op jit(solution)/shard_map/ppermute | solution.py:14
  34.8 0.4 first_rim.1
  35.2 0.2 collective-permute-start.8
  35.4 1.3 %collective-permute-start.9 = (f32[8,256]{1,0:T(8,128)S(1)}, f32[8,256]{1,0:T(8,128)S(1)}, u32[]{:S(2)}, u32[]{:S(2)}) collective-permute-start(f32[8,256]{1,0:T(8,128)S(1)} %get-tuple-element.37), channel_id=1, source_target_pairs={{0,7},{1,0},{2,1},{3,2},{4,3},{5,4},{6,5},{7,6},{8,15},{9,8},{10,9... | collective-permute-start | bytes 24584 | tf_op jit(solution)/shard_map/ppermute | solution.py:14
  36.7 0.6 collective-permute-done.8.w_lo
  37.3 1.2 %collective-permute-done.9.w_hi = f32[8,256]{1,0:T(8,128)S(1)} collective-permute-done((f32[8,256]{1,0:T(8,128)S(1)}, f32[8,256]{1,0:T(8,128)S(1)}, u32[]{:S(2)}, u32[]{:S(2)}) %collective-permute-start.9) | collective-permute-done | bytes 8224 | tf_op jit(solution)/shard_map/ppermute | solution.py:14
  38.5 0.1 collective-permute-start.10
  38.6 4.9 %collective-permute-start.11 = (f32[18,256]{1,0:T(8,128)S(1)}, f32[18,256]{1,0:T(8,128)S(1)}, u32[]{:S(2)}, u32[]{:S(2)}) collective-permute-start(f32[18,256]{1,0:T(8,128)S(1)} %pad_maximum_fusion.1), channel_id=1, source_target_pairs={{0,120},{8,0},{16,8},{24,16},{32,24},{40,32},{48,40},{56,48},{64,5... | collective-permute-start | bytes 55304 | tf_op jit(solution)/shard_map/ppermute | solution.py:14
  43.5 3.6 %second_core.1 = (f32[8,16,256]{2,1,0:T(8,128)S(1)}, f32[10,16,256]{2,1,0:T(8,128)S(1)}) custom-call(bf16[6,16,32,256]{3,2,1,0:T(8,128)(2,1)S(1)} %conv_inner.1.inner, bf16[4,16,32,256]{3,2,1,0:T(8,128)(2,1)S(1)} %get-tuple-element.31.edge, f32[8,16,256]{2,1,0:T(8,128)S(1)} %copy-done.1, f32[8,16,256]{2,1,0:T(8,128)S(1)} %get-tuple-element.35.first, ...), custom_call_target="tpu_custom_call" | custom-call | tf_op jit(solution)/shard_map/second_core/pallas_call | solution.py:553
  47.1 1.5 %second_rim.1 = (f32[8,16,256]{2,1,0:T(8,128)S(1)}, f32[1,128]{1,0:T(1,128)S(1)}) custom-call(bf16[6,16,32,256]{3,2,1,0:T(8,128)(2,1)S(1)} %conv_inner.1.inner, bf16[4,16,32,256]{3,2,1,0:T(8,128)(2,1)S(1)} %get-tuple-element.31.edge, bf16[10,32,256]{2,1,0:T(8,128)(2,1)S(1)} %collective-permute-done.6.f_lo, ...), custom_call_target="tpu_custom_call" | custom-call | tf_op jit(solution)/shard_map/second_rim/pallas_call | solution.py:553
  48.7 17.6 %all_to_all.5 = f32[128,1,128]{2,1,0:T(1,128)S(1)} all-to-all(f32[128,1,128]{2,1,0:T(1,128)S(1)} %broadcast_in_dim.13), channel_id=1, replica_groups=mesh['sx'=16,'sy'=8] {'sx','sy'}, dimensions={0} | all-to-all | bytes 131072 | tf_op jit(solution)/shard_map/all_to_all | solution.py:663
  66.3 0.9 %final.1 = (f32[8,16,256]{2,1,0:T(8,128)}, f32[8,16,256]{2,1,0:T(8,128)}) custom-call(f32[128,128]{1,0:T(8,128)S(1)} %bitcast.8, f32[8,16,256]{2,1,0:T(8,128)S(1)} %copy-done.1, f32[8,16,256]{2,1,0:T(8,128)S(1)} %get-tuple-element.35.first, f32[8,16,256]{2,1,0:T(8,128)S(1)} %get-tuple-element.41.second), custom_call_target="tpu_custom_call" | custom-call | tf_op jit(solution)/shard_map/final/pallas_call | solution.py:553
  (23 shorter events, 0.1 us)
Async XLA Ops:
  0.6 22.4 %copy-start = (bf16[8,16,32,256]{3,2,1,0:T(8,128)(2,1)S(1)}, bf16[8,16,32,256]{3,2,1,0:T(8,128)(2,1)}, u32[]{:S(2)}) copy-start(bf16[8,16,32,256]{3,2,1,0:T(8,128)(2,1)} %own.5) | copy-start | bytes 6291460
  0.6 22.0 %copy-start.6 = (f32[32]{0:T(128)S(1)}, f32[32]{0:T(128)}, u32[]{:S(2)}) copy-start(f32[32]{0:T(128)} %param.9) | copy-start | bytes 388
  0.7 21.9 %copy-start.5 = (bf16[27,32,32]{2,1,0:T(8,128)(2,1)S(1)}, bf16[27,32,32]{2,1,0:T(8,128)(2,1)}, u32[]{:S(2)}) copy-start(bf16[27,32,32]{2,1,0:T(8,128)(2,1)} %taps.1) | copy-start | bytes 165892
  3.6 24.0 %collective-permute-start.2 = (bf16[35,32,256]{2,1,0:T(8,128)(2,1)}, bf16[35,32,256]{2,1,0:T(8,128)(2,1)S(1)}, u32[]{:S(2)}, u32[]{:S(2)}) collective-permute-start(bf16[35,32,256]{2,1,0:T(8,128)(2,1)} %get-tuple-element.27), channel_id=1, source_target_pairs={{0,8},{8,16},{16,24},{24,32},{32,40},{40,48},{48,56},{56,64},{64,7... | collective-permute-start | bytes 1720328 | tf_op jit(solution)/shard_map/ppermute | solution.py:14
  5.7 21.9 %collective-permute-start.3 = (bf16[35,32,256]{2,1,0:T(8,128)(2,1)}, bf16[35,32,256]{2,1,0:T(8,128)(2,1)S(1)}, u32[]{:S(2)}, u32[]{:S(2)}) collective-permute-start(bf16[35,32,256]{2,1,0:T(8,128)(2,1)} %get-tuple-element.28), channel_id=1, source_target_pairs={{0,120},{8,0},{16,8},{24,16},{32,24},{40,32},{48,40},{56,48},{64,5... | collective-permute-start | bytes 1720328 | tf_op jit(solution)/shard_map/ppermute | solution.py:14
  10.5 4.6 %collective-permute-start = (bf16[9,32,256]{2,1,0:T(8,128)(2,1)}, bf16[9,32,256]{2,1,0:T(8,128)(2,1)S(1)}, u32[]{:S(2)}, u32[]{:S(2)}) collective-permute-start(bf16[9,32,256]{2,1,0:T(8,128)(2,1)} %get-tuple-element.22), channel_id=1, source_target_pairs={{0,1},{1,2},{2,3},{3,4},{4,5},{5,6},{6,7},{7,0},{8,9},{9,10},{10,1... | collective-permute-start | bytes 442376 | tf_op jit(solution)/shard_map/ppermute | solution.py:14
  12.6 5.1 %collective-permute-start.1 = (bf16[9,32,256]{2,1,0:T(8,128)(2,1)}, bf16[9,32,256]{2,1,0:T(8,128)(2,1)S(1)}, u32[]{:S(2)}, u32[]{:S(2)}) collective-permute-start(bf16[9,32,256]{2,1,0:T(8,128)(2,1)} %get-tuple-element.23), channel_id=1, source_target_pairs={{0,7},{1,0},{2,1},{3,2},{4,3},{5,4},{6,5},{7,6},{8,15},{9,8},{10,9... | collective-permute-start | bytes 442376 | tf_op jit(solution)/shard_map/ppermute | solution.py:14
  17.7 9.8 %collective-permute-start.4 = (bf16[5,32,256]{2,1,0:T(8,128)(2,1)S(1)}, bf16[5,32,256]{2,1,0:T(8,128)(2,1)S(1)}, u32[]{:S(2)}, u32[]{:S(2)}) collective-permute-start(bf16[5,32,256]{2,1,0:T(8,128)(2,1)S(1)} %get-tuple-element.29), channel_id=1, source_target_pairs={{0,8},{8,16},{16,24},{24,32},{32,40},{40,48},{48,56},{56,64},{64,7... | collective-permute-start | bytes 245768 | tf_op jit(solution)/shard_map/ppermute | solution.py:14
  17.8 9.7 %collective-permute-start.5 = (bf16[5,32,256]{2,1,0:T(8,128)(2,1)S(1)}, bf16[5,32,256]{2,1,0:T(8,128)(2,1)S(1)}, u32[]{:S(2)}, u32[]{:S(2)}) collective-permute-start(bf16[5,32,256]{2,1,0:T(8,128)(2,1)S(1)} %get-tuple-element.30), channel_id=1, source_target_pairs={{0,120},{8,0},{16,8},{24,16},{32,24},{40,32},{48,40},{56,48},{64,5... | collective-permute-start | bytes 245768 | tf_op jit(solution)/shard_map/ppermute | solution.py:14
  23.0 0.9 %copy-start.3 = (f32[8,16,256]{2,1,0:T(8,128)S(1)}, f32[8,16,256]{2,1,0:T(8,128)}, u32[]{:S(2)}) copy-start(f32[8,16,256]{2,1,0:T(8,128)} %get-tuple-element.24.mask) | copy-start | bytes 393220
  23.9 3.6 %copy-start.4 = (f32[8,16,256]{2,1,0:T(8,128)S(1)}, f32[8,16,256]{2,1,0:T(8,128)}, u32[]{:S(2)}) copy-start(f32[8,16,256]{2,1,0:T(8,128)} %get-tuple-element.24.mask) | copy-start | bytes 393220
  27.5 2.5 %copy-start.1 = (f32[8,16,256]{2,1,0:T(8,128)S(1)}, f32[8,16,256]{2,1,0:T(8,128)}, u32[]{:S(2)}) copy-start(f32[8,16,256]{2,1,0:T(8,128)} %get-tuple-element.34.start) | copy-start | bytes 393220
  27.5 2.5 %copy-start.2 = (f32[8,16,256]{2,1,0:T(8,128)S(1)}, f32[8,16,256]{2,1,0:T(8,128)}, u32[]{:S(2)}) copy-start(f32[8,16,256]{2,1,0:T(8,128)} %ridge.3) | copy-start | bytes 393220
  29.5 4.0 %collective-permute-start.6 = (bf16[10,32,256]{2,1,0:T(8,128)(2,1)S(1)}, bf16[10,32,256]{2,1,0:T(8,128)(2,1)S(1)}, u32[]{:S(2)}, u32[]{:S(2)}) collective-permute-start(bf16[10,32,256]{2,1,0:T(8,128)(2,1)S(1)} %get-tuple-element.32), channel_id=1, source_target_pairs={{0,1},{1,2},{2,3},{3,4},{4,5},{5,6},{6,7},{7,0},{8,9},{9,10},{10,1... | collective-permute-start | bytes 491528 | tf_op jit(solution)/shard_map/ppermute | solution.py:14
  29.8 5.0 %collective-permute-start.7 = (bf16[10,32,256]{2,1,0:T(8,128)(2,1)S(1)}, bf16[10,32,256]{2,1,0:T(8,128)(2,1)S(1)}, u32[]{:S(2)}, u32[]{:S(2)}) collective-permute-start(bf16[10,32,256]{2,1,0:T(8,128)(2,1)S(1)} %get-tuple-element.33), channel_id=1, source_target_pairs={{0,7},{1,0},{2,1},{3,2},{4,3},{5,4},{6,5},{7,6},{8,15},{9,8},{10,9... | collective-permute-start | bytes 491528 | tf_op jit(solution)/shard_map/ppermute | solution.py:14
  35.2 2.1 %collective-permute-start.8 = (f32[8,256]{1,0:T(8,128)S(1)}, f32[8,256]{1,0:T(8,128)S(1)}, u32[]{:S(2)}, u32[]{:S(2)}) collective-permute-start(f32[8,256]{1,0:T(8,128)S(1)} %get-tuple-element.36), channel_id=1, source_target_pairs={{0,1},{1,2},{2,3},{3,4},{4,5},{5,6},{6,7},{7,0},{8,9},{9,10},{10,1... | collective-permute-start | bytes 24584 | tf_op jit(solution)/shard_map/ppermute | solution.py:14
  35.4 3.1 %collective-permute-start.9 = (f32[8,256]{1,0:T(8,128)S(1)}, f32[8,256]{1,0:T(8,128)S(1)}, u32[]{:S(2)}, u32[]{:S(2)}) collective-permute-start(f32[8,256]{1,0:T(8,128)S(1)} %get-tuple-element.37), channel_id=1, source_target_pairs={{0,7},{1,0},{2,1},{3,2},{4,3},{5,4},{6,5},{7,6},{8,15},{9,8},{10,9... | collective-permute-start | bytes 24584 | tf_op jit(solution)/shard_map/ppermute | solution.py:14
  38.5 8.6 %collective-permute-start.10 = (f32[18,256]{1,0:T(8,128)S(1)}, f32[18,256]{1,0:T(8,128)S(1)}, u32[]{:S(2)}, u32[]{:S(2)}) collective-permute-start(f32[18,256]{1,0:T(8,128)S(1)} %pad_maximum_fusion), channel_id=1, source_target_pairs={{0,8},{8,16},{16,24},{24,32},{32,40},{40,48},{48,56},{56,64},{64,7... | collective-permute-start | bytes 55304 | tf_op jit(solution)/shard_map/ppermute | solution.py:14
  38.6 8.5 %collective-permute-start.11 = (f32[18,256]{1,0:T(8,128)S(1)}, f32[18,256]{1,0:T(8,128)S(1)}, u32[]{:S(2)}, u32[]{:S(2)}) collective-permute-start(f32[18,256]{1,0:T(8,128)S(1)} %pad_maximum_fusion.1), channel_id=1, source_target_pairs={{0,120},{8,0},{16,8},{24,16},{32,24},{40,32},{48,40},{56,48},{64,5... | collective-permute-start | bytes 55304 | tf_op jit(solution)/shard_map/ppermute | solution.py:14

commit v9 on v8

--- a/solution.py
+++ b/solution.py
@@ -26,6 +26,7 @@
     ids_in,
     occupancy_in,
     target_in,
+    ridge_in,
     mask,
     start,
     y_hi,
@@ -35,6 +36,7 @@
     ids,
     occupancy,
     target,
+    ridge,
     columns,
     present,
     sems,
@@ -54,6 +56,7 @@
                 (own.at[rows - 1], x_hi.at[cols : 2 * cols]),
                 (own.at[0], x_lo.at[0:cols]),
                 (own.at[1], x_lo.at[cols : 2 * cols]),
+                (ridge_in, ridge),
             )
         )
     ]
@@ -72,18 +75,20 @@
         start[x] = mask[x] * target[x]
     copies[3].wait()
     copies[4].wait()
-    for k, (out, y) in enumerate(((y_lo, 0), (y_hi, cols - 1))):
+    copies[9].wait()
+    blank = jnp.zeros((channels - 3 * rows, depth), jnp.float32)
+    for k, (out, y, far) in enumerate(((y_lo, 0, 1), (y_hi, cols - 1, cols - 2))):
         for x in range(rows):
             out[x] = columns[k, x, 0] * mask[x, y : y + 1, :].astype(jnp.bfloat16)
-        edge = jnp.concatenate([start[x, y : y + 1, :] for x in range(rows)], axis=0)
-        blank = jnp.zeros((channels - 3 * rows, depth), jnp.float32)
-        out[rows] = jnp.concatenate([*three(edge), blank], axis=0).astype(jnp.bfloat16)
+        for at, value in enumerate((column_of(start, y), column_of(start, far), column_of(ridge, y))):
+            terms = jnp.concatenate([*three(value), blank], axis=0)
+            out[rows + at] = terms.astype(jnp.bfloat16)
     for out, pair, row in ((x_hi, (rows - 2, rows - 1), rows - 1), (x_lo, (0, 1), 0)):
         out[2 * cols] = jnp.concatenate([mask[x] for x in pair], axis=0).astype(jnp.bfloat16)
         high, mid, low = three(start[row])
         out[2 * cols + 1] = jnp.concatenate([high, mid], axis=0).astype(jnp.bfloat16)
         out[2 * cols + 2] = jnp.concatenate([low, jnp.zeros_like(low)], axis=0).astype(jnp.bfloat16)
-    for copy in copies[5:]:
+    for copy in copies[5:9]:
         copy.wait()
 
 
@@ -182,21 +187,18 @@
 
 
 def sides_kernel(y_lo, y_hi, out_hi, out_lo):
-    rows = y_lo.shape[0] - 1
+    rows = y_lo.shape[0] - 3
     channels, depth = y_lo.shape[1:]
     clear = [splat(flag, y_lo.shape[1:]) for flag in mesh_flags()[:2]]
-    low_terms = y_lo[rows].astype(jnp.float32)
-    high_terms = y_hi[rows].astype(jnp.float32)
+    sources = [ref[rows + far].astype(jnp.float32) for far in range(2) for ref in (y_lo, y_hi)]
     for out, pair, row in ((out_hi, (rows - 2, rows - 1), rows - 1), (out_lo, (0, 1), 0)):
         for k, x in enumerate(pair):
             out[2 * k] = y_lo[x] * clear[0]
             out[2 * k + 1] = y_hi[x] * clear[1]
         rims = [
-            terms[at : at + 1]
-            for at in (row, rows + row, 2 * rows + row)
-            for terms in (low_terms, high_terms)
+            terms[at : at + 1] for at in (row, rows + row, 2 * rows + row) for terms in sources
         ]
-        blank = jnp.zeros((channels - 6, depth), jnp.float32)
+        blank = jnp.zeros((channels - 12, depth), jnp.float32)
         out[4] = jnp.concatenate([*rims, blank], axis=0).astype(jnp.bfloat16)
 
 
@@ -245,10 +247,11 @@
     ):
         for y in range(0, cols, 2):
             conv_block(grid, masks, wide, bias_all, lane, 4 * side, y, out, 2 * side)
-    for ref, y in ((out_hi, cols - 1), (out_lo, 0)):
-        for x in range(rows + 2):
-            at = field_at(inner, out, x)
-            ref[x] = at[0][at[1], y]
+    for ref, ys in ((out_hi, (cols - 1, cols - 2)), (out_lo, (0, 1))):
+        for far, y in enumerate(ys):
+            for x in range(rows + 2):
+                at = field_at(inner, out, x)
+                ref[far * (rows + 2) + x] = at[0][at[1], y]
 
 
 def two_sum(a, b):
@@ -380,28 +383,74 @@
     return jnp.concatenate([ref[x, y : y + 1, :] for x in range(ref.shape[0])], axis=0)
 
 
+def joined(terms, count, step):
+    return (terms[:count] + terms[step : step + count]) + terms[2 * step : 2 * step + count]
+
+
 def first_rim_kernel(
-    inner, edge, f_lo, f_hi, y_lo, y_hi, side_lo, side_hi, core, out, out_hi, out_lo
+    inner,
+    edge,
+    f_lo,
+    f_hi,
+    y_lo,
+    y_hi,
+    x_lo,
+    x_hi,
+    side_lo,
+    side_hi,
+    start,
+    core,
+    out,
+    w_lo,
+    w_hi,
+    out_hi,
+    out_lo,
 ):
     n, cols, channels, depth = inner.shape
     rows = n + 2
+    scale = 1.0 / (8 * channels)
     lane = lanes((channels, depth))
     out[...] = core[...]
-    ends = []
-    for side in (side_lo, side_hi):
-        terms = side[4].astype(jnp.float32)
-        ends.append((terms[0:2] + terms[2:4]) + terms[4:6])
-    for k, (ref, rim, flag, y, send) in enumerate(
-        zip((f_lo, f_hi), (y_lo, y_hi), mesh_flags(), (0, cols - 1), (out_lo, out_hi))
+    corners = [joined(side[4].astype(jnp.float32), 4, 4) for side in (side_lo, side_hi)]
+    for k, (ref, rim, keep, flag, y) in enumerate(
+        zip((f_lo, f_hi), (y_lo, y_hi), (w_lo, w_hi), mesh_flags(), (0, cols - 1))
     ):
-        terms = rim[rows].astype(jnp.float32)
-        values = (terms[:rows] + terms[rows : 2 * rows]) + terms[2 * rows : 3 * rows]
-        values = [ends[0][k : k + 1], *(values[x : x + 1] for x in range(rows)), ends[1][k : k + 1]]
-        g = [ref[x].astype(jnp.float32) * (value * flag) for x, value in enumerate(values)]
-        column = column_of(core, y) + rim_rows(g, inner, edge, y, lane, 1.0 / (8 * channels))
-        send[...] = column
+        near, far, ridge = (
+            joined(rim[rows + at].astype(jnp.float32), rows, rows) for at in range(3)
+        )
+        ends = []
+        for side in (x_lo, x_hi):
+            upper = side[2 * cols + 1].astype(jnp.float32)
+            lower = side[2 * cols + 2].astype(jnp.float32)
+            ends.append((upper[y : y + 1] + upper[cols + y : cols + y + 1]) + lower[y : y + 1])
+
+        def products(fields, values, low, high):
+            lines = [low, *(values[x : x + 1] for x in range(rows)), high]
+            return [field.astype(jnp.float32) * line for field, line in zip(fields, lines)]
+
+        beyond = [ref[x] for x in range(rows + 2)]
+        g = products(beyond, near * flag, corners[0][k : k + 1] * flag, corners[1][k : k + 1] * flag)
+        g_far = products(
+            [ref[rows + 2 + x] for x in range(rows + 2)],
+            far,
+            corners[0][2 + k : 3 + k],
+            corners[1][2 + k : 3 + k],
+        )
+        own = [field_at(inner, edge, x) for x in range(rows + 2)]
+        g_own = products([at[0][at[1], y] for at in own], column_of(start, y), ends[0], ends[1])
+        column = column_of(core, y) + rim_rows(g, inner, edge, y, lane, scale)
+        smooth = [(a + b) + (b + c) for a, b, c in zip(g_far, g, g_own)]
+        image = [
+            close_column((smooth[x] + smooth[x + 1]) + (smooth[x + 1] + smooth[x + 2]), lane, beyond[x + 1])
+            for x in range(rows)
+        ]
+        keep[...] = (ridge * near + jnp.concatenate(image, axis=0) * scale) * flag
         for x in range(rows):
             out[x, y : y + 1, :] = column[x : x + 1]
+    for ref, x in ((out_hi, rows - 1), (out_lo, 0)):
+        ref[0:1] = w_lo[x : x + 1]
+        ref[1 : 1 + cols] = out[x]
+        ref[1 + cols : 2 + cols] = w_hi[x : x + 1]
 
 
 PRODUCTS = ((0, 0), (0, 1), (1, 1), (0, 2), (1, 2))
@@ -562,25 +611,26 @@
 
     plane = ((rows, cols, depth), f32)
     blocks = block_ids.reshape(-1, block_ids.shape[3])
-    edge_column = ((rows + 1, channels, depth), bf16)
+    edge_column = ((rows + 3, channels, depth), bf16)
     edge_rows = ((2 * cols + 3, channels, depth), bf16)
     outs = [plane, plane, edge_column, edge_column, edge_rows, edge_rows]
     weight_mask, residual, y_hi, y_lo, x_hi, x_lo = pl.pallas_call(
         prep_kernel,
         out_shape=[jax.ShapeDtypeStruct(shape, dtype) for shape, dtype in outs],
-        in_specs=[pl.BlockSpec(memory_space=pl.ANY)] * 4,
+        in_specs=[pl.BlockSpec(memory_space=pl.ANY)] * 5,
         out_specs=[vmem for _ in outs],
         scratch_shapes=[
             pltpu.VMEM(blocks.shape, jnp.int32),
             pltpu.VMEM(occupancy.shape, jnp.int32),
             pltpu.VMEM(target.shape, f32),
+            pltpu.VMEM(ridge.shape, f32),
             pltpu.VMEM((2, rows, 1, channels, depth), bf16),
             pltpu.VMEM((blocks.shape[0], depth // block_ids.shape[2]), f32),
-            pltpu.SemaphoreType.DMA((9,)),
+            pltpu.SemaphoreType.DMA((10,)),
         ],
         compiler_params=pltpu.CompilerParams(vmem_limit_bytes=PREP_LIMIT << 20),
         name="prep",
-    )(features, blocks, occupancy, target)
+    )(features, blocks, occupancy, target, ridge)
     y_lo, y_hi = (shift(y_hi, "sy", 1), shift(y_lo, "sy", -1))
     x_lo, x_hi = (shift(x_hi, "sx", 1), shift(x_lo, "sx", -1))
     wide, bias = call(
@@ -612,7 +662,7 @@
         12,
         "conv_inner",
     )
-    column = ((rows + 2, channels, depth), bf16)
+    column = ((2 * (rows + 2), channels, depth), bf16)
     edge, f_hi, f_lo = call(
         conv_edge_kernel,
         (features, y_lo, y_hi, x_lo, x_hi, side_lo, side_hi, weight_mask, wide, bias, inner),
@@ -631,17 +681,16 @@
         "first_core",
     )
     line = ((rows, depth), f32)
-    first, w_hi, w_lo = call(
+    row = ((cols + 2, depth), f32)
+    first, w_lo, w_hi, r_hi, r_lo = call(
         first_rim_kernel,
-        (inner, edge, f_lo, f_hi, y_lo, y_hi, side_lo, side_hi, core),
-        [plane, line, line],
+        (inner, edge, f_lo, f_hi, y_lo, y_hi, x_lo, x_hi, side_lo, side_hi, residual, core),
+        [plane, line, line, row, row],
         [],
         4,
         "first_rim",
     )
-    w_lo, w_hi = (shift(w_hi, "sy", 1), shift(w_lo, "sy", -1))
-    rims = [jnp.concatenate([w_lo[x : x + 1], first[x], w_hi[x : x + 1]]) for x in (rows - 1, 0)]
-    r_lo, r_hi = (shift(rims[0], "sx", 1), shift(rims[1], "sx", -1))
+    r_lo, r_hi = (shift(r_hi, "sx", 1), shift(r_lo, "sx", -1))
     core, grams = call(
         second_core_kernel,
         (inner, edge, residual, first, ridge),

time: 67.4 us -> 65.2 us (0.967)
  starting transfers between devices: 20.9 us -> 19.3 us
  blocking collectives: 17.6 us -> 16.3 us
    ppermute x12 -> x10, starting transfers between devices: 20.9 us -> 19.3 us  [shift(): lax.ppermute(value, axis, [(i, (i + step) % peers) for i in range(peers)])]
    all_to_all x1, blocking collectives: 17.6 us -> 16.3 us  [per_device(): lax.all_to_all(jnp.broadcast_to(share[None], (peers, 1, 128)), AXES, 0, 0)]
    ppermute x12 -> x10, waiting for transfers between devices: 8.2 us -> 8.52 us  [shift(): lax.ppermute(value, axis, [(i, (i + step) % peers) for i in range(peers)])]
  transfers between devices with their start and end apart: 12 -> 10, of which waited for: 5 -> 4; matrix products, arithmetic and copies ran while one was open for 0% -> 0% of each run, Pallas kernels for 16% -> 17%
where the time goes in v9:
time: 65.2 us; the launch traced here: 65.1 us
  starting transfers between devices  19.3 us (30%)
  Pallas kernels  19.2 us (29%)
  blocking collectives  16.3 us (25%)
  waiting for transfers between devices  8.52 us (13%)
  local copies, waits for them, and re-layouts  0.97 us (1%)
  between operations  0.83 us (1%)
    ppermute x10, starting transfers between devices, shift(): lax.ppermute(value, axis, [(i, (i + step) % peers) for i in range(peers)])  19.3 us
    all_to_all x1, blocking collectives, per_device(): lax.all_to_all(jnp.broadcast_to(share[None], (peers, 1, 128)), AXES, 0, 0)  16.3 us
    pallas_call x9, Pallas kernels, call(): pl.pallas_call(kernel, out_shape=[jax.ShapeDtypeStruct(shape, dtype) for...  16.2 us
    ppermute x10, waiting for transfers between devices, shift(): lax.ppermute(value, axis, [(i, (i + step) % peers) for i in range(peers)])  8.52 us
    pallas_call x1, Pallas kernels, per_device(): pl.pallas_call(prep_kernel, out_shape=[jax.ShapeDtypeStruct(shape, dtype)...  3.05 us
  transfers between devices with their start and end apart: 10, of which 4 were waited for; matrix products, arithmetic and copies ran while one was open for 0% of the time, Pallas kernels for 17%

profile of v9, /device:TPU:1, one launch (start us, length us, event | category | flops | bytes accessed | tf_op | source)
XLA Modules:
  0.0 65.1 jit_solution(12442916445622190625)
XLA Ops:
  0.7 3.0 %prep.1 = (f32[8,16,256]{2,1,0:T(8,128)}, f32[8,16,256]{2,1,0:T(8,128)}, bf16[11,32,256]{2,1,0:T(8,128)(2,1)}, bf16[11,32,256]{2,1,0:T(8,128)(2,1)}, bf16[35,32,...) custom-call(bf16[8,16,32,256]{3,2,1,0:T(8,128)(2,1)} %own.5, s32[256,27]{1,0:T(8,128)} %bitcast.7, ...), custom_call_target="tpu_custom_call" | custom-call | tf_op jit(solution)/shard_map/prep/pallas_call | solution.py:617
  3.7 2.1 %collective-permute-start.2 = (bf16[35,32,256]{2,1,0:T(8,128)(2,1)}, bf16[35,32,256]{2,1,0:T(8,128)(2,1)S(1)}, u32[]{:S(2)}, u32[]{:S(2)}) collective-permute-start(bf16[35,32,256]{2,1,0:T(8,128)(2,1)} %get-tuple-element.29), channel_id=1, source_target_pairs={{0,8},{8,16},{16,24},{24,32},{32,40},{40,48},{48,56},{56,64},{64,7... | collective-permute-start | bytes 1720328 | tf_op jit(solution)/shard_map/ppermute | solution.py:14
  5.8 4.8 %collective-permute-start.3 = (bf16[35,32,256]{2,1,0:T(8,128)(2,1)}, bf16[35,32,256]{2,1,0:T(8,128)(2,1)S(1)}, u32[]{:S(2)}, u32[]{:S(2)}) collective-permute-start(bf16[35,32,256]{2,1,0:T(8,128)(2,1)} %get-tuple-element.30), channel_id=1, source_target_pairs={{0,120},{8,0},{16,8},{24,16},{32,24},{40,32},{48,40},{56,48},{64,5... | collective-permute-start | bytes 1720328 | tf_op jit(solution)/shard_map/ppermute | solution.py:14
  10.6 2.1 %collective-permute-start = (bf16[11,32,256]{2,1,0:T(8,128)(2,1)}, bf16[11,32,256]{2,1,0:T(8,128)(2,1)S(1)}, u32[]{:S(2)}, u32[]{:S(2)}) collective-permute-start(bf16[11,32,256]{2,1,0:T(8,128)(2,1)} %get-tuple-element.24), channel_id=1, source_target_pairs={{0,1},{1,2},{2,3},{3,4},{4,5},{5,6},{6,7},{7,0},{8,9},{9,10},{10,1... | collective-permute-start | bytes 540680 | tf_op jit(solution)/shard_map/ppermute | solution.py:14
  12.8 0.0 collective-permute-start.1
  12.8 2.8 %collective-permute-done.y_lo = bf16[11,32,256]{2,1,0:T(8,128)(2,1)S(1)} collective-permute-done((bf16[11,32,256]{2,1,0:T(8,128)(2,1)}, bf16[11,32,256]{2,1,0:T(8,128)(2,1)S(1)}, u32[]{:S(2)}, u32[]{:S(2)}) %collective-permute-start) | collective-permute-done | bytes 180256 | tf_op jit(solution)/shard_map/ppermute | solution.py:14
  15.5 2.7 %collective-permute-done.1.y_hi = bf16[11,32,256]{2,1,0:T(8,128)(2,1)S(1)} collective-permute-done((bf16[11,32,256]{2,1,0:T(8,128)(2,1)}, bf16[11,32,256]{2,1,0:T(8,128)(2,1)S(1)}, u32[]{:S(2)}, u32[]{:S(2)}) %collective-permute-start.1) | collective-permute-done | bytes 180256 | tf_op jit(solution)/shard_map/ppermute | solution.py:14
  18.2 0.1 collective-permute-start.4
  18.3 4.8 %collective-permute-start.5 = (bf16[5,32,256]{2,1,0:T(8,128)(2,1)S(1)}, bf16[5,32,256]{2,1,0:T(8,128)(2,1)S(1)}, u32[]{:S(2)}, u32[]{:S(2)}) collective-permute-start(bf16[5,32,256]{2,1,0:T(8,128)(2,1)S(1)} %get-tuple-element.32), channel_id=1, source_target_pairs={{0,120},{8,0},{16,8},{24,16},{32,24},{40,32},{48,40},{56,48},{64,5... | collective-permute-start | bytes 245768 | tf_op jit(solution)/shard_map/ppermute | solution.py:14
  23.1 0.4 weights.1
  23.5 0.0 copy-start.3
  23.6 0.9 %copy-done.3 = f32[8,16,256]{2,1,0:T(8,128)S(1)} copy-done((f32[8,16,256]{2,1,0:T(8,128)S(1)}, f32[8,16,256]{2,1,0:T(8,128)}, u32[]{:S(2)}) %copy-start.3) | copy-done | bytes 131096
  24.5 3.5 %conv_inner.1.inner = bf16[6,16,32,256]{3,2,1,0:T(8,128)(2,1)S(1)} custom-call(bf16[8,16,32,256]{3,2,1,0:T(8,128)(2,1)S(1)} %copy-done, bf16[11,32,256]{2,1,0:T(8,128)(2,1)S(1)} %collective-permute-done.y_lo, bf16[11,32,256]{2,1,0:T(8,128)(2,1)S(1)} %collective-permute-done.1.y_hi, f32[8,16,256]{2,1,0:T(8,128)S(1)} %copy-done.3, ...), custom_call_target="tpu_custom_call" | custom-call | tf_op jit(solution)/shard_map/conv_inner/pallas_call | solution.py:602
  28.0 0.0 copy-start.1
  28.0 0.0 copy-start.2
  28.0 0.0 collective-permute-done.4.side_lo
  28.0 0.0 collective-permute-done.5.side_hi
  28.0 0.0 collective-permute-done.2.x_lo
  28.1 1.9 %conv_edge.1 = (bf16[4,16,32,256]{3,2,1,0:T(8,128)(2,1)S(1)}, bf16[20,32,256]{2,1,0:T(8,128)(2,1)S(1)}, bf16[20,32,256]{2,1,0:T(8,128)(2,1)S(1)}) custom-call(bf16[8,16,32,256]{3,2,1,0:T(8,128)(2,1)S(1)} %copy-done, bf16[11,32,256]{2,1,0:T(8,128)(2,1)S(1)} %collective-permute-done.y_lo, bf16[11,32,256]{2,1,0:T(8,128)(2,1)S(1)} %collective-permute-done.1.y_hi, ...), custom_call_target="tpu_custom_call" | custom-call | tf_op jit(solution)/shard_map/conv_edge/pallas_call | solution.py:602
  30.0 0.3 collective-permute-start.6
  30.3 0.2 collective-permute-start.7
  30.6 3.5 %first_core.1.core = f32[8,16,256]{2,1,0:T(8,128)S(1)} custom-call(bf16[6,16,32,256]{3,2,1,0:T(8,128)(2,1)S(1)} %conv_inner.1.inner, bf16[4,16,32,256]{3,2,1,0:T(8,128)(2,1)S(1)} %get-tuple-element.33.edge, f32[8,16,256]{2,1,0:T(8,128)S(1)} %copy-done.1, bf16[35,32,256]{2,1,0:T(8,128)(2,1)S(1)} %collective-permute-done.2.x_lo, ...), custom_call_target="tpu_custom_call" | custom-call | tf_op jit(solution)/shard_map/first_core/pallas_call | solution.py:602
  34.0 0.3 collective-permute-done.6.f_lo
  34.3 2.8 %collective-permute-done.7.f_hi = bf16[20,32,256]{2,1,0:T(8,128)(2,1)S(1)} collective-permute-done((bf16[20,32,256]{2,1,0:T(8,128)(2,1)S(1)}, bf16[20,32,256]{2,1,0:T(8,128)(2,1)S(1)}, u32[]{:S(2)}, u32[]{:S(2)}) %collective-permute-start.7) | collective-permute-done | bytes 327712 | tf_op jit(solution)/shard_map/ppermute | solution.py:14
  37.1 0.8 %first_rim.1 = (f32[8,16,256]{2,1,0:T(8,128)S(1)}, f32[8,256]{1,0:T(8,128)S(1)}, f32[8,256]{1,0:T(8,128)S(1)}, f32[18,256]{1,0:T(8,128)S(1)}, f32[18,256]{1,0:T(8,128)S(1)}) custom-call(bf16[6,16,32,256]{3,2,1,0:T(8,128)(2,1)S(1)} %conv_inner.1.inner, bf16[4,16,32,256]{3,2,1,0:T(8,128)(2,1)S(1)} %get-tuple-element.33.edge, ...), custom_call_target="tpu_custom_call" | custom-call | tf_op jit(solution)/shard_map/first_rim/pallas_call | solution.py:602
  37.9 0.1 collective-permute-start.8
  37.9 4.8 %collective-permute-start.9 = (f32[18,256]{1,0:T(8,128)S(1)}, f32[18,256]{1,0:T(8,128)S(1)}, u32[]{:S(2)}, u32[]{:S(2)}) collective-permute-start(f32[18,256]{1,0:T(8,128)S(1)} %get-tuple-element.41), channel_id=1, source_target_pairs={{0,120},{8,0},{16,8},{24,16},{32,24},{40,32},{48,40},{56,48},{64,5... | collective-permute-start | bytes 55304 | tf_op jit(solution)/shard_map/ppermute | solution.py:14
  42.7 3.6 %second_core.1 = (f32[8,16,256]{2,1,0:T(8,128)S(1)}, f32[10,16,256]{2,1,0:T(8,128)S(1)}) custom-call(bf16[6,16,32,256]{3,2,1,0:T(8,128)(2,1)S(1)} %conv_inner.1.inner, bf16[4,16,32,256]{3,2,1,0:T(8,128)(2,1)S(1)} %get-tuple-element.33.edge, f32[8,16,256]{2,1,0:T(8,128)S(1)} %copy-done.1, f32[8,16,256]{2,1,0:T(8,128)S(1)} %get-tuple-element.37.first, ...), custom_call_target="tpu_custom_call" | custom-call | tf_op jit(solution)/shard_map/second_core/pallas_call | solution.py:602
  46.3 0.0 collective-permute-done.9.x_hi
  46.3 1.5 %second_rim.1 = (f32[8,16,256]{2,1,0:T(8,128)S(1)}, f32[1,128]{1,0:T(1,128)S(1)}) custom-call(bf16[6,16,32,256]{3,2,1,0:T(8,128)(2,1)S(1)} %conv_inner.1.inner, bf16[4,16,32,256]{3,2,1,0:T(8,128)(2,1)S(1)} %get-tuple-element.33.edge, bf16[20,32,256]{2,1,0:T(8,128)(2,1)S(1)} %collective-permute-done.6.f_lo, ...), custom_call_target="tpu_custom_call" | custom-call | tf_op jit(solution)/shard_map/second_rim/pallas_call | solution.py:602
  47.9 16.3 %all_to_all.5 = f32[128,1,128]{2,1,0:T(1,128)S(1)} all-to-all(f32[128,1,128]{2,1,0:T(1,128)S(1)} %broadcast_in_dim.13), channel_id=1, replica_groups=mesh['sx'=16,'sy'=8] {'sx','sy'}, dimensions={0} | all-to-all | bytes 131072 | tf_op jit(solution)/shard_map/all_to_all | solution.py:712
  64.2 0.9 %final.1 = (f32[8,16,256]{2,1,0:T(8,128)}, f32[8,16,256]{2,1,0:T(8,128)}) custom-call(f32[128,128]{1,0:T(8,128)S(1)} %bitcast.4, f32[8,16,256]{2,1,0:T(8,128)S(1)} %copy-done.1, f32[8,16,256]{2,1,0:T(8,128)S(1)} %get-tuple-element.37.first, f32[8,16,256]{2,1,0:T(8,128)S(1)} %get-tuple-element.45.second), custom_call_target="tpu_custom_call" | custom-call | tf_op jit(solution)/shard_map/final/pallas_call | solution.py:602
  (14 shorter events, 0.1 us)
Async XLA Ops:
  0.6 22.9 %copy-start = (bf16[8,16,32,256]{3,2,1,0:T(8,128)(2,1)S(1)}, bf16[8,16,32,256]{3,2,1,0:T(8,128)(2,1)}, u32[]{:S(2)}) copy-start(bf16[8,16,32,256]{3,2,1,0:T(8,128)(2,1)} %own.5) | copy-start | bytes 6291460
  0.6 22.5 %copy-start.6 = (f32[32]{0:T(128)S(1)}, f32[32]{0:T(128)}, u32[]{:S(2)}) copy-start(f32[32]{0:T(128)} %param.9) | copy-start | bytes 388
  0.7 22.4 %copy-start.5 = (bf16[27,32,32]{2,1,0:T(8,128)(2,1)S(1)}, bf16[27,32,32]{2,1,0:T(8,128)(2,1)}, u32[]{:S(2)}) copy-start(bf16[27,32,32]{2,1,0:T(8,128)(2,1)} %taps.1) | copy-start | bytes 165892
  3.7 24.3 %collective-permute-start.2 = (bf16[35,32,256]{2,1,0:T(8,128)(2,1)}, bf16[35,32,256]{2,1,0:T(8,128)(2,1)S(1)}, u32[]{:S(2)}, u32[]{:S(2)}) collective-permute-start(bf16[35,32,256]{2,1,0:T(8,128)(2,1)} %get-tuple-element.29), channel_id=1, source_target_pairs={{0,8},{8,16},{16,24},{24,32},{32,40},{40,48},{48,56},{56,64},{64,7... | collective-permute-start | bytes 1720328 | tf_op jit(solution)/shard_map/ppermute | solution.py:14
  5.8 22.2 %collective-permute-start.3 = (bf16[35,32,256]{2,1,0:T(8,128)(2,1)}, bf16[35,32,256]{2,1,0:T(8,128)(2,1)S(1)}, u32[]{:S(2)}, u32[]{:S(2)}) collective-permute-start(bf16[35,32,256]{2,1,0:T(8,128)(2,1)} %get-tuple-element.30), channel_id=1, source_target_pairs={{0,120},{8,0},{16,8},{24,16},{32,24},{40,32},{48,40},{56,48},{64,5... | collective-permute-start | bytes 1720328 | tf_op jit(solution)/shard_map/ppermute | solution.py:14
  10.6 4.9 %collective-permute-start = (bf16[11,32,256]{2,1,0:T(8,128)(2,1)}, bf16[11,32,256]{2,1,0:T(8,128)(2,1)S(1)}, u32[]{:S(2)}, u32[]{:S(2)}) collective-permute-start(bf16[11,32,256]{2,1,0:T(8,128)(2,1)} %get-tuple-element.24), channel_id=1, source_target_pairs={{0,1},{1,2},{2,3},{3,4},{4,5},{5,6},{6,7},{7,0},{8,9},{9,10},{10,1... | collective-permute-start | bytes 540680 | tf_op jit(solution)/shard_map/ppermute | solution.py:14
  12.8 5.4 %collective-permute-start.1 = (bf16[11,32,256]{2,1,0:T(8,128)(2,1)}, bf16[11,32,256]{2,1,0:T(8,128)(2,1)S(1)}, u32[]{:S(2)}, u32[]{:S(2)}) collective-permute-start(bf16[11,32,256]{2,1,0:T(8,128)(2,1)} %get-tuple-element.25), channel_id=1, source_target_pairs={{0,7},{1,0},{2,1},{3,2},{4,3},{5,4},{6,5},{7,6},{8,15},{9,8},{10,9... | collective-permute-start | bytes 540680 | tf_op jit(solution)/shard_map/ppermute | solution.py:14
  18.2 9.8 %collective-permute-start.4 = (bf16[5,32,256]{2,1,0:T(8,128)(2,1)S(1)}, bf16[5,32,256]{2,1,0:T(8,128)(2,1)S(1)}, u32[]{:S(2)}, u32[]{:S(2)}) collective-permute-start(bf16[5,32,256]{2,1,0:T(8,128)(2,1)S(1)} %get-tuple-element.31), channel_id=1, source_target_pairs={{0,8},{8,16},{16,24},{24,32},{32,40},{40,48},{48,56},{56,64},{64,7... | collective-permute-start | bytes 245768 | tf_op jit(solution)/shard_map/ppermute | solution.py:14
  18.3 9.7 %collective-permute-start.5 = (bf16[5,32,256]{2,1,0:T(8,128)(2,1)S(1)}, bf16[5,32,256]{2,1,0:T(8,128)(2,1)S(1)}, u32[]{:S(2)}, u32[]{:S(2)}) collective-permute-start(bf16[5,32,256]{2,1,0:T(8,128)(2,1)S(1)} %get-tuple-element.32), channel_id=1, source_target_pairs={{0,120},{8,0},{16,8},{24,16},{32,24},{40,32},{48,40},{56,48},{64,5... | collective-permute-start | bytes 245768 | tf_op jit(solution)/shard_map/ppermute | solution.py:14
  23.5 0.9 %copy-start.3 = (f32[8,16,256]{2,1,0:T(8,128)S(1)}, f32[8,16,256]{2,1,0:T(8,128)}, u32[]{:S(2)}) copy-start(f32[8,16,256]{2,1,0:T(8,128)} %get-tuple-element.26.mask) | copy-start | bytes 393220
  24.5 3.6 %copy-start.4 = (f32[8,16,256]{2,1,0:T(8,128)S(1)}, f32[8,16,256]{2,1,0:T(8,128)}, u32[]{:S(2)}) copy-start(f32[8,16,256]{2,1,0:T(8,128)} %get-tuple-element.26.mask) | copy-start | bytes 393220
  28.0 2.6 %copy-start.1 = (f32[8,16,256]{2,1,0:T(8,128)S(1)}, f32[8,16,256]{2,1,0:T(8,128)}, u32[]{:S(2)}) copy-start(f32[8,16,256]{2,1,0:T(8,128)} %get-tuple-element.36.start) | copy-start | bytes 393220
  28.0 2.5 %copy-start.2 = (f32[8,16,256]{2,1,0:T(8,128)S(1)}, f32[8,16,256]{2,1,0:T(8,128)}, u32[]{:S(2)}) copy-start(f32[8,16,256]{2,1,0:T(8,128)} %ridge.3) | copy-start | bytes 393220
  30.0 4.3 %collective-permute-start.6 = (bf16[20,32,256]{2,1,0:T(8,128)(2,1)S(1)}, bf16[20,32,256]{2,1,0:T(8,128)(2,1)S(1)}, u32[]{:S(2)}, u32[]{:S(2)}) collective-permute-start(bf16[20,32,256]{2,1,0:T(8,128)(2,1)S(1)} %get-tuple-element.34), channel_id=1, source_target_pairs={{0,1},{1,2},{2,3},{3,4},{4,5},{5,6},{6,7},{7,0},{8,9},{9,10},{10,1... | collective-permute-start | bytes 983048 | tf_op jit(solution)/shard_map/ppermute | solution.py:14
  30.3 6.8 %collective-permute-start.7 = (bf16[20,32,256]{2,1,0:T(8,128)(2,1)S(1)}, bf16[20,32,256]{2,1,0:T(8,128)(2,1)S(1)}, u32[]{:S(2)}, u32[]{:S(2)}) collective-permute-start(bf16[20,32,256]{2,1,0:T(8,128)(2,1)S(1)} %get-tuple-element.35), channel_id=1, source_target_pairs={{0,7},{1,0},{2,1},{3,2},{4,3},{5,4},{6,5},{7,6},{8,15},{9,8},{10,9... | collective-permute-start | bytes 983048 | tf_op jit(solution)/shard_map/ppermute | solution.py:14
  37.9 8.5 %collective-permute-start.8 = (f32[18,256]{1,0:T(8,128)S(1)}, f32[18,256]{1,0:T(8,128)S(1)}, u32[]{:S(2)}, u32[]{:S(2)}) collective-permute-start(f32[18,256]{1,0:T(8,128)S(1)} %get-tuple-element.40), channel_id=1, source_target_pairs={{0,8},{8,16},{16,24},{24,32},{32,40},{40,48},{48,56},{56,64},{64,7... | collective-permute-start | bytes 55304 | tf_op jit(solution)/shard_map/ppermute | solution.py:14
  37.9 8.4 %collective-permute-start.9 = (f32[18,256]{1,0:T(8,128)S(1)}, f32[18,256]{1,0:T(8,128)S(1)}, u32[]{:S(2)}, u32[]{:S(2)}) collective-permute-start(f32[18,256]{1,0:T(8,128)S(1)} %get-tuple-element.41), channel_id=1, source_target_pairs={{0,120},{8,0},{16,8},{24,16},{32,24},{40,32},{48,40},{56,48},{64,5... | collective-permute-start | bytes 55304 | tf_op jit(solution)/shard_map/ppermute | solution.py:14

commit v10 on v9

--- a/solution.py
+++ b/solution.py
@@ -26,7 +26,6 @@
     ids_in,
     occupancy_in,
     target_in,
-    ridge_in,
     mask,
     start,
     y_hi,
@@ -36,7 +35,6 @@
     ids,
     occupancy,
     target,
-    ridge,
     columns,
     present,
     sems,
@@ -56,7 +54,6 @@
                 (own.at[rows - 1], x_hi.at[cols : 2 * cols]),
                 (own.at[0], x_lo.at[0:cols]),
                 (own.at[1], x_lo.at[cols : 2 * cols]),
-                (ridge_in, ridge),
             )
         )
     ]
@@ -75,14 +72,12 @@
         start[x] = mask[x] * target[x]
     copies[3].wait()
     copies[4].wait()
-    copies[9].wait()
     blank = jnp.zeros((channels - 3 * rows, depth), jnp.float32)
-    for k, (out, y, far) in enumerate(((y_lo, 0, 1), (y_hi, cols - 1, cols - 2))):
+    for k, (out, y) in enumerate(((y_lo, 0), (y_hi, cols - 1))):
         for x in range(rows):
             out[x] = columns[k, x, 0] * mask[x, y : y + 1, :].astype(jnp.bfloat16)
-        for at, value in enumerate((column_of(start, y), column_of(start, far), column_of(ridge, y))):
-            terms = jnp.concatenate([*three(value), blank], axis=0)
-            out[rows + at] = terms.astype(jnp.bfloat16)
+        terms = jnp.concatenate([*three(column_of(start, y)), blank], axis=0)
+        out[rows] = terms.astype(jnp.bfloat16)
     for out, pair, row in ((x_hi, (rows - 2, rows - 1), rows - 1), (x_lo, (0, 1), 0)):
         out[2 * cols] = jnp.concatenate([mask[x] for x in pair], axis=0).astype(jnp.bfloat16)
         high, mid, low = three(start[row])
@@ -187,10 +182,10 @@
 
 
 def sides_kernel(y_lo, y_hi, out_hi, out_lo):
-    rows = y_lo.shape[0] - 3
+    rows = y_lo.shape[0] - 1
     channels, depth = y_lo.shape[1:]
     clear = [splat(flag, y_lo.shape[1:]) for flag in mesh_flags()[:2]]
-    sources = [ref[rows + far].astype(jnp.float32) for far in range(2) for ref in (y_lo, y_hi)]
+    sources = [ref[rows].astype(jnp.float32) for ref in (y_lo, y_hi)]
     for out, pair, row in ((out_hi, (rows - 2, rows - 1), rows - 1), (out_lo, (0, 1), 0)):
         for k, x in enumerate(pair):
             out[2 * k] = y_lo[x] * clear[0]
@@ -198,7 +193,7 @@
         rims = [
             terms[at : at + 1] for at in (row, rows + row, 2 * rows + row) for terms in sources
         ]
-        blank = jnp.zeros((channels - 12, depth), jnp.float32)
+        blank = jnp.zeros((channels - 6, depth), jnp.float32)
         out[4] = jnp.concatenate([*rims, blank], axis=0).astype(jnp.bfloat16)
 
 
@@ -214,6 +209,8 @@
     wide,
     bias,
     inner,
+    start,
+    ridge,
     out,
     out_hi,
     out_lo,
@@ -247,11 +244,22 @@
     ):
         for y in range(0, cols, 2):
             conv_block(grid, masks, wide, bias_all, lane, 4 * side, y, out, 2 * side)
-    for ref, ys in ((out_hi, (cols - 1, cols - 2)), (out_lo, (0, 1))):
-        for far, y in enumerate(ys):
-            for x in range(rows + 2):
-                at = field_at(inner, out, x)
-                ref[far * (rows + 2) + x] = at[0][at[1], y]
+    lane = lanes((channels, depth))
+    places = [field_at(inner, out, x) for x in range(rows + 2)]
+    blank = jnp.zeros((channels - 3 * rows, depth), jnp.float32)
+    for ref, y, beside in ((out_hi, cols - 1, cols - 2), (out_lo, 0, 1)):
+        smooth = []
+        for x, (field, at) in enumerate(places):
+            ref[x] = field[at, y]
+            near, next_in = (
+                field[at, k].astype(jnp.float32) * start_at(start, x_lo, x_hi, x, k)
+                for k in (y, beside)
+            )
+            smooth.append((near + near) + next_in)
+        image = column_of(ridge, y) * column_of(start, y) + rim_rows(
+            smooth, inner, out, y, lane, 1.0 / (8 * channels)
+        )
+        ref[rows + 2] = jnp.concatenate([*three(image), blank], axis=0).astype(jnp.bfloat16)
 
 
 def two_sum(a, b):
@@ -381,6 +389,16 @@
 
 def column_of(ref, y):
     return jnp.concatenate([ref[x, y : y + 1, :] for x in range(ref.shape[0])], axis=0)
+
+
+def start_at(start, x_lo, x_hi, x, y):
+    rows, cols = start.shape[:2]
+    if 0 < x <= rows:
+        return start[x - 1, y : y + 1, :]
+    side = x_lo if x == 0 else x_hi
+    upper = side[2 * cols + 1].astype(jnp.float32)
+    lower = side[2 * cols + 2].astype(jnp.float32)
+    return (upper[y : y + 1] + upper[cols + y : cols + y + 1]) + lower[y : y + 1]
 
 
 def joined(terms, count, step):
@@ -411,40 +429,25 @@
     scale = 1.0 / (8 * channels)
     lane = lanes((channels, depth))
     out[...] = core[...]
-    corners = [joined(side[4].astype(jnp.float32), 4, 4) for side in (side_lo, side_hi)]
+    corners = [joined(side[4].astype(jnp.float32), 2, 2) for side in (side_lo, side_hi)]
     for k, (ref, rim, keep, flag, y) in enumerate(
         zip((f_lo, f_hi), (y_lo, y_hi), (w_lo, w_hi), mesh_flags(), (0, cols - 1))
     ):
-        near, far, ridge = (
-            joined(rim[rows + at].astype(jnp.float32), rows, rows) for at in range(3)
-        )
-        ends = []
-        for side in (x_lo, x_hi):
-            upper = side[2 * cols + 1].astype(jnp.float32)
-            lower = side[2 * cols + 2].astype(jnp.float32)
-            ends.append((upper[y : y + 1] + upper[cols + y : cols + y + 1]) + lower[y : y + 1])
-
-        def products(fields, values, low, high):
-            lines = [low, *(values[x : x + 1] for x in range(rows)), high]
-            return [field.astype(jnp.float32) * line for field, line in zip(fields, lines)]
-
+        near = joined(rim[rows].astype(jnp.float32), rows, rows)
+        values = [corners[0][k : k + 1], *(near[x : x + 1] for x in range(rows)), corners[1][k : k + 1]]
         beyond = [ref[x] for x in range(rows + 2)]
-        g = products(beyond, near * flag, corners[0][k : k + 1] * flag, corners[1][k : k + 1] * flag)
-        g_far = products(
-            [ref[rows + 2 + x] for x in range(rows + 2)],
-            far,
-            corners[0][2 + k : 3 + k],
-            corners[1][2 + k : 3 + k],
-        )
-        own = [field_at(inner, edge, x) for x in range(rows + 2)]
-        g_own = products([at[0][at[1], y] for at in own], column_of(start, y), ends[0], ends[1])
+        g = [field.astype(jnp.float32) * (value * flag) for field, value in zip(beyond, values)]
         column = column_of(core, y) + rim_rows(g, inner, edge, y, lane, scale)
-        smooth = [(a + b) + (b + c) for a, b, c in zip(g_far, g, g_own)]
+        g = [
+            at[0][at[1], y].astype(jnp.float32) * start_at(start, x_lo, x_hi, x, y)
+            for x, at in enumerate(field_at(inner, edge, x) for x in range(rows + 2))
+        ]
         image = [
-            close_column((smooth[x] + smooth[x + 1]) + (smooth[x + 1] + smooth[x + 2]), lane, beyond[x + 1])
+            close_column((g[x] + g[x + 1]) + (g[x + 1] + g[x + 2]), lane, beyond[x + 1])
             for x in range(rows)
         ]
-        keep[...] = (ridge * near + jnp.concatenate(image, axis=0) * scale) * flag
+        theirs = joined(ref[rows + 2].astype(jnp.float32), rows, rows)
+        keep[...] = (theirs + jnp.concatenate(image, axis=0) * scale) * flag
         for x in range(rows):
             out[x, y : y + 1, :] = column[x : x + 1]
     for ref, x in ((out_hi, rows - 1), (out_lo, 0)):
@@ -611,26 +614,25 @@
 
     plane = ((rows, cols, depth), f32)
     blocks = block_ids.reshape(-1, block_ids.shape[3])
-    edge_column = ((rows + 3, channels, depth), bf16)
+    edge_column = ((rows + 1, channels, depth), bf16)
     edge_rows = ((2 * cols + 3, channels, depth), bf16)
     outs = [plane, plane, edge_column, edge_column, edge_rows, edge_rows]
     weight_mask, residual, y_hi, y_lo, x_hi, x_lo = pl.pallas_call(
         prep_kernel,
         out_shape=[jax.ShapeDtypeStruct(shape, dtype) for shape, dtype in outs],
-        in_specs=[pl.BlockSpec(memory_space=pl.ANY)] * 5,
+        in_specs=[pl.BlockSpec(memory_space=pl.ANY)] * 4,
         out_specs=[vmem for _ in outs],
         scratch_shapes=[
             pltpu.VMEM(blocks.shape, jnp.int32),
             pltpu.VMEM(occupancy.shape, jnp.int32),
             pltpu.VMEM(target.shape, f32),
-            pltpu.VMEM(ridge.shape, f32),
             pltpu.VMEM((2, rows, 1, channels, depth), bf16),
             pltpu.VMEM((blocks.shape[0], depth // block_ids.shape[2]), f32),
-            pltpu.SemaphoreType.DMA((10,)),
+            pltpu.SemaphoreType.DMA((9,)),
         ],
         compiler_params=pltpu.CompilerParams(vmem_limit_bytes=PREP_LIMIT << 20),
         name="prep",
-    )(features, blocks, occupancy, target, ridge)
+    )(features, blocks, occupancy, target)
     y_lo, y_hi = (shift(y_hi, "sy", 1), shift(y_lo, "sy", -1))
     x_lo, x_hi = (shift(x_hi, "sx", 1), shift(x_lo, "sx", -1))
     wide, bias = call(
@@ -662,10 +664,24 @@
         12,
         "conv_inner",
     )
-    column = ((2 * (rows + 2), channels, depth), bf16)
+    column = ((rows + 3, channels, depth), bf16)
     edge, f_hi, f_lo = call(
         conv_edge_kernel,
-        (features, y_lo, y_hi, x_lo, x_hi, side_lo, side_hi, weight_mask, wide, bias, inner),
+        (
+            features,
+            y_lo,
+            y_hi,
+            x_lo,
+            x_hi,
+            side_lo,
+            side_hi,
+            weight_mask,
+            wide,
+            bias,
+            inner,
+            residual,
+            ridge,
+        ),
         [(edge_shape, bf16), column, column],
         [grid_scratch, ((4, cols, depth), f32)],
         12,

time: 65.2 us -> 63.2 us (0.969)
  waiting for transfers between devices: 8.52 us -> 6.58 us
    ppermute x10, waiting for transfers between devices: 8.52 us -> 6.58 us  [shift(): lax.ppermute(value, axis, [(i, (i + step) % peers) for i in range(peers)])]
  transfers between devices with their start and end apart: 10 -> 10, of which waited for: 4 -> 3; matrix products, arithmetic and copies ran while one was open for 0% -> 0% of each run, Pallas kernels for 17% -> 18%
where the time goes in v10:
time: 63.2 us; the launch traced here: 63.1 us
  starting transfers between devices  19.3 us (31%)
  Pallas kernels  19.1 us (30%)
  blocking collectives  16.3 us (26%)
  waiting for transfers between devices  6.58 us (10%)
  local copies, waits for them, and re-layouts  0.96 us (2%)
  between operations  0.83 us (1%)
    ppermute x10, starting transfers between devices, shift(): lax.ppermute(value, axis, [(i, (i + step) % peers) for i in range(peers)])  19.3 us
    all_to_all x1, blocking collectives, per_device(): lax.all_to_all(jnp.broadcast_to(share[None], (peers, 1, 128)), AXES, 0, 0)  16.3 us
    pallas_call x9, Pallas kernels, call(): pl.pallas_call(kernel, out_shape=[jax.ShapeDtypeStruct(shape, dtype) for...  16.2 us
    ppermute x10, waiting for transfers between devices, shift(): lax.ppermute(value, axis, [(i, (i + step) % peers) for i in range(peers)])  6.58 us
    pallas_call x1, Pallas kernels, per_device(): pl.pallas_call(prep_kernel, out_shape=[jax.ShapeDtypeStruct(shape, dtype)...  2.92 us
  transfers between devices with their start and end apart: 10, of which 3 were waited for; matrix products, arithmetic and copies ran while one was open for 0% of the time, Pallas kernels for 18%

profile of v10, /device:TPU:1, one launch (start us, length us, event | category | flops | bytes accessed | tf_op | source)
XLA Modules:
  0.0 63.1 jit_solution(9922247075094643)
XLA Ops:
  0.7 2.9 %prep.1 = (f32[8,16,256]{2,1,0:T(8,128)}, f32[8,16,256]{2,1,0:T(8,128)}, bf16[9,32,256]{2,1,0:T(8,128)(2,1)}, bf16[9,32,256]{2,1,0:T(8,128)(2,1)}, bf16[35,32,25...) custom-call(bf16[8,16,32,256]{3,2,1,0:T(8,128)(2,1)} %own.5, s32[256,27]{1,0:T(8,128)} %bitcast.7, ...), custom_call_target="tpu_custom_call" | custom-call | tf_op jit(solution)/shard_map/prep/pallas_call | solution.py:620
  3.6 2.1 %collective-permute-start.2 = (bf16[35,32,256]{2,1,0:T(8,128)(2,1)}, bf16[35,32,256]{2,1,0:T(8,128)(2,1)S(1)}, u32[]{:S(2)}, u32[]{:S(2)}) collective-permute-start(bf16[35,32,256]{2,1,0:T(8,128)(2,1)} %get-tuple-element.29), channel_id=1, source_target_pairs={{0,8},{8,16},{16,24},{24,32},{32,40},{40,48},{48,56},{56,64},{64,7... | collective-permute-start | bytes 1720328 | tf_op jit(solution)/shard_map/ppermute | solution.py:14
  5.7 4.8 %collective-permute-start.3 = (bf16[35,32,256]{2,1,0:T(8,128)(2,1)}, bf16[35,32,256]{2,1,0:T(8,128)(2,1)S(1)}, u32[]{:S(2)}, u32[]{:S(2)}) collective-permute-start(bf16[35,32,256]{2,1,0:T(8,128)(2,1)} %get-tuple-element.30), channel_id=1, source_target_pairs={{0,120},{8,0},{16,8},{24,16},{32,24},{40,32},{48,40},{56,48},{64,5... | collective-permute-start | bytes 1720328 | tf_op jit(solution)/shard_map/ppermute | solution.py:14
  10.5 2.1 %collective-permute-start = (bf16[9,32,256]{2,1,0:T(8,128)(2,1)}, bf16[9,32,256]{2,1,0:T(8,128)(2,1)S(1)}, u32[]{:S(2)}, u32[]{:S(2)}) collective-permute-start(bf16[9,32,256]{2,1,0:T(8,128)(2,1)} %get-tuple-element.24), channel_id=1, source_target_pairs={{0,1},{1,2},{2,3},{3,4},{4,5},{5,6},{6,7},{7,0},{8,9},{9,10},{10,1... | collective-permute-start | bytes 442376 | tf_op jit(solution)/shard_map/ppermute | solution.py:14
  12.7 0.0 collective-permute-start.1
  12.7 2.4 %collective-permute-done.y_lo = bf16[9,32,256]{2,1,0:T(8,128)(2,1)S(1)} collective-permute-done((bf16[9,32,256]{2,1,0:T(8,128)(2,1)}, bf16[9,32,256]{2,1,0:T(8,128)(2,1)S(1)}, u32[]{:S(2)}, u32[]{:S(2)}) %collective-permute-start) | collective-permute-done | bytes 147488 | tf_op jit(solution)/shard_map/ppermute | solution.py:14
  15.1 2.7 %collective-permute-done.1.y_hi = bf16[9,32,256]{2,1,0:T(8,128)(2,1)S(1)} collective-permute-done((bf16[9,32,256]{2,1,0:T(8,128)(2,1)}, bf16[9,32,256]{2,1,0:T(8,128)(2,1)S(1)}, u32[]{:S(2)}, u32[]{:S(2)}) %collective-permute-start.1) | collective-permute-done | bytes 147488 | tf_op jit(solution)/shard_map/ppermute | solution.py:14
  17.8 0.1 collective-permute-start.4
  17.8 4.8 %collective-permute-start.5 = (bf16[5,32,256]{2,1,0:T(8,128)(2,1)S(1)}, bf16[5,32,256]{2,1,0:T(8,128)(2,1)S(1)}, u32[]{:S(2)}, u32[]{:S(2)}) collective-permute-start(bf16[5,32,256]{2,1,0:T(8,128)(2,1)S(1)} %get-tuple-element.32), channel_id=1, source_target_pairs={{0,120},{8,0},{16,8},{24,16},{32,24},{40,32},{48,40},{56,48},{64,5... | collective-permute-start | bytes 245768 | tf_op jit(solution)/shard_map/ppermute | solution.py:14
  22.6 0.4 weights.1
  23.1 0.0 copy-start.3
  23.1 0.9 %copy-done.3 = f32[8,16,256]{2,1,0:T(8,128)S(1)} copy-done((f32[8,16,256]{2,1,0:T(8,128)S(1)}, f32[8,16,256]{2,1,0:T(8,128)}, u32[]{:S(2)}) %copy-start.3) | copy-done | bytes 131096
  24.0 3.5 %conv_inner.1.inner = bf16[6,16,32,256]{3,2,1,0:T(8,128)(2,1)S(1)} custom-call(bf16[8,16,32,256]{3,2,1,0:T(8,128)(2,1)S(1)} %copy-done, bf16[9,32,256]{2,1,0:T(8,128)(2,1)S(1)} %collective-permute-done.y_lo, bf16[9,32,256]{2,1,0:T(8,128)(2,1)S(1)} %collective-permute-done.1.y_hi, f32[8,16,256]{2,1,0:T(8,128)S(1)} %copy-done.3, ...), custom_call_target="tpu_custom_call" | custom-call | tf_op jit(solution)/shard_map/conv_inner/pallas_call | solution.py:605
  27.5 0.0 collective-permute-done.4.side_lo
  27.5 0.0 collective-permute-done.5.side_hi
  27.5 0.0 collective-permute-done.2.x_lo
  27.5 0.0 collective-permute-done.3.x_hi
  27.6 2.1 %conv_edge.1 = (bf16[4,16,32,256]{3,2,1,0:T(8,128)(2,1)S(1)}, bf16[11,32,256]{2,1,0:T(8,128)(2,1)S(1)}, bf16[11,32,256]{2,1,0:T(8,128)(2,1)S(1)}) custom-call(bf16[8,16,32,256]{3,2,1,0:T(8,128)(2,1)S(1)} %copy-done, bf16[9,32,256]{2,1,0:T(8,128)(2,1)S(1)} %collective-permute-done.y_lo, bf16[9,32,256]{2,1,0:T(8,128)(2,1)S(1)} %collective-permute-done.1.y_hi, ...), custom_call_target="tpu_custom_call" | custom-call | tf_op jit(solution)/shard_map/conv_edge/pallas_call | solution.py:605
  29.7 0.3 collective-permute-start.6
  29.9 0.2 collective-permute-start.7
  30.2 3.5 %first_core.1.core = f32[8,16,256]{2,1,0:T(8,128)S(1)} custom-call(bf16[6,16,32,256]{3,2,1,0:T(8,128)(2,1)S(1)} %conv_inner.1.inner, bf16[4,16,32,256]{3,2,1,0:T(8,128)(2,1)S(1)} %get-tuple-element.34.edge, f32[8,16,256]{2,1,0:T(8,128)S(1)} %copy-done.1, bf16[35,32,256]{2,1,0:T(8,128)(2,1)S(1)} %collective-permute-done.2.x_lo, ...), custom_call_target="tpu_custom_call" | custom-call | tf_op jit(solution)/shard_map/first_core/pallas_call | solution.py:605
  33.6 0.0 collective-permute-done.6.f_lo
  33.7 1.5 %collective-permute-done.7.f_hi = bf16[11,32,256]{2,1,0:T(8,128)(2,1)S(1)} collective-permute-done((bf16[11,32,256]{2,1,0:T(8,128)(2,1)S(1)}, bf16[11,32,256]{2,1,0:T(8,128)(2,1)S(1)}, u32[]{:S(2)}, u32[]{:S(2)}) %collective-permute-start.7) | collective-permute-done | bytes 180256 | tf_op jit(solution)/shard_map/ppermute | solution.py:14
  35.2 0.7 %first_rim.1 = (f32[8,16,256]{2,1,0:T(8,128)S(1)}, f32[8,256]{1,0:T(8,128)S(1)}, f32[8,256]{1,0:T(8,128)S(1)}, f32[18,256]{1,0:T(8,128)S(1)}, f32[18,256]{1,0:T(8,128)S(1)}) custom-call(bf16[6,16,32,256]{3,2,1,0:T(8,128)(2,1)S(1)} %conv_inner.1.inner, bf16[4,16,32,256]{3,2,1,0:T(8,128)(2,1)S(1)} %get-tuple-element.34.edge, ...), custom_call_target="tpu_custom_call" | custom-call | tf_op jit(solution)/shard_map/first_rim/pallas_call | solution.py:605
  35.8 0.1 collective-permute-start.8
  35.9 4.8 %collective-permute-start.9 = (f32[18,256]{1,0:T(8,128)S(1)}, f32[18,256]{1,0:T(8,128)S(1)}, u32[]{:S(2)}, u32[]{:S(2)}) collective-permute-start(f32[18,256]{1,0:T(8,128)S(1)} %get-tuple-element.41), channel_id=1, source_target_pairs={{0,120},{8,0},{16,8},{24,16},{32,24},{40,32},{48,40},{56,48},{64,5... | collective-permute-start | bytes 55304 | tf_op jit(solution)/shard_map/ppermute | solution.py:14
  40.7 3.6 %second_core.1 = (f32[8,16,256]{2,1,0:T(8,128)S(1)}, f32[10,16,256]{2,1,0:T(8,128)S(1)}) custom-call(bf16[6,16,32,256]{3,2,1,0:T(8,128)(2,1)S(1)} %conv_inner.1.inner, bf16[4,16,32,256]{3,2,1,0:T(8,128)(2,1)S(1)} %get-tuple-element.34.edge, f32[8,16,256]{2,1,0:T(8,128)S(1)} %copy-done.1, f32[8,16,256]{2,1,0:T(8,128)S(1)} %get-tuple-element.37.first, ...), custom_call_target="tpu_custom_call" | custom-call | tf_op jit(solution)/shard_map/second_core/pallas_call | solution.py:605
  44.3 0.0 collective-permute-done.8.x_lo
  44.3 0.0 collective-permute-done.9.x_hi
  44.3 1.5 %second_rim.1 = (f32[8,16,256]{2,1,0:T(8,128)S(1)}, f32[1,128]{1,0:T(1,128)S(1)}) custom-call(bf16[6,16,32,256]{3,2,1,0:T(8,128)(2,1)S(1)} %conv_inner.1.inner, bf16[4,16,32,256]{3,2,1,0:T(8,128)(2,1)S(1)} %get-tuple-element.34.edge, bf16[11,32,256]{2,1,0:T(8,128)(2,1)S(1)} %collective-permute-done.6.f_lo, ...), custom_call_target="tpu_custom_call" | custom-call | tf_op jit(solution)/shard_map/second_rim/pallas_call | solution.py:605
  45.9 16.3 %all_to_all.5 = f32[128,1,128]{2,1,0:T(1,128)S(1)} all-to-all(f32[128,1,128]{2,1,0:T(1,128)S(1)} %broadcast_in_dim.13), channel_id=1, replica_groups=mesh['sx'=16,'sy'=8] {'sx','sy'}, dimensions={0} | all-to-all | bytes 131072 | tf_op jit(solution)/shard_map/all_to_all | solution.py:728
  62.1 0.9 %final.1 = (f32[8,16,256]{2,1,0:T(8,128)}, f32[8,16,256]{2,1,0:T(8,128)}) custom-call(f32[128,128]{1,0:T(8,128)S(1)} %bitcast.4, f32[8,16,256]{2,1,0:T(8,128)S(1)} %copy-done.1, f32[8,16,256]{2,1,0:T(8,128)S(1)} %get-tuple-element.37.first, f32[8,16,256]{2,1,0:T(8,128)S(1)} %get-tuple-element.45.second), custom_call_target="tpu_custom_call" | custom-call | tf_op jit(solution)/shard_map/final/pallas_call | solution.py:605
  (12 shorter events, 0.1 us)
Async XLA Ops:
  0.6 22.4 %copy-start = (bf16[8,16,32,256]{3,2,1,0:T(8,128)(2,1)S(1)}, bf16[8,16,32,256]{3,2,1,0:T(8,128)(2,1)}, u32[]{:S(2)}) copy-start(bf16[8,16,32,256]{3,2,1,0:T(8,128)(2,1)} %own.5) | copy-start | bytes 6291460
  0.6 22.0 %copy-start.5 = (f32[32]{0:T(128)S(1)}, f32[32]{0:T(128)}, u32[]{:S(2)}) copy-start(f32[32]{0:T(128)} %param.9) | copy-start | bytes 388
  0.7 22.0 %copy-start.4 = (bf16[27,32,32]{2,1,0:T(8,128)(2,1)S(1)}, bf16[27,32,32]{2,1,0:T(8,128)(2,1)}, u32[]{:S(2)}) copy-start(bf16[27,32,32]{2,1,0:T(8,128)(2,1)} %taps.1) | copy-start | bytes 165892
  3.6 24.0 %collective-permute-start.2 = (bf16[35,32,256]{2,1,0:T(8,128)(2,1)}, bf16[35,32,256]{2,1,0:T(8,128)(2,1)S(1)}, u32[]{:S(2)}, u32[]{:S(2)}) collective-permute-start(bf16[35,32,256]{2,1,0:T(8,128)(2,1)} %get-tuple-element.29), channel_id=1, source_target_pairs={{0,8},{8,16},{16,24},{24,32},{32,40},{40,48},{48,56},{56,64},{64,7... | collective-permute-start | bytes 1720328 | tf_op jit(solution)/shard_map/ppermute | solution.py:14
  5.7 21.9 %collective-permute-start.3 = (bf16[35,32,256]{2,1,0:T(8,128)(2,1)}, bf16[35,32,256]{2,1,0:T(8,128)(2,1)S(1)}, u32[]{:S(2)}, u32[]{:S(2)}) collective-permute-start(bf16[35,32,256]{2,1,0:T(8,128)(2,1)} %get-tuple-element.30), channel_id=1, source_target_pairs={{0,120},{8,0},{16,8},{24,16},{32,24},{40,32},{48,40},{56,48},{64,5... | collective-permute-start | bytes 1720328 | tf_op jit(solution)/shard_map/ppermute | solution.py:14
  10.5 4.6 %collective-permute-start = (bf16[9,32,256]{2,1,0:T(8,128)(2,1)}, bf16[9,32,256]{2,1,0:T(8,128)(2,1)S(1)}, u32[]{:S(2)}, u32[]{:S(2)}) collective-permute-start(bf16[9,32,256]{2,1,0:T(8,128)(2,1)} %get-tuple-element.24), channel_id=1, source_target_pairs={{0,1},{1,2},{2,3},{3,4},{4,5},{5,6},{6,7},{7,0},{8,9},{9,10},{10,1... | collective-permute-start | bytes 442376 | tf_op jit(solution)/shard_map/ppermute | solution.py:14
  12.7 5.1 %collective-permute-start.1 = (bf16[9,32,256]{2,1,0:T(8,128)(2,1)}, bf16[9,32,256]{2,1,0:T(8,128)(2,1)S(1)}, u32[]{:S(2)}, u32[]{:S(2)}) collective-permute-start(bf16[9,32,256]{2,1,0:T(8,128)(2,1)} %get-tuple-element.25), channel_id=1, source_target_pairs={{0,7},{1,0},{2,1},{3,2},{4,3},{5,4},{6,5},{7,6},{8,15},{9,8},{10,9... | collective-permute-start | bytes 442376 | tf_op jit(solution)/shard_map/ppermute | solution.py:14
  17.8 9.8 %collective-permute-start.4 = (bf16[5,32,256]{2,1,0:T(8,128)(2,1)S(1)}, bf16[5,32,256]{2,1,0:T(8,128)(2,1)S(1)}, u32[]{:S(2)}, u32[]{:S(2)}) collective-permute-start(bf16[5,32,256]{2,1,0:T(8,128)(2,1)S(1)} %get-tuple-element.31), channel_id=1, source_target_pairs={{0,8},{8,16},{16,24},{24,32},{32,40},{40,48},{48,56},{56,64},{64,7... | collective-permute-start | bytes 245768 | tf_op jit(solution)/shard_map/ppermute | solution.py:14
  17.8 9.7 %collective-permute-start.5 = (bf16[5,32,256]{2,1,0:T(8,128)(2,1)S(1)}, bf16[5,32,256]{2,1,0:T(8,128)(2,1)S(1)}, u32[]{:S(2)}, u32[]{:S(2)}) collective-permute-start(bf16[5,32,256]{2,1,0:T(8,128)(2,1)S(1)} %get-tuple-element.32), channel_id=1, source_target_pairs={{0,120},{8,0},{16,8},{24,16},{32,24},{40,32},{48,40},{56,48},{64,5... | collective-permute-start | bytes 245768 | tf_op jit(solution)/shard_map/ppermute | solution.py:14
  23.1 0.9 %copy-start.3 = (f32[8,16,256]{2,1,0:T(8,128)S(1)}, f32[8,16,256]{2,1,0:T(8,128)}, u32[]{:S(2)}) copy-start(f32[8,16,256]{2,1,0:T(8,128)} %get-tuple-element.26.mask) | copy-start | bytes 393220
  24.0 3.6 %copy-start.1 = (f32[8,16,256]{2,1,0:T(8,128)S(1)}, f32[8,16,256]{2,1,0:T(8,128)}, u32[]{:S(2)}) copy-start(f32[8,16,256]{2,1,0:T(8,128)} %get-tuple-element.33.start) | copy-start | bytes 393220
  24.0 3.6 %copy-start.2 = (f32[8,16,256]{2,1,0:T(8,128)S(1)}, f32[8,16,256]{2,1,0:T(8,128)}, u32[]{:S(2)}) copy-start(f32[8,16,256]{2,1,0:T(8,128)} %ridge.5) | copy-start | bytes 393220
  29.7 4.0 %collective-permute-start.6 = (bf16[11,32,256]{2,1,0:T(8,128)(2,1)S(1)}, bf16[11,32,256]{2,1,0:T(8,128)(2,1)S(1)}, u32[]{:S(2)}, u32[]{:S(2)}) collective-permute-start(bf16[11,32,256]{2,1,0:T(8,128)(2,1)S(1)} %get-tuple-element.35), channel_id=1, source_target_pairs={{0,1},{1,2},{2,3},{3,4},{4,5},{5,6},{6,7},{7,0},{8,9},{9,10},{10,1... | collective-permute-start | bytes 540680 | tf_op jit(solution)/shard_map/ppermute | solution.py:14
  29.9 5.2 %collective-permute-start.7 = (bf16[11,32,256]{2,1,0:T(8,128)(2,1)S(1)}, bf16[11,32,256]{2,1,0:T(8,128)(2,1)S(1)}, u32[]{:S(2)}, u32[]{:S(2)}) collective-permute-start(bf16[11,32,256]{2,1,0:T(8,128)(2,1)S(1)} %get-tuple-element.36), channel_id=1, source_target_pairs={{0,7},{1,0},{2,1},{3,2},{4,3},{5,4},{6,5},{7,6},{8,15},{9,8},{10,9... | collective-permute-start | bytes 540680 | tf_op jit(solution)/shard_map/ppermute | solution.py:14
  35.8 8.5 %collective-permute-start.8 = (f32[18,256]{1,0:T(8,128)S(1)}, f32[18,256]{1,0:T(8,128)S(1)}, u32[]{:S(2)}, u32[]{:S(2)}) collective-permute-start(f32[18,256]{1,0:T(8,128)S(1)} %get-tuple-element.40), channel_id=1, source_target_pairs={{0,8},{8,16},{16,24},{24,32},{32,40},{40,48},{48,56},{56,64},{64,7... | collective-permute-start | bytes 55304 | tf_op jit(solution)/shard_map/ppermute | solution.py:14
  35.9 8.4 %collective-permute-start.9 = (f32[18,256]{1,0:T(8,128)S(1)}, f32[18,256]{1,0:T(8,128)S(1)}, u32[]{:S(2)}, u32[]{:S(2)}) collective-permute-start(f32[18,256]{1,0:T(8,128)S(1)} %get-tuple-element.41), channel_id=1, source_target_pairs={{0,120},{8,0},{16,8},{24,16},{32,24},{40,32},{48,40},{56,48},{64,5... | collective-permute-start | bytes 55304 | tf_op jit(solution)/shard_map/ppermute | solution.py:14

commit v11 on v10

--- a/solution.py
+++ b/solution.py
@@ -19,6 +19,11 @@
     rest = value - high
     mid = rest.astype(jnp.bfloat16).astype(jnp.float32)
     return high, mid, rest - mid
+
+
+def paired(value):
+    high, mid, low = three(value)
+    return jnp.concatenate([high, mid], axis=0), jnp.concatenate([low, jnp.zeros_like(low)], axis=0)
 
 
 def prep_kernel(
@@ -37,6 +42,7 @@
     target,
     columns,
     present,
+    message,
     sems,
 ):
     rows, cols, channels, depth = own.shape
@@ -50,15 +56,23 @@
                 (target_in, target),
                 (own.at[:, 0:1], columns.at[0]),
                 (own.at[:, cols - 1 : cols], columns.at[1]),
-                (own.at[rows - 2], x_hi.at[0:cols]),
-                (own.at[rows - 1], x_hi.at[cols : 2 * cols]),
-                (own.at[0], x_lo.at[0:cols]),
-                (own.at[1], x_lo.at[cols : 2 * cols]),
+                (own.at[rows - 2], message.at[0, 0:cols]),
+                (own.at[rows - 1], message.at[0, cols : 2 * cols]),
+                (own.at[0], message.at[1, 0:cols]),
+                (own.at[1], message.at[1, cols : 2 * cols]),
+                (message.at[0, 0 : 2 * cols], x_hi.at[0 : 2 * cols]),
+                (message.at[1, 0 : 2 * cols], x_lo.at[0 : 2 * cols]),
+                (message.at[0, 2 * cols :], x_hi.at[2 * cols :]),
+                (message.at[1, 2 * cols :], x_lo.at[2 * cols :]),
             )
         )
     ]
-    for copy in copies:
+    for copy in (*copies[5:9], *copies[:5]):
         copy.start()
+    for k in range(2):
+        copies[5 + 2 * k].wait()
+        copies[6 + 2 * k].wait()
+        copies[9 + k].start()
     copies[0].wait()
     copies[1].wait()
     present[...] = jnp.broadcast_to(
@@ -70,6 +84,11 @@
     copies[2].wait()
     for x in range(rows):
         start[x] = mask[x] * target[x]
+    for k, (pair, row) in enumerate((((rows - 2, rows - 1), rows - 1), ((0, 1), 0))):
+        pieces = (jnp.concatenate([mask[x] for x in pair], axis=0), *paired(start[row]))
+        for at, piece in enumerate(pieces):
+            message[k, 2 * cols + at] = piece.astype(jnp.bfloat16)
+        copies[11 + k].start()
     copies[3].wait()
     copies[4].wait()
     blank = jnp.zeros((channels - 3 * rows, depth), jnp.float32)
@@ -78,16 +97,12 @@
             out[x] = columns[k, x, 0] * mask[x, y : y + 1, :].astype(jnp.bfloat16)
         terms = jnp.concatenate([*three(column_of(start, y)), blank], axis=0)
         out[rows] = terms.astype(jnp.bfloat16)
-    for out, pair, row in ((x_hi, (rows - 2, rows - 1), rows - 1), (x_lo, (0, 1), 0)):
-        out[2 * cols] = jnp.concatenate([mask[x] for x in pair], axis=0).astype(jnp.bfloat16)
-        high, mid, low = three(start[row])
-        out[2 * cols + 1] = jnp.concatenate([high, mid], axis=0).astype(jnp.bfloat16)
-        out[2 * cols + 2] = jnp.concatenate([low, jnp.zeros_like(low)], axis=0).astype(jnp.bfloat16)
-    for copy in copies[5:9]:
+    for copy in copies[9:]:
         copy.wait()
 
 
-def weights_kernel(taps, bias, wide, bias_col):
+def weights_kernel(taps, bias, mask, wide, bias_col, mask_out):
+    mask_out[...] = mask[...]
     channels = taps.shape[1]
     width = 16 * channels
     row = lax.broadcasted_iota(jnp.int32, (channels, width), 0)
@@ -181,7 +196,7 @@
     lax.fori_loop(0, rows // 2 - 1, pair, 0)
 
 
-def sides_kernel(y_lo, y_hi, out_hi, out_lo):
+def sides_kernel(y_lo, y_hi, _, out_hi, out_lo):
     rows = y_lo.shape[0] - 1
     channels, depth = y_lo.shape[1:]
     clear = [splat(flag, y_lo.shape[1:]) for flag in mesh_flags()[:2]]
@@ -621,24 +636,25 @@
         prep_kernel,
         out_shape=[jax.ShapeDtypeStruct(shape, dtype) for shape, dtype in outs],
         in_specs=[pl.BlockSpec(memory_space=pl.ANY)] * 4,
-        out_specs=[vmem for _ in outs],
+        out_specs=[vmem] * 4 + [pl.BlockSpec(memory_space=pl.ANY)] * 2,
         scratch_shapes=[
             pltpu.VMEM(blocks.shape, jnp.int32),
             pltpu.VMEM(occupancy.shape, jnp.int32),
             pltpu.VMEM(target.shape, f32),
             pltpu.VMEM((2, rows, 1, channels, depth), bf16),
             pltpu.VMEM((blocks.shape[0], depth // block_ids.shape[2]), f32),
-            pltpu.SemaphoreType.DMA((9,)),
+            pltpu.VMEM((2, *edge_rows[0]), bf16),
+            pltpu.SemaphoreType.DMA((13,)),
         ],
         compiler_params=pltpu.CompilerParams(vmem_limit_bytes=PREP_LIMIT << 20),
         name="prep",
     )(features, blocks, occupancy, target)
     y_lo, y_hi = (shift(y_hi, "sy", 1), shift(y_lo, "sy", -1))
     x_lo, x_hi = (shift(x_hi, "sx", 1), shift(x_lo, "sx", -1))
-    wide, bias = call(
+    wide, bias, weight_mask = call(
         weights_kernel,
-        (conv_weight, conv_bias[None]),
-        [((12 * channels, 16 * channels), bf16), ((channels, depth), f32)],
+        (conv_weight, conv_bias[None], weight_mask),
+        [((12 * channels, 16 * channels), bf16), ((channels, depth), f32), plane],
         [],
         8,
         "weights",
@@ -649,7 +665,7 @@
     side_shape = (5, channels, depth)
     side_hi, side_lo = call(
         sides_kernel,
-        (y_lo, y_hi),
+        (y_lo, y_hi, bias),
         [(side_shape, bf16), (side_shape, bf16)],
         [],
         4,

time: 63.2 us -> 62.9 us (level)
  waiting for transfers between devices: 6.58 us -> 5.17 us
  starting transfers between devices: 19.3 us -> 20.3 us
    ppermute x10, waiting for transfers between devices: 6.58 us -> 5.17 us  [shift(): lax.ppermute(value, axis, [(i, (i + step) % peers) for i in range(peers)])]
    ppermute x10, starting transfers between devices: 19.3 us -> 20.3 us  [shift(): lax.ppermute(value, axis, [(i, (i + step) % peers) for i in range(peers)])]
where the time goes in v11:
time: 62.9 us; the launch traced here: 62.8 us
  starting transfers between devices  20.3 us (32%)
  Pallas kernels  19.4 us (31%)
  blocking collectives  16.2 us (26%)
  waiting for transfers between devices  5.17 us (8%)
  local copies, waits for them, and re-layouts  0.96 us (2%)
  between operations  0.82 us (1%)
    ppermute x10, starting transfers between devices, shift(): lax.ppermute(value, axis, [(i, (i + step) % peers) for i in range(peers)])  20.3 us
    pallas_call x9, Pallas kernels, call(): pl.pallas_call(kernel, out_shape=[jax.ShapeDtypeStruct(shape, dtype) for...  16.2 us
    all_to_all x1, blocking collectives, per_device(): lax.all_to_all(jnp.broadcast_to(share[None], (peers, 1, 128)), AXES, 0, 0)  16.2 us
    ppermute x10, waiting for transfers between devices, shift(): lax.ppermute(value, axis, [(i, (i + step) % peers) for i in range(peers)])  5.17 us
    pallas_call x1, Pallas kernels, per_device(): pl.pallas_call(prep_kernel, out_shape=[jax.ShapeDtypeStruct(shape, dtype)...  3.12 us
  transfers between devices with their start and end apart: 10, of which 3 were waited for; matrix products, arithmetic and copies ran while one was open for 0% of the time, Pallas kernels for 18%

profile of v11, /device:TPU:1, one launch (start us, length us, event | category | flops | bytes accessed | tf_op | source)
XLA Modules:
  0.0 62.8 jit_solution(10639819056823743797)
XLA Ops:
  0.7 3.1 %prep.1 = (f32[8,16,256]{2,1,0:T(8,128)}, f32[8,16,256]{2,1,0:T(8,128)}, bf16[9,32,256]{2,1,0:T(8,128)(2,1)}, bf16[9,32,256]{2,1,0:T(8,128)(2,1)}, bf16[35,32,25...) custom-call(bf16[8,16,32,256]{3,2,1,0:T(8,128)(2,1)} %own.5, s32[256,27]{1,0:T(8,128)} %bitcast.7, ...), custom_call_target="tpu_custom_call" | custom-call | tf_op jit(solution)/shard_map/prep/pallas_call | solution.py:635
  3.8 2.1 %collective-permute-start.2 = (bf16[35,32,256]{2,1,0:T(8,128)(2,1)}, bf16[35,32,256]{2,1,0:T(8,128)(2,1)S(1)}, u32[]{:S(2)}, u32[]{:S(2)}) collective-permute-start(bf16[35,32,256]{2,1,0:T(8,128)(2,1)} %get-tuple-element.31), channel_id=1, source_target_pairs={{0,8},{8,16},{16,24},{24,32},{32,40},{40,48},{48,56},{56,64},{64,7... | collective-permute-start | bytes 1720328 | tf_op jit(solution)/shard_map/ppermute | solution.py:14
  5.9 4.8 %collective-permute-start.3 = (bf16[35,32,256]{2,1,0:T(8,128)(2,1)}, bf16[35,32,256]{2,1,0:T(8,128)(2,1)S(1)}, u32[]{:S(2)}, u32[]{:S(2)}) collective-permute-start(bf16[35,32,256]{2,1,0:T(8,128)(2,1)} %get-tuple-element.32), channel_id=1, source_target_pairs={{0,120},{8,0},{16,8},{24,16},{32,24},{40,32},{48,40},{56,48},{64,5... | collective-permute-start | bytes 1720328 | tf_op jit(solution)/shard_map/ppermute | solution.py:14
  10.7 2.1 %collective-permute-start = (bf16[9,32,256]{2,1,0:T(8,128)(2,1)}, bf16[9,32,256]{2,1,0:T(8,128)(2,1)S(1)}, u32[]{:S(2)}, u32[]{:S(2)}) collective-permute-start(bf16[9,32,256]{2,1,0:T(8,128)(2,1)} %get-tuple-element.25), channel_id=1, source_target_pairs={{0,1},{1,2},{2,3},{3,4},{4,5},{5,6},{6,7},{7,0},{8,9},{9,10},{10,1... | collective-permute-start | bytes 442376 | tf_op jit(solution)/shard_map/ppermute | solution.py:14
  12.9 0.0 collective-permute-start.1
  12.9 0.0 copy-start.4
  12.9 0.9 %copy-done.4 = f32[8,16,256]{2,1,0:T(8,128)S(1)} copy-done((f32[8,16,256]{2,1,0:T(8,128)S(1)}, f32[8,16,256]{2,1,0:T(8,128)}, u32[]{:S(2)}) %copy-start.4) | copy-done | bytes 131096
  13.8 0.4 weights.1
  14.2 1.1 %collective-permute-done.y_lo = bf16[9,32,256]{2,1,0:T(8,128)(2,1)S(1)} collective-permute-done((bf16[9,32,256]{2,1,0:T(8,128)(2,1)}, bf16[9,32,256]{2,1,0:T(8,128)(2,1)S(1)}, u32[]{:S(2)}, u32[]{:S(2)}) %collective-permute-start) | collective-permute-done | bytes 147488 | tf_op jit(solution)/shard_map/ppermute | solution.py:14
  15.3 2.7 %collective-permute-done.1.y_hi = bf16[9,32,256]{2,1,0:T(8,128)(2,1)S(1)} collective-permute-done((bf16[9,32,256]{2,1,0:T(8,128)(2,1)}, bf16[9,32,256]{2,1,0:T(8,128)(2,1)S(1)}, u32[]{:S(2)}, u32[]{:S(2)}) %collective-permute-start.1) | collective-permute-done | bytes 147488 | tf_op jit(solution)/shard_map/ppermute | solution.py:14
  18.0 0.1 collective-permute-start.4
  18.0 4.8 %collective-permute-start.5 = (bf16[5,32,256]{2,1,0:T(8,128)(2,1)S(1)}, bf16[5,32,256]{2,1,0:T(8,128)(2,1)S(1)}, u32[]{:S(2)}, u32[]{:S(2)}) collective-permute-start(bf16[5,32,256]{2,1,0:T(8,128)(2,1)S(1)} %get-tuple-element.34), channel_id=1, source_target_pairs={{0,120},{8,0},{16,8},{24,16},{32,24},{40,32},{48,40},{56,48},{64,5... | collective-permute-start | bytes 245768 | tf_op jit(solution)/shard_map/ppermute | solution.py:14
  22.8 3.5 %conv_inner.1.inner = bf16[6,16,32,256]{3,2,1,0:T(8,128)(2,1)S(1)} custom-call(bf16[8,16,32,256]{3,2,1,0:T(8,128)(2,1)S(1)} %copy-done, bf16[9,32,256]{2,1,0:T(8,128)(2,1)S(1)} %collective-permute-done.y_lo, bf16[9,32,256]{2,1,0:T(8,128)(2,1)S(1)} %collective-permute-done.1.y_hi, f32[8,16,256]{2,1,0:T(8,128)S(1)} %get-tuple-element.28.mask, ...), custom_call_target="tpu_custom_call" | custom-call | tf_op jit(solution)/shard_map/conv_inner/pallas_call | solution.py:620
  26.4 0.0 collective-permute-done.4.side_lo
  26.4 0.0 collective-permute-done.5.side_hi
  26.4 0.0 collective-permute-done.2.x_lo
  26.4 0.0 collective-permute-done.3.x_hi
  26.4 2.1 %conv_edge.1 = (bf16[4,16,32,256]{3,2,1,0:T(8,128)(2,1)S(1)}, bf16[11,32,256]{2,1,0:T(8,128)(2,1)S(1)}, bf16[11,32,256]{2,1,0:T(8,128)(2,1)S(1)}) custom-call(bf16[8,16,32,256]{3,2,1,0:T(8,128)(2,1)S(1)} %copy-done, bf16[9,32,256]{2,1,0:T(8,128)(2,1)S(1)} %collective-permute-done.y_lo, bf16[9,32,256]{2,1,0:T(8,128)(2,1)S(1)} %collective-permute-done.1.y_hi, ...), custom_call_target="tpu_custom_call" | custom-call | tf_op jit(solution)/shard_map/conv_edge/pallas_call | solution.py:620
  28.5 1.3 %collective-permute-start.6 = (bf16[11,32,256]{2,1,0:T(8,128)(2,1)S(1)}, bf16[11,32,256]{2,1,0:T(8,128)(2,1)S(1)}, u32[]{:S(2)}, u32[]{:S(2)}) collective-permute-start(bf16[11,32,256]{2,1,0:T(8,128)(2,1)S(1)} %get-tuple-element.37), channel_id=1, source_target_pairs={{0,1},{1,2},{2,3},{3,4},{4,5},{5,6},{6,7},{7,0},{8,9},{9,10},{10,1... | collective-permute-start | bytes 540680 | tf_op jit(solution)/shard_map/ppermute | solution.py:14
  29.9 0.0 collective-permute-start.7
  29.9 3.5 %first_core.1.core = f32[8,16,256]{2,1,0:T(8,128)S(1)} custom-call(bf16[6,16,32,256]{3,2,1,0:T(8,128)(2,1)S(1)} %conv_inner.1.inner, bf16[4,16,32,256]{3,2,1,0:T(8,128)(2,1)S(1)} %get-tuple-element.36.edge, f32[8,16,256]{2,1,0:T(8,128)S(1)} %copy-done.1, bf16[35,32,256]{2,1,0:T(8,128)(2,1)S(1)} %collective-permute-done.2.x_lo, ...), custom_call_target="tpu_custom_call" | custom-call | tf_op jit(solution)/shard_map/first_core/pallas_call | solution.py:620
  33.3 0.0 collective-permute-done.6.f_lo
  33.3 1.4 %collective-permute-done.7.f_hi = bf16[11,32,256]{2,1,0:T(8,128)(2,1)S(1)} collective-permute-done((bf16[11,32,256]{2,1,0:T(8,128)(2,1)S(1)}, bf16[11,32,256]{2,1,0:T(8,128)(2,1)S(1)}, u32[]{:S(2)}, u32[]{:S(2)}) %collective-permute-start.7) | collective-permute-done | bytes 180256 | tf_op jit(solution)/shard_map/ppermute | solution.py:14
  34.8 0.7 %first_rim.1 = (f32[8,16,256]{2,1,0:T(8,128)S(1)}, f32[8,256]{1,0:T(8,128)S(1)}, f32[8,256]{1,0:T(8,128)S(1)}, f32[18,256]{1,0:T(8,128)S(1)}, f32[18,256]{1,0:T(8,128)S(1)}) custom-call(bf16[6,16,32,256]{3,2,1,0:T(8,128)(2,1)S(1)} %conv_inner.1.inner, bf16[4,16,32,256]{3,2,1,0:T(8,128)(2,1)S(1)} %get-tuple-element.36.edge, ...), custom_call_target="tpu_custom_call" | custom-call | tf_op jit(solution)/shard_map/first_rim/pallas_call | solution.py:620
  35.5 0.1 collective-permute-start.8
  35.5 4.9 %collective-permute-start.9 = (f32[18,256]{1,0:T(8,128)S(1)}, f32[18,256]{1,0:T(8,128)S(1)}, u32[]{:S(2)}, u32[]{:S(2)}) collective-permute-start(f32[18,256]{1,0:T(8,128)S(1)} %get-tuple-element.43), channel_id=1, source_target_pairs={{0,120},{8,0},{16,8},{24,16},{32,24},{40,32},{48,40},{56,48},{64,5... | collective-permute-start | bytes 55304 | tf_op jit(solution)/shard_map/ppermute | solution.py:14
  40.5 3.6 %second_core.1 = (f32[8,16,256]{2,1,0:T(8,128)S(1)}, f32[10,16,256]{2,1,0:T(8,128)S(1)}) custom-call(bf16[6,16,32,256]{3,2,1,0:T(8,128)(2,1)S(1)} %conv_inner.1.inner, bf16[4,16,32,256]{3,2,1,0:T(8,128)(2,1)S(1)} %get-tuple-element.36.edge, f32[8,16,256]{2,1,0:T(8,128)S(1)} %copy-done.1, f32[8,16,256]{2,1,0:T(8,128)S(1)} %get-tuple-element.39.first, ...), custom_call_target="tpu_custom_call" | custom-call | tf_op jit(solution)/shard_map/second_core/pallas_call | solution.py:620
  44.1 0.0 collective-permute-done.8.x_lo
  44.1 0.0 collective-permute-done.9.x_hi
  44.1 1.5 %second_rim.1 = (f32[8,16,256]{2,1,0:T(8,128)S(1)}, f32[1,128]{1,0:T(1,128)S(1)}) custom-call(bf16[6,16,32,256]{3,2,1,0:T(8,128)(2,1)S(1)} %conv_inner.1.inner, bf16[4,16,32,256]{3,2,1,0:T(8,128)(2,1)S(1)} %get-tuple-element.36.edge, bf16[11,32,256]{2,1,0:T(8,128)(2,1)S(1)} %collective-permute-done.6.f_lo, ...), custom_call_target="tpu_custom_call" | custom-call | tf_op jit(solution)/shard_map/second_rim/pallas_call | solution.py:620
  45.6 16.2 %all_to_all.5 = f32[128,1,128]{2,1,0:T(1,128)S(1)} all-to-all(f32[128,1,128]{2,1,0:T(1,128)S(1)} %broadcast_in_dim.13), channel_id=1, replica_groups=mesh['sx'=16,'sy'=8] {'sx','sy'}, dimensions={0} | all-to-all | bytes 131072 | tf_op jit(solution)/shard_map/all_to_all | solution.py:744
  61.8 0.9 %final.1 = (f32[8,16,256]{2,1,0:T(8,128)}, f32[8,16,256]{2,1,0:T(8,128)}) custom-call(f32[128,128]{1,0:T(8,128)S(1)} %bitcast.4, f32[8,16,256]{2,1,0:T(8,128)S(1)} %copy-done.1, f32[8,16,256]{2,1,0:T(8,128)S(1)} %get-tuple-element.39.first, f32[8,16,256]{2,1,0:T(8,128)S(1)} %get-tuple-element.47.second), custom_call_target="tpu_custom_call" | custom-call | tf_op jit(solution)/shard_map/final/pallas_call | solution.py:620
  (12 shorter events, 0.1 us)
Async XLA Ops:
  0.6 22.2 %copy-start = (bf16[8,16,32,256]{3,2,1,0:T(8,128)(2,1)S(1)}, bf16[8,16,32,256]{3,2,1,0:T(8,128)(2,1)}, u32[]{:S(2)}) copy-start(bf16[8,16,32,256]{3,2,1,0:T(8,128)(2,1)} %own.5) | copy-start | bytes 6291460
  0.6 12.2 %copy-start.5 = (f32[32]{0:T(128)S(1)}, f32[32]{0:T(128)}, u32[]{:S(2)}) copy-start(f32[32]{0:T(128)} %param.9) | copy-start | bytes 388
  0.7 12.2 %copy-start.3 = (bf16[27,32,32]{2,1,0:T(8,128)(2,1)S(1)}, bf16[27,32,32]{2,1,0:T(8,128)(2,1)}, u32[]{:S(2)}) copy-start(bf16[27,32,32]{2,1,0:T(8,128)(2,1)} %taps.1) | copy-start | bytes 165892
  3.8 22.6 %collective-permute-start.2 = (bf16[35,32,256]{2,1,0:T(8,128)(2,1)}, bf16[35,32,256]{2,1,0:T(8,128)(2,1)S(1)}, u32[]{:S(2)}, u32[]{:S(2)}) collective-permute-start(bf16[35,32,256]{2,1,0:T(8,128)(2,1)} %get-tuple-element.31), channel_id=1, source_target_pairs={{0,8},{8,16},{16,24},{24,32},{32,40},{40,48},{48,56},{56,64},{64,7... | collective-permute-start | bytes 1720328 | tf_op jit(solution)/shard_map/ppermute | solution.py:14
  5.9 20.5 %collective-permute-start.3 = (bf16[35,32,256]{2,1,0:T(8,128)(2,1)}, bf16[35,32,256]{2,1,0:T(8,128)(2,1)S(1)}, u32[]{:S(2)}, u32[]{:S(2)}) collective-permute-start(bf16[35,32,256]{2,1,0:T(8,128)(2,1)} %get-tuple-element.32), channel_id=1, source_target_pairs={{0,120},{8,0},{16,8},{24,16},{32,24},{40,32},{48,40},{56,48},{64,5... | collective-permute-start | bytes 1720328 | tf_op jit(solution)/shard_map/ppermute | solution.py:14
  10.7 4.6 %collective-permute-start = (bf16[9,32,256]{2,1,0:T(8,128)(2,1)}, bf16[9,32,256]{2,1,0:T(8,128)(2,1)S(1)}, u32[]{:S(2)}, u32[]{:S(2)}) collective-permute-start(bf16[9,32,256]{2,1,0:T(8,128)(2,1)} %get-tuple-element.25), channel_id=1, source_target_pairs={{0,1},{1,2},{2,3},{3,4},{4,5},{5,6},{6,7},{7,0},{8,9},{9,10},{10,1... | collective-permute-start | bytes 442376 | tf_op jit(solution)/shard_map/ppermute | solution.py:14
  12.9 5.1 %collective-permute-start.1 = (bf16[9,32,256]{2,1,0:T(8,128)(2,1)}, bf16[9,32,256]{2,1,0:T(8,128)(2,1)S(1)}, u32[]{:S(2)}, u32[]{:S(2)}) collective-permute-start(bf16[9,32,256]{2,1,0:T(8,128)(2,1)} %get-tuple-element.26), channel_id=1, source_target_pairs={{0,7},{1,0},{2,1},{3,2},{4,3},{5,4},{6,5},{7,6},{8,15},{9,8},{10,9... | collective-permute-start | bytes 442376 | tf_op jit(solution)/shard_map/ppermute | solution.py:14
  12.9 0.9 %copy-start.4 = (f32[8,16,256]{2,1,0:T(8,128)S(1)}, f32[8,16,256]{2,1,0:T(8,128)}, u32[]{:S(2)}) copy-start(f32[8,16,256]{2,1,0:T(8,128)} %get-tuple-element.27.mask) | copy-start | bytes 393220
  18.0 8.4 %collective-permute-start.4 = (bf16[5,32,256]{2,1,0:T(8,128)(2,1)S(1)}, bf16[5,32,256]{2,1,0:T(8,128)(2,1)S(1)}, u32[]{:S(2)}, u32[]{:S(2)}) collective-permute-start(bf16[5,32,256]{2,1,0:T(8,128)(2,1)S(1)} %get-tuple-element.33), channel_id=1, source_target_pairs={{0,8},{8,16},{16,24},{24,32},{32,40},{40,48},{48,56},{56,64},{64,7... | collective-permute-start | bytes 245768 | tf_op jit(solution)/shard_map/ppermute | solution.py:14
  18.0 8.3 %collective-permute-start.5 = (bf16[5,32,256]{2,1,0:T(8,128)(2,1)S(1)}, bf16[5,32,256]{2,1,0:T(8,128)(2,1)S(1)}, u32[]{:S(2)}, u32[]{:S(2)}) collective-permute-start(bf16[5,32,256]{2,1,0:T(8,128)(2,1)S(1)} %get-tuple-element.34), channel_id=1, source_target_pairs={{0,120},{8,0},{16,8},{24,16},{32,24},{40,32},{48,40},{56,48},{64,5... | collective-permute-start | bytes 245768 | tf_op jit(solution)/shard_map/ppermute | solution.py:14
  22.8 3.6 %copy-start.1 = (f32[8,16,256]{2,1,0:T(8,128)S(1)}, f32[8,16,256]{2,1,0:T(8,128)}, u32[]{:S(2)}) copy-start(f32[8,16,256]{2,1,0:T(8,128)} %get-tuple-element.35.start) | copy-start | bytes 393220
  22.8 3.6 %copy-start.2 = (f32[8,16,256]{2,1,0:T(8,128)S(1)}, f32[8,16,256]{2,1,0:T(8,128)}, u32[]{:S(2)}) copy-start(f32[8,16,256]{2,1,0:T(8,128)} %ridge.5) | copy-start | bytes 393220
  28.5 4.8 %collective-permute-start.6 = (bf16[11,32,256]{2,1,0:T(8,128)(2,1)S(1)}, bf16[11,32,256]{2,1,0:T(8,128)(2,1)S(1)}, u32[]{:S(2)}, u32[]{:S(2)}) collective-permute-start(bf16[11,32,256]{2,1,0:T(8,128)(2,1)S(1)} %get-tuple-element.37), channel_id=1, source_target_pairs={{0,1},{1,2},{2,3},{3,4},{4,5},{5,6},{6,7},{7,0},{8,9},{9,10},{10,1... | collective-permute-start | bytes 540680 | tf_op jit(solution)/shard_map/ppermute | solution.py:14
  29.9 4.9 %collective-permute-start.7 = (bf16[11,32,256]{2,1,0:T(8,128)(2,1)S(1)}, bf16[11,32,256]{2,1,0:T(8,128)(2,1)S(1)}, u32[]{:S(2)}, u32[]{:S(2)}) collective-permute-start(bf16[11,32,256]{2,1,0:T(8,128)(2,1)S(1)} %get-tuple-element.38), channel_id=1, source_target_pairs={{0,7},{1,0},{2,1},{3,2},{4,3},{5,4},{6,5},{7,6},{8,15},{9,8},{10,9... | collective-permute-start | bytes 540680 | tf_op jit(solution)/shard_map/ppermute | solution.py:14
  35.5 8.6 %collective-permute-start.8 = (f32[18,256]{1,0:T(8,128)S(1)}, f32[18,256]{1,0:T(8,128)S(1)}, u32[]{:S(2)}, u32[]{:S(2)}) collective-permute-start(f32[18,256]{1,0:T(8,128)S(1)} %get-tuple-element.42), channel_id=1, source_target_pairs={{0,8},{8,16},{16,24},{24,32},{32,40},{40,48},{48,56},{56,64},{64,7... | collective-permute-start | bytes 55304 | tf_op jit(solution)/shard_map/ppermute | solution.py:14
  35.5 8.5 %collective-permute-start.9 = (f32[18,256]{1,0:T(8,128)S(1)}, f32[18,256]{1,0:T(8,128)S(1)}, u32[]{:S(2)}, u32[]{:S(2)}) collective-permute-start(f32[18,256]{1,0:T(8,128)S(1)} %get-tuple-element.43), channel_id=1, source_target_pairs={{0,120},{8,0},{16,8},{24,16},{32,24},{40,32},{48,40},{56,48},{64,5... | collective-permute-start | bytes 55304 | tf_op jit(solution)/shard_map/ppermute | solution.py:14

commit v12 on v11

--- a/solution.py
+++ b/solution.py
@@ -649,6 +649,7 @@
         compiler_params=pltpu.CompilerParams(vmem_limit_bytes=PREP_LIMIT << 20),
         name="prep",
     )(features, blocks, occupancy, target)
+    features, weight_mask = lax.optimization_barrier((features, weight_mask))
     y_lo, y_hi = (shift(y_hi, "sy", 1), shift(y_lo, "sy", -1))
     x_lo, x_hi = (shift(x_hi, "sx", 1), shift(x_lo, "sx", -1))
     wide, bias, weight_mask = call(

time: 62.9 us -> 62.9 us (level)
  no operation moved by 1% of the time
where the time goes in v12:
time: 62.9 us; the launch traced here: 62.8 us
  starting transfers between devices  20.3 us (32%)
  Pallas kernels  19.4 us (31%)
  blocking collectives  16.2 us (26%)
  waiting for transfers between devices  5.17 us (8%)
  local copies, waits for them, and re-layouts  0.96 us (2%)
  between operations  0.82 us (1%)
    ppermute x10, starting transfers between devices, shift(): lax.ppermute(value, axis, [(i, (i + step) % peers) for i in range(peers)])  20.3 us
    pallas_call x9, Pallas kernels, call(): pl.pallas_call(kernel, out_shape=[jax.ShapeDtypeStruct(shape, dtype) for...  16.2 us
    all_to_all x1, blocking collectives, per_device(): lax.all_to_all(jnp.broadcast_to(share[None], (peers, 1, 128)), AXES, 0, 0)  16.2 us
    ppermute x10, waiting for transfers between devices, shift(): lax.ppermute(value, axis, [(i, (i + step) % peers) for i in range(peers)])  5.17 us
    pallas_call x1, Pallas kernels, per_device(): pl.pallas_call(prep_kernel, out_shape=[jax.ShapeDtypeStruct(shape, dtype)...  3.12 us
  transfers between devices with their start and end apart: 10, of which 3 were waited for; matrix products, arithmetic and copies ran while one was open for 0% of the time, Pallas kernels for 18%

profile of v12, /device:TPU:1, one launch (start us, length us, event | category | flops | bytes accessed | tf_op | source)
XLA Modules:
  0.0 62.8 jit_solution(10639819056823743797)
XLA Ops:
  0.7 3.1 %prep.1 = (f32[8,16,256]{2,1,0:T(8,128)}, f32[8,16,256]{2,1,0:T(8,128)}, bf16[9,32,256]{2,1,0:T(8,128)(2,1)}, bf16[9,32,256]{2,1,0:T(8,128)(2,1)}, bf16[35,32,25...) custom-call(bf16[8,16,32,256]{3,2,1,0:T(8,128)(2,1)} %own.3, s32[256,27]{1,0:T(8,128)} %bitcast.7, ...), custom_call_target="tpu_custom_call" | custom-call | tf_op jit(solution)/shard_map/prep/pallas_call | solution.py:635
  3.8 2.1 %collective-permute-start.2 = (bf16[35,32,256]{2,1,0:T(8,128)(2,1)}, bf16[35,32,256]{2,1,0:T(8,128)(2,1)S(1)}, u32[]{:S(2)}, u32[]{:S(2)}) collective-permute-start(bf16[35,32,256]{2,1,0:T(8,128)(2,1)} %get-tuple-element.35), channel_id=1, source_target_pairs={{0,8},{8,16},{16,24},{24,32},{32,40},{40,48},{48,56},{56,64},{64,7... | collective-permute-start | bytes 1720328 | tf_op jit(solution)/shard_map/ppermute | solution.py:14
  5.9 4.8 %collective-permute-start.3 = (bf16[35,32,256]{2,1,0:T(8,128)(2,1)}, bf16[35,32,256]{2,1,0:T(8,128)(2,1)S(1)}, u32[]{:S(2)}, u32[]{:S(2)}) collective-permute-start(bf16[35,32,256]{2,1,0:T(8,128)(2,1)} %get-tuple-element.36), channel_id=1, source_target_pairs={{0,120},{8,0},{16,8},{24,16},{32,24},{40,32},{48,40},{56,48},{64,5... | collective-permute-start | bytes 1720328 | tf_op jit(solution)/shard_map/ppermute | solution.py:14
  10.7 2.1 %collective-permute-start = (bf16[9,32,256]{2,1,0:T(8,128)(2,1)}, bf16[9,32,256]{2,1,0:T(8,128)(2,1)S(1)}, u32[]{:S(2)}, u32[]{:S(2)}) collective-permute-start(bf16[9,32,256]{2,1,0:T(8,128)(2,1)} %get-tuple-element.29), channel_id=1, source_target_pairs={{0,1},{1,2},{2,3},{3,4},{4,5},{5,6},{6,7},{7,0},{8,9},{9,10},{10,1... | collective-permute-start | bytes 442376 | tf_op jit(solution)/shard_map/ppermute | solution.py:14
  12.9 0.0 collective-permute-start.1
  12.9 0.0 copy-start.4
  12.9 0.9 %copy-done.4 = f32[8,16,256]{2,1,0:T(8,128)S(1)} copy-done((f32[8,16,256]{2,1,0:T(8,128)S(1)}, f32[8,16,256]{2,1,0:T(8,128)}, u32[]{:S(2)}) %copy-start.4) | copy-done | bytes 131096
  13.8 0.4 weights.1
  14.2 1.1 %collective-permute-done.y_lo = bf16[9,32,256]{2,1,0:T(8,128)(2,1)S(1)} collective-permute-done((bf16[9,32,256]{2,1,0:T(8,128)(2,1)}, bf16[9,32,256]{2,1,0:T(8,128)(2,1)S(1)}, u32[]{:S(2)}, u32[]{:S(2)}) %collective-permute-start) | collective-permute-done | bytes 147488 | tf_op jit(solution)/shard_map/ppermute | solution.py:14
  15.3 2.7 %collective-permute-done.1.y_hi = bf16[9,32,256]{2,1,0:T(8,128)(2,1)S(1)} collective-permute-done((bf16[9,32,256]{2,1,0:T(8,128)(2,1)}, bf16[9,32,256]{2,1,0:T(8,128)(2,1)S(1)}, u32[]{:S(2)}, u32[]{:S(2)}) %collective-permute-start.1) | collective-permute-done | bytes 147488 | tf_op jit(solution)/shard_map/ppermute | solution.py:14
  18.0 0.1 collective-permute-start.4
  18.0 4.8 %collective-permute-start.5 = (bf16[5,32,256]{2,1,0:T(8,128)(2,1)S(1)}, bf16[5,32,256]{2,1,0:T(8,128)(2,1)S(1)}, u32[]{:S(2)}, u32[]{:S(2)}) collective-permute-start(bf16[5,32,256]{2,1,0:T(8,128)(2,1)S(1)} %get-tuple-element.38), channel_id=1, source_target_pairs={{0,120},{8,0},{16,8},{24,16},{32,24},{40,32},{48,40},{56,48},{64,5... | collective-permute-start | bytes 245768 | tf_op jit(solution)/shard_map/ppermute | solution.py:14
  22.8 3.5 %conv_inner.1.inner = bf16[6,16,32,256]{3,2,1,0:T(8,128)(2,1)S(1)} custom-call(bf16[8,16,32,256]{3,2,1,0:T(8,128)(2,1)S(1)} %copy-done, bf16[9,32,256]{2,1,0:T(8,128)(2,1)S(1)} %collective-permute-done.y_lo, bf16[9,32,256]{2,1,0:T(8,128)(2,1)S(1)} %collective-permute-done.1.y_hi, f32[8,16,256]{2,1,0:T(8,128)S(1)} %get-tuple-element.32.mask, ...), custom_call_target="tpu_custom_call" | custom-call | tf_op jit(solution)/shard_map/conv_inner/pallas_call | solution.py:620
  26.4 0.0 collective-permute-done.4.side_lo
  26.4 0.0 collective-permute-done.5.side_hi
  26.4 0.0 collective-permute-done.2.x_lo
  26.4 0.0 collective-permute-done.3.x_hi
  26.4 2.1 %conv_edge.1 = (bf16[4,16,32,256]{3,2,1,0:T(8,128)(2,1)S(1)}, bf16[11,32,256]{2,1,0:T(8,128)(2,1)S(1)}, bf16[11,32,256]{2,1,0:T(8,128)(2,1)S(1)}) custom-call(bf16[8,16,32,256]{3,2,1,0:T(8,128)(2,1)S(1)} %copy-done, bf16[9,32,256]{2,1,0:T(8,128)(2,1)S(1)} %collective-permute-done.y_lo, bf16[9,32,256]{2,1,0:T(8,128)(2,1)S(1)} %collective-permute-done.1.y_hi, ...), custom_call_target="tpu_custom_call" | custom-call | tf_op jit(solution)/shard_map/conv_edge/pallas_call | solution.py:620
  28.5 1.3 %collective-permute-start.6 = (bf16[11,32,256]{2,1,0:T(8,128)(2,1)S(1)}, bf16[11,32,256]{2,1,0:T(8,128)(2,1)S(1)}, u32[]{:S(2)}, u32[]{:S(2)}) collective-permute-start(bf16[11,32,256]{2,1,0:T(8,128)(2,1)S(1)} %get-tuple-element.41), channel_id=1, source_target_pairs={{0,1},{1,2},{2,3},{3,4},{4,5},{5,6},{6,7},{7,0},{8,9},{9,10},{10,1... | collective-permute-start | bytes 540680 | tf_op jit(solution)/shard_map/ppermute | solution.py:14
  29.9 0.0 collective-permute-start.7
  29.9 3.5 %first_core.1.core = f32[8,16,256]{2,1,0:T(8,128)S(1)} custom-call(bf16[6,16,32,256]{3,2,1,0:T(8,128)(2,1)S(1)} %conv_inner.1.inner, bf16[4,16,32,256]{3,2,1,0:T(8,128)(2,1)S(1)} %get-tuple-element.40.edge, f32[8,16,256]{2,1,0:T(8,128)S(1)} %copy-done.1, bf16[35,32,256]{2,1,0:T(8,128)(2,1)S(1)} %collective-permute-done.2.x_lo, ...), custom_call_target="tpu_custom_call" | custom-call | tf_op jit(solution)/shard_map/first_core/pallas_call | solution.py:620
  33.3 0.0 collective-permute-done.6.f_lo
  33.3 1.4 %collective-permute-done.7.f_hi = bf16[11,32,256]{2,1,0:T(8,128)(2,1)S(1)} collective-permute-done((bf16[11,32,256]{2,1,0:T(8,128)(2,1)S(1)}, bf16[11,32,256]{2,1,0:T(8,128)(2,1)S(1)}, u32[]{:S(2)}, u32[]{:S(2)}) %collective-permute-start.7) | collective-permute-done | bytes 180256 | tf_op jit(solution)/shard_map/ppermute | solution.py:14
  34.8 0.7 %first_rim.1 = (f32[8,16,256]{2,1,0:T(8,128)S(1)}, f32[8,256]{1,0:T(8,128)S(1)}, f32[8,256]{1,0:T(8,128)S(1)}, f32[18,256]{1,0:T(8,128)S(1)}, f32[18,256]{1,0:T(8,128)S(1)}) custom-call(bf16[6,16,32,256]{3,2,1,0:T(8,128)(2,1)S(1)} %conv_inner.1.inner, bf16[4,16,32,256]{3,2,1,0:T(8,128)(2,1)S(1)} %get-tuple-element.40.edge, ...), custom_call_target="tpu_custom_call" | custom-call | tf_op jit(solution)/shard_map/first_rim/pallas_call | solution.py:620
  35.5 0.1 collective-permute-start.8
  35.5 4.9 %collective-permute-start.9 = (f32[18,256]{1,0:T(8,128)S(1)}, f32[18,256]{1,0:T(8,128)S(1)}, u32[]{:S(2)}, u32[]{:S(2)}) collective-permute-start(f32[18,256]{1,0:T(8,128)S(1)} %get-tuple-element.47), channel_id=1, source_target_pairs={{0,120},{8,0},{16,8},{24,16},{32,24},{40,32},{48,40},{56,48},{64,5... | collective-permute-start | bytes 55304 | tf_op jit(solution)/shard_map/ppermute | solution.py:14
  40.5 3.6 %second_core.1 = (f32[8,16,256]{2,1,0:T(8,128)S(1)}, f32[10,16,256]{2,1,0:T(8,128)S(1)}) custom-call(bf16[6,16,32,256]{3,2,1,0:T(8,128)(2,1)S(1)} %conv_inner.1.inner, bf16[4,16,32,256]{3,2,1,0:T(8,128)(2,1)S(1)} %get-tuple-element.40.edge, f32[8,16,256]{2,1,0:T(8,128)S(1)} %copy-done.1, f32[8,16,256]{2,1,0:T(8,128)S(1)} %get-tuple-element.43.first, ...), custom_call_target="tpu_custom_call" | custom-call | tf_op jit(solution)/shard_map/second_core/pallas_call | solution.py:620
  44.1 0.0 collective-permute-done.8.x_lo
  44.1 0.0 collective-permute-done.9.x_hi
  44.1 1.5 %second_rim.1 = (f32[8,16,256]{2,1,0:T(8,128)S(1)}, f32[1,128]{1,0:T(1,128)S(1)}) custom-call(bf16[6,16,32,256]{3,2,1,0:T(8,128)(2,1)S(1)} %conv_inner.1.inner, bf16[4,16,32,256]{3,2,1,0:T(8,128)(2,1)S(1)} %get-tuple-element.40.edge, bf16[11,32,256]{2,1,0:T(8,128)(2,1)S(1)} %collective-permute-done.6.f_lo, ...), custom_call_target="tpu_custom_call" | custom-call | tf_op jit(solution)/shard_map/second_rim/pallas_call | solution.py:620
  45.6 16.2 %all_to_all.5 = f32[128,1,128]{2,1,0:T(1,128)S(1)} all-to-all(f32[128,1,128]{2,1,0:T(1,128)S(1)} %broadcast_in_dim.13), channel_id=1, replica_groups=mesh['sx'=16,'sy'=8] {'sx','sy'}, dimensions={0} | all-to-all | bytes 131072 | tf_op jit(solution)/shard_map/all_to_all | solution.py:745
  61.8 0.9 %final.1 = (f32[8,16,256]{2,1,0:T(8,128)}, f32[8,16,256]{2,1,0:T(8,128)}) custom-call(f32[128,128]{1,0:T(8,128)S(1)} %bitcast.4, f32[8,16,256]{2,1,0:T(8,128)S(1)} %copy-done.1, f32[8,16,256]{2,1,0:T(8,128)S(1)} %get-tuple-element.43.first, f32[8,16,256]{2,1,0:T(8,128)S(1)} %get-tuple-element.51.second), custom_call_target="tpu_custom_call" | custom-call | tf_op jit(solution)/shard_map/final/pallas_call | solution.py:620
  (12 shorter events, 0.1 us)
Async XLA Ops:
  0.6 22.2 %copy-start = (bf16[8,16,32,256]{3,2,1,0:T(8,128)(2,1)S(1)}, bf16[8,16,32,256]{3,2,1,0:T(8,128)(2,1)}, u32[]{:S(2)}) copy-start(bf16[8,16,32,256]{3,2,1,0:T(8,128)(2,1)} %own.3) | copy-start | bytes 6291460
  0.6 12.2 %copy-start.5 = (f32[32]{0:T(128)S(1)}, f32[32]{0:T(128)}, u32[]{:S(2)}) copy-start(f32[32]{0:T(128)} %param.9) | copy-start | bytes 388
  0.7 12.2 %copy-start.3 = (bf16[27,32,32]{2,1,0:T(8,128)(2,1)S(1)}, bf16[27,32,32]{2,1,0:T(8,128)(2,1)}, u32[]{:S(2)}) copy-start(bf16[27,32,32]{2,1,0:T(8,128)(2,1)} %taps.1) | copy-start | bytes 165892
  3.8 22.6 %collective-permute-start.2 = (bf16[35,32,256]{2,1,0:T(8,128)(2,1)}, bf16[35,32,256]{2,1,0:T(8,128)(2,1)S(1)}, u32[]{:S(2)}, u32[]{:S(2)}) collective-permute-start(bf16[35,32,256]{2,1,0:T(8,128)(2,1)} %get-tuple-element.35), channel_id=1, source_target_pairs={{0,8},{8,16},{16,24},{24,32},{32,40},{40,48},{48,56},{56,64},{64,7... | collective-permute-start | bytes 1720328 | tf_op jit(solution)/shard_map/ppermute | solution.py:14
  5.9 20.5 %collective-permute-start.3 = (bf16[35,32,256]{2,1,0:T(8,128)(2,1)}, bf16[35,32,256]{2,1,0:T(8,128)(2,1)S(1)}, u32[]{:S(2)}, u32[]{:S(2)}) collective-permute-start(bf16[35,32,256]{2,1,0:T(8,128)(2,1)} %get-tuple-element.36), channel_id=1, source_target_pairs={{0,120},{8,0},{16,8},{24,16},{32,24},{40,32},{48,40},{56,48},{64,5... | collective-permute-start | bytes 1720328 | tf_op jit(solution)/shard_map/ppermute | solution.py:14
  10.7 4.6 %collective-permute-start = (bf16[9,32,256]{2,1,0:T(8,128)(2,1)}, bf16[9,32,256]{2,1,0:T(8,128)(2,1)S(1)}, u32[]{:S(2)}, u32[]{:S(2)}) collective-permute-start(bf16[9,32,256]{2,1,0:T(8,128)(2,1)} %get-tuple-element.29), channel_id=1, source_target_pairs={{0,1},{1,2},{2,3},{3,4},{4,5},{5,6},{6,7},{7,0},{8,9},{9,10},{10,1... | collective-permute-start | bytes 442376 | tf_op jit(solution)/shard_map/ppermute | solution.py:14
  12.9 5.1 %collective-permute-start.1 = (bf16[9,32,256]{2,1,0:T(8,128)(2,1)}, bf16[9,32,256]{2,1,0:T(8,128)(2,1)S(1)}, u32[]{:S(2)}, u32[]{:S(2)}) collective-permute-start(bf16[9,32,256]{2,1,0:T(8,128)(2,1)} %get-tuple-element.30), channel_id=1, source_target_pairs={{0,7},{1,0},{2,1},{3,2},{4,3},{5,4},{6,5},{7,6},{8,15},{9,8},{10,9... | collective-permute-start | bytes 442376 | tf_op jit(solution)/shard_map/ppermute | solution.py:14
  12.9 0.9 %copy-start.4 = (f32[8,16,256]{2,1,0:T(8,128)S(1)}, f32[8,16,256]{2,1,0:T(8,128)}, u32[]{:S(2)}) copy-start(f32[8,16,256]{2,1,0:T(8,128)} %get-tuple-element.31.mask) | copy-start | bytes 393220
  18.0 8.4 %collective-permute-start.4 = (bf16[5,32,256]{2,1,0:T(8,128)(2,1)S(1)}, bf16[5,32,256]{2,1,0:T(8,128)(2,1)S(1)}, u32[]{:S(2)}, u32[]{:S(2)}) collective-permute-start(bf16[5,32,256]{2,1,0:T(8,128)(2,1)S(1)} %get-tuple-element.37), channel_id=1, source_target_pairs={{0,8},{8,16},{16,24},{24,32},{32,40},{40,48},{48,56},{56,64},{64,7... | collective-permute-start | bytes 245768 | tf_op jit(solution)/shard_map/ppermute | solution.py:14
  18.0 8.3 %collective-permute-start.5 = (bf16[5,32,256]{2,1,0:T(8,128)(2,1)S(1)}, bf16[5,32,256]{2,1,0:T(8,128)(2,1)S(1)}, u32[]{:S(2)}, u32[]{:S(2)}) collective-permute-start(bf16[5,32,256]{2,1,0:T(8,128)(2,1)S(1)} %get-tuple-element.38), channel_id=1, source_target_pairs={{0,120},{8,0},{16,8},{24,16},{32,24},{40,32},{48,40},{56,48},{64,5... | collective-permute-start | bytes 245768 | tf_op jit(solution)/shard_map/ppermute | solution.py:14
  22.8 3.6 %copy-start.1 = (f32[8,16,256]{2,1,0:T(8,128)S(1)}, f32[8,16,256]{2,1,0:T(8,128)}, u32[]{:S(2)}) copy-start(f32[8,16,256]{2,1,0:T(8,128)} %get-tuple-element.39.start) | copy-start | bytes 393220
  22.8 3.6 %copy-start.2 = (f32[8,16,256]{2,1,0:T(8,128)S(1)}, f32[8,16,256]{2,1,0:T(8,128)}, u32[]{:S(2)}) copy-start(f32[8,16,256]{2,1,0:T(8,128)} %ridge.5) | copy-start | bytes 393220
  28.5 4.8 %collective-permute-start.6 = (bf16[11,32,256]{2,1,0:T(8,128)(2,1)S(1)}, bf16[11,32,256]{2,1,0:T(8,128)(2,1)S(1)}, u32[]{:S(2)}, u32[]{:S(2)}) collective-permute-start(bf16[11,32,256]{2,1,0:T(8,128)(2,1)S(1)} %get-tuple-element.41), channel_id=1, source_target_pairs={{0,1},{1,2},{2,3},{3,4},{4,5},{5,6},{6,7},{7,0},{8,9},{9,10},{10,1... | collective-permute-start | bytes 540680 | tf_op jit(solution)/shard_map/ppermute | solution.py:14
  29.9 4.9 %collective-permute-start.7 = (bf16[11,32,256]{2,1,0:T(8,128)(2,1)S(1)}, bf16[11,32,256]{2,1,0:T(8,128)(2,1)S(1)}, u32[]{:S(2)}, u32[]{:S(2)}) collective-permute-start(bf16[11,32,256]{2,1,0:T(8,128)(2,1)S(1)} %get-tuple-element.42), channel_id=1, source_target_pairs={{0,7},{1,0},{2,1},{3,2},{4,3},{5,4},{6,5},{7,6},{8,15},{9,8},{10,9... | collective-permute-start | bytes 540680 | tf_op jit(solution)/shard_map/ppermute | solution.py:14
  35.5 8.6 %collective-permute-start.8 = (f32[18,256]{1,0:T(8,128)S(1)}, f32[18,256]{1,0:T(8,128)S(1)}, u32[]{:S(2)}, u32[]{:S(2)}) collective-permute-start(f32[18,256]{1,0:T(8,128)S(1)} %get-tuple-element.46), channel_id=1, source_target_pairs={{0,8},{8,16},{16,24},{24,32},{32,40},{40,48},{48,56},{56,64},{64,7... | collective-permute-start | bytes 55304 | tf_op jit(solution)/shard_map/ppermute | solution.py:14
  35.5 8.5 %collective-permute-start.9 = (f32[18,256]{1,0:T(8,128)S(1)}, f32[18,256]{1,0:T(8,128)S(1)}, u32[]{:S(2)}, u32[]{:S(2)}) collective-permute-start(f32[18,256]{1,0:T(8,128)S(1)} %get-tuple-element.47), channel_id=1, source_target_pairs={{0,120},{8,0},{16,8},{24,16},{32,24},{40,32},{48,40},{56,48},{64,5... | collective-permute-start | bytes 55304 | tf_op jit(solution)/shard_map/ppermute | solution.py:14

commit v13 on v11

--- a/solution.py
+++ b/solution.py
@@ -31,10 +31,10 @@
     ids_in,
     occupancy_in,
     target_in,
-    mask,
-    start,
-    y_hi,
-    y_lo,
+    mask_out,
+    start_out,
+    y_hi_out,
+    y_lo_out,
     x_hi,
     x_lo,
     ids,
@@ -43,6 +43,10 @@
     columns,
     present,
     message,
+    mask,
+    start,
+    y_hi,
+    y_lo,
     sems,
 ):
     rows, cols, channels, depth = own.shape
@@ -64,6 +68,10 @@
                 (message.at[1, 0 : 2 * cols], x_lo.at[0 : 2 * cols]),
                 (message.at[0, 2 * cols :], x_hi.at[2 * cols :]),
                 (message.at[1, 2 * cols :], x_lo.at[2 * cols :]),
+                (mask, mask_out),
+                (start, start_out),
+                (y_lo, y_lo_out),
+                (y_hi, y_hi_out),
             )
         )
     ]
@@ -81,9 +89,11 @@
     for x in range(rows):
         blocks = [present[pl.ds(2 * cols * x + z, cols, stride=2), :] for z in range(depth // half)]
         mask[x] = occupancy[x].astype(jnp.float32) * jnp.concatenate(blocks, axis=1)
+    copies[13].start()
     copies[2].wait()
     for x in range(rows):
         start[x] = mask[x] * target[x]
+    copies[14].start()
     for k, (pair, row) in enumerate((((rows - 2, rows - 1), rows - 1), ((0, 1), 0))):
         pieces = (jnp.concatenate([mask[x] for x in pair], axis=0), *paired(start[row]))
         for at, piece in enumerate(pieces):
@@ -97,6 +107,7 @@
             out[x] = columns[k, x, 0] * mask[x, y : y + 1, :].astype(jnp.bfloat16)
         terms = jnp.concatenate([*three(column_of(start, y)), blank], axis=0)
         out[rows] = terms.astype(jnp.bfloat16)
+        copies[15 + k].start()
     for copy in copies[9:]:
         copy.wait()
 
@@ -552,8 +563,17 @@
         delta = jnp.concatenate(parts, axis=0) * scale
         add_products(sums, (3, 4), (start[x], first[x], delta))
         out[x] = out[x] + delta
-    row = jnp.zeros((8, 128), jnp.float32)
     lane = lanes((8, 128))
+    line = lax.broadcasted_iota(jnp.int32, (8, 128), 0)
+
+    def fold(s, e, axis, steps):
+        for step in steps:
+            t, d = two_sum(s, pltpu.roll(s, step, axis))
+            s, e = (t, (e + pltpu.roll(e, step, axis)) + d)
+        return s, e
+
+    total = jnp.zeros((8, 128), jnp.float32)
+    error = jnp.zeros((8, 128), jnp.float32)
     for k, (s, e) in enumerate(sums):
         while s.shape[0] > 8:
             half = s.shape[0] // 2
@@ -563,13 +583,12 @@
             half = s.shape[1] // 2
             t, d = two_sum(s[:, :half], s[:, half:])
             s, e = (t, e[:, :half] + e[:, half:] + d)
-        for axis, steps in ((0, (4, 2, 1)), (1, (64, 32, 16, 8, 4, 2, 1))):
-            for step in steps:
-                t, d = two_sum(s, pltpu.roll(s, step, axis))
-                s, e = (t, (e + pltpu.roll(e, step, axis)) + d)
-        row = jnp.where(lane == k, s, row)
-        row = jnp.where(lane == 8 + k, e, row)
-    share[...] = row[0:1]
+        s, e = fold(s, e, 0, (4, 2, 1))
+        total = jnp.where(line == k, s, total)
+        error = jnp.where(line == k, e, error)
+    total, error = fold(total, error, 1, (64, 32, 16, 8, 4, 2, 1))
+    placed = jnp.where(lane == line, total, 0.0) + jnp.where(lane == line + 8, error, 0.0)
+    share[...] = jnp.sum(placed, axis=0, keepdims=True)
 
 
 def final_kernel(shares, start, first, second, solution_out, residual_out):
@@ -636,7 +655,7 @@
         prep_kernel,
         out_shape=[jax.ShapeDtypeStruct(shape, dtype) for shape, dtype in outs],
         in_specs=[pl.BlockSpec(memory_space=pl.ANY)] * 4,
-        out_specs=[vmem] * 4 + [pl.BlockSpec(memory_space=pl.ANY)] * 2,
+        out_specs=[pl.BlockSpec(memory_space=pl.ANY)] * 6,
         scratch_shapes=[
             pltpu.VMEM(blocks.shape, jnp.int32),
             pltpu.VMEM(occupancy.shape, jnp.int32),
@@ -644,7 +663,8 @@
             pltpu.VMEM((2, rows, 1, channels, depth), bf16),
             pltpu.VMEM((blocks.shape[0], depth // block_ids.shape[2]), f32),
             pltpu.VMEM((2, *edge_rows[0]), bf16),
-            pltpu.SemaphoreType.DMA((13,)),
+            *(pltpu.VMEM(shape, dtype) for shape, dtype in outs[:4]),
+            pltpu.SemaphoreType.DMA((17,)),
         ],
         compiler_params=pltpu.CompilerParams(vmem_limit_bytes=PREP_LIMIT << 20),
         name="prep",

time: 62.9 us -> 62.3 us (level)
  Pallas kernels: 19.4 us -> 18.7 us
    pallas_call x1, Pallas kernels: 3.12 us -> 2.48 us  [per_device(): pl.pallas_call(prep_kernel, out_shape=[jax.ShapeDtypeStruct(shape, dtype)...]
where the time goes in v13:
time: 62.3 us; the launch traced here: 62.1 us
  starting transfers between devices  20.3 us (33%)
  Pallas kernels  18.7 us (30%)
  blocking collectives  16.2 us (26%)
  waiting for transfers between devices  5.17 us (8%)
  local copies, waits for them, and re-layouts  0.96 us (2%)
  between operations  0.82 us (1%)
    ppermute x10, starting transfers between devices, shift(): lax.ppermute(value, axis, [(i, (i + step) % peers) for i in range(peers)])  20.3 us
    pallas_call x9, Pallas kernels, call(): pl.pallas_call(kernel, out_shape=[jax.ShapeDtypeStruct(shape, dtype) for...  16.2 us
    all_to_all x1, blocking collectives, per_device(): lax.all_to_all(jnp.broadcast_to(share[None], (peers, 1, 128)), AXES, 0, 0)  16.2 us
    ppermute x10, waiting for transfers between devices, shift(): lax.ppermute(value, axis, [(i, (i + step) % peers) for i in range(peers)])  5.17 us
    pallas_call x1, Pallas kernels, per_device(): pl.pallas_call(prep_kernel, out_shape=[jax.ShapeDtypeStruct(shape, dtype)...  2.48 us
  transfers between devices with their start and end apart: 10, of which 3 were waited for; matrix products, arithmetic and copies ran while one was open for 0% of the time, Pallas kernels for 18%

profile of v13, /device:TPU:1, one launch (start us, length us, event | category | flops | bytes accessed | tf_op | source)
XLA Modules:
  0.0 62.1 jit_solution(10137964334125031524)
XLA Ops:
  0.7 2.5 %prep.1 = (f32[8,16,256]{2,1,0:T(8,128)}, f32[8,16,256]{2,1,0:T(8,128)}, bf16[9,32,256]{2,1,0:T(8,128)(2,1)}, bf16[9,32,256]{2,1,0:T(8,128)(2,1)}, bf16[35,32,25...) custom-call(bf16[8,16,32,256]{3,2,1,0:T(8,128)(2,1)} %own.5, s32[256,27]{1,0:T(8,128)} %bitcast.7, ...), custom_call_target="tpu_custom_call" | custom-call | tf_op jit(solution)/shard_map/prep/pallas_call | solution.py:654
  3.2 2.1 %collective-permute-start.2 = (bf16[35,32,256]{2,1,0:T(8,128)(2,1)}, bf16[35,32,256]{2,1,0:T(8,128)(2,1)S(1)}, u32[]{:S(2)}, u32[]{:S(2)}) collective-permute-start(bf16[35,32,256]{2,1,0:T(8,128)(2,1)} %get-tuple-element.31), channel_id=1, source_target_pairs={{0,8},{8,16},{16,24},{24,32},{32,40},{40,48},{48,56},{56,64},{64,7... | collective-permute-start | bytes 1720328 | tf_op jit(solution)/shard_map/ppermute | solution.py:14
  5.3 4.8 %collective-permute-start.3 = (bf16[35,32,256]{2,1,0:T(8,128)(2,1)}, bf16[35,32,256]{2,1,0:T(8,128)(2,1)S(1)}, u32[]{:S(2)}, u32[]{:S(2)}) collective-permute-start(bf16[35,32,256]{2,1,0:T(8,128)(2,1)} %get-tuple-element.32), channel_id=1, source_target_pairs={{0,120},{8,0},{16,8},{24,16},{32,24},{40,32},{48,40},{56,48},{64,5... | collective-permute-start | bytes 1720328 | tf_op jit(solution)/shard_map/ppermute | solution.py:14
  10.1 2.1 %collective-permute-start = (bf16[9,32,256]{2,1,0:T(8,128)(2,1)}, bf16[9,32,256]{2,1,0:T(8,128)(2,1)S(1)}, u32[]{:S(2)}, u32[]{:S(2)}) collective-permute-start(bf16[9,32,256]{2,1,0:T(8,128)(2,1)} %get-tuple-element.25), channel_id=1, source_target_pairs={{0,1},{1,2},{2,3},{3,4},{4,5},{5,6},{6,7},{7,0},{8,9},{9,10},{10,1... | collective-permute-start | bytes 442376 | tf_op jit(solution)/shard_map/ppermute | solution.py:14
  12.2 0.0 collective-permute-start.1
  12.2 0.0 copy-start.4
  12.2 0.9 %copy-done.4 = f32[8,16,256]{2,1,0:T(8,128)S(1)} copy-done((f32[8,16,256]{2,1,0:T(8,128)S(1)}, f32[8,16,256]{2,1,0:T(8,128)}, u32[]{:S(2)}) %copy-start.4) | copy-done | bytes 131096
  13.1 0.4 weights.1
  13.6 1.1 %collective-permute-done.y_lo = bf16[9,32,256]{2,1,0:T(8,128)(2,1)S(1)} collective-permute-done((bf16[9,32,256]{2,1,0:T(8,128)(2,1)}, bf16[9,32,256]{2,1,0:T(8,128)(2,1)S(1)}, u32[]{:S(2)}, u32[]{:S(2)}) %collective-permute-start) | collective-permute-done | bytes 147488 | tf_op jit(solution)/shard_map/ppermute | solution.py:14
  14.6 2.7 %collective-permute-done.1.y_hi = bf16[9,32,256]{2,1,0:T(8,128)(2,1)S(1)} collective-permute-done((bf16[9,32,256]{2,1,0:T(8,128)(2,1)}, bf16[9,32,256]{2,1,0:T(8,128)(2,1)S(1)}, u32[]{:S(2)}, u32[]{:S(2)}) %collective-permute-start.1) | collective-permute-done | bytes 147488 | tf_op jit(solution)/shard_map/ppermute | solution.py:14
  17.3 0.1 collective-permute-start.4
  17.4 4.8 %collective-permute-start.5 = (bf16[5,32,256]{2,1,0:T(8,128)(2,1)S(1)}, bf16[5,32,256]{2,1,0:T(8,128)(2,1)S(1)}, u32[]{:S(2)}, u32[]{:S(2)}) collective-permute-start(bf16[5,32,256]{2,1,0:T(8,128)(2,1)S(1)} %get-tuple-element.34), channel_id=1, source_target_pairs={{0,120},{8,0},{16,8},{24,16},{32,24},{40,32},{48,40},{56,48},{64,5... | collective-permute-start | bytes 245768 | tf_op jit(solution)/shard_map/ppermute | solution.py:14
  22.2 3.5 %conv_inner.1.inner = bf16[6,16,32,256]{3,2,1,0:T(8,128)(2,1)S(1)} custom-call(bf16[8,16,32,256]{3,2,1,0:T(8,128)(2,1)S(1)} %copy-done, bf16[9,32,256]{2,1,0:T(8,128)(2,1)S(1)} %collective-permute-done.y_lo, bf16[9,32,256]{2,1,0:T(8,128)(2,1)S(1)} %collective-permute-done.1.y_hi, f32[8,16,256]{2,1,0:T(8,128)S(1)} %get-tuple-element.28.mask, ...), custom_call_target="tpu_custom_call" | custom-call | tf_op jit(solution)/shard_map/conv_inner/pallas_call | solution.py:639
  25.7 0.0 collective-permute-done.4.side_lo
  25.7 0.0 collective-permute-done.5.side_hi
  25.7 0.0 collective-permute-done.2.x_lo
  25.8 0.0 collective-permute-done.3.x_hi
  25.8 2.1 %conv_edge.1 = (bf16[4,16,32,256]{3,2,1,0:T(8,128)(2,1)S(1)}, bf16[11,32,256]{2,1,0:T(8,128)(2,1)S(1)}, bf16[11,32,256]{2,1,0:T(8,128)(2,1)S(1)}) custom-call(bf16[8,16,32,256]{3,2,1,0:T(8,128)(2,1)S(1)} %copy-done, bf16[9,32,256]{2,1,0:T(8,128)(2,1)S(1)} %collective-permute-done.y_lo, bf16[9,32,256]{2,1,0:T(8,128)(2,1)S(1)} %collective-permute-done.1.y_hi, ...), custom_call_target="tpu_custom_call" | custom-call | tf_op jit(solution)/shard_map/conv_edge/pallas_call | solution.py:639
  27.9 1.3 %collective-permute-start.6 = (bf16[11,32,256]{2,1,0:T(8,128)(2,1)S(1)}, bf16[11,32,256]{2,1,0:T(8,128)(2,1)S(1)}, u32[]{:S(2)}, u32[]{:S(2)}) collective-permute-start(bf16[11,32,256]{2,1,0:T(8,128)(2,1)S(1)} %get-tuple-element.37), channel_id=1, source_target_pairs={{0,1},{1,2},{2,3},{3,4},{4,5},{5,6},{6,7},{7,0},{8,9},{9,10},{10,1... | collective-permute-start | bytes 540680 | tf_op jit(solution)/shard_map/ppermute | solution.py:14
  29.2 0.0 collective-permute-start.7
  29.2 3.5 %first_core.1.core = f32[8,16,256]{2,1,0:T(8,128)S(1)} custom-call(bf16[6,16,32,256]{3,2,1,0:T(8,128)(2,1)S(1)} %conv_inner.1.inner, bf16[4,16,32,256]{3,2,1,0:T(8,128)(2,1)S(1)} %get-tuple-element.36.edge, f32[8,16,256]{2,1,0:T(8,128)S(1)} %copy-done.1, bf16[35,32,256]{2,1,0:T(8,128)(2,1)S(1)} %collective-permute-done.2.x_lo, ...), custom_call_target="tpu_custom_call" | custom-call | tf_op jit(solution)/shard_map/first_core/pallas_call | solution.py:639
  32.7 0.0 collective-permute-done.6.f_lo
  32.7 1.4 %collective-permute-done.7.f_hi = bf16[11,32,256]{2,1,0:T(8,128)(2,1)S(1)} collective-permute-done((bf16[11,32,256]{2,1,0:T(8,128)(2,1)S(1)}, bf16[11,32,256]{2,1,0:T(8,128)(2,1)S(1)}, u32[]{:S(2)}, u32[]{:S(2)}) %collective-permute-start.7) | collective-permute-done | bytes 180256 | tf_op jit(solution)/shard_map/ppermute | solution.py:14
  34.1 0.7 %first_rim.1 = (f32[8,16,256]{2,1,0:T(8,128)S(1)}, f32[8,256]{1,0:T(8,128)S(1)}, f32[8,256]{1,0:T(8,128)S(1)}, f32[18,256]{1,0:T(8,128)S(1)}, f32[18,256]{1,0:T(8,128)S(1)}) custom-call(bf16[6,16,32,256]{3,2,1,0:T(8,128)(2,1)S(1)} %conv_inner.1.inner, bf16[4,16,32,256]{3,2,1,0:T(8,128)(2,1)S(1)} %get-tuple-element.36.edge, ...), custom_call_target="tpu_custom_call" | custom-call | tf_op jit(solution)/shard_map/first_rim/pallas_call | solution.py:639
  34.8 0.1 collective-permute-start.8
  34.9 4.9 %collective-permute-start.9 = (f32[18,256]{1,0:T(8,128)S(1)}, f32[18,256]{1,0:T(8,128)S(1)}, u32[]{:S(2)}, u32[]{:S(2)}) collective-permute-start(f32[18,256]{1,0:T(8,128)S(1)} %get-tuple-element.43), channel_id=1, source_target_pairs={{0,120},{8,0},{16,8},{24,16},{32,24},{40,32},{48,40},{56,48},{64,5... | collective-permute-start | bytes 55304 | tf_op jit(solution)/shard_map/ppermute | solution.py:14
  39.8 3.6 %second_core.1 = (f32[8,16,256]{2,1,0:T(8,128)S(1)}, f32[10,16,256]{2,1,0:T(8,128)S(1)}) custom-call(bf16[6,16,32,256]{3,2,1,0:T(8,128)(2,1)S(1)} %conv_inner.1.inner, bf16[4,16,32,256]{3,2,1,0:T(8,128)(2,1)S(1)} %get-tuple-element.36.edge, f32[8,16,256]{2,1,0:T(8,128)S(1)} %copy-done.1, f32[8,16,256]{2,1,0:T(8,128)S(1)} %get-tuple-element.39.first, ...), custom_call_target="tpu_custom_call" | custom-call | tf_op jit(solution)/shard_map/second_core/pallas_call | solution.py:639
  43.4 0.0 collective-permute-done.8.x_lo
  43.4 0.0 collective-permute-done.9.x_hi
  43.4 1.5 %second_rim.1 = (f32[8,16,256]{2,1,0:T(8,128)S(1)}, f32[1,128]{1,0:T(1,128)S(1)}) custom-call(bf16[6,16,32,256]{3,2,1,0:T(8,128)(2,1)S(1)} %conv_inner.1.inner, bf16[4,16,32,256]{3,2,1,0:T(8,128)(2,1)S(1)} %get-tuple-element.36.edge, bf16[11,32,256]{2,1,0:T(8,128)(2,1)S(1)} %collective-permute-done.6.f_lo, ...), custom_call_target="tpu_custom_call" | custom-call | tf_op jit(solution)/shard_map/second_rim/pallas_call | solution.py:639
  45.0 16.2 %all_to_all.5 = f32[128,1,128]{2,1,0:T(1,128)S(1)} all-to-all(f32[128,1,128]{2,1,0:T(1,128)S(1)} %broadcast_in_dim.13), channel_id=1, replica_groups=mesh['sx'=16,'sy'=8] {'sx','sy'}, dimensions={0} | all-to-all | bytes 131072 | tf_op jit(solution)/shard_map/all_to_all | solution.py:764
  61.2 0.9 %final.1 = (f32[8,16,256]{2,1,0:T(8,128)}, f32[8,16,256]{2,1,0:T(8,128)}) custom-call(f32[128,128]{1,0:T(8,128)S(1)} %bitcast.4, f32[8,16,256]{2,1,0:T(8,128)S(1)} %copy-done.1, f32[8,16,256]{2,1,0:T(8,128)S(1)} %get-tuple-element.39.first, f32[8,16,256]{2,1,0:T(8,128)S(1)} %get-tuple-element.47.second), custom_call_target="tpu_custom_call" | custom-call | tf_op jit(solution)/shard_map/final/pallas_call | solution.py:639
  (12 shorter events, 0.1 us)
Async XLA Ops:
  0.6 21.5 %copy-start = (bf16[8,16,32,256]{3,2,1,0:T(8,128)(2,1)S(1)}, bf16[8,16,32,256]{3,2,1,0:T(8,128)(2,1)}, u32[]{:S(2)}) copy-start(bf16[8,16,32,256]{3,2,1,0:T(8,128)(2,1)} %own.5) | copy-start | bytes 6291460
  0.6 11.6 %copy-start.5 = (f32[32]{0:T(128)S(1)}, f32[32]{0:T(128)}, u32[]{:S(2)}) copy-start(f32[32]{0:T(128)} %param.9) | copy-start | bytes 388
  0.7 11.6 %copy-start.3 = (bf16[27,32,32]{2,1,0:T(8,128)(2,1)S(1)}, bf16[27,32,32]{2,1,0:T(8,128)(2,1)}, u32[]{:S(2)}) copy-start(bf16[27,32,32]{2,1,0:T(8,128)(2,1)} %taps.1) | copy-start | bytes 165892
  3.2 22.6 %collective-permute-start.2 = (bf16[35,32,256]{2,1,0:T(8,128)(2,1)}, bf16[35,32,256]{2,1,0:T(8,128)(2,1)S(1)}, u32[]{:S(2)}, u32[]{:S(2)}) collective-permute-start(bf16[35,32,256]{2,1,0:T(8,128)(2,1)} %get-tuple-element.31), channel_id=1, source_target_pairs={{0,8},{8,16},{16,24},{24,32},{32,40},{40,48},{48,56},{56,64},{64,7... | collective-permute-start | bytes 1720328 | tf_op jit(solution)/shard_map/ppermute | solution.py:14
  5.3 20.5 %collective-permute-start.3 = (bf16[35,32,256]{2,1,0:T(8,128)(2,1)}, bf16[35,32,256]{2,1,0:T(8,128)(2,1)S(1)}, u32[]{:S(2)}, u32[]{:S(2)}) collective-permute-start(bf16[35,32,256]{2,1,0:T(8,128)(2,1)} %get-tuple-element.32), channel_id=1, source_target_pairs={{0,120},{8,0},{16,8},{24,16},{32,24},{40,32},{48,40},{56,48},{64,5... | collective-permute-start | bytes 1720328 | tf_op jit(solution)/shard_map/ppermute | solution.py:14
  10.1 4.6 %collective-permute-start = (bf16[9,32,256]{2,1,0:T(8,128)(2,1)}, bf16[9,32,256]{2,1,0:T(8,128)(2,1)S(1)}, u32[]{:S(2)}, u32[]{:S(2)}) collective-permute-start(bf16[9,32,256]{2,1,0:T(8,128)(2,1)} %get-tuple-element.25), channel_id=1, source_target_pairs={{0,1},{1,2},{2,3},{3,4},{4,5},{5,6},{6,7},{7,0},{8,9},{9,10},{10,1... | collective-permute-start | bytes 442376 | tf_op jit(solution)/shard_map/ppermute | solution.py:14
  12.2 5.1 %collective-permute-start.1 = (bf16[9,32,256]{2,1,0:T(8,128)(2,1)}, bf16[9,32,256]{2,1,0:T(8,128)(2,1)S(1)}, u32[]{:S(2)}, u32[]{:S(2)}) collective-permute-start(bf16[9,32,256]{2,1,0:T(8,128)(2,1)} %get-tuple-element.26), channel_id=1, source_target_pairs={{0,7},{1,0},{2,1},{3,2},{4,3},{5,4},{6,5},{7,6},{8,15},{9,8},{10,9... | collective-permute-start | bytes 442376 | tf_op jit(solution)/shard_map/ppermute | solution.py:14
  12.2 0.9 %copy-start.4 = (f32[8,16,256]{2,1,0:T(8,128)S(1)}, f32[8,16,256]{2,1,0:T(8,128)}, u32[]{:S(2)}) copy-start(f32[8,16,256]{2,1,0:T(8,128)} %get-tuple-element.27.mask) | copy-start | bytes 393220
  17.3 8.4 %collective-permute-start.4 = (bf16[5,32,256]{2,1,0:T(8,128)(2,1)S(1)}, bf16[5,32,256]{2,1,0:T(8,128)(2,1)S(1)}, u32[]{:S(2)}, u32[]{:S(2)}) collective-permute-start(bf16[5,32,256]{2,1,0:T(8,128)(2,1)S(1)} %get-tuple-element.33), channel_id=1, source_target_pairs={{0,8},{8,16},{16,24},{24,32},{32,40},{40,48},{48,56},{56,64},{64,7... | collective-permute-start | bytes 245768 | tf_op jit(solution)/shard_map/ppermute | solution.py:14
  17.4 8.3 %collective-permute-start.5 = (bf16[5,32,256]{2,1,0:T(8,128)(2,1)S(1)}, bf16[5,32,256]{2,1,0:T(8,128)(2,1)S(1)}, u32[]{:S(2)}, u32[]{:S(2)}) collective-permute-start(bf16[5,32,256]{2,1,0:T(8,128)(2,1)S(1)} %get-tuple-element.34), channel_id=1, source_target_pairs={{0,120},{8,0},{16,8},{24,16},{32,24},{40,32},{48,40},{56,48},{64,5... | collective-permute-start | bytes 245768 | tf_op jit(solution)/shard_map/ppermute | solution.py:14
  22.2 3.6 %copy-start.1 = (f32[8,16,256]{2,1,0:T(8,128)S(1)}, f32[8,16,256]{2,1,0:T(8,128)}, u32[]{:S(2)}) copy-start(f32[8,16,256]{2,1,0:T(8,128)} %get-tuple-element.35.start) | copy-start | bytes 393220
  22.2 3.6 %copy-start.2 = (f32[8,16,256]{2,1,0:T(8,128)S(1)}, f32[8,16,256]{2,1,0:T(8,128)}, u32[]{:S(2)}) copy-start(f32[8,16,256]{2,1,0:T(8,128)} %ridge.5) | copy-start | bytes 393220
  27.9 4.8 %collective-permute-start.6 = (bf16[11,32,256]{2,1,0:T(8,128)(2,1)S(1)}, bf16[11,32,256]{2,1,0:T(8,128)(2,1)S(1)}, u32[]{:S(2)}, u32[]{:S(2)}) collective-permute-start(bf16[11,32,256]{2,1,0:T(8,128)(2,1)S(1)} %get-tuple-element.37), channel_id=1, source_target_pairs={{0,1},{1,2},{2,3},{3,4},{4,5},{5,6},{6,7},{7,0},{8,9},{9,10},{10,1... | collective-permute-start | bytes 540680 | tf_op jit(solution)/shard_map/ppermute | solution.py:14
  29.2 4.9 %collective-permute-start.7 = (bf16[11,32,256]{2,1,0:T(8,128)(2,1)S(1)}, bf16[11,32,256]{2,1,0:T(8,128)(2,1)S(1)}, u32[]{:S(2)}, u32[]{:S(2)}) collective-permute-start(bf16[11,32,256]{2,1,0:T(8,128)(2,1)S(1)} %get-tuple-element.38), channel_id=1, source_target_pairs={{0,7},{1,0},{2,1},{3,2},{4,3},{5,4},{6,5},{7,6},{8,15},{9,8},{10,9... | collective-permute-start | bytes 540680 | tf_op jit(solution)/shard_map/ppermute | solution.py:14
  34.8 8.6 %collective-permute-start.8 = (f32[18,256]{1,0:T(8,128)S(1)}, f32[18,256]{1,0:T(8,128)S(1)}, u32[]{:S(2)}, u32[]{:S(2)}) collective-permute-start(f32[18,256]{1,0:T(8,128)S(1)} %get-tuple-element.42), channel_id=1, source_target_pairs={{0,8},{8,16},{16,24},{24,32},{32,40},{40,48},{48,56},{56,64},{64,7... | collective-permute-start | bytes 55304 | tf_op jit(solution)/shard_map/ppermute | solution.py:14
  34.9 8.5 %collective-permute-start.9 = (f32[18,256]{1,0:T(8,128)S(1)}, f32[18,256]{1,0:T(8,128)S(1)}, u32[]{:S(2)}, u32[]{:S(2)}) collective-permute-start(f32[18,256]{1,0:T(8,128)S(1)} %get-tuple-element.43), channel_id=1, source_target_pairs={{0,120},{8,0},{16,8},{24,16},{32,24},{40,32},{48,40},{56,48},{64,5... | collective-permute-start | bytes 55304 | tf_op jit(solution)/shard_map/ppermute | solution.py:14

commit v14 on v13

--- a/solution.py
+++ b/solution.py
@@ -493,7 +493,9 @@
         sums[k] = (s, sums[k][1] + (t + e))
 
 
-def second_core_kernel(inner, edge, start, first, ridge, out, grams, smooth):
+def second_core_kernel(
+    inner, edge, f_lo, f_hi, start, first, w_lo, w_hi, ridge, out, grams, smooth
+):
     n, cols, channels, depth = inner.shape
     scale = 1.0 / (8 * channels)
 
@@ -517,21 +519,9 @@
     sums = [(zero, zero) for _ in PRODUCTS]
     for x in range(n + 2):
         add_products(sums, range(5), (start[x], first[x], out[x]))
-    for k, (s, e) in enumerate(sums):
-        grams[2 * k] = s
-        grams[2 * k + 1] = e
-
-
-def second_rim_kernel(
-    inner, edge, f_lo, f_hi, start, first, w_lo, w_hi, x_lo, x_hi, core, grams, out, share
-):
-    n, cols, channels, depth = inner.shape
     rows = n + 2
-    scale = 1.0 / (8 * channels)
     lane = lanes((channels, depth))
     flags = mesh_flags()
-    out[...] = core[...]
-    sums = [(grams[2 * k], grams[2 * k + 1]) for k in range(5)]
     added = []
     for ref, rim, flag, y in ((f_lo, w_lo, flags[0], 0), (f_hi, w_hi, flags[1], cols - 1)):
         g = [ref[x + 1].astype(jnp.float32) * (rim[x : x + 1] * flag) for x in range(rows)]
@@ -541,6 +531,21 @@
     for delta, y in zip(added, (0, cols - 1)):
         for x in range(rows):
             out[x, y : y + 1, :] = out[x, y : y + 1, :] + delta[x : x + 1]
+    for k, (s, e) in enumerate(sums):
+        grams[2 * k] = s
+        grams[2 * k + 1] = e
+
+
+def second_rim_kernel(
+    edge, f_lo, f_hi, start, first, x_lo, x_hi, core, grams, out, share
+):
+    rows, cols, depth = start.shape
+    channels = edge.shape[2]
+    scale = 1.0 / (8 * channels)
+    lane = lanes((channels, depth))
+    flags = mesh_flags()
+    out[...] = core[...]
+    sums = [(grams[2 * k], grams[2 * k + 1]) for k in range(5)]
     for rim, at, row, x, far in ((x_lo, 0, 1, 0, 0), (x_hi, 3, 2, rows - 1, rows + 1)):
 
         def product(y):
@@ -745,7 +750,7 @@
     r_lo, r_hi = (shift(r_hi, "sx", 1), shift(r_lo, "sx", -1))
     core, grams = call(
         second_core_kernel,
-        (inner, edge, residual, first, ridge),
+        (inner, edge, f_lo, f_hi, residual, first, w_lo, w_hi, ridge),
         [plane, ((2 * len(PRODUCTS), cols, depth), f32)],
         [((rows, cols, channels, depth), f32)],
         10,
@@ -753,7 +758,7 @@
     )
     second, share = call(
         second_rim_kernel,
-        (inner, edge, f_lo, f_hi, residual, first, w_lo, w_hi, r_lo, r_hi, core, grams),
+        (edge, f_lo, f_hi, residual, first, r_lo, r_hi, core, grams),
         [plane, ((1, 128), f32)],
         [],
         4,

time: 62.3 us -> 62 us (level)
  no operation moved by 1% of the time
where the time goes in v14:
time: 62 us; the launch traced here: 61.9 us
  starting transfers between devices  20.3 us (33%)
  Pallas kernels  18.8 us (30%)
  blocking collectives  15.9 us (26%)
  waiting for transfers between devices  5.17 us (8%)
  local copies, waits for them, and re-layouts  0.96 us (2%)
  between operations  0.82 us (1%)
    ppermute x10, starting transfers between devices, shift(): lax.ppermute(value, axis, [(i, (i + step) % peers) for i in range(peers)])  20.3 us
    pallas_call x9, Pallas kernels, call(): pl.pallas_call(kernel, out_shape=[jax.ShapeDtypeStruct(shape, dtype) for...  16.3 us
    all_to_all x1, blocking collectives, per_device(): lax.all_to_all(jnp.broadcast_to(share[None], (peers, 1, 128)), AXES, 0, 0)  15.9 us
    ppermute x10, waiting for transfers between devices, shift(): lax.ppermute(value, axis, [(i, (i + step) % peers) for i in range(peers)])  5.17 us
    pallas_call x1, Pallas kernels, per_device(): pl.pallas_call(prep_kernel, out_shape=[jax.ShapeDtypeStruct(shape, dtype)...  2.48 us
  transfers between devices with their start and end apart: 10, of which 3 were waited for; matrix products, arithmetic and copies ran while one was open for 0% of the time, Pallas kernels for 18%

profile of v14, /device:TPU:1, one launch (start us, length us, event | category | flops | bytes accessed | tf_op | source)
XLA Modules:
  0.0 61.9 jit_solution(12195706546003076208)
XLA Ops:
  0.7 2.5 %prep.1 = (f32[8,16,256]{2,1,0:T(8,128)}, f32[8,16,256]{2,1,0:T(8,128)}, bf16[9,32,256]{2,1,0:T(8,128)(2,1)}, bf16[9,32,256]{2,1,0:T(8,128)(2,1)}, bf16[35,32,25...) custom-call(bf16[8,16,32,256]{3,2,1,0:T(8,128)(2,1)} %own.5, s32[256,27]{1,0:T(8,128)} %bitcast.7, ...), custom_call_target="tpu_custom_call" | custom-call | tf_op jit(solution)/shard_map/prep/pallas_call | solution.py:659
  3.2 2.1 %collective-permute-start.2 = (bf16[35,32,256]{2,1,0:T(8,128)(2,1)}, bf16[35,32,256]{2,1,0:T(8,128)(2,1)S(1)}, u32[]{:S(2)}, u32[]{:S(2)}) collective-permute-start(bf16[35,32,256]{2,1,0:T(8,128)(2,1)} %get-tuple-element.27), channel_id=1, source_target_pairs={{0,8},{8,16},{16,24},{24,32},{32,40},{40,48},{48,56},{56,64},{64,7... | collective-permute-start | bytes 1720328 | tf_op jit(solution)/shard_map/ppermute | solution.py:14
  5.3 4.8 %collective-permute-start.3 = (bf16[35,32,256]{2,1,0:T(8,128)(2,1)}, bf16[35,32,256]{2,1,0:T(8,128)(2,1)S(1)}, u32[]{:S(2)}, u32[]{:S(2)}) collective-permute-start(bf16[35,32,256]{2,1,0:T(8,128)(2,1)} %get-tuple-element.28), channel_id=1, source_target_pairs={{0,120},{8,0},{16,8},{24,16},{32,24},{40,32},{48,40},{56,48},{64,5... | collective-permute-start | bytes 1720328 | tf_op jit(solution)/shard_map/ppermute | solution.py:14
  10.1 2.1 %collective-permute-start = (bf16[9,32,256]{2,1,0:T(8,128)(2,1)}, bf16[9,32,256]{2,1,0:T(8,128)(2,1)S(1)}, u32[]{:S(2)}, u32[]{:S(2)}) collective-permute-start(bf16[9,32,256]{2,1,0:T(8,128)(2,1)} %get-tuple-element.25), channel_id=1, source_target_pairs={{0,1},{1,2},{2,3},{3,4},{4,5},{5,6},{6,7},{7,0},{8,9},{9,10},{10,1... | collective-permute-start | bytes 442376 | tf_op jit(solution)/shard_map/ppermute | solution.py:14
  12.2 0.0 collective-permute-start.1
  12.2 0.0 copy-start.4
  12.2 0.9 %copy-done.4 = f32[8,16,256]{2,1,0:T(8,128)S(1)} copy-done((f32[8,16,256]{2,1,0:T(8,128)S(1)}, f32[8,16,256]{2,1,0:T(8,128)}, u32[]{:S(2)}) %copy-start.4) | copy-done | bytes 131096
  13.1 0.4 weights.1
  13.6 1.1 %collective-permute-done.y_lo = bf16[9,32,256]{2,1,0:T(8,128)(2,1)S(1)} collective-permute-done((bf16[9,32,256]{2,1,0:T(8,128)(2,1)}, bf16[9,32,256]{2,1,0:T(8,128)(2,1)S(1)}, u32[]{:S(2)}, u32[]{:S(2)}) %collective-permute-start) | collective-permute-done | bytes 147488 | tf_op jit(solution)/shard_map/ppermute | solution.py:14
  14.6 2.7 %collective-permute-done.1.y_hi = bf16[9,32,256]{2,1,0:T(8,128)(2,1)S(1)} collective-permute-done((bf16[9,32,256]{2,1,0:T(8,128)(2,1)}, bf16[9,32,256]{2,1,0:T(8,128)(2,1)S(1)}, u32[]{:S(2)}, u32[]{:S(2)}) %collective-permute-start.1) | collective-permute-done | bytes 147488 | tf_op jit(solution)/shard_map/ppermute | solution.py:14
  17.3 0.1 collective-permute-start.4
  17.4 4.8 %collective-permute-start.5 = (bf16[5,32,256]{2,1,0:T(8,128)(2,1)S(1)}, bf16[5,32,256]{2,1,0:T(8,128)(2,1)S(1)}, u32[]{:S(2)}, u32[]{:S(2)}) collective-permute-start(bf16[5,32,256]{2,1,0:T(8,128)(2,1)S(1)} %get-tuple-element.32), channel_id=1, source_target_pairs={{0,120},{8,0},{16,8},{24,16},{32,24},{40,32},{48,40},{56,48},{64,5... | collective-permute-start | bytes 245768 | tf_op jit(solution)/shard_map/ppermute | solution.py:14
  22.2 3.5 %conv_inner.1.inner = bf16[6,16,32,256]{3,2,1,0:T(8,128)(2,1)S(1)} custom-call(bf16[8,16,32,256]{3,2,1,0:T(8,128)(2,1)S(1)} %copy-done, bf16[9,32,256]{2,1,0:T(8,128)(2,1)S(1)} %collective-permute-done.y_lo, bf16[9,32,256]{2,1,0:T(8,128)(2,1)S(1)} %collective-permute-done.1.y_hi, f32[8,16,256]{2,1,0:T(8,128)S(1)} %get-tuple-element.33.mask, ...), custom_call_target="tpu_custom_call" | custom-call | tf_op jit(solution)/shard_map/conv_inner/pallas_call | solution.py:644
  25.7 0.0 collective-permute-done.4.side_lo
  25.7 0.0 collective-permute-done.5.side_hi
  25.7 0.0 collective-permute-done.2.x_lo
  25.8 0.0 collective-permute-done.3.x_hi
  25.8 2.1 %conv_edge.1 = (bf16[4,16,32,256]{3,2,1,0:T(8,128)(2,1)S(1)}, bf16[11,32,256]{2,1,0:T(8,128)(2,1)S(1)}, bf16[11,32,256]{2,1,0:T(8,128)(2,1)S(1)}) custom-call(bf16[8,16,32,256]{3,2,1,0:T(8,128)(2,1)S(1)} %copy-done, bf16[9,32,256]{2,1,0:T(8,128)(2,1)S(1)} %collective-permute-done.y_lo, bf16[9,32,256]{2,1,0:T(8,128)(2,1)S(1)} %collective-permute-done.1.y_hi, ...), custom_call_target="tpu_custom_call" | custom-call | tf_op jit(solution)/shard_map/conv_edge/pallas_call | solution.py:644
  27.9 1.3 %collective-permute-start.6 = (bf16[11,32,256]{2,1,0:T(8,128)(2,1)S(1)}, bf16[11,32,256]{2,1,0:T(8,128)(2,1)S(1)}, u32[]{:S(2)}, u32[]{:S(2)}) collective-permute-start(bf16[11,32,256]{2,1,0:T(8,128)(2,1)S(1)} %get-tuple-element.37), channel_id=1, source_target_pairs={{0,1},{1,2},{2,3},{3,4},{4,5},{5,6},{6,7},{7,0},{8,9},{9,10},{10,1... | collective-permute-start | bytes 540680 | tf_op jit(solution)/shard_map/ppermute | solution.py:14
  29.2 0.0 collective-permute-start.7
  29.2 3.5 %first_core.1.core = f32[8,16,256]{2,1,0:T(8,128)S(1)} custom-call(bf16[6,16,32,256]{3,2,1,0:T(8,128)(2,1)S(1)} %conv_inner.1.inner, bf16[4,16,32,256]{3,2,1,0:T(8,128)(2,1)S(1)} %get-tuple-element.36.edge, f32[8,16,256]{2,1,0:T(8,128)S(1)} %copy-done.1, bf16[35,32,256]{2,1,0:T(8,128)(2,1)S(1)} %collective-permute-done.2.x_lo, ...), custom_call_target="tpu_custom_call" | custom-call | tf_op jit(solution)/shard_map/first_core/pallas_call | solution.py:644
  32.7 0.0 collective-permute-done.6.f_lo
  32.7 1.4 %collective-permute-done.7.f_hi = bf16[11,32,256]{2,1,0:T(8,128)(2,1)S(1)} collective-permute-done((bf16[11,32,256]{2,1,0:T(8,128)(2,1)S(1)}, bf16[11,32,256]{2,1,0:T(8,128)(2,1)S(1)}, u32[]{:S(2)}, u32[]{:S(2)}) %collective-permute-start.7) | collective-permute-done | bytes 180256 | tf_op jit(solution)/shard_map/ppermute | solution.py:14
  34.1 0.7 %first_rim.1 = (f32[8,16,256]{2,1,0:T(8,128)S(1)}, f32[8,256]{1,0:T(8,128)S(1)}, f32[8,256]{1,0:T(8,128)S(1)}, f32[18,256]{1,0:T(8,128)S(1)}, f32[18,256]{1,0:T(8,128)S(1)}) custom-call(bf16[6,16,32,256]{3,2,1,0:T(8,128)(2,1)S(1)} %conv_inner.1.inner, bf16[4,16,32,256]{3,2,1,0:T(8,128)(2,1)S(1)} %get-tuple-element.36.edge, ...), custom_call_target="tpu_custom_call" | custom-call | tf_op jit(solution)/shard_map/first_rim/pallas_call | solution.py:644
  34.8 0.1 collective-permute-start.8
  34.9 4.9 %collective-permute-start.9 = (f32[18,256]{1,0:T(8,128)S(1)}, f32[18,256]{1,0:T(8,128)S(1)}, u32[]{:S(2)}, u32[]{:S(2)}) collective-permute-start(f32[18,256]{1,0:T(8,128)S(1)} %get-tuple-element.41), channel_id=1, source_target_pairs={{0,120},{8,0},{16,8},{24,16},{32,24},{40,32},{48,40},{56,48},{64,5... | collective-permute-start | bytes 55304 | tf_op jit(solution)/shard_map/ppermute | solution.py:14
  39.8 3.9 %second_core.1 = (f32[8,16,256]{2,1,0:T(8,128)S(1)}, f32[10,16,256]{2,1,0:T(8,128)S(1)}) custom-call(bf16[6,16,32,256]{3,2,1,0:T(8,128)(2,1)S(1)} %conv_inner.1.inner, bf16[4,16,32,256]{3,2,1,0:T(8,128)(2,1)S(1)} %get-tuple-element.36.edge, bf16[11,32,256]{2,1,0:T(8,128)(2,1)S(1)} %collective-permute-done.6.f_lo, ...), custom_call_target="tpu_custom_call" | custom-call | tf_op jit(solution)/shard_map/second_core/pallas_call | solution.py:644
  43.7 0.0 collective-permute-done.8.x_lo
  43.8 0.0 collective-permute-done.9.x_hi
  43.8 1.2 %second_rim.1 = (f32[8,16,256]{2,1,0:T(8,128)S(1)}, f32[1,128]{1,0:T(1,128)S(1)}) custom-call(bf16[4,16,32,256]{3,2,1,0:T(8,128)(2,1)S(1)} %get-tuple-element.36.edge, bf16[11,32,256]{2,1,0:T(8,128)(2,1)S(1)} %collective-permute-done.6.f_lo, bf16[11,32,256]{2,1,0:T(8,128)(2,1)S(1)} %collective-permute-done.7.f_hi, f32[8,16,256]{2,1,0:T(8,128)S(1)} %copy-done.1, ...), custom_call_target="tpu_custom_call" | custom-call | tf_op jit(solution)/shard_map/second_rim/pallas_call | solution.py:644
  45.0 15.9 %all_to_all.5 = f32[128,1,128]{2,1,0:T(1,128)S(1)} all-to-all(f32[128,1,128]{2,1,0:T(1,128)S(1)} %broadcast_in_dim.13), channel_id=1, replica_groups=mesh['sx'=16,'sy'=8] {'sx','sy'}, dimensions={0} | all-to-all | bytes 131072 | tf_op jit(solution)/shard_map/all_to_all | solution.py:769
  60.9 0.9 %final.1 = (f32[8,16,256]{2,1,0:T(8,128)}, f32[8,16,256]{2,1,0:T(8,128)}) custom-call(f32[128,128]{1,0:T(8,128)S(1)} %bitcast.4, f32[8,16,256]{2,1,0:T(8,128)S(1)} %copy-done.1, f32[8,16,256]{2,1,0:T(8,128)S(1)} %get-tuple-element.39.first, f32[8,16,256]{2,1,0:T(8,128)S(1)} %get-tuple-element.47.second), custom_call_target="tpu_custom_call" | custom-call | tf_op jit(solution)/shard_map/final/pallas_call | solution.py:644
  (12 shorter events, 0.1 us)
Async XLA Ops:
  0.6 21.5 %copy-start = (bf16[8,16,32,256]{3,2,1,0:T(8,128)(2,1)S(1)}, bf16[8,16,32,256]{3,2,1,0:T(8,128)(2,1)}, u32[]{:S(2)}) copy-start(bf16[8,16,32,256]{3,2,1,0:T(8,128)(2,1)} %own.5) | copy-start | bytes 6291460
  0.6 11.6 %copy-start.5 = (f32[32]{0:T(128)S(1)}, f32[32]{0:T(128)}, u32[]{:S(2)}) copy-start(f32[32]{0:T(128)} %param.9) | copy-start | bytes 388
  0.7 11.6 %copy-start.3 = (bf16[27,32,32]{2,1,0:T(8,128)(2,1)S(1)}, bf16[27,32,32]{2,1,0:T(8,128)(2,1)}, u32[]{:S(2)}) copy-start(bf16[27,32,32]{2,1,0:T(8,128)(2,1)} %taps.1) | copy-start | bytes 165892
  3.2 22.6 %collective-permute-start.2 = (bf16[35,32,256]{2,1,0:T(8,128)(2,1)}, bf16[35,32,256]{2,1,0:T(8,128)(2,1)S(1)}, u32[]{:S(2)}, u32[]{:S(2)}) collective-permute-start(bf16[35,32,256]{2,1,0:T(8,128)(2,1)} %get-tuple-element.27), channel_id=1, source_target_pairs={{0,8},{8,16},{16,24},{24,32},{32,40},{40,48},{48,56},{56,64},{64,7... | collective-permute-start | bytes 1720328 | tf_op jit(solution)/shard_map/ppermute | solution.py:14
  5.3 20.5 %collective-permute-start.3 = (bf16[35,32,256]{2,1,0:T(8,128)(2,1)}, bf16[35,32,256]{2,1,0:T(8,128)(2,1)S(1)}, u32[]{:S(2)}, u32[]{:S(2)}) collective-permute-start(bf16[35,32,256]{2,1,0:T(8,128)(2,1)} %get-tuple-element.28), channel_id=1, source_target_pairs={{0,120},{8,0},{16,8},{24,16},{32,24},{40,32},{48,40},{56,48},{64,5... | collective-permute-start | bytes 1720328 | tf_op jit(solution)/shard_map/ppermute | solution.py:14
  10.1 4.6 %collective-permute-start = (bf16[9,32,256]{2,1,0:T(8,128)(2,1)}, bf16[9,32,256]{2,1,0:T(8,128)(2,1)S(1)}, u32[]{:S(2)}, u32[]{:S(2)}) collective-permute-start(bf16[9,32,256]{2,1,0:T(8,128)(2,1)} %get-tuple-element.25), channel_id=1, source_target_pairs={{0,1},{1,2},{2,3},{3,4},{4,5},{5,6},{6,7},{7,0},{8,9},{9,10},{10,1... | collective-permute-start | bytes 442376 | tf_op jit(solution)/shard_map/ppermute | solution.py:14
  12.2 5.1 %collective-permute-start.1 = (bf16[9,32,256]{2,1,0:T(8,128)(2,1)}, bf16[9,32,256]{2,1,0:T(8,128)(2,1)S(1)}, u32[]{:S(2)}, u32[]{:S(2)}) collective-permute-start(bf16[9,32,256]{2,1,0:T(8,128)(2,1)} %get-tuple-element.26), channel_id=1, source_target_pairs={{0,7},{1,0},{2,1},{3,2},{4,3},{5,4},{6,5},{7,6},{8,15},{9,8},{10,9... | collective-permute-start | bytes 442376 | tf_op jit(solution)/shard_map/ppermute | solution.py:14
  12.2 0.9 %copy-start.4 = (f32[8,16,256]{2,1,0:T(8,128)S(1)}, f32[8,16,256]{2,1,0:T(8,128)}, u32[]{:S(2)}) copy-start(f32[8,16,256]{2,1,0:T(8,128)} %get-tuple-element.29.mask) | copy-start | bytes 393220
  17.3 8.4 %collective-permute-start.4 = (bf16[5,32,256]{2,1,0:T(8,128)(2,1)S(1)}, bf16[5,32,256]{2,1,0:T(8,128)(2,1)S(1)}, u32[]{:S(2)}, u32[]{:S(2)}) collective-permute-start(bf16[5,32,256]{2,1,0:T(8,128)(2,1)S(1)} %get-tuple-element.31), channel_id=1, source_target_pairs={{0,8},{8,16},{16,24},{24,32},{32,40},{40,48},{48,56},{56,64},{64,7... | collective-permute-start | bytes 245768 | tf_op jit(solution)/shard_map/ppermute | solution.py:14
  17.4 8.3 %collective-permute-start.5 = (bf16[5,32,256]{2,1,0:T(8,128)(2,1)S(1)}, bf16[5,32,256]{2,1,0:T(8,128)(2,1)S(1)}, u32[]{:S(2)}, u32[]{:S(2)}) collective-permute-start(bf16[5,32,256]{2,1,0:T(8,128)(2,1)S(1)} %get-tuple-element.32), channel_id=1, source_target_pairs={{0,120},{8,0},{16,8},{24,16},{32,24},{40,32},{48,40},{56,48},{64,5... | collective-permute-start | bytes 245768 | tf_op jit(solution)/shard_map/ppermute | solution.py:14
  22.2 3.6 %copy-start.1 = (f32[8,16,256]{2,1,0:T(8,128)S(1)}, f32[8,16,256]{2,1,0:T(8,128)}, u32[]{:S(2)}) copy-start(f32[8,16,256]{2,1,0:T(8,128)} %get-tuple-element.35.start) | copy-start | bytes 393220
  22.2 3.6 %copy-start.2 = (f32[8,16,256]{2,1,0:T(8,128)S(1)}, f32[8,16,256]{2,1,0:T(8,128)}, u32[]{:S(2)}) copy-start(f32[8,16,256]{2,1,0:T(8,128)} %ridge.5) | copy-start | bytes 393220
  27.9 4.8 %collective-permute-start.6 = (bf16[11,32,256]{2,1,0:T(8,128)(2,1)S(1)}, bf16[11,32,256]{2,1,0:T(8,128)(2,1)S(1)}, u32[]{:S(2)}, u32[]{:S(2)}) collective-permute-start(bf16[11,32,256]{2,1,0:T(8,128)(2,1)S(1)} %get-tuple-element.37), channel_id=1, source_target_pairs={{0,1},{1,2},{2,3},{3,4},{4,5},{5,6},{6,7},{7,0},{8,9},{9,10},{10,1... | collective-permute-start | bytes 540680 | tf_op jit(solution)/shard_map/ppermute | solution.py:14
  29.2 4.9 %collective-permute-start.7 = (bf16[11,32,256]{2,1,0:T(8,128)(2,1)S(1)}, bf16[11,32,256]{2,1,0:T(8,128)(2,1)S(1)}, u32[]{:S(2)}, u32[]{:S(2)}) collective-permute-start(bf16[11,32,256]{2,1,0:T(8,128)(2,1)S(1)} %get-tuple-element.38), channel_id=1, source_target_pairs={{0,7},{1,0},{2,1},{3,2},{4,3},{5,4},{6,5},{7,6},{8,15},{9,8},{10,9... | collective-permute-start | bytes 540680 | tf_op jit(solution)/shard_map/ppermute | solution.py:14
  34.8 8.9 %collective-permute-start.8 = (f32[18,256]{1,0:T(8,128)S(1)}, f32[18,256]{1,0:T(8,128)S(1)}, u32[]{:S(2)}, u32[]{:S(2)}) collective-permute-start(f32[18,256]{1,0:T(8,128)S(1)} %get-tuple-element.40), channel_id=1, source_target_pairs={{0,8},{8,16},{16,24},{24,32},{32,40},{40,48},{48,56},{56,64},{64,7... | collective-permute-start | bytes 55304 | tf_op jit(solution)/shard_map/ppermute | solution.py:14
  34.9 8.9 %collective-permute-start.9 = (f32[18,256]{1,0:T(8,128)S(1)}, f32[18,256]{1,0:T(8,128)S(1)}, u32[]{:S(2)}, u32[]{:S(2)}) collective-permute-start(f32[18,256]{1,0:T(8,128)S(1)} %get-tuple-element.41), channel_id=1, source_target_pairs={{0,120},{8,0},{16,8},{24,16},{32,24},{40,32},{48,40},{56,48},{64,5... | collective-permute-start | bytes 55304 | tf_op jit(solution)/shard_map/ppermute | solution.py:14

commit v15 on v14

--- a/solution.py
+++ b/solution.py
@@ -146,10 +146,10 @@
     return [jnp.where(k, 1.0, 0.0) for k in keep]
 
 
-def conv_block(grid, masks, wide, bias_all, lane, grid_x, y, out, out_x):
+def conv_block(window_rows, masks, wide, bias_all, lane, y, out, out_x):
     channels, depth = bias_all.shape
     window = jnp.concatenate(
-        [grid[grid_x + k, y : y + 4].reshape(4 * channels, depth) for k in range(4)], axis=0
+        [ref[x, y : y + 4].reshape(4 * channels, depth) for ref, x in window_rows], axis=0
     )
     parts = jnp.dot(wide[...], window, preferred_element_type=jnp.float32)
     low = pltpu.roll(parts[0 : 4 * channels], 1, 1)
@@ -186,7 +186,7 @@
     return lambda y: mask[x, y : y + 1, :]
 
 
-def conv_inner_kernel(own, y_lo, y_hi, mask, wide, bias, out, grid):
+def conv_inner_kernel(own, y_lo, y_hi, mask, wide, bias, out, kept, grid):
     rows, cols, channels, depth = own.shape
     flags = mesh_flags()
 
@@ -195,13 +195,16 @@
         return carry
 
     lax.fori_loop(0, rows, fill, 0)
+    for k, x in enumerate((0, 1, rows - 2, rows - 1)):
+        kept[k] = grid[x]
     lane = lax.broadcasted_iota(jnp.int32, (4 * channels, depth), 1)
     bias_all = bias[...]
 
     def pair(i, carry):
         masks = (mask_of(mask, 2 * i + 1), mask_of(mask, 2 * i + 2))
         for y in range(0, cols, 2):
-            conv_block(grid, masks, wide, bias_all, lane, 2 * i, y, out, 2 * i)
+            window_rows = [(grid, 2 * i + k) for k in range(4)]
+            conv_block(window_rows, masks, wide, bias_all, lane, y, out, 2 * i)
         return carry
 
     lax.fori_loop(0, rows // 2 - 1, pair, 0)
@@ -224,9 +227,7 @@
 
 
 def conv_edge_kernel(
-    own,
-    y_lo,
-    y_hi,
+    kept,
     x_lo,
     x_hi,
     side_lo,
@@ -243,7 +244,8 @@
     grid,
     side_mask,
 ):
-    rows, cols, channels, depth = own.shape
+    rows, cols, depth = mask.shape
+    channels = kept.shape[2]
     flags = mesh_flags()
     for k, side in enumerate((x_lo, x_hi)):
         both = side[2 * cols].astype(jnp.float32) * flags[2 + k]
@@ -254,14 +256,12 @@
             clear = splat(flags[2 + k], (channels, depth))
             fill_row(
                 grid,
-                6 * k + x,
+                2 * k + x,
                 mask_of(side_mask, 2 * k + x),
                 lambda y: ref[x * cols + y],
                 side[2 * x] * clear,
                 side[2 * x + 1] * clear,
             )
-        fill_own(grid, 2 + x, own, mask, y_lo, y_hi, flags, x)
-        fill_own(grid, 4 + x, own, mask, y_lo, y_hi, flags, rows - 2 + x)
     lane = lax.broadcasted_iota(jnp.int32, (4 * channels, depth), 1)
     bias_all = bias[...]
     for side, masks in (
@@ -269,7 +269,9 @@
         (1, (mask_of(mask, rows - 1), mask_of(side_mask, 2))),
     ):
         for y in range(0, cols, 2):
-            conv_block(grid, masks, wide, bias_all, lane, 4 * side, y, out, 2 * side)
+            pairs = (grid, kept) if side == 0 else (kept, grid)
+            window_rows = [(ref, 2 * side + k) for ref in pairs for k in range(2)]
+            conv_block(window_rows, masks, wide, bias_all, lane, y, out, 2 * side)
     lane = lanes((channels, depth))
     places = [field_at(inner, out, x) for x in range(rows + 2)]
     blank = jnp.zeros((channels - 3 * rows, depth), jnp.float32)
@@ -685,6 +687,7 @@
         "weights",
     )
     grid_scratch = ((rows, cols + 2, channels, depth), bf16)
+    kept_grid = ((4, cols + 2, channels, depth), bf16)
     inner_shape = (rows - 2, cols, channels, depth)
     edge_shape = (4, cols, channels, depth)
     side_shape = (5, channels, depth)
@@ -697,10 +700,10 @@
         "sides",
     )
     side_lo, side_hi = (shift(side_hi, "sx", 1), shift(side_lo, "sx", -1))
-    (inner,) = call(
+    inner, kept = call(
         conv_inner_kernel,
         (features, y_lo, y_hi, weight_mask, wide, bias),
-        [(inner_shape, bf16)],
+        [(inner_shape, bf16), kept_grid],
         [grid_scratch],
         12,
         "conv_inner",
@@ -709,9 +712,7 @@
     edge, f_hi, f_lo = call(
         conv_edge_kernel,
         (
-            features,
-            y_lo,
-            y_hi,
+            kept,
             x_lo,
             x_hi,
             side_lo,
@@ -724,7 +725,7 @@
             ridge,
         ),
         [(edge_shape, bf16), column, column],
-        [grid_scratch, ((4, cols, depth), f32)],
+        [kept_grid, ((4, cols, depth), f32)],
         12,
         "conv_edge",
     )

time: 62 us -> 62 us (level)
  no operation moved by 1% of the time
where the time goes in v15:
time: 62 us; the launch traced here: 61.9 us
  starting transfers between devices  20.2 us (33%)
  Pallas kernels  18.8 us (30%)
  blocking collectives  15.9 us (26%)
  waiting for transfers between devices  5.17 us (8%)
  local copies, waits for them, and re-layouts  0.96 us (2%)
  between operations  0.82 us (1%)
    ppermute x10, starting transfers between devices, shift(): lax.ppermute(value, axis, [(i, (i + step) % peers) for i in range(peers)])  20.2 us
    pallas_call x9, Pallas kernels, call(): pl.pallas_call(kernel, out_shape=[jax.ShapeDtypeStruct(shape, dtype) for...  16.3 us
    all_to_all x1, blocking collectives, per_device(): lax.all_to_all(jnp.broadcast_to(share[None], (peers, 1, 128)), AXES, 0, 0)  15.9 us
    ppermute x10, waiting for transfers between devices, shift(): lax.ppermute(value, axis, [(i, (i + step) % peers) for i in range(peers)])  5.17 us
    pallas_call x1, Pallas kernels, per_device(): pl.pallas_call(prep_kernel, out_shape=[jax.ShapeDtypeStruct(shape, dtype)...  2.49 us
  transfers between devices with their start and end apart: 10, of which 3 were waited for; matrix products, arithmetic and copies ran while one was open for 0% of the time, Pallas kernels for 18%

profile of v15, /device:TPU:1, one launch (start us, length us, event | category | flops | bytes accessed | tf_op | source)
XLA Modules:
  0.0 61.9 jit_solution(10571364765208644314)
XLA Ops:
  0.7 2.5 %prep.1 = (f32[8,16,256]{2,1,0:T(8,128)}, f32[8,16,256]{2,1,0:T(8,128)}, bf16[9,32,256]{2,1,0:T(8,128)(2,1)}, bf16[9,32,256]{2,1,0:T(8,128)(2,1)}, bf16[35,32,25...) custom-call(bf16[8,16,32,256]{3,2,1,0:T(8,128)(2,1)} %own.3, s32[256,27]{1,0:T(8,128)} %bitcast.7, ...), custom_call_target="tpu_custom_call" | custom-call | tf_op jit(solution)/shard_map/prep/pallas_call | solution.py:661
  3.2 2.1 %collective-permute-start.2 = (bf16[35,32,256]{2,1,0:T(8,128)(2,1)}, bf16[35,32,256]{2,1,0:T(8,128)(2,1)S(1)}, u32[]{:S(2)}, u32[]{:S(2)}) collective-permute-start(bf16[35,32,256]{2,1,0:T(8,128)(2,1)} %get-tuple-element.34), channel_id=1, source_target_pairs={{0,8},{8,16},{16,24},{24,32},{32,40},{40,48},{48,56},{56,64},{64,7... | collective-permute-start | bytes 1720328 | tf_op jit(solution)/shard_map/ppermute | solution.py:14
  5.3 4.8 %collective-permute-start.3 = (bf16[35,32,256]{2,1,0:T(8,128)(2,1)}, bf16[35,32,256]{2,1,0:T(8,128)(2,1)S(1)}, u32[]{:S(2)}, u32[]{:S(2)}) collective-permute-start(bf16[35,32,256]{2,1,0:T(8,128)(2,1)} %get-tuple-element.35), channel_id=1, source_target_pairs={{0,120},{8,0},{16,8},{24,16},{32,24},{40,32},{48,40},{56,48},{64,5... | collective-permute-start | bytes 1720328 | tf_op jit(solution)/shard_map/ppermute | solution.py:14
  10.1 2.1 %collective-permute-start = (bf16[9,32,256]{2,1,0:T(8,128)(2,1)}, bf16[9,32,256]{2,1,0:T(8,128)(2,1)S(1)}, u32[]{:S(2)}, u32[]{:S(2)}) collective-permute-start(bf16[9,32,256]{2,1,0:T(8,128)(2,1)} %get-tuple-element.27), channel_id=1, source_target_pairs={{0,1},{1,2},{2,3},{3,4},{4,5},{5,6},{6,7},{7,0},{8,9},{9,10},{10,1... | collective-permute-start | bytes 442376 | tf_op jit(solution)/shard_map/ppermute | solution.py:14
  12.2 0.0 collective-permute-start.1
  12.2 0.0 copy-start.4
  12.3 0.9 %copy-done.4 = f32[8,16,256]{2,1,0:T(8,128)S(1)} copy-done((f32[8,16,256]{2,1,0:T(8,128)S(1)}, f32[8,16,256]{2,1,0:T(8,128)}, u32[]{:S(2)}) %copy-start.4) | copy-done | bytes 131096
  13.2 0.4 weights.1
  13.6 1.1 %collective-permute-done.y_lo = bf16[9,32,256]{2,1,0:T(8,128)(2,1)S(1)} collective-permute-done((bf16[9,32,256]{2,1,0:T(8,128)(2,1)}, bf16[9,32,256]{2,1,0:T(8,128)(2,1)S(1)}, u32[]{:S(2)}, u32[]{:S(2)}) %collective-permute-start) | collective-permute-done | bytes 147488 | tf_op jit(solution)/shard_map/ppermute | solution.py:14
  14.7 2.7 %collective-permute-done.1.y_hi = bf16[9,32,256]{2,1,0:T(8,128)(2,1)S(1)} collective-permute-done((bf16[9,32,256]{2,1,0:T(8,128)(2,1)}, bf16[9,32,256]{2,1,0:T(8,128)(2,1)S(1)}, u32[]{:S(2)}, u32[]{:S(2)}) %collective-permute-start.1) | collective-permute-done | bytes 147488 | tf_op jit(solution)/shard_map/ppermute | solution.py:14
  17.3 0.1 collective-permute-start.4
  17.4 4.8 %collective-permute-start.5 = (bf16[5,32,256]{2,1,0:T(8,128)(2,1)S(1)}, bf16[5,32,256]{2,1,0:T(8,128)(2,1)S(1)}, u32[]{:S(2)}, u32[]{:S(2)}) collective-permute-start(bf16[5,32,256]{2,1,0:T(8,128)(2,1)S(1)} %get-tuple-element.37), channel_id=1, source_target_pairs={{0,120},{8,0},{16,8},{24,16},{32,24},{40,32},{48,40},{56,48},{64,5... | collective-permute-start | bytes 245768 | tf_op jit(solution)/shard_map/ppermute | solution.py:14
  22.2 3.6 %conv_inner.1 = (bf16[6,16,32,256]{3,2,1,0:T(8,128)(2,1)S(1)}, bf16[4,18,32,256]{3,2,1,0:T(8,128)(2,1)S(1)}) custom-call(bf16[8,16,32,256]{3,2,1,0:T(8,128)(2,1)S(1)} %copy-done, bf16[9,32,256]{2,1,0:T(8,128)(2,1)S(1)} %collective-permute-done.y_lo, bf16[9,32,256]{2,1,0:T(8,128)(2,1)S(1)} %collective-permute-done.1.y_hi, ...), custom_call_target="tpu_custom_call" | custom-call | tf_op jit(solution)/shard_map/conv_inner/pallas_call | solution.py:646
  25.8 0.0 collective-permute-done.4.side_lo
  25.8 0.0 collective-permute-done.5.side_hi
  25.8 0.0 collective-permute-done.2.x_lo
  25.8 0.0 collective-permute-done.3.x_hi
  25.9 2.1 %conv_edge.1 = (bf16[4,16,32,256]{3,2,1,0:T(8,128)(2,1)S(1)}, bf16[11,32,256]{2,1,0:T(8,128)(2,1)S(1)}, bf16[11,32,256]{2,1,0:T(8,128)(2,1)S(1)}) custom-call(bf16[4,18,32,256]{3,2,1,0:T(8,128)(2,1)S(1)} %get-tuple-element.33.kept, bf16[35,32,256]{2,1,0:T(8,128)(2,1)S(1)} %collective-permute-done.2.x_lo, ...), custom_call_target="tpu_custom_call" | custom-call | tf_op jit(solution)/shard_map/conv_edge/pallas_call | solution.py:646
  27.9 1.3 %collective-permute-start.6 = (bf16[11,32,256]{2,1,0:T(8,128)(2,1)S(1)}, bf16[11,32,256]{2,1,0:T(8,128)(2,1)S(1)}, u32[]{:S(2)}, u32[]{:S(2)}) collective-permute-start(bf16[11,32,256]{2,1,0:T(8,128)(2,1)S(1)} %get-tuple-element.41), channel_id=1, source_target_pairs={{0,1},{1,2},{2,3},{3,4},{4,5},{5,6},{6,7},{7,0},{8,9},{9,10},{10,1... | collective-permute-start | bytes 540680 | tf_op jit(solution)/shard_map/ppermute | solution.py:14
  29.2 0.0 collective-permute-start.7
  29.2 3.5 %first_core.1.core = f32[8,16,256]{2,1,0:T(8,128)S(1)} custom-call(bf16[6,16,32,256]{3,2,1,0:T(8,128)(2,1)S(1)} %get-tuple-element.38.inner, bf16[4,16,32,256]{3,2,1,0:T(8,128)(2,1)S(1)} %get-tuple-element.40.edge, f32[8,16,256]{2,1,0:T(8,128)S(1)} %copy-done.1, bf16[35,32,256]{2,1,0:T(8,128)(2,1)S(1)} %collective-permute-done.2.x_lo, ...), custom_call_target="tpu_custom_call" | custom-call | tf_op jit(solution)/shard_map/first_core/pallas_call | solution.py:646
  32.7 0.0 collective-permute-done.6.f_lo
  32.7 1.4 %collective-permute-done.7.f_hi = bf16[11,32,256]{2,1,0:T(8,128)(2,1)S(1)} collective-permute-done((bf16[11,32,256]{2,1,0:T(8,128)(2,1)S(1)}, bf16[11,32,256]{2,1,0:T(8,128)(2,1)S(1)}, u32[]{:S(2)}, u32[]{:S(2)}) %collective-permute-start.7) | collective-permute-done | bytes 180256 | tf_op jit(solution)/shard_map/ppermute | solution.py:14
  34.1 0.7 %first_rim.1 = (f32[8,16,256]{2,1,0:T(8,128)S(1)}, f32[8,256]{1,0:T(8,128)S(1)}, f32[8,256]{1,0:T(8,128)S(1)}, f32[18,256]{1,0:T(8,128)S(1)}, f32[18,256]{1,0:T(8,128)S(1)}) custom-call(bf16[6,16,32,256]{3,2,1,0:T(8,128)(2,1)S(1)} %get-tuple-element.38.inner, bf16[4,16,32,256]{3,2,1,0:T(8,128)(2,1)S(1)} %get-tuple-element.40.edge, ...), custom_call_target="tpu_custom_call" | custom-call | tf_op jit(solution)/shard_map/first_rim/pallas_call | solution.py:646
  34.8 0.1 collective-permute-start.8
  34.9 4.9 %collective-permute-start.9 = (f32[18,256]{1,0:T(8,128)S(1)}, f32[18,256]{1,0:T(8,128)S(1)}, u32[]{:S(2)}, u32[]{:S(2)}) collective-permute-start(f32[18,256]{1,0:T(8,128)S(1)} %get-tuple-element.45), channel_id=1, source_target_pairs={{0,120},{8,0},{16,8},{24,16},{32,24},{40,32},{48,40},{56,48},{64,5... | collective-permute-start | bytes 55304 | tf_op jit(solution)/shard_map/ppermute | solution.py:14
  39.8 3.9 %second_core.1 = (f32[8,16,256]{2,1,0:T(8,128)S(1)}, f32[10,16,256]{2,1,0:T(8,128)S(1)}) custom-call(bf16[6,16,32,256]{3,2,1,0:T(8,128)(2,1)S(1)} %get-tuple-element.38.inner, bf16[4,16,32,256]{3,2,1,0:T(8,128)(2,1)S(1)} %get-tuple-element.40.edge, bf16[11,32,256]{2,1,0:T(8,128)(2,1)S(1)} %collective-permute-done.6.f_lo, ...), custom_call_target="tpu_custom_call" | custom-call | tf_op jit(solution)/shard_map/second_core/pallas_call | solution.py:646
  43.8 0.0 collective-permute-done.8.x_lo
  43.8 0.0 collective-permute-done.9.x_hi
  43.8 1.2 %second_rim.1 = (f32[8,16,256]{2,1,0:T(8,128)S(1)}, f32[1,128]{1,0:T(1,128)S(1)}) custom-call(bf16[4,16,32,256]{3,2,1,0:T(8,128)(2,1)S(1)} %get-tuple-element.40.edge, bf16[11,32,256]{2,1,0:T(8,128)(2,1)S(1)} %collective-permute-done.6.f_lo, bf16[11,32,256]{2,1,0:T(8,128)(2,1)S(1)} %collective-permute-done.7.f_hi, f32[8,16,256]{2,1,0:T(8,128)S(1)} %copy-done.1, ...), custom_call_target="tpu_custom_call" | custom-call | tf_op jit(solution)/shard_map/second_rim/pallas_call | solution.py:646
  45.0 15.9 %all_to_all.5 = f32[128,1,128]{2,1,0:T(1,128)S(1)} all-to-all(f32[128,1,128]{2,1,0:T(1,128)S(1)} %broadcast_in_dim.13), channel_id=1, replica_groups=mesh['sx'=16,'sy'=8] {'sx','sy'}, dimensions={0} | all-to-all | bytes 131072 | tf_op jit(solution)/shard_map/all_to_all | solution.py:770
  60.9 0.9 %final.1 = (f32[8,16,256]{2,1,0:T(8,128)}, f32[8,16,256]{2,1,0:T(8,128)}) custom-call(f32[128,128]{1,0:T(8,128)S(1)} %bitcast.4, f32[8,16,256]{2,1,0:T(8,128)S(1)} %copy-done.1, f32[8,16,256]{2,1,0:T(8,128)S(1)} %get-tuple-element.43.first, f32[8,16,256]{2,1,0:T(8,128)S(1)} %get-tuple-element.51.second), custom_call_target="tpu_custom_call" | custom-call | tf_op jit(solution)/shard_map/final/pallas_call | solution.py:646
  (12 shorter events, 0.1 us)
Async XLA Ops:
  0.6 11.6 %copy-start.5 = (f32[32]{0:T(128)S(1)}, f32[32]{0:T(128)}, u32[]{:S(2)}) copy-start(f32[32]{0:T(128)} %param.9) | copy-start | bytes 388
  0.6 11.6 %copy-start.3 = (bf16[27,32,32]{2,1,0:T(8,128)(2,1)S(1)}, bf16[27,32,32]{2,1,0:T(8,128)(2,1)}, u32[]{:S(2)}) copy-start(bf16[27,32,32]{2,1,0:T(8,128)(2,1)} %taps.1) | copy-start | bytes 165892
  0.7 21.5 %copy-start = (bf16[8,16,32,256]{3,2,1,0:T(8,128)(2,1)S(1)}, bf16[8,16,32,256]{3,2,1,0:T(8,128)(2,1)}, u32[]{:S(2)}) copy-start(bf16[8,16,32,256]{3,2,1,0:T(8,128)(2,1)} %own.3) | copy-start | bytes 6291460
  3.2 22.7 %collective-permute-start.2 = (bf16[35,32,256]{2,1,0:T(8,128)(2,1)}, bf16[35,32,256]{2,1,0:T(8,128)(2,1)S(1)}, u32[]{:S(2)}, u32[]{:S(2)}) collective-permute-start(bf16[35,32,256]{2,1,0:T(8,128)(2,1)} %get-tuple-element.34), channel_id=1, source_target_pairs={{0,8},{8,16},{16,24},{24,32},{32,40},{40,48},{48,56},{56,64},{64,7... | collective-permute-start | bytes 1720328 | tf_op jit(solution)/shard_map/ppermute | solution.py:14
  5.3 20.6 %collective-permute-start.3 = (bf16[35,32,256]{2,1,0:T(8,128)(2,1)}, bf16[35,32,256]{2,1,0:T(8,128)(2,1)S(1)}, u32[]{:S(2)}, u32[]{:S(2)}) collective-permute-start(bf16[35,32,256]{2,1,0:T(8,128)(2,1)} %get-tuple-element.35), channel_id=1, source_target_pairs={{0,120},{8,0},{16,8},{24,16},{32,24},{40,32},{48,40},{56,48},{64,5... | collective-permute-start | bytes 1720328 | tf_op jit(solution)/shard_map/ppermute | solution.py:14
  10.1 4.6 %collective-permute-start = (bf16[9,32,256]{2,1,0:T(8,128)(2,1)}, bf16[9,32,256]{2,1,0:T(8,128)(2,1)S(1)}, u32[]{:S(2)}, u32[]{:S(2)}) collective-permute-start(bf16[9,32,256]{2,1,0:T(8,128)(2,1)} %get-tuple-element.27), channel_id=1, source_target_pairs={{0,1},{1,2},{2,3},{3,4},{4,5},{5,6},{6,7},{7,0},{8,9},{9,10},{10,1... | collective-permute-start | bytes 442376 | tf_op jit(solution)/shard_map/ppermute | solution.py:14
  12.2 5.1 %collective-permute-start.1 = (bf16[9,32,256]{2,1,0:T(8,128)(2,1)}, bf16[9,32,256]{2,1,0:T(8,128)(2,1)S(1)}, u32[]{:S(2)}, u32[]{:S(2)}) collective-permute-start(bf16[9,32,256]{2,1,0:T(8,128)(2,1)} %get-tuple-element.28), channel_id=1, source_target_pairs={{0,7},{1,0},{2,1},{3,2},{4,3},{5,4},{6,5},{7,6},{8,15},{9,8},{10,9... | collective-permute-start | bytes 442376 | tf_op jit(solution)/shard_map/ppermute | solution.py:14
  12.2 0.9 %copy-start.4 = (f32[8,16,256]{2,1,0:T(8,128)S(1)}, f32[8,16,256]{2,1,0:T(8,128)}, u32[]{:S(2)}) copy-start(f32[8,16,256]{2,1,0:T(8,128)} %get-tuple-element.29.mask) | copy-start | bytes 393220
  17.3 8.5 %copy-start.1 = (f32[8,16,256]{2,1,0:T(8,128)S(1)}, f32[8,16,256]{2,1,0:T(8,128)}, u32[]{:S(2)}) copy-start(f32[8,16,256]{2,1,0:T(8,128)} %get-tuple-element.39.start) | copy-start | bytes 393220
  17.3 8.6 %copy-start.2 = (f32[8,16,256]{2,1,0:T(8,128)S(1)}, f32[8,16,256]{2,1,0:T(8,128)}, u32[]{:S(2)}) copy-start(f32[8,16,256]{2,1,0:T(8,128)} %ridge.5) | copy-start | bytes 393220
  17.3 8.5 %collective-permute-start.4 = (bf16[5,32,256]{2,1,0:T(8,128)(2,1)S(1)}, bf16[5,32,256]{2,1,0:T(8,128)(2,1)S(1)}, u32[]{:S(2)}, u32[]{:S(2)}) collective-permute-start(bf16[5,32,256]{2,1,0:T(8,128)(2,1)S(1)} %get-tuple-element.36), channel_id=1, source_target_pairs={{0,8},{8,16},{16,24},{24,32},{32,40},{40,48},{48,56},{56,64},{64,7... | collective-permute-start | bytes 245768 | tf_op jit(solution)/shard_map/ppermute | solution.py:14
  17.4 8.4 %collective-permute-start.5 = (bf16[5,32,256]{2,1,0:T(8,128)(2,1)S(1)}, bf16[5,32,256]{2,1,0:T(8,128)(2,1)S(1)}, u32[]{:S(2)}, u32[]{:S(2)}) collective-permute-start(bf16[5,32,256]{2,1,0:T(8,128)(2,1)S(1)} %get-tuple-element.37), channel_id=1, source_target_pairs={{0,120},{8,0},{16,8},{24,16},{32,24},{40,32},{48,40},{56,48},{64,5... | collective-permute-start | bytes 245768 | tf_op jit(solution)/shard_map/ppermute | solution.py:14
  27.9 4.7 %collective-permute-start.6 = (bf16[11,32,256]{2,1,0:T(8,128)(2,1)S(1)}, bf16[11,32,256]{2,1,0:T(8,128)(2,1)S(1)}, u32[]{:S(2)}, u32[]{:S(2)}) collective-permute-start(bf16[11,32,256]{2,1,0:T(8,128)(2,1)S(1)} %get-tuple-element.41), channel_id=1, source_target_pairs={{0,1},{1,2},{2,3},{3,4},{4,5},{5,6},{6,7},{7,0},{8,9},{9,10},{10,1... | collective-permute-start | bytes 540680 | tf_op jit(solution)/shard_map/ppermute | solution.py:14
  29.2 4.9 %collective-permute-start.7 = (bf16[11,32,256]{2,1,0:T(8,128)(2,1)S(1)}, bf16[11,32,256]{2,1,0:T(8,128)(2,1)S(1)}, u32[]{:S(2)}, u32[]{:S(2)}) collective-permute-start(bf16[11,32,256]{2,1,0:T(8,128)(2,1)S(1)} %get-tuple-element.42), channel_id=1, source_target_pairs={{0,7},{1,0},{2,1},{3,2},{4,3},{5,4},{6,5},{7,6},{8,15},{9,8},{10,9... | collective-permute-start | bytes 540680 | tf_op jit(solution)/shard_map/ppermute | solution.py:14
  34.8 8.9 %collective-permute-start.8 = (f32[18,256]{1,0:T(8,128)S(1)}, f32[18,256]{1,0:T(8,128)S(1)}, u32[]{:S(2)}, u32[]{:S(2)}) collective-permute-start(f32[18,256]{1,0:T(8,128)S(1)} %get-tuple-element.44), channel_id=1, source_target_pairs={{0,8},{8,16},{16,24},{24,32},{32,40},{40,48},{48,56},{56,64},{64,7... | collective-permute-start | bytes 55304 | tf_op jit(solution)/shard_map/ppermute | solution.py:14
  34.9 8.9 %collective-permute-start.9 = (f32[18,256]{1,0:T(8,128)S(1)}, f32[18,256]{1,0:T(8,128)S(1)}, u32[]{:S(2)}, u32[]{:S(2)}) collective-permute-start(f32[18,256]{1,0:T(8,128)S(1)} %get-tuple-element.45), channel_id=1, source_target_pairs={{0,120},{8,0},{16,8},{24,16},{32,24},{40,32},{48,40},{56,48},{64,5... | collective-permute-start | bytes 55304 | tf_op jit(solution)/shard_map/ppermute | solution.py:14
